TPU v7x, 512 devices: a whole 4x4x16 slice. The times are simulated.
512 devices in a mesh: seq: 16 (over y, z_hi, core), blk: 32 (over z_lo, x).
Axes of the slice: x: 4, y: 4, z: 16 (z_hi: 2, z_lo: 8; z = z_hi * 8 + z_lo), core: 2. Of those that a mesh axis runs over, the one named last changes fastest.
Arguments:
- hidden_states: bfloat16 [2048, 4096], P('seq'), may hold values from -6 to 6
- query_weight: bfloat16 [4096, 4096], P('seq', 'blk')
- key_weight: bfloat16 [4096, 4096], P('seq', 'blk')
- value_weight: bfloat16 [4096, 4096], P('seq', 'blk'), may hold values from -0.09375 to 0.09375
- output_weight: bfloat16 [4096, 4096], P('blk', 'seq'), may hold values from -0.1875 to 0.1875
- query_gain: float32 [4096], P('blk'), may hold values from 0.7 to 3
- key_gain: float32 [4096], P('blk'), may hold values from 0.7 to 3
- attention_gain: float32 [4096], replicated, may hold values from 0.5 to 1.5
- gate_weight: bfloat16 [4096, 11008], P('seq', 'blk'), may hold values from -0.09375 to 0.09375
- up_weight: bfloat16 [4096, 11008], P('seq', 'blk'), may hold values from -0.09375 to 0.09375
- down_weight: bfloat16 [11008, 4096], P('blk', 'seq'), may hold values from -0.109375 to 0.109375
- feedforward_gain: float32 [4096], replicated, may hold values from 0.5 to 1.5
- cached_keys: bfloat16 [16, 1024, 4096], P('seq', None, 'blk'), may hold values from -6 to 6
- cached_values: bfloat16 [16, 1024, 4096], P('seq', None, 'blk'), may hold values from -6 to 6
- passage_order: int32 [16], replicated, may hold values from 0 to 15, each once
- separators: int32 [8, 2], replicated, may hold values from 1 to 64
- recompute_index: int32 [16, 96], replicated, may hold values from 0 to 1023, as said below
- prompt_lengths: int32 [8], replicated, may hold values from 16 to 64, as said below
Outputs:
- hidden_out: bfloat16 [2048, 4096], P(('seq', 'blk'))
- blended_keys: bfloat16 [16, 1024, 4096], P('seq', None, 'blk')
- blended_values: bfloat16 [16, 1024, 4096], P('seq', None, 'blk')
Inputs may be any that keep to these rules, and one draw needn't show every extreme that they name: `passage_order`: each passage id appears once. `recompute_index`: distinct within each passage. `prompt_lengths`: some request has all 64 of its new tokens live.
All inputs are finite; a program needn't handle non-finite values.
Results may differ from a plain program's by a relative error of at most 0.035.
Values may be sent and summed in bfloat16 or wider, within the bound.
No kernel may reach another device: no remote copies, remote signals or barrier semaphores. Data moves between devices by JAX's collectives and lax.ppermute only.
A program may use at most 64 MiB of HBM per device.

v0:
```python
import math

import jax
import jax.numpy as jnp
from jax import lax
from jax.sharding import PartitionSpec as P

HD = 128
PLEN = 1024
SEL = 96
PPR = 2
TOKN_DEV = 32


EPSILON = 1e-06
ROPE_THETA = 500000.0
MASKED_SCORE = -1e30


def joined(part, axis, combine):
    gathered = jax.tree.map(lambda a: lax.all_gather(a, axis), part)

    def take(source):
        return jax.tree.map(lambda a: lax.dynamic_index_in_dim(a, source, 0, False), gathered)

    return lax.fori_loop(
        1, lax.axis_size(axis), lambda source, state: combine(state, take(source)), take(0)
    )


def frequencies():
    indices = jnp.arange(HD // 2, dtype=jnp.float32)
    return jnp.exp(indices * (-2.0 * math.log(ROPE_THETA) / HD))


def rotate(values, angles):
    half_width = values.shape[-1] // 2
    cosine = jnp.cos(angles)[:, None, :]
    sine = jnp.sin(angles)[:, None, :]
    first = values[..., :half_width]
    second = values[..., half_width:]
    return jnp.concatenate(
        [first * cosine - second * sine, second * cosine + first * sine], axis=-1
    )


def normalize(matrix):
    return matrix * lax.rsqrt(jnp.mean(matrix * matrix, axis=-1, keepdims=True) + EPSILON)


def layout(passage_order, separators, recompute_index, prompt_lengths, seq_count):
    request_count = seq_count // PPR
    ordering = passage_order.reshape(request_count, PPR)
    slot_ids = jnp.arange(PPR, dtype=jnp.int32)
    opening = slot_ids[None, :] * PLEN + jnp.cumsum(separators, axis=1)
    flattened = ordering.reshape(-1)
    starts = jnp.zeros((seq_count,), jnp.int32).at[flattened].set(opening.reshape(-1))
    request_ids = jnp.repeat(jnp.arange(request_count, dtype=jnp.int32), PPR)
    owners = jnp.zeros((seq_count,), jnp.int32).at[flattened].set(request_ids)
    prompt_start = opening[:, PPR - 1] + PLEN
    devices = jnp.arange(seq_count, dtype=jnp.int32)
    new_request = devices // PPR
    new_index = (devices % PPR)[:, None] * TOKN_DEV + jnp.arange(TOKN_DEV, dtype=jnp.int32)[None, :]
    new_positions = prompt_start[new_request][:, None] + new_index
    new_live = new_index < prompt_lengths[new_request][:, None]
    picked_positions = starts[:, None] + recompute_index
    row_positions = jnp.concatenate([picked_positions, new_positions], axis=1).reshape(-1)
    row_live = jnp.concatenate([jnp.ones(picked_positions.shape, bool), new_live], axis=1).reshape(
        -1
    )
    return (starts, owners, row_positions, row_live)


def partial_attention(queries, key_block, value_block, visible, head_count):
    query_count = queries.shape[0]
    key_count = key_block.shape[0]
    query_heads = queries.reshape(query_count, head_count, HD)
    key_heads = key_block.reshape(key_count, head_count, HD)
    value_heads = value_block.reshape(key_count, head_count, HD)
    scores = jnp.einsum(
        "qhd,khd->hqk", query_heads, key_heads, preferred_element_type=jnp.float32
    ) * HD ** (-0.5)
    masked = jnp.where(visible[None], scores, MASKED_SCORE)
    peaks = jnp.max(masked, axis=2)
    exponentials = jnp.where(visible[None], jnp.exp(masked - peaks[:, :, None]), 0.0)
    totals = jnp.sum(exponentials, axis=2)
    weighted = jnp.einsum(
        "hqk,khd->qhd",
        exponentials.astype(jnp.bfloat16),
        value_heads,
        preferred_element_type=jnp.float32,
    )
    return (weighted, peaks.T, totals.T)


def spread(parts, indices, total_rows):
    weighted, peaks, totals = parts
    head_count = peaks.shape[1]
    full_weighted = jnp.zeros((total_rows, head_count, HD), jnp.float32).at[indices].set(weighted)
    full_peaks = (
        jnp.full((total_rows, head_count), MASKED_SCORE, jnp.float32).at[indices].set(peaks)
    )
    full_totals = jnp.zeros((total_rows, head_count), jnp.float32).at[indices].set(totals)
    return (full_weighted, full_peaks, full_totals)


def combine(first, second):
    peaks = jnp.maximum(first[1], second[1])
    first_factor = jnp.exp(first[1] - peaks)
    second_factor = jnp.exp(second[1] - peaks)
    weighted = first[0] * first_factor[:, :, None] + second[0] * second_factor[:, :, None]
    return (weighted, peaks, first[2] * first_factor + second[2] * second_factor)


def shards(
    hidden_states,
    query_weight,
    key_weight,
    value_weight,
    output_weight,
    query_gain,
    key_gain,
    attention_gain,
    gate_weight,
    up_weight,
    down_weight,
    feedforward_gain,
    cached_keys,
    cached_values,
    passage_order,
    separators,
    recompute_index,
    prompt_lengths,
):
    seq_count = lax.axis_size("seq")
    blk_count = lax.axis_size("blk")
    seq_index = lax.axis_index("seq")
    blk_index = lax.axis_index("blk")
    row_count = hidden_states.shape[0]
    local_width = query_weight.shape[1]
    head_count = local_width // HD
    total_rows = row_count * seq_count
    part_rows = row_count // blk_count
    starts, owners, row_positions, row_live = layout(
        passage_order, separators, recompute_index, prompt_lengths, seq_count
    )
    frequency = frequencies()
    pieces = (
        lax.all_gather(query_weight, "seq", axis=0, tiled=True),
        lax.all_gather(key_weight, "seq", axis=0, tiled=True),
        lax.all_gather(value_weight, "seq", axis=0, tiled=True),
    )
    query_raw = jnp.dot(hidden_states, pieces[0], preferred_element_type=jnp.float32)
    key_raw = jnp.dot(hidden_states, pieces[1], preferred_element_type=jnp.float32)
    value_raw = jnp.dot(hidden_states, pieces[2], preferred_element_type=jnp.float32)
    query_squares, key_squares = lax.psum(
        (jnp.sum(query_raw * query_raw, axis=1), jnp.sum(key_raw * key_raw, axis=1)), "blk"
    )
    full_width = local_width * blk_count
    my_positions = lax.dynamic_slice_in_dim(row_positions, seq_index * row_count, row_count)
    my_live = lax.dynamic_slice_in_dim(row_live, seq_index * row_count, row_count)
    angles = my_positions.astype(jnp.float32)[:, None] * frequency[None, :]
    query_scaled = query_raw * lax.rsqrt(query_squares / full_width + EPSILON)[:, None] * query_gain
    key_scaled = key_raw * lax.rsqrt(key_squares / full_width + EPSILON)[:, None] * key_gain
    query = (
        rotate(query_scaled.reshape(row_count, head_count, HD), angles)
        .reshape(row_count, local_width)
        .astype(jnp.bfloat16)
    )
    key_rows = (
        rotate(key_scaled.reshape(row_count, head_count, HD), angles)
        .reshape(row_count, local_width)
        .astype(jnp.bfloat16)
    )
    value_rows = value_raw.astype(jnp.bfloat16)
    passage_start = lax.dynamic_index_in_dim(starts, seq_index, 0, keepdims=False)
    turned = jnp.broadcast_to(passage_start.astype(jnp.float32) * frequency, (PLEN, HD // 2))
    old_keys = cached_keys[0].astype(jnp.float32).reshape(PLEN, head_count, HD)
    picked = lax.dynamic_index_in_dim(recompute_index, seq_index, 0, keepdims=False)
    passage_keys = (
        rotate(old_keys, turned)
        .reshape(PLEN, local_width)
        .astype(jnp.bfloat16)
        .at[picked]
        .set(key_rows[:SEL])
    )
    passage_values = cached_values[0].at[picked].set(value_rows[:SEL])
    all_queries = lax.all_gather(query, "seq", axis=0, tiled=True)
    request = lax.dynamic_index_in_dim(owners, seq_index, 0, keepdims=False)
    ordering = passage_order.reshape(-1, PPR)
    retrieved = lax.dynamic_index_in_dim(ordering, request, 0, keepdims=False)
    slot_ids = jnp.arange(PPR, dtype=jnp.int32)
    new_offsets = SEL + jnp.arange(TOKN_DEV, dtype=jnp.int32)
    picked_offsets = jnp.arange(SEL, dtype=jnp.int32)
    chosen_rows = (retrieved[:, None] * row_count + picked_offsets[None, :]).reshape(-1)
    group_rows = ((request * PPR + slot_ids)[:, None] * row_count + new_offsets[None, :]).reshape(
        -1
    )
    rows_first = jnp.concatenate([chosen_rows, group_rows])
    passage_positions = passage_start + jnp.arange(PLEN, dtype=jnp.int32)
    first_visible = passage_positions[None, :] <= row_positions[rows_first][:, None]
    first_parts = partial_attention(
        all_queries[rows_first], passage_keys, passage_values, first_visible, head_count
    )
    own_request = seq_index // PPR
    rows_second = (
        (own_request * PPR + slot_ids)[:, None] * row_count + new_offsets[None, :]
    ).reshape(-1)
    second_visible = (my_positions[SEL:][None, :] <= row_positions[rows_second][:, None]) & my_live[
        SEL:
    ][None, :]
    second_parts = partial_attention(
        all_queries[rows_second], key_rows[SEL:], value_rows[SEL:], second_visible, head_count
    )
    local_parts = combine(
        spread(first_parts, rows_first, total_rows), spread(second_parts, rows_second, total_rows)
    )
    merged = joined(local_parts, "seq", combine)
    weighted = lax.dynamic_slice_in_dim(merged[0], seq_index * row_count, row_count, 0)
    totals = lax.dynamic_slice_in_dim(merged[2], seq_index * row_count, row_count, 0)
    attention = (weighted / totals[:, :, None]).reshape(row_count, local_width).astype(jnp.bfloat16)
    gate_full, up_full, down_full = (
        lax.all_gather(gate_weight, "seq", axis=0, tiled=True),
        lax.all_gather(up_weight, "seq", axis=0, tiled=True),
        lax.all_gather(down_weight, "seq", axis=1, tiled=True),
    )
    output_full = lax.all_gather(output_weight, "seq", axis=1, tiled=True)
    summed = lax.psum_scatter(
        jnp.dot(attention, output_full, preferred_element_type=jnp.float32).astype(jnp.bfloat16),
        "blk",
        scatter_dimension=0,
        tiled=True,
    ).astype(jnp.float32)
    input_rows = lax.dynamic_slice_in_dim(hidden_states, blk_index * part_rows, part_rows, 0)
    mixed_rows = (input_rows.astype(jnp.float32) + normalize(summed) * attention_gain).astype(
        jnp.bfloat16
    )
    pieces = lax.all_gather(mixed_rows, "blk", axis=0, tiled=True)
    gate_values = jnp.dot(pieces, gate_full, preferred_element_type=jnp.float32)
    up_values = jnp.dot(pieces, up_full, preferred_element_type=jnp.float32)
    activation = (jax.nn.silu(gate_values) * up_values).astype(jnp.bfloat16)
    feedforward = lax.psum_scatter(
        jnp.dot(activation, down_full, preferred_element_type=jnp.float32).astype(jnp.bfloat16),
        "blk",
        scatter_dimension=0,
        tiled=True,
    ).astype(jnp.float32)
    hidden_out = (
        mixed_rows.astype(jnp.float32) + normalize(feedforward) * feedforward_gain
    ).astype(jnp.bfloat16)
    return (hidden_out, passage_keys[None], passage_values[None])


def solution(mesh):
    return jax.shard_map(
        shards,
        mesh=mesh,
        in_specs=(
            P("seq", None),
            P("seq", "blk"),
            P("seq", "blk"),
            P("seq", "blk"),
            P("blk", "seq"),
            P("blk"),
            P("blk"),
            P(),
            P("seq", "blk"),
            P("seq", "blk"),
            P("blk", "seq"),
            P(),
            P("seq", None, "blk"),
            P("seq", None, "blk"),
            P(),
            P(),
            P(),
            P(),
        ),
        out_specs=(P(("seq", "blk"), None), P("seq", None, "blk"), P("seq", None, "blk")),
        check_vma=False,
    )
```

profile of v0, /device:TPU:8, one launch (start us, length us, event | category | flops | bytes accessed | tf_op | source)
XLA Modules:
  0.0 2227.4 jit_solution(16655705783078409144)
XLA Ops:
  26.4 66.8 %all-gather.17.cloned.1.call-done = bf16[4096,128]{1,0:T(8,128)(2,1)} async-done(((bf16[256,128]{1,0:T(8,128)(2,1)}), bf16[4096,128]{1,0:T(8,128)(2,1)}) %all-gather.17.cloned.1.call-update) | async-done | bytes 1048592 | tf_op jit(solution)/shard_map/all_gather | solution.py:149
  95.0 70.1 %all-gather.19.cloned.1.call-done = bf16[4096,128]{1,0:T(8,128)(2,1)} async-done(((bf16[256,128]{1,0:T(8,128)(2,1)}), bf16[4096,128]{1,0:T(8,128)(2,1)}) %all-gather.19.cloned.1.call-update) | async-done | bytes 1048592 | tf_op jit(solution)/shard_map/all_gather | solution.py:150
  166.9 117.8 %all-reduce.3 = (f32[128]{0:T(128)S(1)}, f32[128]{0:T(128)S(1)}) all-reduce(f32[128]{0:T(128)S(1)} %get-tuple-element.239, f32[128]{0:T(128)S(1)} %get-tuple-element.241), channel_id=1, replica_groups=mesh['seq'=16,'blk'=32] {'blk'}, use_global_device_ids=true, to_apply=%region_5.6 | all-reduce | flops 256 | bytes 2048 | tf_op jit(solution)/shard_map/psum | solution.py:156
  285.1 47.5 %all-gather = bf16[2048,1,128]{0,2,1:T(8,128)(2,1)S(1)} all-gather(bf16[128,1,128]{0,2,1:T(8,128)(2,1)S(1)} %pad_maximum_fusion.1), channel_id=2, replica_groups=mesh['seq'=16,'blk'=32] {'seq'}, dimensions={0}, use_global_device_ids=true | all-gather | bytes 557056 | tf_op jit(solution)/shard_map/all_gather | solution.py:188
  349.5 38.7 %all-gather.2 = f32[32768,1]{0,1:T(1,128)S(1)} all-gather(f32[2048,1]{0,1:T(1,128)S(1)} %get-tuple-element.226), channel_id=4, replica_groups=mesh['seq'=16,'blk'=32] {'seq'}, dimensions={0}, use_global_device_ids=true | all-gather | bytes 139264 | tf_op jit(solution)/shard_map/all_gather | solution.py:21
  388.2 52.1 %all-gather.3 = f32[32768,1]{0,1:T(1,128)S(1)} all-gather(f32[2048,1]{0,1:T(1,128)S(1)} %get-tuple-element.223), channel_id=5, replica_groups=mesh['seq'=16,'blk'=32] {'seq'}, dimensions={0}, use_global_device_ids=true | all-gather | bytes 139264 | tf_op jit(solution)/shard_map/all_gather | solution.py:21
  440.3 190.9 %all-gather.29.cloned.1.call-done = f32[32768,1,128]{2,0,1:T(8,128)} async-done(((f32[2048,1,128]{2,0,1:T(8,128)}), f32[32768,1,128]{2,0,1:T(8,128)}) %all-gather.29.cloned.1.call-update) | async-done | bytes 16777232 | tf_op jit(solution)/shard_map/all_gather | solution.py:21
  632.5 156.0 %while.19 = (s32[]{:T(128)}, f32[2048,1,128]{2,1,0:T(1,128)S(1)}, f32[2048,1]{0,1:T(1,128)S(1)}, f32[2048,1]{0,1:T(1,128)S(1)}, f32[16,2048,1]{1,2,0:T(1,128)S(1...) while((s32[]{:T(128)}, f32[2048,1,128]{2,1,0:T(1,128)S(1)}, ...), condition=%wide.region_20.21_spmd, body=%wide.region_19.20_spmd.sunk | while | flops 798725 | bytes 5324951 | solution.py:26
  633.8 9.0 multiply_add_fusion.3
  644.2 9.0 multiply_add_fusion.3
  654.6 9.0 multiply_add_fusion.3
  665.0 9.0 multiply_add_fusion.3
  675.4 9.0 multiply_add_fusion.3
  685.8 9.0 multiply_add_fusion.3
  696.2 9.0 multiply_add_fusion.3
  706.6 9.0 multiply_add_fusion.3
  717.0 9.0 multiply_add_fusion.3
  727.4 9.0 multiply_add_fusion.3
  737.8 9.0 multiply_add_fusion.3
  748.2 9.0 multiply_add_fusion.3
  758.6 9.0 multiply_add_fusion.3
  769.0 9.0 multiply_add_fusion.3
  779.4 9.0 multiply_add_fusion.3
  788.5 2.7 convolution_convert_fusion.1
  793.2 456.0 %all-reduce.7.cloned.1.call-done = bf16[128,4096]{1,0:T(8,128)(2,1)} async-done(((bf16[128,4096]{1,0:T(8,128)(2,1)}), bf16[128,4096]{1,0:T(8,128)(2,1)}) %all-reduce.7.cloned.1.call-update) | async-done | bytes 1048592
  1253.9 218.1 %all-gather.31.cloned.1.call-done = bf16[32,4,4096]{2,1,0:T(4,128)(2,1)} async-done(((bf16[1,4,4096]{2,1,0:T(4,128)(2,1)}), bf16[32,4,4096]{2,1,0:T(4,128)(2,1)}) %all-gather.31.cloned.1.call-update) | async-done | bytes 1048592 | tf_op jit(solution)/shard_map/all_gather | solution.py:238
  1473.4 100.8 %all-gather.23.cloned.1.call-done = bf16[4096,344]{0,1:T(8,128)(2,1)} async-done(((bf16[256,344]{0,1:T(8,128)(2,1)}), bf16[4096,344]{0,1:T(8,128)(2,1)}) %all-gather.23.cloned.1.call-update) | async-done | bytes 2818064 | tf_op jit(solution)/shard_map/all_gather | solution.py:223
  1574.1 2.8 fusion.93
  1576.9 92.7 %all-gather.25.cloned.1.call-done = bf16[4096,344]{0,1:T(8,128)(2,1)} async-done(((bf16[256,344]{0,1:T(8,128)(2,1)}), bf16[4096,344]{0,1:T(8,128)(2,1)}) %all-gather.25.cloned.1.call-update) | async-done | bytes 2818064 | tf_op jit(solution)/shard_map/all_gather | solution.py:224
  1669.7 95.4 %all-gather.27.cloned.1.call-done = bf16[344,4096]{1,0:T(8,128)(2,1)} async-done(((bf16[344,256]{1,0:T(8,128)(2,1)}), bf16[344,4096]{1,0:T(8,128)(2,1)}) %all-gather.27.cloned.1.call-update) | async-done | bytes 2818064 | tf_op jit(solution)/shard_map/all_gather | solution.py:225
  1765.0 6.3 convolution_convert_fusion
  1771.4 446.9 %all-reduce.9.cloned.1.call-done = bf16[128,4096]{1,0:T(8,128)(2,1)} async-done(((bf16[128,4096]{1,0:T(8,128)(2,1)}), bf16[128,4096]{1,0:T(8,128)(2,1)}) %all-reduce.9.cloned.1.call-update) | async-done | bytes 1048592
  (166 shorter events, 67.8 us)
Async XLA Ops:
  7.2 17.8 copy-start
  7.2 86.0 %all-gather.17.cloned.1.call-start = ((), (), s32[]{:S(2)}) async-start(), calls=%async_computation.1 | async-start | bytes 1114112 | tf_op jit(solution)/shard_map/all_gather | solution.py:149
  7.9 157.2 %all-gather.19.cloned.1.call-start = ((), (), s32[]{:S(2)}) async-start(), calls=%async_computation.2 | async-start | bytes 1114112 | tf_op jit(solution)/shard_map/all_gather | solution.py:150
  8.7 332.5 %all-gather.15.cloned.1.call-start = ((), (), s32[]{:S(2)}) async-start(), calls=%async_computation | async-start | bytes 1114112 | tf_op jit(solution)/shard_map/all_gather | solution.py:151
  9.4 621.8 %all-gather.29.cloned.1.call-start = ((), (), s32[]{:S(2)}) async-start(), calls=%async_computation.7 | async-start | bytes 17825792 | tf_op jit(solution)/shard_map/all_gather | solution.py:21
  16.0 77.3 %copy-start.1 = (bf16[128,4096]{1,0:T(8,128)(2,1)S(1)}, bf16[128,4096]{1,0:T(8,128)(2,1)}, u32[]{:S(2)}) copy-start(bf16[128,4096]{1,0:T(8,128)(2,1)} %param.20) | copy-start | bytes 3145732
  26.2 258.5 %copy-start.8 = (f32[128]{0:T(128)S(1)}, f32[128]{0:T(128)}, u32[]{:S(2)}) copy-start(f32[128]{0:T(128)} %param.25) | copy-start | bytes 1540
  26.2 258.6 %copy-start.9 = (f32[128]{0:T(128)S(1)}, f32[128]{0:T(128)}, u32[]{:S(2)}) copy-start(f32[128]{0:T(128)} %param.26) | copy-start | bytes 1540
  333.8 9.3 copy-start.5
  335.5 9.0 copy-start.2
  344.1 0.7 copy-start.4
  348.9 439.6 %all-gather.21.cloned.1.call-start = ((), (), s32[]{:S(2)}) async-start(), calls=%async_computation.3 | async-start | bytes 1114112 | tf_op jit(solution)/shard_map/all_gather | solution.py:227
  349.5 899.7 %all-reduce.7.cloned.1.call-start = ((), (), s32[]{:S(2)}) async-start(), calls=%async_computation.9 | async-start | bytes 2097152
  788.5 461.7 %copy-start.6 = (f32[4096]{0:T(1024)S(1)}, f32[4096]{0:T(1024)}, u32[]{:S(2)}) copy-start(f32[4096]{0:T(1024)} %param.27) | copy-start | bytes 49156
  791.3 680.8 %all-gather.31.cloned.1.call-start = ((), (), s32[]{:S(2)}) async-start(), calls=%async_computation.8 | async-start | bytes 1081344 | tf_op jit(solution)/shard_map/all_gather | solution.py:238
  1251.8 322.3 %all-gather.23.cloned.1.call-start = ((), (), s32[]{:S(2)}) async-start(), calls=%async_computation.4 | async-start | bytes 2994176 | tf_op jit(solution)/shard_map/all_gather | solution.py:223
  1252.5 417.1 %all-gather.25.cloned.1.call-start = ((), (), s32[]{:S(2)}) async-start(), calls=%async_computation.5 | async-start | bytes 2994176 | tf_op jit(solution)/shard_map/all_gather | solution.py:224
  1253.3 511.8 %all-gather.27.cloned.1.call-start = ((), (), s32[]{:S(2)}) async-start(), calls=%async_computation.6 | async-start | bytes 2994176 | tf_op jit(solution)/shard_map/all_gather | solution.py:225
  1253.9 964.4 %all-reduce.9.cloned.1.call-start = ((), (), s32[]{:S(2)}) async-start(), calls=%async_computation.10 | async-start | bytes 2097152
  1576.9 642.3 %copy-start.3 = (bf16[4,4096]{1,0:T(4,128)(2,1)S(1)}, bf16[4,4096]{1,0:T(4,128)(2,1)}, u32[]{:S(2)}) copy-start(bf16[4,4096]{1,0:T(4,128)(2,1)} %fusion.26) | copy-start | bytes 98308
  1576.9 642.3 %copy-start.7 = (f32[4096]{0:T(1024)S(1)}, f32[4096]{0:T(1024)}, u32[]{:S(2)}) copy-start(f32[4096]{0:T(1024)} %param.31) | copy-start | bytes 49156
Sparse Core Ops, SparseCore 0:
  11.3 81.8 all-gather.16
  96.5 68.5 all-gather.18
  168.4 68.6 all-gather.14
  349.0 282.1 all-gather.28
  634.1 79.2 all-gather.20
  791.4 457.7 all-reduce.6
  1252.1 219.9 all-gather.30
  1475.6 98.4 all-gather.22
  1577.7 91.8 all-gather.24
  1673.1 91.8 all-gather.26
  1771.5 446.7 all-reduce.8
where the time goes:
time: 2230 us
  waiting for transfers between devices  1740 us (78%)
  blocking collectives  256 us (11%)
  other arithmetic  149 us (7%)
  local copies, waits for them, and re-layouts  42.2 us (2%)
    unnamed x13, waiting for transfers between devices  907 us
    all_gather x1, waiting for transfers between devices, shards(): pieces = lax.all_gather(mixed_rows, 'blk', axis=0, tiled=True)  218 us
    all_gather x1, waiting for transfers between devices, joined(): gathered = jax.tree.map(lambda a: lax.all_gather(a, axis), part)  191 us
    add x16, other arithmetic, combine(): first[0] * first_factor[:, :, None] + second[0] * second_factor[:, :, None]  137 us
    psum x1, blocking collectives, shards(): lax.psum((jnp.sum(query_raw * query_raw, axis=1), jnp.sum(key_raw * key_r...  118 us
    all_gather x1, waiting for transfers between devices, shards(): lax.all_gather(gate_weight, 'seq', axis=0, tiled=True)  101 us
    all_gather x1, waiting for transfers between devices, shards(): lax.all_gather(down_weight, 'seq', axis=1, tiled=True)  95.4 us
    all_gather x1, waiting for transfers between devices, shards(): lax.all_gather(up_weight, 'seq', axis=0, tiled=True)  92.7 us
  transfers between devices with their start and end apart: 11, of which 9 were waited for; matrix products, arithmetic and copies ran while one was open for 8% of the time, Pallas kernels for 0%

commit v1 on v0

v1 whole, which is shorter than its diff:
```python
import math

import jax
import jax.numpy as jnp
from jax import lax
from jax.sharding import Mesh, PartitionSpec as P

HD = 128
PLEN = 1024
SEL = 96
PPR = 2
TOKN_DEV = 32
ROW_DEV = 128

EPSILON = 1e-06
ROPE_THETA = 500000.0
MASKED = -1e30

SEQ = ("y", "zh", "core")
BLK = ("zl", "x")
NY, NZH, NCORE, NZL, NX = 4, 2, 2, 8, 4
N_SEQ = NY * NZH * NCORE
bf16 = jnp.bfloat16
f32 = jnp.float32


def frequencies():
    indices = jnp.arange(HD // 2, dtype=f32)
    return jnp.exp(indices * (-2.0 * math.log(ROPE_THETA) / HD))


def rotate(values, cosine, sine):
    first = values[:, : HD // 2]
    second = values[:, HD // 2 :]
    return jnp.concatenate(
        [first * cosine - second * sine, second * cosine + first * sine], axis=-1
    )


def copies_to_all(a, axis, count):
    return lax.all_to_all(
        jnp.broadcast_to(a[None], (count,) + a.shape), axis, 0, 0, tiled=True
    )


def gather_seq(a):
    a = copies_to_all(a, "zh", NZH)
    a = copies_to_all(a, "y", NY)
    a = copies_to_all(a, "core", NCORE)
    return a.reshape((N_SEQ,) + a.shape[3:])


def seq_slot(s):
    return (s % 2) * 8 + (s // 4) * 2 + (s // 2) % 2


def swap(a, axis, count):
    return lax.ppermute(a, axis, [(i, i ^ 1) for i in range(count)])


def layout(passage_order, separators, recompute_index, prompt_lengths):
    requests = N_SEQ // PPR
    slot_ids = jnp.arange(PPR, dtype=jnp.int32)
    opening = slot_ids[None, :] * PLEN + jnp.cumsum(separators, axis=1)
    flat = passage_order.reshape(-1)
    hit = flat[None, :] == jnp.arange(N_SEQ, dtype=jnp.int32)[:, None]
    starts = jnp.sum(jnp.where(hit, opening.reshape(-1)[None, :], 0), axis=1)
    place = jnp.sum(jnp.where(hit, jnp.arange(N_SEQ, dtype=jnp.int32)[None, :], 0), axis=1)
    owners = place // PPR
    prompt_start = opening[:, PPR - 1] + PLEN
    new_index = jnp.arange(PPR * TOKN_DEV, dtype=jnp.int32)
    new_positions = (prompt_start[:, None] + new_index[None, :]).reshape(N_SEQ, TOKN_DEV)
    new_live = (new_index[None, :] < prompt_lengths[:, None]).reshape(N_SEQ, TOKN_DEV)
    picked = starts[:, None] + recompute_index
    positions = jnp.concatenate([picked, new_positions], axis=1)
    return starts, owners, positions, new_live


def partial_attention(queries, keys, values, visible):
    scores = lax.dot_general(
        queries, keys, (((1,), (1,)), ((), ())), preferred_element_type=f32
    ) * HD ** (-0.5)
    scores = jnp.where(visible, scores, MASKED)
    peak = jnp.max(scores, axis=1, keepdims=True)
    weights = jnp.where(visible, jnp.exp(scores - peak), 0.0)
    total = jnp.sum(weights, axis=1, keepdims=True)
    some = total > 0.0
    safe = jnp.where(some, total, 1.0)
    out = jnp.dot(weights.astype(bf16), values, preferred_element_type=f32) / safe
    return out, jnp.where(some, peak + jnp.log(safe), MASKED)


def merge(parts):
    top = parts[0][1]
    for _, level in parts[1:]:
        top = jnp.maximum(top, level)
    num = 0.0
    den = 0.0
    for out, level in parts:
        w = jnp.exp(level - top)
        num = num + w * out
        den = den + w
    return num / den


def pack(out, level):
    high = lax.reduce_precision(level, 8, 7)
    rest = level - high
    mid = lax.reduce_precision(rest, 8, 7)
    low = rest - mid
    tail = jnp.zeros((out.shape[0], HD - 3), f32)
    return jnp.concatenate([out, high, mid, low, tail], axis=1).astype(bf16)


def unpack(block):
    block = block.astype(f32)
    level = block[:, HD : HD + 1] + block[:, HD + 1 : HD + 2] + block[:, HD + 2 : HD + 3]
    return block[:, :HD], level


def shards(
    hidden_states,
    query_weight,
    key_weight,
    value_weight,
    output_weight,
    query_gain,
    key_gain,
    attention_gain,
    gate_weight,
    up_weight,
    down_weight,
    feedforward_gain,
    cached_keys,
    cached_values,
    passage_order,
    separators,
    recompute_index,
    prompt_lengths,
):
    zh = lax.axis_index("zh")
    core = lax.axis_index("core")
    zl = lax.axis_index("zl")
    x_at = lax.axis_index("x")
    seq = lax.axis_index("y") * 4 + zh * 2 + core
    width = query_weight.shape[1]
    hidden_units = gate_weight.shape[1]
    model = hidden_states.shape[1]
    depth = query_weight.shape[0]

    out_all = lax.all_gather(output_weight.T, SEQ, axis=0, tiled=True)
    pad = (-hidden_units) % 128
    ff_mine = jnp.concatenate(
        [jnp.pad(down_weight.T, ((0, 0), (0, pad))), gate_weight, up_weight], axis=1
    )
    ff_all = lax.all_gather(ff_mine, SEQ, axis=0, tiled=True)
    up_from = hidden_units + pad

    mine = jnp.concatenate([query_weight, key_weight, value_weight], axis=1)
    theirs = swap(mine, "zh", NZH)
    near = copies_to_all(mine, "y", NY)
    near_other = swap(near, "core", NCORE)
    far = copies_to_all(theirs, "y", NY)
    far_other = swap(far, "core", NCORE)

    columns = hidden_states.reshape(ROW_DEV, NY, NZH, NCORE, depth)

    def block(i, j):
        return columns[:, :, i, j].reshape(ROW_DEV, NY * depth)

    by_zh = [
        [jnp.where(zh == 0, block(i, j), block(1 - i, j)) for j in range(2)] for i in range(2)
    ]
    picked_x = [
        [jnp.where(core == 0, by_zh[i][j], by_zh[i][1 - j]) for j in range(2)] for i in range(2)
    ]

    def product(x, w):
        return jnp.dot(x, w.reshape(NY * depth, 3 * width), preferred_element_type=f32)

    raw = product(picked_x[0][0], near) + product(picked_x[0][1], near_other)
    raw = raw + product(picked_x[1][0], far) + product(picked_x[1][1], far_other)
    query_raw, key_raw, value_raw = (raw[:, i * width : (i + 1) * width] for i in range(3))

    starts, owners, positions, new_live = layout(
        passage_order, separators, recompute_index, prompt_lengths
    )
    frequency = frequencies()
    my_positions = lax.dynamic_index_in_dim(positions, seq, 0, False)
    angles = my_positions.astype(f32)[:, None] * frequency[None, :]
    cosine, sine = jnp.cos(angles), jnp.sin(angles)
    start = lax.dynamic_index_in_dim(starts, seq, 0, False)
    turn = (start.astype(f32) * frequency)[None, :]
    moved = rotate(cached_keys[0].astype(f32), jnp.cos(turn), jnp.sin(turn)).astype(bf16)

    squares = jnp.stack(
        [jnp.sum(query_raw * query_raw, axis=1), jnp.sum(key_raw * key_raw, axis=1)]
    )
    squares = lax.all_to_all(
        jnp.broadcast_to(squares[None], (NZL * NX,) + squares.shape), BLK, 0, 0, tiled=True
    )
    squares = jnp.sum(squares, axis=0)
    scale = lax.rsqrt(squares / model + EPSILON)
    query = rotate(query_raw * scale[0][:, None] * query_gain, cosine, sine).astype(bf16)
    key = rotate(key_raw * scale[1][:, None] * key_gain, cosine, sine).astype(bf16)
    value = value_raw.astype(bf16)

    picked = lax.dynamic_index_in_dim(recompute_index, seq, 0, False)
    passage_keys = moved.at[picked].set(key[:SEL], unique_indices=True)
    passage_values = cached_values[0].at[picked].set(value[:SEL], unique_indices=True)

    request = lax.dynamic_index_in_dim(owners, seq, 0, False)
    order = passage_order.reshape(-1, PPR)
    chosen = lax.dynamic_index_in_dim(order, request, 0, False)
    all_queries = gather_seq(query)

    def rows_of(table, s):
        return lax.dynamic_index_in_dim(table, s, 0, False)

    sources = [chosen[0], chosen[1], request * 2, request * 2 + 1]
    cuts = [slice(0, SEL), slice(0, SEL), slice(SEL, None), slice(SEL, None)]
    wanted = jnp.concatenate(
        [rows_of(all_queries, seq_slot(s))[c] for s, c in zip(sources, cuts)]
    )
    wanted_at = jnp.concatenate([rows_of(positions, s)[c] for s, c in zip(sources, cuts)])
    key_at = start + jnp.arange(PLEN, dtype=jnp.int32)
    part, level = partial_attention(
        wanted, passage_keys, passage_values, key_at[None, :] <= wanted_at[:, None]
    )

    new_mine = jnp.concatenate([key[SEL:], value[SEL:]])
    new_other = swap(new_mine, "core", NCORE)
    new_keys = jnp.concatenate([key[SEL:], new_other[:TOKN_DEV]])
    new_values = jnp.concatenate([value[SEL:], new_other[TOKN_DEV:]])
    partner = seq + 1 - 2 * core
    new_at = jnp.concatenate([my_positions[SEL:], rows_of(positions, partner)[SEL:]])
    live = jnp.concatenate([rows_of(new_live, seq), rows_of(new_live, partner)])
    new_part = partial_attention(
        query[SEL:],
        new_keys,
        new_values,
        (new_at[None, :] <= my_positions[SEL:][:, None]) & live[None, :],
    )

    returned = gather_seq(pack(part[SEL:], level[SEL:]))
    first = chosen[0] == seq
    own = (
        jnp.where(first, part[:SEL], part[SEL : 2 * SEL]),
        jnp.where(first, level[:SEL], level[SEL : 2 * SEL]),
    )
    remote, remote_level = unpack(rows_of(returned, seq_slot(chosen[0]))[:SEL])
    old_rows = merge([own, (remote, jnp.where(first, MASKED, remote_level))])
    my_order = rows_of(order, seq // 2)
    parts = [new_part]
    for i in range(PPR):
        theirs_back = rows_of(returned, seq_slot(my_order[i]))
        parts.append(
            unpack(
                jnp.where(
                    core == 0,
                    theirs_back[SEL : SEL + TOKN_DEV],
                    theirs_back[SEL + TOKN_DEV : SEL + 2 * TOKN_DEV],
                )
            )
        )
    attention = jnp.concatenate([old_rows, merge(parts)]).astype(bf16)

    blocks = NX * NZL
    out_blocks = out_all.reshape(blocks, model // blocks, width)
    terms = jnp.einsum("rk,bck->brc", attention, out_blocks, preferred_element_type=f32)
    terms = terms.astype(bf16).reshape(NX, NZL, ROW_DEV, model // blocks)
    terms = lax.all_to_all(terms, "x", 0, 0, tiled=True)
    terms = jnp.sum(terms.astype(f32), axis=0).astype(bf16)
    terms = lax.all_to_all(terms, "zl", 0, 0, tiled=True)
    summed = jnp.sum(terms.astype(f32), axis=0).astype(bf16)
    summed = copies_to_all(summed, "zl", NZL)
    summed = copies_to_all(summed, "x", NX).reshape(blocks, ROW_DEV, model // blocks)
    summed = summed.transpose(1, 0, 2).reshape(ROW_DEV, model).astype(f32)
    norm = lax.rsqrt(jnp.mean(summed * summed, axis=1, keepdims=True) + EPSILON)
    mixed = (hidden_states.astype(f32) + summed * norm * attention_gain).astype(bf16)

    both = jnp.dot(mixed, ff_all[:, up_from:], preferred_element_type=f32)
    gate_values, up_values = both[:, :hidden_units], both[:, hidden_units:]
    activation = (jax.nn.silu(gate_values) * up_values).astype(bf16)
    rows = ROW_DEV // blocks
    activation = (
        activation.reshape(NZL, NX, rows, hidden_units)
        .transpose(1, 0, 2, 3)
        .reshape(ROW_DEV, hidden_units)
    )
    terms = lax.dot_general(
        activation,
        ff_all[:, :hidden_units],
        (((1,), (1,)), ((), ())),
        preferred_element_type=f32,
    ).astype(bf16)
    terms = lax.all_to_all(terms.reshape(NX, NZL * rows, model), "x", 0, 0, tiled=True)
    terms = jnp.sum(terms.astype(f32), axis=0).astype(bf16)
    terms = lax.all_to_all(terms.reshape(NZL, rows, model), "zl", 0, 0, tiled=True)
    total = jnp.sum(terms.astype(f32), axis=0)
    norm = lax.rsqrt(jnp.mean(total * total, axis=1, keepdims=True) + EPSILON)
    my_rows = lax.dynamic_slice_in_dim(mixed, (zl * NX + x_at) * rows, rows, 0)
    hidden_out = (my_rows.astype(f32) + total * norm * feedforward_gain).astype(bf16)
    return (hidden_out, passage_keys[None], passage_values[None])


def solution(mesh):
    fine = Mesh(
        mesh.devices.reshape(NY, NZH, NCORE, NZL, NX), ("y", "zh", "core", "zl", "x")
    )
    by_both = P(SEQ, BLK)
    return jax.shard_map(
        shards,
        mesh=fine,
        in_specs=(
            P(SEQ, None),
            by_both,
            by_both,
            by_both,
            P(BLK, SEQ),
            P(BLK),
            P(BLK),
            P(),
            by_both,
            by_both,
            P(BLK, SEQ),
            P(),
            P(SEQ, None, BLK),
            P(SEQ, None, BLK),
            P(),
            P(),
            P(),
            P(),
        ),
        out_specs=(P(SEQ + BLK, None), P(SEQ, None, BLK), P(SEQ, None, BLK)),
        check_vma=False,
    )
```

time: 2230 us -> 376 us (0.17)
  waiting for transfers between devices: 1740 us -> 61.1 us
  other arithmetic: 149 us -> 10.9 us
  blocking collectives: 256 us -> 153 us
  starting transfers between devices: 0.43 us -> 80.1 us
    unnamed x13 -> x2, waiting for transfers between devices: 907 us -> 0.7 us
    all_gather x9 -> x2, waiting for transfers between devices: 835 us -> 0.04 us  [the longest x1 0.02 us: shards(): out_all = lax.all_gather(output_weight.T, SEQ, axis=0, tiled=True)]
    all_to_all x0 -> x7, blocking collectives: none -> 153 us  [the longest x1 77.7 us: shards(): terms = lax.all_to_all(terms, 'zl', 0, 0, tiled=True)]
    add x39 -> x5, other arithmetic: 139 us -> 0.81 us  [the longest x1 0.65 us: shards(): key_at = start + jnp.arange(PLEN, dtype=jnp.int32)]
    all_gather x3 -> x0, blocking collectives: 138 us -> none  [the longest x2 90.7 us: joined(): gathered = jax.tree.map(lambda a: lax.all_gather(a, axis), part)]
    psum x1 -> x0, blocking collectives: 118 us -> none  [shards(): lax.psum((jnp.sum(query_raw * query_raw, axis=1), jnp.sum(key_raw * key_r...]
    all_to_all x0 -> x8, waiting for transfers between devices: none -> 60.4 us  [the longest x6 34.2 us: copies_to_all(): lax.all_to_all(jnp.broadcast_to(a[None], (count,) + a.shape), axis, 0, 0,...]
    all_to_all x0 -> x8, starting transfers between devices: none -> 58.4 us  [the longest x6 35 us: copies_to_all(): lax.all_to_all(jnp.broadcast_to(a[None], (count,) + a.shape), axis, 0, 0,...]
  transfers between devices with their start and end apart: 11 -> 14, of which waited for: 9 -> 8; matrix products, arithmetic and copies ran while one was open for 8% -> 10% of each run, Pallas kernels for 0% -> 0%
where the time goes in v1:
time: 376 us; the launch traced here: 374 us
  blocking collectives  153 us (41%)
  starting transfers between devices  80.1 us (21%)
  waiting for transfers between devices  61.1 us (16%)
  between operations  31.1 us (8%)
  local copies, waits for them, and re-layouts  23.8 us (6%)
  matrix products  14.2 us (4%)
  other arithmetic  10.9 us (3%)
    all_to_all x1, blocking collectives, shards(): terms = lax.all_to_all(terms, 'zl', 0, 0, tiled=True)  77.7 us
    all_to_all x4, blocking collectives, copies_to_all(): lax.all_to_all(jnp.broadcast_to(a[None], (count,) + a.shape), axis, 0, 0,...  43.8 us
    all_to_all x6, starting transfers between devices, copies_to_all(): lax.all_to_all(jnp.broadcast_to(a[None], (count,) + a.shape), axis, 0, 0,...  35 us
    all_to_all x6, waiting for transfers between devices, copies_to_all(): lax.all_to_all(jnp.broadcast_to(a[None], (count,) + a.shape), axis, 0, 0,...  34.2 us
    ppermute x4, starting transfers between devices, swap(): return lax.ppermute(a, axis, [(i, i ^ 1) for i in range(count)])  21.6 us
    all_to_all x1, blocking collectives, shards(): terms = lax.all_to_all(terms, 'x', 0, 0, tiled=True)  18.1 us
    all_to_all x1, waiting for transfers between devices, shards(): lax.all_to_all(terms.reshape(NZL, rows, model), 'zl', 0, 0, tiled=True)  14.2 us
    all_to_all x1, blocking collectives, shards(): lax.all_to_all(terms.reshape(NX, NZL * rows, model), 'x', 0, 0, tiled=True)  13.3 us
  transfers between devices with their start and end apart: 14, of which 8 were waited for; matrix products, arithmetic and copies ran while one was open for 10% of the time, Pallas kernels for 0%

profile of v1, /device:TPU:8, one launch (start us, length us, event | category | flops | bytes accessed | tf_op | source)
XLA Modules:
  0.0 374.2 jit_solution(7568273035372770461)
XLA Ops:
  10.6 15.9 %collective-permute-start.1 = (bf16[256,384]{1,0:T(8,128)(2,1)S(1)}, bf16[256,384]{1,0:T(8,128)(2,1)S(1)}, u32[]{:S(2)}, u32[]{:S(2)}) collective-permute-start(bf16[256,384]{1,0:T(8,128)(2,1)S(1)} %constant_dynamic-update-slice_fusion), channel_id=1, source_target_pairs={{0,64},{64,0},{1,65},{65,1},{2,66},{66,2},{3,67},{67,3},{4,68},{68... | collective-permute-start | bytes 589832 | tf_op jit(solution)/shard_map/ppermute | solution.py:58
  27.4 4.9 %all-to-all-start = ((bf16[4,256,384]{2,1,0:T(8,128)(2,1)}), bf16[4,256,384]{2,1,0:T(8,128)(2,1)S(1)}, u32[]{:S(2)}, u32[]{:S(2)}) async-start(bf16[4,256,384]{2,1,0:T(8,128)(2,1)} %broadcast_in_dim.85), calls=%async_computation | async-start | bytes 1572864 | tf_op jit(solution)/shard_map/all_to_all | solution.py:41
  44.5 5.6 %all-to-all-start.1 = ((bf16[4,256,384]{2,1,0:T(8,128)(2,1)}), bf16[4,256,384]{2,1,0:T(8,128)(2,1)}, u32[]{:S(2)}, u32[]{:S(2)}) async-start(bf16[4,256,384]{2,1,0:T(8,128)(2,1)} %broadcast_in_dim.86), calls=%async_computation.1 | async-start | bytes 1572864 | tf_op jit(solution)/shard_map/all_to_all | solution.py:41
  51.7 1.9 collective-permute-start
  53.7 6.5 %all-to-all-done.1 = bf16[4,256,384]{2,1,0:T(8,128)(2,1)} async-done(((bf16[4,256,384]{2,1,0:T(8,128)(2,1)}), bf16[4,256,384]{2,1,0:T(8,128)(2,1)}, u32[]{:S(2)}, u32[]{:S(2)}) %all-to-all-start.1) | async-done | bytes 786464 | tf_op jit(solution)/shard_map/all_to_all | solution.py:41
  60.2 1.9 collective-permute-start.2
  68.9 12.0 %all-to-all-start.2 = ((f32[32,2,128]{2,1,0:T(2,128)}), f32[32,2,128]{2,1,0:T(2,128)S(1)}, u32[]{:S(2)}, u32[]{:S(2)}) async-start(f32[32,2,128]{2,1,0:T(2,128)} %broadcast_in_dim.87), calls=%async_computation.2 | async-start | bytes 65536 | tf_op jit(solution)/shard_map/all_to_all | solution.py:199
  81.6 12.0 %all-to-all-done.2 = f32[32,2,128]{2,1,0:T(2,128)S(1)} async-done(((f32[32,2,128]{2,1,0:T(2,128)}), f32[32,2,128]{2,1,0:T(2,128)S(1)}, u32[]{:S(2)}, u32[]{:S(2)}) %all-to-all-start.2) | async-done | bytes 32800 | tf_op jit(solution)/shard_map/all_to_all | solution.py:199
  94.8 8.5 %all-to-all-start.3 = ((bf16[2,128,128]{2,1,0:T(8,128)(2,1)}), bf16[2,128,128]{2,1,0:T(8,128)(2,1)S(1)}, u32[]{:S(2)}, u32[]{:S(2)}) async-start(bf16[2,128,128]{2,1,0:T(8,128)(2,1)} %broadcast_in_dim.88), calls=%async_computation.3 | async-start | bytes 131072 | tf_op jit(solution)/shard_map/all_to_all | solution.py:41
  108.5 7.7 %all-to-all-done.3 = bf16[2,128,128]{2,1,0:T(8,128)(2,1)S(1)} async-done(((bf16[2,128,128]{2,1,0:T(8,128)(2,1)}), bf16[2,128,128]{2,1,0:T(8,128)(2,1)S(1)}, u32[]{:S(2)}, u32[]{:S(2)}) %all-to-all-start.3) | async-done | bytes 65568 | tf_op jit(solution)/shard_map/all_to_all | solution.py:41
  116.9 4.8 %all-to-all-start.4 = ((bf16[4,2,128,128]{3,2,1,0:T(8,128)(2,1)}), bf16[4,2,128,128]{3,2,1,0:T(8,128)(2,1)S(1)}, u32[]{:S(2)}, u32[]{:S(2)}) async-start(bf16[4,2,128,128]{3,2,1,0:T(8,128)(2,1)} %broadcast_in_dim.89), calls=%async_computation.4 | async-start | bytes 524288 | tf_op jit(solution)/shard_map/all_to_all | solution.py:41
  121.9 1.9 collective-permute-start.3
  124.9 2.1 all-to-all-done.4
  127.0 4.2 %all_to_all.75 = bf16[2,4,2,128,128]{4,3,2,1,0:T(8,128)(2,1)S(1)} all-to-all(bf16[2,4,2,128,128]{4,3,2,1,0:T(8,128)(2,1)S(1)} %broadcast_in_dim.90), channel_id=1, replica_groups=mesh['y'=4,'zh'=2,'core'=2,'zl'=8,'x'=4] {'core'}, dimensions={0} | all-to-all | bytes 1048576 | tf_op jit(solution)/shard_map/all_to_all | solution.py:41
  133.7 6.5 %all-to-all-start.6 = ((bf16[2,160,256]{2,1,0:T(8,128)(2,1)}), bf16[2,160,256]{2,1,0:T(8,128)(2,1)S(1)}, u32[]{:S(2)}, u32[]{:S(2)}) async-start(bf16[2,160,256]{2,1,0:T(8,128)(2,1)} %broadcast_in_dim.174), calls=%async_computation.6 | async-start | bytes 327680 | tf_op jit(solution)/shard_map/all_to_all | solution.py:41
  146.0 7.6 %all-to-all-done.6 = bf16[2,160,256]{2,1,0:T(8,128)(2,1)S(1)} async-done(((bf16[2,160,256]{2,1,0:T(8,128)(2,1)}), bf16[2,160,256]{2,1,0:T(8,128)(2,1)S(1)}, u32[]{:S(2)}, u32[]{:S(2)}) %all-to-all-start.6) | async-done | bytes 163872 | tf_op jit(solution)/shard_map/all_to_all | solution.py:41
  154.5 4.6 %all-to-all-start.7 = ((bf16[4,2,160,256]{3,2,1,0:T(8,128)(2,1)}), bf16[4,2,160,256]{3,2,1,0:T(8,128)(2,1)S(1)}, u32[]{:S(2)}, u32[]{:S(2)}) async-start(bf16[4,2,160,256]{3,2,1,0:T(8,128)(2,1)} %broadcast_in_dim.175), calls=%async_computation.7 | async-start | bytes 1310720 | tf_op jit(solution)/shard_map/all_to_all | solution.py:41
  159.7 1.6 copy.190
  161.4 9.0 %all-to-all-done.7 = bf16[4,2,160,256]{3,2,1,0:T(8,128)(2,1)S(1)} async-done(((bf16[4,2,160,256]{3,2,1,0:T(8,128)(2,1)}), bf16[4,2,160,256]{3,2,1,0:T(8,128)(2,1)S(1)}, u32[]{:S(2)}, u32[]{:S(2)}) %all-to-all-start.7) | async-done | bytes 655392 | tf_op jit(solution)/shard_map/all_to_all | solution.py:41
  170.5 4.8 %all_to_all.76 = bf16[2,4,2,160,256]{4,3,2,1,0:T(8,128)(2,1)S(1)} all-to-all(bf16[2,4,2,160,256]{4,3,2,1,0:T(8,128)(2,1)S(1)} %broadcast_in_dim.176), channel_id=1, replica_groups=mesh['y'=4,'zh'=2,'core'=2,'zl'=8,'x'=4] {'core'}, dimensions={0} | all-to-all | bytes 2621440 | tf_op jit(solution)/shard_map/all_to_all | solution.py:41
  175.2 2.4 copy.188
  180.5 18.1 %all_to_all.77 = bf16[4,8,128,128]{3,2,1,0:T(8,128)(2,1)S(1)} all-to-all(bf16[4,8,128,128]{3,2,1,0:T(8,128)(2,1)S(1)} %bitcast.132), channel_id=1, replica_groups=mesh['y'=4,'zh'=2,'core'=2,'zl'=8,'x'=4] {'x'}, dimensions={0} | all-to-all | bytes 2097152 | tf_op jit(solution)/shard_map/all_to_all | solution.py:272
  198.8 77.7 %all_to_all.78 = bf16[8,128,128]{2,1,0:T(8,128)(2,1)S(1)} all-to-all(bf16[8,128,128]{2,1,0:T(8,128)(2,1)S(1)} %reduce_sum.139), channel_id=1, replica_groups=mesh['y'=4,'zh'=2,'core'=2,'zl'=8,'x'=4] {'zl'}, dimensions={0} | all-to-all | bytes 524288 | tf_op jit(solution)/shard_map/all_to_all | solution.py:274
  276.6 20.0 %all_to_all.79 = bf16[8,128,128]{2,1,0:T(8,128)(2,1)S(1)} all-to-all(bf16[8,128,128]{2,1,0:T(8,128)(2,1)S(1)} %broadcast_in_dim.182), channel_id=1, replica_groups=mesh['y'=4,'zh'=2,'core'=2,'zl'=8,'x'=4] {'zl'}, dimensions={0} | all-to-all | bytes 524288 | tf_op jit(solution)/shard_map/all_to_all | solution.py:41
  296.9 14.9 %all_to_all.80 = bf16[4,8,128,128]{3,1,2,0:T(8,128)(2,1)S(1)} all-to-all(bf16[4,8,128,128]{3,1,2,0:T(8,128)(2,1)S(1)} %broadcast_in_dim.183), channel_id=1, replica_groups=mesh['y'=4,'zh'=2,'core'=2,'zl'=8,'x'=4] {'x'}, dimensions={0} | all-to-all | bytes 2097152 | tf_op jit(solution)/shard_map/all_to_all | solution.py:41
  312.0 1.9 copy.194
  313.9 1.9 copy.195
  317.8 4.6 %fusion = f32[128,688]{0,1:T(8,128)S(1)} fusion(bf16[128,4096]{1,0:T(8,128)(2,1)S(1)} %add_convert_fusion, bf16[4096,1072]{0,1:T(8,128)(2,1)} %all-gather.5.cloned.1.call-done), kind=kOutput, calls=%fused_computation.2 | convolution fusion | flops 721420288 | bytes 7036928 | tf_op jit(solution)/shard_map/dot_general | solution.py:282
  322.7 2.6 convolution_convert_fusion
  325.3 13.3 %all_to_all.81 = bf16[4,32,4096]{2,1,0:T(8,128)(2,1)S(1)} all-to-all(bf16[4,32,4096]{2,1,0:T(8,128)(2,1)S(1)} %bitcast.137), channel_id=1, replica_groups=mesh['y'=4,'zh'=2,'core'=2,'zl'=8,'x'=4] {'x'}, dimensions={0} | all-to-all | bytes 2097152 | tf_op jit(solution)/shard_map/all_to_all | solution.py:297
  339.6 11.5 %all-to-all-start.14 = ((bf16[8,4,4096]{2,1,0:T(4,128)(2,1)}), bf16[8,4,4096]{2,1,0:T(4,128)(2,1)S(1)}, u32[]{:S(2)}, u32[]{:S(2)}) async-start(bf16[8,4,4096]{2,1,0:T(4,128)(2,1)} %reshape.334), calls=%async_computation.14 | async-start | bytes 524288 | tf_op jit(solution)/shard_map/all_to_all | solution.py:299
  351.1 14.2 %all-to-all-done.14 = bf16[8,4,4096]{2,1,0:T(4,128)(2,1)S(1)} async-done(((bf16[8,4,4096]{2,1,0:T(4,128)(2,1)}), bf16[8,4,4096]{2,1,0:T(4,128)(2,1)S(1)}, u32[]{:S(2)}, u32[]{:S(2)}) %all-to-all-start.14) | async-done | bytes 262176 | tf_op jit(solution)/shard_map/all_to_all | solution.py:299
  (166 shorter events, 36.3 us)
Async XLA Ops:
  7.2 25.1 %copy-start.8 = (bf16[256,344]{0,1:T(8,128)(2,1)S(1)}, bf16[256,344]{0,1:T(8,128)(2,1)}, u32[]{:S(2)}) copy-start(bf16[256,344]{0,1:T(8,128)(2,1)} %param.26) | copy-start | bytes 528388
  7.2 25.1 %copy-start.7 = (bf16[256,344]{0,1:T(8,128)(2,1)S(1)}, bf16[256,344]{0,1:T(8,128)(2,1)}, u32[]{:S(2)}) copy-start(bf16[256,344]{0,1:T(8,128)(2,1)} %param.27) | copy-start | bytes 528388
  7.2 25.1 %copy-start.6 = (bf16[344,256]{1,0:T(8,128)(2,1)S(1)}, bf16[344,256]{1,0:T(8,128)(2,1)}, u32[]{:S(2)}) copy-start(bf16[344,256]{1,0:T(8,128)(2,1)} %param.28) | copy-start | bytes 528388
  7.2 152.5 %all-gather.3.cloned.1.call-start = ((), (), s32[]{:S(2)}) async-start(), calls=%async_computation.15 | async-start | bytes 1114112 | tf_op jit(solution)/shard_map/all_gather | solution.py:151
  10.5 22.7 %copy-start.13 = (s32[8,2]{0,1:T(2,128)S(1)}, s32[8,2]{0,1:T(2,128)}, u32[]{:S(2)}) copy-start(s32[8,2]{0,1:T(2,128)} %param.33) | copy-start | bytes 196
  10.5 23.0 %copy-start.12 = (s32[16]{0:T(128)S(1)}, s32[16]{0:T(128)}, u32[]{:S(2)}) copy-start(s32[16]{0:T(128)} %param.32) | copy-start | bytes 196
  10.5 29.6 %copy-start.16 = (s32[8]{0:T(128)S(1)}, s32[8]{0:T(128)}, u32[]{:S(2)}) copy-start(s32[8]{0:T(128)} %param.35) | copy-start | bytes 100
  10.5 31.0 %copy-start.11 = (s32[16,96]{1,0:T(8,128)S(1)}, s32[16,96]{1,0:T(8,128)}, u32[]{:S(2)}) copy-start(s32[16,96]{1,0:T(8,128)} %param.34) | copy-start | bytes 18436
  10.6 31.5 %copy-start.5 = (bf16[1,1024,128]{2,1,0:T(8,128)(2,1)S(1)}, bf16[1,1024,128]{2,1,0:T(8,128)(2,1)}, u32[]{:S(2)}) copy-start(bf16[1,1024,128]{2,1,0:T(8,128)(2,1)} %param.30) | copy-start | bytes 786436
  10.6 31.6 %collective-permute-start.1 = (bf16[256,384]{1,0:T(8,128)(2,1)S(1)}, bf16[256,384]{1,0:T(8,128)(2,1)S(1)}, u32[]{:S(2)}, u32[]{:S(2)}) collective-permute-start(bf16[256,384]{1,0:T(8,128)(2,1)S(1)} %constant_dynamic-update-slice_fusion), channel_id=1, source_target_pairs={{0,64},{64,0},{1,65},{65,1},{2,66},{66,2},{3,67},{67,3},{4,68},{68... | collective-permute-start | bytes 589832 | tf_op jit(solution)/shard_map/ppermute | solution.py:58
  27.4 16.2 %all-to-all-start = ((bf16[4,256,384]{2,1,0:T(8,128)(2,1)}), bf16[4,256,384]{2,1,0:T(8,128)(2,1)S(1)}, u32[]{:S(2)}, u32[]{:S(2)}) async-start(bf16[4,256,384]{2,1,0:T(8,128)(2,1)} %broadcast_in_dim.85), calls=%async_computation | async-start | bytes 1572864 | tf_op jit(solution)/shard_map/all_to_all | solution.py:41
  32.3 285.5 %all-gather.5.cloned.1.call-start = ((), (), s32[]{:S(2)}) async-start(), calls=%async_computation.16 | async-start | bytes 9330688 | tf_op jit(solution)/shard_map/all_gather | solution.py:156
  42.1 20.1 %copy-start = (bf16[128,4096]{1,0:T(8,128)(2,1)S(1)}, bf16[128,4096]{1,0:T(8,128)(2,1)}, u32[]{:S(2)}) copy-start(bf16[128,4096]{1,0:T(8,128)(2,1)} %param.18) | copy-start | bytes 3145732
  44.5 15.7 %all-to-all-start.1 = ((bf16[4,256,384]{2,1,0:T(8,128)(2,1)}), bf16[4,256,384]{2,1,0:T(8,128)(2,1)}, u32[]{:S(2)}, u32[]{:S(2)}) async-start(bf16[4,256,384]{2,1,0:T(8,128)(2,1)} %broadcast_in_dim.86), calls=%async_computation.1 | async-start | bytes 1572864 | tf_op jit(solution)/shard_map/all_to_all | solution.py:41
  51.7 11.6 %collective-permute-start = (bf16[4,256,384]{2,1,0:T(8,128)(2,1)S(1)}, bf16[4,256,384]{2,1,0:T(8,128)(2,1)}, u32[]{:S(2)}, u32[]{:S(2)}) collective-permute-start(bf16[4,256,384]{2,1,0:T(8,128)(2,1)S(1)} %all-to-all-done), channel_id=1, source_target_pairs={{0,32},{32,0},{1,33},{33,1},{2,34},{34,2},{3,35},{35,3},{4,36},{36... | collective-permute-start | bytes 2359304 | tf_op jit(solution)/shard_map/ppermute | solution.py:58
  60.2 4.8 %collective-permute-start.2 = (bf16[4,256,384]{2,1,0:T(8,128)(2,1)}, bf16[4,256,384]{2,1,0:T(8,128)(2,1)}, u32[]{:S(2)}, u32[]{:S(2)}) collective-permute-start(bf16[4,256,384]{2,1,0:T(8,128)(2,1)} %all-to-all-done.1), channel_id=1, source_target_pairs={{0,32},{32,0},{1,33},{33,1},{2,34},{34,2},{3,35},{35,3},{4,36},{36... | collective-permute-start | bytes 2359304 | tf_op jit(solution)/shard_map/ppermute | solution.py:58
  63.4 30.3 %copy-start.14 = (f32[128]{0:T(128)S(1)}, f32[128]{0:T(128)}, u32[]{:S(2)}) copy-start(f32[128]{0:T(128)} %param.23) | copy-start | bytes 1540
  63.4 30.3 %copy-start.15 = (f32[128]{0:T(128)S(1)}, f32[128]{0:T(128)}, u32[]{:S(2)}) copy-start(f32[128]{0:T(128)} %param.24) | copy-start | bytes 1540
  66.6 40.9 %copy-start.4 = (bf16[1,1024,128]{2,1,0:T(8,128)(2,1)S(1)}, bf16[1,1024,128]{2,1,0:T(8,128)(2,1)}, u32[]{:S(2)}) copy-start(bf16[1,1024,128]{2,1,0:T(8,128)(2,1)} %param.31) | copy-start | bytes 786436
  68.9 24.7 %all-to-all-start.2 = ((f32[32,2,128]{2,1,0:T(2,128)}), f32[32,2,128]{2,1,0:T(2,128)S(1)}, u32[]{:S(2)}, u32[]{:S(2)}) async-start(f32[32,2,128]{2,1,0:T(2,128)} %broadcast_in_dim.87), calls=%async_computation.2 | async-start | bytes 65536 | tf_op jit(solution)/shard_map/all_to_all | solution.py:199
  94.8 21.4 %all-to-all-start.3 = ((bf16[2,128,128]{2,1,0:T(8,128)(2,1)}), bf16[2,128,128]{2,1,0:T(8,128)(2,1)S(1)}, u32[]{:S(2)}, u32[]{:S(2)}) async-start(bf16[2,128,128]{2,1,0:T(8,128)(2,1)} %broadcast_in_dim.88), calls=%async_computation.3 | async-start | bytes 131072 | tf_op jit(solution)/shard_map/all_to_all | solution.py:41
  108.5 23.5 %copy-start.3 = (bf16[1024,128]{1,0:T(8,128)(2,1)}, bf16[1024,128]{1,0:T(8,128)(2,1)S(1)}, u32[]{:S(2)}) copy-start(bf16[1024,128]{1,0:T(8,128)(2,1)S(1)} %scatter_fusion.1) | copy-start | bytes 786436
  116.9 10.0 %all-to-all-start.4 = ((bf16[4,2,128,128]{3,2,1,0:T(8,128)(2,1)}), bf16[4,2,128,128]{3,2,1,0:T(8,128)(2,1)S(1)}, u32[]{:S(2)}, u32[]{:S(2)}) async-start(bf16[4,2,128,128]{3,2,1,0:T(8,128)(2,1)} %broadcast_in_dim.89), calls=%async_computation.4 | async-start | bytes 524288 | tf_op jit(solution)/shard_map/all_to_all | solution.py:41
  121.9 24.0 %collective-permute-start.3 = (bf16[64,128]{0,1:T(8,128)(2,1)S(1)}, bf16[64,128]{0,1:T(8,128)(2,1)S(1)}, u32[]{:S(2)}, u32[]{:S(2)}) collective-permute-start(bf16[64,128]{0,1:T(8,128)(2,1)S(1)} %pad_maximum_fusion.3), channel_id=1, source_target_pairs={{0,32},{32,0},{1,33},{33,1},{2,34},{34,2},{3,35},{35,3},{4,36},{36... | collective-permute-start | bytes 49160 | tf_op jit(solution)/shard_map/ppermute | solution.py:58
  124.9 7.1 %copy-start.2 = (bf16[1024,128]{1,0:T(8,128)(2,1)}, bf16[1024,128]{1,0:T(8,128)(2,1)S(1)}, u32[]{:S(2)}) copy-start(bf16[1024,128]{1,0:T(8,128)(2,1)S(1)} %scatter_fusion) | copy-start | bytes 786436
  133.7 19.9 %all-to-all-start.6 = ((bf16[2,160,256]{2,1,0:T(8,128)(2,1)}), bf16[2,160,256]{2,1,0:T(8,128)(2,1)S(1)}, u32[]{:S(2)}, u32[]{:S(2)}) async-start(bf16[2,160,256]{2,1,0:T(8,128)(2,1)} %broadcast_in_dim.174), calls=%async_computation.6 | async-start | bytes 327680 | tf_op jit(solution)/shard_map/all_to_all | solution.py:41
  154.5 15.8 %all-to-all-start.7 = ((bf16[4,2,160,256]{3,2,1,0:T(8,128)(2,1)}), bf16[4,2,160,256]{3,2,1,0:T(8,128)(2,1)S(1)}, u32[]{:S(2)}, u32[]{:S(2)}) async-start(bf16[4,2,160,256]{3,2,1,0:T(8,128)(2,1)} %broadcast_in_dim.175), calls=%async_computation.7 | async-start | bytes 1310720 | tf_op jit(solution)/shard_map/all_to_all | solution.py:41
  313.9 2.2 copy-start.9
  317.7 4.6 %copy-start.1 = (bf16[128,4096]{1,0:T(8,128)(2,1)}, bf16[128,4096]{1,0:T(8,128)(2,1)S(1)}, u32[]{:S(2)}) copy-start(bf16[128,4096]{1,0:T(8,128)(2,1)S(1)} %add_convert_fusion) | copy-start | bytes 3145732
  325.3 40.5 %copy-start.10 = (f32[4096]{0:T(1024)S(1)}, f32[4096]{0:T(1024)}, u32[]{:S(2)}) copy-start(f32[4096]{0:T(1024)} %param.29) | copy-start | bytes 49156
  339.6 25.7 %all-to-all-start.14 = ((bf16[8,4,4096]{2,1,0:T(4,128)(2,1)}), bf16[8,4,4096]{2,1,0:T(4,128)(2,1)S(1)}, u32[]{:S(2)}, u32[]{:S(2)}) async-start(bf16[8,4,4096]{2,1,0:T(4,128)(2,1)} %reshape.334), calls=%async_computation.14 | async-start | bytes 524288 | tf_op jit(solution)/shard_map/all_to_all | solution.py:299
Sparse Core Ops, SparseCore 0:
  11.2 85.6 all-gather.2
  100.0 169.8 all-gather.4

commit v2 on v1

--- a/solution.py
+++ b/solution.py
@@ -3,6 +3,8 @@
 import jax
 import jax.numpy as jnp
 from jax import lax
+from jax.experimental import pallas as pl
+from jax.experimental.pallas import tpu as pltpu
 from jax.sharding import Mesh, PartitionSpec as P
 
 HD = 128
@@ -116,6 +118,131 @@
     block = block.astype(f32)
     level = block[:, HD : HD + 1] + block[:, HD + 1 : HD + 2] + block[:, HD + 2 : HD + 3]
     return block[:, :HD], level
+
+
+def merge_and_project(control, own, new_part, returned, later):
+    own_out, own_level = own
+    new_out, new_level = new_part
+    width = own_out.shape[1]
+    blocks = later.shape[0] // width
+
+    def kernel(c_ref, own_ref, own_l_ref, new_ref, new_l_ref, back_ref, w_ref, out_ref, att_ref):
+        remote, remote_level = unpack(back_ref[c_ref[0], :SEL, :])
+        remote_level = jnp.where(c_ref[4] == 1, MASKED, remote_level)
+        att_ref[:SEL, :] = merge([(own_ref[...], own_l_ref[...]), (remote, remote_level)])
+        at = pl.multiple_of(SEL + c_ref[3] * TOKN_DEV, TOKN_DEV)
+        parts = [(new_ref[...], new_l_ref[...])]
+        for i in range(PPR):
+            parts.append(unpack(back_ref[c_ref[1 + i], pl.ds(at, TOKN_DEV), :]))
+        att_ref[SEL:, :] = merge(parts)
+        attention = att_ref[...].astype(bf16)
+        for b in range(blocks):
+            out_ref[b] = lax.dot_general(
+                attention,
+                w_ref[b * width : (b + 1) * width, :],
+                (((1,), (1,)), ((), ())),
+                preferred_element_type=f32,
+            ).astype(bf16)
+
+    def whole(a):
+        return pl.BlockSpec(a.shape, lambda i: (0,) * a.ndim)
+
+    return pl.pallas_call(
+        kernel,
+        grid=(1,),
+        out_shape=jax.ShapeDtypeStruct((blocks, ROW_DEV, width), bf16),
+        in_specs=[
+            pl.BlockSpec(memory_space=pltpu.SMEM),
+            whole(own_out),
+            whole(own_level),
+            whole(new_out),
+            whole(new_level),
+            whole(returned),
+            pl.BlockSpec((later.shape[0], width), lambda i: (0, 0)),
+        ],
+        out_specs=pl.BlockSpec((blocks, ROW_DEV, width), lambda i: (0, 0, 0)),
+        scratch_shapes=[pltpu.VMEM((ROW_DEV, width), f32)],
+        compiler_params=pltpu.CompilerParams(vmem_limit_bytes=24 << 20),
+        name="merge_and_project",
+    )(control, own_out, own_level, new_out, new_level, returned, later)
+
+
+def feed_forward(summed, hidden, gain, later, width, units):
+    blocks, rows, part = summed.shape
+    model = blocks * part
+    steps = 8
+    chunk = model // steps
+    each = chunk // part
+    down_from, gate_from = width, width + units
+    per = rows // (NZL * NX)
+
+    def kernel(s_ref, x_ref, g_ref, w_ref, out_ref, mixed_ref, norm_ref, acc_ref, down_ref):
+        k = pl.program_id(0)
+
+        @pl.when(k == 0)
+        def _():
+            squares = jnp.zeros((rows, part), f32)
+            for b in range(blocks):
+                block = s_ref[b].astype(f32)
+                squares = squares + block * block
+            norm_ref[...] = lax.rsqrt(
+                jnp.sum(squares, axis=1, keepdims=True) / model + EPSILON
+            )
+            acc_ref[...] = jnp.zeros_like(acc_ref)
+
+        for j in range(each):
+            cols = slice(j * part, (j + 1) * part)
+            mixed_ref[:, cols] = (
+                x_ref[:, cols].astype(f32)
+                + s_ref[k * each + j].astype(f32) * norm_ref[...] * g_ref[:, cols]
+            ).astype(bf16)
+        acc_ref[...] += jnp.dot(
+            mixed_ref[...], w_ref[:, gate_from:], preferred_element_type=f32
+        )
+        down_ref[k] = w_ref[:, down_from:gate_from]
+
+        @pl.when(k == steps - 1)
+        def _():
+            gate, up = acc_ref[:, :units], acc_ref[:, units:]
+            activation = (gate / (1.0 + jnp.exp(-gate)) * up).astype(bf16)
+            to = lax.broadcasted_iota(jnp.int32, (rows, rows), 0)
+            at = lax.broadcasted_iota(jnp.int32, (rows, rows), 1)
+            source = (to // per) % NZL * (NX * per) + to // (NZL * per) * per + to % per
+            move = jnp.where(at == source, 1.0, 0.0).astype(bf16)
+            activation = jnp.dot(move, activation, preferred_element_type=f32).astype(bf16)
+            for c in range(steps):
+                out_ref[:, c * chunk : (c + 1) * chunk] = lax.dot_general(
+                    activation,
+                    down_ref[c],
+                    (((1,), (1,)), ((), ())),
+                    preferred_element_type=f32,
+                ).astype(bf16)
+
+    return pl.pallas_call(
+        kernel,
+        grid=(steps,),
+        out_shape=(
+            jax.ShapeDtypeStruct((rows, model), bf16),
+            jax.ShapeDtypeStruct((rows, model), bf16),
+        ),
+        in_specs=[
+            pl.BlockSpec((blocks, rows, part), lambda k: (0, 0, 0)),
+            pl.BlockSpec((rows, chunk), lambda k: (0, k)),
+            pl.BlockSpec((1, chunk), lambda k: (0, k)),
+            pl.BlockSpec((chunk, later.shape[1]), lambda k: (k, 0)),
+        ],
+        out_specs=(
+            pl.BlockSpec((rows, model), lambda k: (0, 0)),
+            pl.BlockSpec((rows, chunk), lambda k: (0, k)),
+        ),
+        scratch_shapes=[
+            pltpu.VMEM((rows, 1), f32),
+            pltpu.VMEM((rows, 2 * units), f32),
+            pltpu.VMEM((steps, chunk, units), bf16),
+        ],
+        compiler_params=pltpu.CompilerParams(vmem_limit_bytes=32 << 20),
+        name="feed_forward",
+    )(summed, hidden, gain, later)
 
 
 def shards(
@@ -148,40 +275,24 @@
     model = hidden_states.shape[1]
     depth = query_weight.shape[0]
 
-    out_all = lax.all_gather(output_weight.T, SEQ, axis=0, tiled=True)
     pad = (-hidden_units) % 128
-    ff_mine = jnp.concatenate(
-        [jnp.pad(down_weight.T, ((0, 0), (0, pad))), gate_weight, up_weight], axis=1
-    )
-    ff_all = lax.all_gather(ff_mine, SEQ, axis=0, tiled=True)
-    up_from = hidden_units + pad
+    later = lax.all_gather(
+        jnp.concatenate(
+            [
+                output_weight.T,
+                jnp.pad(down_weight.T, ((0, 0), (0, pad))),
+                jnp.pad(gate_weight, ((0, 0), (0, pad))),
+                jnp.pad(up_weight, ((0, 0), (0, pad))),
+            ],
+            axis=1,
+        ),
+        SEQ,
+        axis=0,
+        tiled=True,
+    )
 
     mine = jnp.concatenate([query_weight, key_weight, value_weight], axis=1)
     theirs = swap(mine, "zh", NZH)
-    near = copies_to_all(mine, "y", NY)
-    near_other = swap(near, "core", NCORE)
-    far = copies_to_all(theirs, "y", NY)
-    far_other = swap(far, "core", NCORE)
-
-    columns = hidden_states.reshape(ROW_DEV, NY, NZH, NCORE, depth)
-
-    def block(i, j):
-        return columns[:, :, i, j].reshape(ROW_DEV, NY * depth)
-
-    by_zh = [
-        [jnp.where(zh == 0, block(i, j), block(1 - i, j)) for j in range(2)] for i in range(2)
-    ]
-    picked_x = [
-        [jnp.where(core == 0, by_zh[i][j], by_zh[i][1 - j]) for j in range(2)] for i in range(2)
-    ]
-
-    def product(x, w):
-        return jnp.dot(x, w.reshape(NY * depth, 3 * width), preferred_element_type=f32)
-
-    raw = product(picked_x[0][0], near) + product(picked_x[0][1], near_other)
-    raw = raw + product(picked_x[1][0], far) + product(picked_x[1][1], far_other)
-    query_raw, key_raw, value_raw = (raw[:, i * width : (i + 1) * width] for i in range(3))
-
     starts, owners, positions, new_live = layout(
         passage_order, separators, recompute_index, prompt_lengths
     )
@@ -192,6 +303,30 @@
     start = lax.dynamic_index_in_dim(starts, seq, 0, False)
     turn = (start.astype(f32) * frequency)[None, :]
     moved = rotate(cached_keys[0].astype(f32), jnp.cos(turn), jnp.sin(turn)).astype(bf16)
+    near = copies_to_all(mine, "y", NY)
+    theirs, cosine, sine, moved = lax.optimization_barrier((theirs, cosine, sine, moved))
+    near_other = swap(near, "core", NCORE)
+    far = copies_to_all(theirs, "y", NY)
+    far_other = swap(far, "core", NCORE)
+
+    columns = hidden_states.reshape(ROW_DEV, NY, NZH, NCORE, depth)
+
+    def block(i, j):
+        return columns[:, :, i, j].reshape(ROW_DEV, NY * depth)
+
+    by_zh = [
+        [jnp.where(zh == 0, block(i, j), block(1 - i, j)) for j in range(2)] for i in range(2)
+    ]
+    picked_x = [
+        [jnp.where(core == 0, by_zh[i][j], by_zh[i][1 - j]) for j in range(2)] for i in range(2)
+    ]
+
+    def product(x, w):
+        return jnp.dot(x, w.reshape(NY * depth, 3 * width), preferred_element_type=f32)
+
+    raw = product(picked_x[0][0], near) + product(picked_x[0][1], near_other)
+    raw = raw + product(picked_x[1][0], far) + product(picked_x[1][1], far_other)
+    query_raw, key_raw, value_raw = (raw[:, i * width : (i + 1) * width] for i in range(3))
 
     squares = jnp.stack(
         [jnp.sum(query_raw * query_raw, axis=1), jnp.sum(key_raw * key_raw, axis=1)]
@@ -248,52 +383,24 @@
         jnp.where(first, part[:SEL], part[SEL : 2 * SEL]),
         jnp.where(first, level[:SEL], level[SEL : 2 * SEL]),
     )
-    remote, remote_level = unpack(rows_of(returned, seq_slot(chosen[0]))[:SEL])
-    old_rows = merge([own, (remote, jnp.where(first, MASKED, remote_level))])
     my_order = rows_of(order, seq // 2)
-    parts = [new_part]
-    for i in range(PPR):
-        theirs_back = rows_of(returned, seq_slot(my_order[i]))
-        parts.append(
-            unpack(
-                jnp.where(
-                    core == 0,
-                    theirs_back[SEL : SEL + TOKN_DEV],
-                    theirs_back[SEL + TOKN_DEV : SEL + 2 * TOKN_DEV],
-                )
-            )
-        )
-    attention = jnp.concatenate([old_rows, merge(parts)]).astype(bf16)
+    control = jnp.stack(
+        [seq_slot(chosen[0]), seq_slot(my_order[0]), seq_slot(my_order[1]), core, first]
+    ).astype(jnp.int32)
 
     blocks = NX * NZL
-    out_blocks = out_all.reshape(blocks, model // blocks, width)
-    terms = jnp.einsum("rk,bck->brc", attention, out_blocks, preferred_element_type=f32)
-    terms = terms.astype(bf16).reshape(NX, NZL, ROW_DEV, model // blocks)
-    terms = lax.all_to_all(terms, "x", 0, 0, tiled=True)
+    terms = merge_and_project(control, own, new_part, returned, later)
+    terms = lax.all_to_all(terms.reshape(NX, NZL, ROW_DEV, width), "x", 0, 0, tiled=True)
     terms = jnp.sum(terms.astype(f32), axis=0).astype(bf16)
     terms = lax.all_to_all(terms, "zl", 0, 0, tiled=True)
     summed = jnp.sum(terms.astype(f32), axis=0).astype(bf16)
     summed = copies_to_all(summed, "zl", NZL)
     summed = copies_to_all(summed, "x", NX).reshape(blocks, ROW_DEV, model // blocks)
-    summed = summed.transpose(1, 0, 2).reshape(ROW_DEV, model).astype(f32)
-    norm = lax.rsqrt(jnp.mean(summed * summed, axis=1, keepdims=True) + EPSILON)
-    mixed = (hidden_states.astype(f32) + summed * norm * attention_gain).astype(bf16)
-
-    both = jnp.dot(mixed, ff_all[:, up_from:], preferred_element_type=f32)
-    gate_values, up_values = both[:, :hidden_units], both[:, hidden_units:]
-    activation = (jax.nn.silu(gate_values) * up_values).astype(bf16)
+
     rows = ROW_DEV // blocks
-    activation = (
-        activation.reshape(NZL, NX, rows, hidden_units)
-        .transpose(1, 0, 2, 3)
-        .reshape(ROW_DEV, hidden_units)
-    )
-    terms = lax.dot_general(
-        activation,
-        ff_all[:, :hidden_units],
-        (((1,), (1,)), ((), ())),
-        preferred_element_type=f32,
-    ).astype(bf16)
+    terms, mixed = feed_forward(
+        summed, hidden_states, attention_gain[None], later, width, hidden_units + pad
+    )
     terms = lax.all_to_all(terms.reshape(NX, NZL * rows, model), "x", 0, 0, tiled=True)
     terms = jnp.sum(terms.astype(f32), axis=0).astype(bf16)
     terms = lax.all_to_all(terms.reshape(NZL, rows, model), "zl", 0, 0, tiled=True)

time: 376 us -> 431 us (1.15)
  the two profiles are of different devices: /device:TPU:8 before, /device:TPU:32 now
where the time goes in v2:
time: 431 us; the launch traced here: 429 us
  waiting for transfers between devices  170 us (39%)
  blocking collectives  93.6 us (22%)
  starting transfers between devices  90.1 us (21%)
  between operations  31.4 us (7%)
  local copies, waits for them, and re-layouts  23.7 us (5%)
  other arithmetic  9.97 us (2%)
  Pallas kernels  6.14 us (1%)
  matrix products  4.85 us (1%)
    all_to_all x1, waiting for transfers between devices, shards(): lax.all_to_all(jnp.broadcast_to(squares[None], (NZL * NX,) + squares.shap...  94.6 us
    all_to_all x6, waiting for transfers between devices, copies_to_all(): lax.all_to_all(jnp.broadcast_to(a[None], (count,) + a.shape), axis, 0, 0,...  48.4 us
    all_to_all x4, blocking collectives, copies_to_all(): lax.all_to_all(jnp.broadcast_to(a[None], (count,) + a.shape), axis, 0, 0,...  43.4 us
    all_to_all x6, starting transfers between devices, copies_to_all(): lax.all_to_all(jnp.broadcast_to(a[None], (count,) + a.shape), axis, 0, 0,...  41.6 us
    ppermute x4, starting transfers between devices, swap(): return lax.ppermute(a, axis, [(i, i ^ 1) for i in range(count)])  20.7 us
    all_to_all x1, blocking collectives, shards(): terms = lax.all_to_all(terms, 'zl', 0, 0, tiled=True)  18.8 us
    all_to_all x1, blocking collectives, shards(): lax.all_to_all(terms.reshape(NX, NZL, ROW_DEV, width), 'x', 0, 0, tiled=T...  18.1 us
    all_to_all x1, starting transfers between devices, shards(): lax.all_to_all(jnp.broadcast_to(squares[None], (NZL * NX,) + squares.shap...  15.1 us
  transfers between devices with their start and end apart: 13, of which 8 were waited for; matrix products, arithmetic and copies ran while one was open for 6% of the time, Pallas kernels for 0%

profile of v2, /device:TPU:32, one launch (start us, length us, event | category | flops | bytes accessed | tf_op | source)
XLA Modules:
  0.0 429.4 jit_solution(14835138523746905396)
XLA Ops:
  11.0 15.0 %collective-permute-start.1 = (bf16[256,384]{1,0:T(8,128)(2,1)S(1)}, bf16[256,384]{1,0:T(8,128)(2,1)S(1)}, u32[]{:S(2)}, u32[]{:S(2)}) collective-permute-start(bf16[256,384]{1,0:T(8,128)(2,1)S(1)} %constant_dynamic-update-slice_fusion), channel_id=1, source_target_pairs={{0,64},{64,0},{1,65},{65,1},{2,66},{66,2},{3,67},{67,3},{4,68},{68... | collective-permute-start | bytes 589832 | tf_op jit(solution)/shard_map/ppermute | solution.py:60
  26.9 4.5 %all-to-all-start = ((bf16[4,256,384]{2,1,0:T(8,128)(2,1)}), bf16[4,256,384]{2,1,0:T(8,128)(2,1)S(1)}, u32[]{:S(2)}, u32[]{:S(2)}) async-start(bf16[4,256,384]{2,1,0:T(8,128)(2,1)} %broadcast_in_dim.83), calls=%async_computation | async-start | bytes 1572864 | tf_op jit(solution)/shard_map/all_to_all | solution.py:43
  43.8 13.0 %collective-permute-done.1 = bf16[256,384]{1,0:T(8,128)(2,1)S(1)} collective-permute-done((bf16[256,384]{1,0:T(8,128)(2,1)S(1)}, bf16[256,384]{1,0:T(8,128)(2,1)S(1)}, u32[]{:S(2)}, u32[]{:S(2)}) %collective-permute-start.1) | collective-permute-done | bytes 196640 | tf_op jit(solution)/shard_map/ppermute | solution.py:60
  57.8 4.7 %all-to-all-start.1 = ((bf16[4,256,384]{2,1,0:T(8,128)(2,1)}), bf16[4,256,384]{2,1,0:T(8,128)(2,1)}, u32[]{:S(2)}, u32[]{:S(2)}) async-start(bf16[4,256,384]{2,1,0:T(8,128)(2,1)} %broadcast_in_dim.84), calls=%async_computation.1 | async-start | bytes 1572864 | tf_op jit(solution)/shard_map/all_to_all | solution.py:43
  63.0 1.9 collective-permute-start
  67.1 5.0 %all-to-all-done.1 = bf16[4,256,384]{2,1,0:T(8,128)(2,1)} async-done(((bf16[4,256,384]{2,1,0:T(8,128)(2,1)}), bf16[4,256,384]{2,1,0:T(8,128)(2,1)}, u32[]{:S(2)}, u32[]{:S(2)}) %all-to-all-start.1) | async-done | bytes 786464 | tf_op jit(solution)/shard_map/all_to_all | solution.py:43
  72.1 1.9 collective-permute-start.2
  76.6 1.5 convolution_add_fusion.1
  79.2 15.1 %all-to-all-start.2 = ((f32[32,2,128]{2,1,0:T(2,128)}), f32[32,2,128]{2,1,0:T(2,128)S(1)}, u32[]{:S(2)}, u32[]{:S(2)}) async-start(f32[32,2,128]{2,1,0:T(2,128)} %broadcast_in_dim.85), calls=%async_computation.2 | async-start | bytes 65536 | tf_op jit(solution)/shard_map/all_to_all | solution.py:334
  105.8 94.6 %all-to-all-done.2 = f32[32,2,128]{2,1,0:T(2,128)S(1)} async-done(((f32[32,2,128]{2,1,0:T(2,128)}), f32[32,2,128]{2,1,0:T(2,128)S(1)}, u32[]{:S(2)}, u32[]{:S(2)}) %all-to-all-start.2) | async-done | bytes 32800 | tf_op jit(solution)/shard_map/all_to_all | solution.py:334
  200.7 1.9 collective-permute-start.3
  203.4 22.2 %all-to-all-start.3 = ((bf16[2,128,128]{2,1,0:T(8,128)(2,1)}), bf16[2,128,128]{2,1,0:T(8,128)(2,1)S(1)}, u32[]{:S(2)}, u32[]{:S(2)}) async-start(bf16[2,128,128]{2,1,0:T(8,128)(2,1)} %broadcast_in_dim.86), calls=%async_computation.3 | async-start | bytes 131072 | tf_op jit(solution)/shard_map/all_to_all | solution.py:43
  226.8 11.6 %all-to-all-done.3 = bf16[2,128,128]{2,1,0:T(8,128)(2,1)S(1)} async-done(((bf16[2,128,128]{2,1,0:T(8,128)(2,1)}), bf16[2,128,128]{2,1,0:T(8,128)(2,1)S(1)}, u32[]{:S(2)}, u32[]{:S(2)}) %all-to-all-start.3) | async-done | bytes 65568 | tf_op jit(solution)/shard_map/all_to_all | solution.py:43
  239.1 3.4 all-to-all-start.4
  243.1 6.1 %all-to-all-done.4 = bf16[4,2,128,128]{3,2,1,0:T(8,128)(2,1)S(1)} async-done(((bf16[4,2,128,128]{3,2,1,0:T(8,128)(2,1)}), bf16[4,2,128,128]{3,2,1,0:T(8,128)(2,1)S(1)}, u32[]{:S(2)}, u32[]{:S(2)}) %all-to-all-start.4) | async-done | bytes 262176 | tf_op jit(solution)/shard_map/all_to_all | solution.py:43
  249.3 4.2 all_to_all.75
  255.9 3.4 all-to-all-start.6
  259.5 14.9 %all-to-all-done.6 = bf16[2,160,256]{2,1,0:T(8,128)(2,1)S(1)} async-done(((bf16[2,160,256]{2,1,0:T(8,128)(2,1)}), bf16[2,160,256]{2,1,0:T(8,128)(2,1)S(1)}, u32[]{:S(2)}, u32[]{:S(2)}) %all-to-all-start.6) | async-done | bytes 163872 | tf_op jit(solution)/shard_map/all_to_all | solution.py:43
  275.3 3.5 all-to-all-start.7
  279.0 10.7 %all-to-all-done.7 = bf16[4,2,160,256]{3,2,1,0:T(8,128)(2,1)S(1)} async-done(((bf16[4,2,160,256]{3,2,1,0:T(8,128)(2,1)}), bf16[4,2,160,256]{3,2,1,0:T(8,128)(2,1)S(1)}, u32[]{:S(2)}, u32[]{:S(2)}) %all-to-all-start.7) | async-done | bytes 655392 | tf_op jit(solution)/shard_map/all_to_all | solution.py:43
  289.9 4.8 %all_to_all.76 = bf16[2,4,2,160,256]{4,3,2,1,0:T(8,128)(2,1)S(1)} all-to-all(bf16[2,4,2,160,256]{4,3,2,1,0:T(8,128)(2,1)S(1)} %broadcast_in_dim.177), channel_id=1, replica_groups=mesh['y'=4,'zh'=2,'core'=2,'zl'=8,'x'=4] {'core'}, dimensions={0} | all-to-all | bytes 2621440 | tf_op jit(solution)/shard_map/all_to_all | solution.py:43
  294.6 4.0 copy-done
  298.6 1.5 merge_and_project.1
  300.2 18.1 %all_to_all.77 = bf16[4,8,128,128]{3,2,1,0:T(8,128)(2,1)S(1)} all-to-all(bf16[4,8,128,128]{3,2,1,0:T(8,128)(2,1)S(1)} %bitcast.90), channel_id=1, replica_groups=mesh['y'=4,'zh'=2,'core'=2,'zl'=8,'x'=4] {'x'}, dimensions={0} | all-to-all | bytes 2097152 | tf_op jit(solution)/shard_map/all_to_all | solution.py:393
  318.4 18.8 %all_to_all.78 = bf16[8,128,128]{2,1,0:T(8,128)(2,1)S(1)} all-to-all(bf16[8,128,128]{2,1,0:T(8,128)(2,1)S(1)} %reduce_sum.130), channel_id=1, replica_groups=mesh['y'=4,'zh'=2,'core'=2,'zl'=8,'x'=4] {'zl'}, dimensions={0} | all-to-all | bytes 524288 | tf_op jit(solution)/shard_map/all_to_all | solution.py:395
  337.4 21.1 %all_to_all.79 = bf16[8,128,128]{2,1,0:T(8,128)(2,1)S(1)} all-to-all(bf16[8,128,128]{2,1,0:T(8,128)(2,1)S(1)} %broadcast_in_dim.178), channel_id=1, replica_groups=mesh['y'=4,'zh'=2,'core'=2,'zl'=8,'x'=4] {'zl'}, dimensions={0} | all-to-all | bytes 524288 | tf_op jit(solution)/shard_map/all_to_all | solution.py:43
  358.7 13.3 %all_to_all.80 = bf16[4,8,128,128]{3,2,1,0:T(8,128)(2,1)S(1)} all-to-all(bf16[4,8,128,128]{3,2,1,0:T(8,128)(2,1)S(1)} %broadcast_in_dim.179), channel_id=1, replica_groups=mesh['y'=4,'zh'=2,'core'=2,'zl'=8,'x'=4] {'x'}, dimensions={0} | all-to-all | bytes 2097152 | tf_op jit(solution)/shard_map/all_to_all | solution.py:43
  372.0 4.0 copy-done.1
  376.0 4.6 %feed_forward.1 = (bf16[128,4096]{1,0:T(8,128)(2,1)S(1)}, bf16[128,4096]{1,0:T(8,128)(2,1)S(1)}) custom-call(bf16[32,128,128]{2,1,0:T(8,128)(2,1)S(1)} %bitcast.91, bf16[128,4096]{1,0:T(8,128)(2,1)S(1)} %copy-done.2, f32[1,4096]{1,0:T(1,128)S(1)} %bitcast.93, bf16[4096,1280]{1,0:T(8,128)(2,1)S(1)} %copy-done.1), custom_call_target="tpu_custom_call" | custom-call | tf_op jit(solution)/shard_map/feed_forward/pallas_call | solution.py:221
  380.6 13.3 %all_to_all.81 = bf16[4,32,4096]{2,1,0:T(8,128)(2,1)S(1)} all-to-all(bf16[4,32,4096]{2,1,0:T(8,128)(2,1)S(1)} %bitcast.92), channel_id=1, replica_groups=mesh['y'=4,'zh'=2,'core'=2,'zl'=8,'x'=4] {'x'}, dimensions={0} | all-to-all | bytes 2097152 | tf_op jit(solution)/shard_map/all_to_all | solution.py:404
  395.0 12.7 %all-to-all-start.14 = ((bf16[8,4,4096]{2,1,0:T(4,128)(2,1)}), bf16[8,4,4096]{2,1,0:T(4,128)(2,1)S(1)}, u32[]{:S(2)}, u32[]{:S(2)}) async-start(bf16[8,4,4096]{2,1,0:T(4,128)(2,1)} %reshape.294), calls=%async_computation.14 | async-start | bytes 524288 | tf_op jit(solution)/shard_map/all_to_all | solution.py:406
  407.7 13.7 %all-to-all-done.14 = bf16[8,4,4096]{2,1,0:T(4,128)(2,1)S(1)} async-done(((bf16[8,4,4096]{2,1,0:T(4,128)(2,1)}), bf16[8,4,4096]{2,1,0:T(4,128)(2,1)S(1)}, u32[]{:S(2)}, u32[]{:S(2)}) %all-to-all-start.14) | async-done | bytes 262176 | tf_op jit(solution)/shard_map/all_to_all | solution.py:406
  (162 shorter events, 29.1 us)
Async XLA Ops:
  7.2 2.5 copy-start.12
  7.2 287.5 %all-gather.2.cloned.1.call-start = ((), (), s32[]{:S(2)}) async-start(), calls=%async_computation.15 | async-start | bytes 11141120 | tf_op jit(solution)/shard_map/all_gather | solution.py:279
  10.9 20.4 %copy-start.19 = (s32[8,2]{0,1:T(2,128)S(1)}, s32[8,2]{0,1:T(2,128)}, u32[]{:S(2)}) copy-start(s32[8,2]{0,1:T(2,128)} %param.33) | copy-start | bytes 196
  10.9 20.7 %copy-start.18 = (s32[16]{0:T(128)S(1)}, s32[16]{0:T(128)}, u32[]{:S(2)}) copy-start(s32[16]{0:T(128)} %param.32) | copy-start | bytes 196
  10.9 28.8 %copy-start.22 = (s32[8]{0:T(128)S(1)}, s32[8]{0:T(128)}, u32[]{:S(2)}) copy-start(s32[8]{0:T(128)} %param.35) | copy-start | bytes 100
  11.0 30.3 %copy-start.17 = (s32[16,96]{1,0:T(8,128)S(1)}, s32[16,96]{1,0:T(8,128)}, u32[]{:S(2)}) copy-start(s32[16,96]{1,0:T(8,128)} %param.34) | copy-start | bytes 18436
  11.0 31.4 %copy-start.6 = (bf16[1,1024,128]{2,1,0:T(8,128)(2,1)S(1)}, bf16[1,1024,128]{2,1,0:T(8,128)(2,1)}, u32[]{:S(2)}) copy-start(bf16[1,1024,128]{2,1,0:T(8,128)(2,1)} %param.30) | copy-start | bytes 786436
  11.0 45.9 %collective-permute-start.1 = (bf16[256,384]{1,0:T(8,128)(2,1)S(1)}, bf16[256,384]{1,0:T(8,128)(2,1)S(1)}, u32[]{:S(2)}, u32[]{:S(2)}) collective-permute-start(bf16[256,384]{1,0:T(8,128)(2,1)S(1)} %constant_dynamic-update-slice_fusion), channel_id=1, source_target_pairs={{0,64},{64,0},{1,65},{65,1},{2,66},{66,2},{3,67},{67,3},{4,68},{68... | collective-permute-start | bytes 589832 | tf_op jit(solution)/shard_map/ppermute | solution.py:60
  26.9 30.0 %all-to-all-start = ((bf16[4,256,384]{2,1,0:T(8,128)(2,1)}), bf16[4,256,384]{2,1,0:T(8,128)(2,1)S(1)}, u32[]{:S(2)}, u32[]{:S(2)}) async-start(bf16[4,256,384]{2,1,0:T(8,128)(2,1)} %broadcast_in_dim.83), calls=%async_computation | async-start | bytes 1572864 | tf_op jit(solution)/shard_map/all_to_all | solution.py:43
  43.7 21.7 %copy-start.2 = (bf16[128,4096]{1,0:T(8,128)(2,1)S(1)}, bf16[128,4096]{1,0:T(8,128)(2,1)}, u32[]{:S(2)}) copy-start(bf16[128,4096]{1,0:T(8,128)(2,1)} %x_ref.1) | copy-start | bytes 3145732
  57.8 14.3 %all-to-all-start.1 = ((bf16[4,256,384]{2,1,0:T(8,128)(2,1)}), bf16[4,256,384]{2,1,0:T(8,128)(2,1)}, u32[]{:S(2)}, u32[]{:S(2)}) async-start(bf16[4,256,384]{2,1,0:T(8,128)(2,1)} %broadcast_in_dim.84), calls=%async_computation.1 | async-start | bytes 1572864 | tf_op jit(solution)/shard_map/all_to_all | solution.py:43
  63.0 12.0 %collective-permute-start = (bf16[4,256,384]{2,1,0:T(8,128)(2,1)S(1)}, bf16[4,256,384]{2,1,0:T(8,128)(2,1)}, u32[]{:S(2)}, u32[]{:S(2)}) collective-permute-start(bf16[4,256,384]{2,1,0:T(8,128)(2,1)S(1)} %all-to-all-done), channel_id=1, source_target_pairs={{0,32},{32,0},{1,33},{33,1},{2,34},{34,2},{3,35},{35,3},{4,36},{36... | collective-permute-start | bytes 2359304 | tf_op jit(solution)/shard_map/ppermute | solution.py:60
  67.0 8.0 %copy-start.5 = (bf16[128,4,1,1,256]{0,4,3,2,1:T(8,128)(2,1)S(1)}, bf16[128,4,1,1,256]{0,4,3,2,1:T(8,128)(2,1)}, u32[]{:S(2)}) copy-start(bf16[128,4,1,1,256]{0,4,3,2,1:T(8,128)(2,1)} %get-tuple-element.24) | copy-start | bytes 786436
  72.1 6.0 %collective-permute-start.2 = (bf16[4,256,384]{2,1,0:T(8,128)(2,1)}, bf16[4,256,384]{2,1,0:T(8,128)(2,1)S(1)}, u32[]{:S(2)}, u32[]{:S(2)}) collective-permute-start(bf16[4,256,384]{2,1,0:T(8,128)(2,1)} %all-to-all-done.1), channel_id=1, source_target_pairs={{0,32},{32,0},{1,33},{33,1},{2,34},{34,2},{3,35},{35,3},{4,36},{36... | collective-permute-start | bytes 2359304 | tf_op jit(solution)/shard_map/ppermute | solution.py:60
  76.5 17.8 %copy-start.23 = (pred[32]{0:T(512)(128)(4,1)S(1)}, pred[32]{0:T(512)(128)(4,1)}, u32[]{:S(2)}) copy-start(pred[32]{0:T(512)(128)(4,1)} %get-tuple-element.56) | copy-start | bytes 100
  78.0 26.6 %copy-start.10 = (bf16[1,1024,128]{2,1,0:T(8,128)(2,1)S(1)}, bf16[1,1024,128]{2,1,0:T(8,128)(2,1)}, u32[]{:S(2)}) copy-start(bf16[1,1024,128]{2,1,0:T(8,128)(2,1)} %param.31) | copy-start | bytes 786436
  78.1 122.4 %copy-start.20 = (f32[128]{0:T(128)S(1)}, f32[128]{0:T(128)}, u32[]{:S(2)}) copy-start(f32[128]{0:T(128)} %param.23) | copy-start | bytes 1540
  78.1 122.4 %copy-start.21 = (f32[128]{0:T(128)S(1)}, f32[128]{0:T(128)}, u32[]{:S(2)}) copy-start(f32[128]{0:T(128)} %param.24) | copy-start | bytes 1540
  78.4 147.2 %copy-start.7 = (bf16[1024,128]{1,0:T(8,128)(2,1)S(1)}, bf16[1024,128]{1,0:T(8,128)(2,1)}, u32[]{:S(2)}) copy-start(bf16[1024,128]{1,0:T(8,128)(2,1)} %pad_maximum_fusion) | copy-start | bytes 786436
  79.2 121.2 %all-to-all-start.2 = ((f32[32,2,128]{2,1,0:T(2,128)}), f32[32,2,128]{2,1,0:T(2,128)S(1)}, u32[]{:S(2)}, u32[]{:S(2)}) async-start(f32[32,2,128]{2,1,0:T(2,128)} %broadcast_in_dim.85), calls=%async_computation.2 | async-start | bytes 65536 | tf_op jit(solution)/shard_map/all_to_all | solution.py:334
  105.8 148.8 %copy-start.9 = (bf16[1024,128]{1,0:T(8,128)(2,1)}, bf16[1024,128]{1,0:T(8,128)(2,1)S(1)}, u32[]{:S(2)}) copy-start(bf16[1024,128]{1,0:T(8,128)(2,1)S(1)} %scatter_custom_fusion.1) | copy-start | bytes 786436
  200.7 26.0 %collective-permute-start.3 = (bf16[64,128]{1,0:T(8,128)(2,1)S(1)}, bf16[64,128]{1,0:T(8,128)(2,1)S(1)}, u32[]{:S(2)}, u32[]{:S(2)}) collective-permute-start(bf16[64,128]{1,0:T(8,128)(2,1)S(1)} %get-tuple-element.19), channel_id=1, source_target_pairs={{0,32},{32,0},{1,33},{33,1},{2,34},{34,2},{3,35},{35,3},{4,36},{36... | collective-permute-start | bytes 49160 | tf_op jit(solution)/shard_map/ppermute | solution.py:60
  203.4 35.0 %all-to-all-start.3 = ((bf16[2,128,128]{2,1,0:T(8,128)(2,1)}), bf16[2,128,128]{2,1,0:T(8,128)(2,1)S(1)}, u32[]{:S(2)}, u32[]{:S(2)}) async-start(bf16[2,128,128]{2,1,0:T(8,128)(2,1)} %broadcast_in_dim.86), calls=%async_computation.3 | async-start | bytes 131072 | tf_op jit(solution)/shard_map/all_to_all | solution.py:43
  226.8 26.7 %copy-start.8 = (bf16[1024,128]{1,0:T(8,128)(2,1)}, bf16[1024,128]{1,0:T(8,128)(2,1)S(1)}, u32[]{:S(2)}) copy-start(bf16[1024,128]{1,0:T(8,128)(2,1)S(1)} %scatter_custom_fusion) | copy-start | bytes 786436
  239.1 10.1 %all-to-all-start.4 = ((bf16[4,2,128,128]{3,2,1,0:T(8,128)(2,1)}), bf16[4,2,128,128]{3,2,1,0:T(8,128)(2,1)S(1)}, u32[]{:S(2)}, u32[]{:S(2)}) async-start(bf16[4,2,128,128]{3,2,1,0:T(8,128)(2,1)} %broadcast_in_dim.87), calls=%async_computation.4 | async-start | bytes 524288 | tf_op jit(solution)/shard_map/all_to_all | solution.py:43
  255.9 18.5 %all-to-all-start.6 = ((bf16[2,160,256]{2,1,0:T(8,128)(2,1)}), bf16[2,160,256]{2,1,0:T(8,128)(2,1)S(1)}, u32[]{:S(2)}, u32[]{:S(2)}) async-start(bf16[2,160,256]{2,1,0:T(8,128)(2,1)} %broadcast_in_dim.175), calls=%async_computation.6 | async-start | bytes 327680 | tf_op jit(solution)/shard_map/all_to_all | solution.py:43
  275.3 14.4 %all-to-all-start.7 = ((bf16[4,2,160,256]{3,2,1,0:T(8,128)(2,1)}), bf16[4,2,160,256]{3,2,1,0:T(8,128)(2,1)S(1)}, u32[]{:S(2)}, u32[]{:S(2)}) async-start(bf16[4,2,160,256]{3,2,1,0:T(8,128)(2,1)} %broadcast_in_dim.176), calls=%async_computation.7 | async-start | bytes 1310720 | tf_op jit(solution)/shard_map/all_to_all | solution.py:43
  294.6 4.0 copy-start
  358.7 13.3 %copy-start.3 = (f32[4096]{0:T(1024)S(1)}, f32[4096]{0:T(1024)}, u32[]{:S(2)}) copy-start(f32[4096]{0:T(1024)} %param.25) | copy-start | bytes 49156
  372.0 4.0 copy-start.1
  394.0 27.9 %copy-start.16 = (f32[4096]{0:T(1024)S(1)}, f32[4096]{0:T(1024)}, u32[]{:S(2)}) copy-start(f32[4096]{0:T(1024)} %param.29) | copy-start | bytes 49156
  395.0 26.4 %all-to-all-start.14 = ((bf16[8,4,4096]{2,1,0:T(4,128)(2,1)}), bf16[8,4,4096]{2,1,0:T(4,128)(2,1)S(1)}, u32[]{:S(2)}, u32[]{:S(2)}) async-start(bf16[8,4,4096]{2,1,0:T(4,128)(2,1)} %reshape.294), calls=%async_computation.14 | async-start | bytes 524288 | tf_op jit(solution)/shard_map/all_to_all | solution.py:406
  (5 other events, 8.2 us)
Sparse Core Ops, SparseCore 0:
  11.3 203.2 all-gather.1

commit v3 on v2

--- a/solution.py
+++ b/solution.py
@@ -1,3 +1,4 @@
+import functools
 import math
 
 import jax
@@ -50,6 +51,15 @@
     a = copies_to_all(a, "y", NY)
     a = copies_to_all(a, "core", NCORE)
     return a.reshape((N_SEQ,) + a.shape[3:])
+
+
+def own_first(blocks, zh, core):
+    by_zh = [
+        [jnp.where(zh == 0, blocks[i][j], blocks[1 - i][j]) for j in range(2)] for i in range(2)
+    ]
+    return [
+        [jnp.where(core == 0, by_zh[i][j], by_zh[i][1 - j]) for j in range(2)] for i in range(2)
+    ]
 
 
 def seq_slot(s):
@@ -120,13 +130,16 @@
     return block[:, :HD], level
 
 
-def merge_and_project(control, own, new_part, returned, later):
+def merge_and_project(control, own, new_part, returned, weights):
     own_out, own_level = own
     new_out, new_level = new_part
     width = own_out.shape[1]
-    blocks = later.shape[0] // width
-
-    def kernel(c_ref, own_ref, own_l_ref, new_ref, new_l_ref, back_ref, w_ref, out_ref, att_ref):
+    count, part, _ = weights[0].shape
+    halves = part // width
+    blocks = len(weights) * count * halves
+
+    def kernel(c_ref, own_ref, own_l_ref, new_ref, new_l_ref, back_ref, *refs):
+        weight_refs, (out_ref, att_ref) = refs[:-2], refs[-2:]
         remote, remote_level = unpack(back_ref[c_ref[0], :SEL, :])
         remote_level = jnp.where(c_ref[4] == 1, MASKED, remote_level)
         att_ref[:SEL, :] = merge([(own_ref[...], own_l_ref[...]), (remote, remote_level)])
@@ -136,17 +149,18 @@
             parts.append(unpack(back_ref[c_ref[1 + i], pl.ds(at, TOKN_DEV), :]))
         att_ref[SEL:, :] = merge(parts)
         attention = att_ref[...].astype(bf16)
-        for b in range(blocks):
-            out_ref[b] = lax.dot_general(
-                attention,
-                w_ref[b * width : (b + 1) * width, :],
-                (((1,), (1,)), ((), ())),
-                preferred_element_type=f32,
-            ).astype(bf16)
+        for j, ref in enumerate(weight_refs):
+            for n in range(count):
+                term = lax.dot_general(
+                    attention, ref[n], (((1,), (1,)), ((), ())), preferred_element_type=f32
+                ).astype(bf16)
+                for h in range(halves):
+                    out_ref[(j * count + n) * halves + h] = term[:, h * width : (h + 1) * width]
 
     def whole(a):
         return pl.BlockSpec(a.shape, lambda i: (0,) * a.ndim)
 
+    out_weights = pl.BlockSpec((count, part, width), lambda i: (0, 0, 3))
     return pl.pallas_call(
         kernel,
         grid=(1,),
@@ -158,25 +172,30 @@
             whole(new_out),
             whole(new_level),
             whole(returned),
-            pl.BlockSpec((later.shape[0], width), lambda i: (0, 0)),
-        ],
+        ]
+        + [out_weights] * len(weights),
         out_specs=pl.BlockSpec((blocks, ROW_DEV, width), lambda i: (0, 0, 0)),
         scratch_shapes=[pltpu.VMEM((ROW_DEV, width), f32)],
         compiler_params=pltpu.CompilerParams(vmem_limit_bytes=24 << 20),
         name="merge_and_project",
-    )(control, own_out, own_level, new_out, new_level, returned, later)
-
-
-def feed_forward(summed, hidden, gain, later, width, units):
+    )(control, own_out, own_level, new_out, new_level, returned, *weights)
+
+
+def feed_forward(summed, hidden, gain, parcels, units):
     blocks, rows, part = summed.shape
     model = blocks * part
-    steps = 8
-    chunk = model // steps
+    count, _, depth = parcels[0].shape
+    group = 2
+    half = count // group
+    parts = len(parcels)
+    steps = parts * half
+    chunk = group * depth
     each = chunk // part
-    down_from, gate_from = width, width + units
     per = rows // (NZL * NX)
 
-    def kernel(s_ref, x_ref, g_ref, w_ref, out_ref, mixed_ref, norm_ref, acc_ref, down_ref):
+    def kernel(s_ref, x_ref, g_ref, *refs):
+        within_refs, down_refs = refs[:parts], refs[parts : 2 * parts]
+        out_ref, mixed_ref, norm_ref, gate_ref, up_ref = refs[2 * parts :]
         k = pl.program_id(0)
 
         @pl.when(k == 0)
@@ -188,7 +207,8 @@
             norm_ref[...] = lax.rsqrt(
                 jnp.sum(squares, axis=1, keepdims=True) / model + EPSILON
             )
-            acc_ref[...] = jnp.zeros_like(acc_ref)
+            gate_ref[...] = jnp.zeros_like(gate_ref)
+            up_ref[...] = jnp.zeros_like(up_ref)
 
         for j in range(each):
             cols = slice(j * part, (j + 1) * part)
@@ -196,27 +216,37 @@
                 x_ref[:, cols].astype(f32)
                 + s_ref[k * each + j].astype(f32) * norm_ref[...] * g_ref[:, cols]
             ).astype(bf16)
-        acc_ref[...] += jnp.dot(
-            mixed_ref[...], w_ref[:, gate_from:], preferred_element_type=f32
-        )
-        down_ref[k] = w_ref[:, down_from:gate_from]
+
+        def add(ref):
+            for n in range(group):
+                mixed = mixed_ref[:, n * depth : (n + 1) * depth]
+
+                def product(weight):
+                    return lax.dot_general(
+                        mixed, weight, (((1,), (1,)), ((), ())), preferred_element_type=f32
+                    )
+
+                gate_ref[...] += product(ref[n, :units])
+                up_ref[...] += product(ref[n, units:])
+
+        for j in range(parts):
+            pl.when(k // half == j)(functools.partial(add, within_refs[j]))
 
         @pl.when(k == steps - 1)
         def _():
-            gate, up = acc_ref[:, :units], acc_ref[:, units:]
-            activation = (gate / (1.0 + jnp.exp(-gate)) * up).astype(bf16)
             to = lax.broadcasted_iota(jnp.int32, (rows, rows), 0)
             at = lax.broadcasted_iota(jnp.int32, (rows, rows), 1)
             source = (to // per) % NZL * (NX * per) + to // (NZL * per) * per + to % per
             move = jnp.where(at == source, 1.0, 0.0).astype(bf16)
-            activation = jnp.dot(move, activation, preferred_element_type=f32).astype(bf16)
-            for c in range(steps):
-                out_ref[:, c * chunk : (c + 1) * chunk] = lax.dot_general(
-                    activation,
-                    down_ref[c],
-                    (((1,), (1,)), ((), ())),
-                    preferred_element_type=f32,
-                ).astype(bf16)
+            gate = gate_ref[...]
+            active = (gate / (1.0 + jnp.exp(-gate)) * up_ref[...]).astype(bf16)
+            active = jnp.dot(move, active, preferred_element_type=f32).astype(bf16)
+            for j in range(parts):
+                for n in range(count):
+                    at_col = (j * count + n) * depth
+                    out_ref[:, at_col : at_col + depth] = jnp.dot(
+                        active, down_refs[j][n], preferred_element_type=f32
+                    ).astype(bf16)
 
     return pl.pallas_call(
         kernel,
@@ -226,23 +256,30 @@
             jax.ShapeDtypeStruct((rows, model), bf16),
         ),
         in_specs=[
-            pl.BlockSpec((blocks, rows, part), lambda k: (0, 0, 0)),
+            pl.BlockSpec(summed.shape, lambda k: (0, 0, 0)),
             pl.BlockSpec((rows, chunk), lambda k: (0, k)),
             pl.BlockSpec((1, chunk), lambda k: (0, k)),
-            pl.BlockSpec((chunk, later.shape[1]), lambda k: (k, 0)),
-        ],
+        ]
+        + [
+            pl.BlockSpec(
+                (group, 2 * units, depth),
+                lambda k, j=j: (jnp.clip(k - j * half, 0, half - 1), 0, 0),
+            )
+            for j in range(parts)
+        ]
+        + [pl.BlockSpec((count, units, depth), lambda k: (0, 2, 0))] * parts,
         out_specs=(
             pl.BlockSpec((rows, model), lambda k: (0, 0)),
             pl.BlockSpec((rows, chunk), lambda k: (0, k)),
         ),
         scratch_shapes=[
             pltpu.VMEM((rows, 1), f32),
-            pltpu.VMEM((rows, 2 * units), f32),
-            pltpu.VMEM((steps, chunk, units), bf16),
+            pltpu.VMEM((rows, units), f32),
+            pltpu.VMEM((rows, units), f32),
         ],
-        compiler_params=pltpu.CompilerParams(vmem_limit_bytes=32 << 20),
+        compiler_params=pltpu.CompilerParams(vmem_limit_bytes=40 << 20),
         name="feed_forward",
-    )(summed, hidden, gain, later)
+    )(summed, hidden, gain, *parcels, *parcels)
 
 
 def shards(
@@ -275,23 +312,9 @@
     model = hidden_states.shape[1]
     depth = query_weight.shape[0]
 
-    pad = (-hidden_units) % 128
-    later = lax.all_gather(
-        jnp.concatenate(
-            [
-                output_weight.T,
-                jnp.pad(down_weight.T, ((0, 0), (0, pad))),
-                jnp.pad(gate_weight, ((0, 0), (0, pad))),
-                jnp.pad(up_weight, ((0, 0), (0, pad))),
-            ],
-            axis=1,
-        ),
-        SEQ,
-        axis=0,
-        tiled=True,
-    )
-
-    mine = jnp.concatenate([query_weight, key_weight, value_weight], axis=1)
+    mine = jnp.concatenate([query_weight, key_weight, value_weight, output_weight.T], axis=1)
+    parcel = jnp.concatenate([gate_weight.T, up_weight.T, down_weight])
+    parcel = jnp.pad(parcel, ((0, -parcel.shape[0] % 16), (0, 0)))
     theirs = swap(mine, "zh", NZH)
     starts, owners, positions, new_live = layout(
         passage_order, separators, recompute_index, prompt_lengths
@@ -307,25 +330,22 @@
     theirs, cosine, sine, moved = lax.optimization_barrier((theirs, cosine, sine, moved))
     near_other = swap(near, "core", NCORE)
     far = copies_to_all(theirs, "y", NY)
+    far, parcel = lax.optimization_barrier((far, parcel))
     far_other = swap(far, "core", NCORE)
+    parcel_near = lax.all_gather(parcel, "y")
 
     columns = hidden_states.reshape(ROW_DEV, NY, NZH, NCORE, depth)
-
-    def block(i, j):
-        return columns[:, :, i, j].reshape(ROW_DEV, NY * depth)
-
-    by_zh = [
-        [jnp.where(zh == 0, block(i, j), block(1 - i, j)) for j in range(2)] for i in range(2)
-    ]
-    picked_x = [
-        [jnp.where(core == 0, by_zh[i][j], by_zh[i][1 - j]) for j in range(2)] for i in range(2)
-    ]
+    ours = own_first(
+        [[columns[:, :, i, j].reshape(ROW_DEV, NY * depth) for j in range(2)] for i in range(2)],
+        zh,
+        core,
+    )
 
     def product(x, w):
-        return jnp.dot(x, w.reshape(NY * depth, 3 * width), preferred_element_type=f32)
-
-    raw = product(picked_x[0][0], near) + product(picked_x[0][1], near_other)
-    raw = raw + product(picked_x[1][0], far) + product(picked_x[1][1], far_other)
+        return jnp.dot(x, w.reshape(NY * depth, 4 * width), preferred_element_type=f32)
+
+    raw = product(ours[0][0], near) + product(ours[0][1], near_other)
+    raw = raw + product(ours[1][0], far) + product(ours[1][1], far_other)
     query_raw, key_raw, value_raw = (raw[:, i * width : (i + 1) * width] for i in range(3))
 
     squares = jnp.stack(
@@ -335,6 +355,8 @@
         jnp.broadcast_to(squares[None], (NZL * NX,) + squares.shape), BLK, 0, 0, tiled=True
     )
     squares = jnp.sum(squares, axis=0)
+    squares, parcel = lax.optimization_barrier((squares, parcel))
+    pair = lax.all_gather(parcel, "zh")
     scale = lax.rsqrt(squares / model + EPSILON)
     query = rotate(query_raw * scale[0][:, None] * query_gain, cosine, sine).astype(bf16)
     key = rotate(key_raw * scale[1][:, None] * key_gain, cosine, sine).astype(bf16)
@@ -377,7 +399,9 @@
         (new_at[None, :] <= my_positions[SEL:][:, None]) & live[None, :],
     )
 
-    returned = gather_seq(pack(part[SEL:], level[SEL:]))
+    returned = copies_to_all(pack(part[SEL:], level[SEL:]), "zh", NZH)
+    returned = copies_to_all(returned, "y", NY)
+    returned = copies_to_all(returned, "core", NCORE).reshape(N_SEQ, -1, 2 * width)
     first = chosen[0] == seq
     own = (
         jnp.where(first, part[:SEL], part[SEL : 2 * SEL]),
@@ -389,7 +413,9 @@
     ).astype(jnp.int32)
 
     blocks = NX * NZL
-    terms = merge_and_project(control, own, new_part, returned, later)
+    terms = merge_and_project(control, own, new_part, returned, [near, near_other, far, far_other])
+    terms, pair = lax.optimization_barrier((terms, pair))
+    parcel_far = lax.all_gather(jnp.where(zh == 0, pair[1], pair[0]), "y")
     terms = lax.all_to_all(terms.reshape(NX, NZL, ROW_DEV, width), "x", 0, 0, tiled=True)
     terms = jnp.sum(terms.astype(f32), axis=0).astype(bf16)
     terms = lax.all_to_all(terms, "zl", 0, 0, tiled=True)
@@ -398,8 +424,20 @@
     summed = copies_to_all(summed, "x", NX).reshape(blocks, ROW_DEV, model // blocks)
 
     rows = ROW_DEV // blocks
+    parcels = [parcel_near, swap(parcel_near, "core", NCORE)]
+    parcels += [parcel_far, swap(parcel_far, "core", NCORE)]
+
+    def own_order(a):
+        a = a.reshape(NY, NZH, NCORE, depth)
+        a = own_first([[a[:, i, j].reshape(1, -1) for j in range(2)] for i in range(2)], zh, core)
+        return jnp.concatenate(a[0] + a[1], axis=1)
+
     terms, mixed = feed_forward(
-        summed, hidden_states, attention_gain[None], later, width, hidden_units + pad
+        summed,
+        jnp.concatenate(ours[0] + ours[1], axis=1),
+        own_order(attention_gain),
+        parcels,
+        hidden_units,
     )
     terms = lax.all_to_all(terms.reshape(NX, NZL * rows, model), "x", 0, 0, tiled=True)
     terms = jnp.sum(terms.astype(f32), axis=0).astype(bf16)
@@ -407,7 +445,10 @@
     total = jnp.sum(terms.astype(f32), axis=0)
     norm = lax.rsqrt(jnp.mean(total * total, axis=1, keepdims=True) + EPSILON)
     my_rows = lax.dynamic_slice_in_dim(mixed, (zl * NX + x_at) * rows, rows, 0)
-    hidden_out = (my_rows.astype(f32) + total * norm * feedforward_gain).astype(bf16)
+    final = my_rows.astype(f32) + total * norm * own_order(feedforward_gain)
+    final = final.astype(bf16).reshape(rows, NZH * NCORE, NY, 1, depth)
+    final = own_first([[final[:, 2 * i + j] for j in range(2)] for i in range(2)], zh, core)
+    hidden_out = jnp.concatenate(final[0] + final[1], axis=2).reshape(rows, model)
     return (hidden_out, passage_keys[None], passage_values[None])
 
 

time: 431 us -> 380 us (0.88)
  waiting for transfers between devices: 170 us -> 101 us
  blocking collectives: 93.6 us -> 41.8 us
  local copies, waits for them, and re-layouts: 23.7 us -> 50 us
  other arithmetic: 9.97 us -> 34 us
  starting transfers between devices: 90.1 us -> 101 us
    all_to_all x1, waiting for transfers between devices: 94.6 us -> 0.01 us  [shards(): lax.all_to_all(jnp.broadcast_to(squares[None], (NZL * NX,) + squares.shap...]
    all_to_all x4 -> x2, blocking collectives: 43.4 us -> 8.94 us  [copies_to_all(): lax.all_to_all(jnp.broadcast_to(a[None], (count,) + a.shape), axis, 0, 0,...]
    all_to_all x6 -> x8, waiting for transfers between devices: 48.4 us -> 76.4 us  [copies_to_all(): lax.all_to_all(jnp.broadcast_to(a[None], (count,) + a.shape), axis, 0, 0,...]
    all_to_all x1 -> x0, blocking collectives: 18.8 us -> none  [shards(): terms = lax.all_to_all(terms, 'zl', 0, 0, tiled=True)]
    all_to_all x0 -> x1, starting transfers between devices: none -> 13 us  [shards(): terms = lax.all_to_all(terms, 'zl', 0, 0, tiled=True)]
    ppermute x4 -> x6, waiting for transfers between devices: 13 us -> 0.02 us  [swap(): return lax.ppermute(a, axis, [(i, i ^ 1) for i in range(count)])]
    all_to_all x0 -> x1, waiting for transfers between devices: none -> 7.97 us  [shards(): terms = lax.all_to_all(terms, 'zl', 0, 0, tiled=True)]
    broadcast_in_dim x10, local copies, waits for them, and re-layouts: 5.33 us -> 11.3 us  [copies_to_all(): jnp.broadcast_to(a[None], (count,) + a.shape)]
  transfers between devices with their start and end apart: 13 -> 20, of which waited for: 8 -> 10; matrix products, arithmetic and copies ran while one was open for 6% -> 19% of each run, Pallas kernels for 0% -> 0%
where the time goes in v3:
time: 380 us; the launch traced here: 376 us
  starting transfers between devices  101 us (27%)
  waiting for transfers between devices  101 us (27%)
  local copies, waits for them, and re-layouts  50 us (13%)
  blocking collectives  41.8 us (11%)
  other arithmetic  34 us (9%)
  between operations  32.3 us (8%)
  Pallas kernels  10 us (3%)
  matrix products  6.19 us (2%)
    all_to_all x8, waiting for transfers between devices, copies_to_all(): lax.all_to_all(jnp.broadcast_to(a[None], (count,) + a.shape), axis, 0, 0,...  76.4 us
    all_to_all x8, starting transfers between devices, copies_to_all(): lax.all_to_all(jnp.broadcast_to(a[None], (count,) + a.shape), axis, 0, 0,...  39.5 us
    ppermute x6, starting transfers between devices, swap(): return lax.ppermute(a, axis, [(i, i ^ 1) for i in range(count)])  24.5 us
    all_to_all x1, blocking collectives, shards(): lax.all_to_all(terms.reshape(NX, NZL, ROW_DEV, width), 'x', 0, 0, tiled=T...  19.4 us
    unnamed x94, local copies, waits for them, and re-layouts  15.9 us
    all_to_all x1, waiting for transfers between devices, shards(): lax.all_to_all(terms.reshape(NZL, rows, model), 'zl', 0, 0, tiled=True)  13.6 us
    all_to_all x1, blocking collectives, shards(): lax.all_to_all(terms.reshape(NX, NZL * rows, model), 'x', 0, 0, tiled=True)  13.4 us
    all_to_all x1, starting transfers between devices, shards(): terms = lax.all_to_all(terms, 'zl', 0, 0, tiled=True)  13 us
  transfers between devices with their start and end apart: 20, of which 10 were waited for; matrix products, arithmetic and copies ran while one was open for 19% of the time, Pallas kernels for 0%

profile of v3, /device:TPU:32, one launch (start us, length us, event | category | flops | bytes accessed | tf_op | source)
XLA Modules:
  0.0 376.3 jit_solution(15403633809265104030)
XLA Ops:
  12.6 15.0 %collective-permute-start.1 = (bf16[256,512]{0,1:T(8,128)(2,1)S(1)}, bf16[256,512]{0,1:T(8,128)(2,1)}, u32[]{:S(2)}, u32[]{:S(2)}) collective-permute-start(bf16[256,512]{0,1:T(8,128)(2,1)S(1)} %pad_maximum_fusion.1), channel_id=1, source_target_pairs={{0,64},{64,0},{1,65},{65,1},{2,66},{66,2},{3,67},{67,3},{4,68},{68... | collective-permute-start | bytes 786440 | tf_op jit(solution)/shard_map/ppermute | solution.py:70
  28.8 4.6 %all-to-all-start = ((bf16[4,256,512]{2,1,0:T(8,128)(2,1)}), bf16[4,256,512]{2,1,0:T(8,128)(2,1)S(1)}, u32[]{:S(2)}, u32[]{:S(2)}) async-start(bf16[4,256,512]{2,1,0:T(8,128)(2,1)} %broadcast_in_dim.81), calls=%async_computation | async-start | bytes 2097152 | tf_op jit(solution)/shard_map/all_to_all | solution.py:44
  47.2 2.3 fusion.64
  53.4 4.8 %all-to-all-start.1 = ((bf16[4,256,512]{2,1,0:T(8,128)(2,1)}), bf16[4,256,512]{2,1,0:T(8,128)(2,1)S(1)}, u32[]{:S(2)}, u32[]{:S(2)}) async-start(bf16[4,256,512]{2,1,0:T(8,128)(2,1)} %broadcast_in_dim.82), calls=%async_computation.1 | async-start | bytes 2097152 | tf_op jit(solution)/shard_map/all_to_all | solution.py:44
  58.8 2.7 broadcast_select_fusion.4
  64.8 7.6 %all-to-all-done.1.refs_2_ = bf16[4,256,512]{2,1,0:T(8,128)(2,1)S(1)} async-done(((bf16[4,256,512]{2,1,0:T(8,128)(2,1)}), bf16[4,256,512]{2,1,0:T(8,128)(2,1)S(1)}, u32[]{:S(2)}, u32[]{:S(2)}) %all-to-all-start.1) | async-done | bytes 1048608 | tf_op jit(solution)/shard_map/all_to_all | solution.py:44
  82.7 10.9 %all-to-all-start.2 = ((f32[32,2,128]{2,1,0:T(2,128)}), f32[32,2,128]{2,1,0:T(2,128)}, u32[]{:S(2)}, u32[]{:S(2)}) async-start(f32[32,2,128]{2,1,0:T(2,128)} %broadcast_in_dim.83), calls=%async_computation.2 | async-start | bytes 65536 | tf_op jit(solution)/shard_map/all_to_all | solution.py:354
  111.0 2.6 scatter_custom_fusion.1
  119.0 8.5 %all-to-all-start.3 = ((bf16[2,128,128]{2,1,0:T(8,128)(2,1)}), bf16[2,128,128]{2,1,0:T(8,128)(2,1)S(1)}, u32[]{:S(2)}, u32[]{:S(2)}) async-start(bf16[2,128,128]{2,1,0:T(8,128)(2,1)} %broadcast_in_dim.84), calls=%async_computation.3 | async-start | bytes 131072 | tf_op jit(solution)/shard_map/all_to_all | solution.py:44
  127.5 2.8 scatter_custom_fusion
  130.9 15.0 %all-to-all-done.3 = bf16[2,128,128]{2,1,0:T(8,128)(2,1)S(1)} async-done(((bf16[2,128,128]{2,1,0:T(8,128)(2,1)}), bf16[2,128,128]{2,1,0:T(8,128)(2,1)S(1)}, u32[]{:S(2)}, u32[]{:S(2)}) %all-to-all-start.3) | async-done | bytes 65568 | tf_op jit(solution)/shard_map/all_to_all | solution.py:44
  146.7 4.3 %all-to-all-start.4 = ((bf16[4,2,128,128]{3,2,1,0:T(8,128)(2,1)}), bf16[4,2,128,128]{3,2,1,0:T(8,128)(2,1)}, u32[]{:S(2)}, u32[]{:S(2)}) async-start(bf16[4,2,128,128]{3,2,1,0:T(8,128)(2,1)} %broadcast_in_dim.85), calls=%async_computation.4 | async-start | bytes 524288 | tf_op jit(solution)/shard_map/all_to_all | solution.py:44
  153.5 4.3 %all-to-all-done.4 = bf16[4,2,128,128]{3,2,1,0:T(8,128)(2,1)} async-done(((bf16[4,2,128,128]{3,2,1,0:T(8,128)(2,1)}), bf16[4,2,128,128]{3,2,1,0:T(8,128)(2,1)}, u32[]{:S(2)}, u32[]{:S(2)}) %all-to-all-start.4) | async-done | bytes 262176 | tf_op jit(solution)/shard_map/all_to_all | solution.py:44
  158.8 4.2 %all_to_all.75 = bf16[2,4,2,128,128]{4,3,2,1,0:T(8,128)(2,1)S(1)} all-to-all(bf16[2,4,2,128,128]{4,3,2,1,0:T(8,128)(2,1)S(1)} %broadcast_in_dim.86), channel_id=1, replica_groups=mesh['y'=4,'zh'=2,'core'=2,'zl'=8,'x'=4] {'core'}, dimensions={0} | all-to-all | bytes 1048576 | tf_op jit(solution)/shard_map/all_to_all | solution.py:44
  174.8 4.1 %all-to-all-start.6 = ((bf16[2,160,256]{2,1,0:T(8,128)(2,1)}), bf16[2,160,256]{2,1,0:T(8,128)(2,1)}, u32[]{:S(2)}, u32[]{:S(2)}) async-start(bf16[2,160,256]{2,1,0:T(8,128)(2,1)} %broadcast_in_dim.171), calls=%async_computation.6 | async-start | bytes 327680 | tf_op jit(solution)/shard_map/all_to_all | solution.py:44
  183.6 8.9 %all-to-all-done.6 = bf16[2,160,256]{2,1,0:T(8,128)(2,1)} async-done(((bf16[2,160,256]{2,1,0:T(8,128)(2,1)}), bf16[2,160,256]{2,1,0:T(8,128)(2,1)}, u32[]{:S(2)}, u32[]{:S(2)}) %all-to-all-start.6) | async-done | bytes 163872 | tf_op jit(solution)/shard_map/all_to_all | solution.py:44
  194.2 4.2 %all-to-all-start.7 = ((bf16[4,2,160,256]{3,2,1,0:T(8,128)(2,1)}), bf16[4,2,160,256]{3,2,1,0:T(8,128)(2,1)}, u32[]{:S(2)}, u32[]{:S(2)}) async-start(bf16[4,2,160,256]{3,2,1,0:T(8,128)(2,1)} %broadcast_in_dim.172), calls=%async_computation.7 | async-start | bytes 1310720 | tf_op jit(solution)/shard_map/all_to_all | solution.py:44
  201.1 16.1 %all-to-all-done.7 = bf16[4,2,160,256]{3,2,1,0:T(8,128)(2,1)} async-done(((bf16[4,2,160,256]{3,2,1,0:T(8,128)(2,1)}), bf16[4,2,160,256]{3,2,1,0:T(8,128)(2,1)}, u32[]{:S(2)}, u32[]{:S(2)}) %all-to-all-start.7) | async-done | bytes 655392 | tf_op jit(solution)/shard_map/all_to_all | solution.py:44
  218.5 4.8 %all_to_all.76 = bf16[2,4,2,160,256]{4,3,2,1,0:T(8,128)(2,1)S(1)} all-to-all(bf16[2,4,2,160,256]{4,3,2,1,0:T(8,128)(2,1)S(1)} %broadcast_in_dim.173), channel_id=1, replica_groups=mesh['y'=4,'zh'=2,'core'=2,'zl'=8,'x'=4] {'core'}, dimensions={0} | all-to-all | bytes 2621440 | tf_op jit(solution)/shard_map/all_to_all | solution.py:44
  227.6 19.4 %all_to_all.77 = bf16[4,8,128,128]{3,2,1,0:T(8,128)(2,1)S(1)} all-to-all(bf16[4,8,128,128]{3,2,1,0:T(8,128)(2,1)S(1)} %bitcast.190), channel_id=1, replica_groups=mesh['y'=4,'zh'=2,'core'=2,'zl'=8,'x'=4] {'x'}, dimensions={0} | all-to-all | bytes 2097152 | tf_op jit(solution)/shard_map/all_to_all | solution.py:419
  248.0 13.0 %all-to-all-start.10 = ((bf16[8,128,128]{2,1,0:T(8,128)(2,1)}), bf16[8,128,128]{2,1,0:T(8,128)(2,1)S(1)}, u32[]{:S(2)}, u32[]{:S(2)}) async-start(bf16[8,128,128]{2,1,0:T(8,128)(2,1)} %reduce_sum.130), calls=%async_computation.10 | async-start | bytes 524288 | tf_op jit(solution)/shard_map/all_to_all | solution.py:421
  262.9 3.3 all-gather.6.cloned.1.call-done.refs_2_.refs_6_
  268.2 8.0 %all-to-all-done.10 = bf16[8,128,128]{2,1,0:T(8,128)(2,1)S(1)} async-done(((bf16[8,128,128]{2,1,0:T(8,128)(2,1)}), bf16[8,128,128]{2,1,0:T(8,128)(2,1)S(1)}, u32[]{:S(2)}, u32[]{:S(2)}) %all-to-all-start.10) | async-done | bytes 262176 | tf_op jit(solution)/shard_map/all_to_all | solution.py:421
  276.9 5.5 %all-to-all-start.11 = ((bf16[8,128,128]{2,1,0:T(8,128)(2,1)}), bf16[8,128,128]{2,1,0:T(8,128)(2,1)S(1)}, u32[]{:S(2)}, u32[]{:S(2)}) async-start(bf16[8,128,128]{2,1,0:T(8,128)(2,1)} %broadcast_in_dim.174), calls=%async_computation.11 | async-start | bytes 524288 | tf_op jit(solution)/shard_map/all_to_all | solution.py:44
  282.4 15.8 %all-to-all-done.11 = bf16[8,128,128]{2,1,0:T(8,128)(2,1)S(1)} async-done(((bf16[8,128,128]{2,1,0:T(8,128)(2,1)}), bf16[8,128,128]{2,1,0:T(8,128)(2,1)S(1)}, u32[]{:S(2)}, u32[]{:S(2)}) %all-to-all-start.11) | async-done | bytes 262176 | tf_op jit(solution)/shard_map/all_to_all | solution.py:44
  299.4 3.6 all-to-all-start.12
  303.1 2.1 pad_maximum_fusion.x_ref
  305.3 8.7 %all-to-all-done.12 = bf16[4,8,128,128]{3,2,1,0:T(8,128)(2,1)S(1)} async-done(((bf16[4,8,128,128]{3,2,1,0:T(8,128)(2,1)}), bf16[4,8,128,128]{3,2,1,0:T(8,128)(2,1)S(1)}, u32[]{:S(2)}, u32[]{:S(2)}) %all-to-all-start.12) | async-done | bytes 1048608 | tf_op jit(solution)/shard_map/all_to_all | solution.py:44
  316.8 8.9 %feed_forward.1 = (bf16[128,4096]{1,0:T(8,128)(2,1)S(1)}, bf16[128,4096]{1,0:T(8,128)(2,1)S(1)}) custom-call(bf16[32,128,128]{2,1,0:T(8,128)(2,1)S(1)} %bitcast.192, bf16[128,4096]{1,0:T(8,128)(2,1)S(1)} %copy-done.6, f32[1,4096]{1,0:T(1,128)S(1)} %pad_maximum_fusion.7.g_ref, bf16[4,1040,256]{2,1,0:T(8,128)(2,1)S(1)} %bitcast.186, ...), custom_call_target="tpu_custom_call" | custom-call | tf_op jit(solution)/shard_map/feed_forward/pallas_call | solution.py:251
  326.7 13.4 %all_to_all.78 = bf16[4,32,4096]{2,1,0:T(8,128)(2,1)S(1)} all-to-all(bf16[4,32,4096]{2,1,0:T(8,128)(2,1)S(1)} %bitcast.193), channel_id=1, replica_groups=mesh['y'=4,'zh'=2,'core'=2,'zl'=8,'x'=4] {'x'}, dimensions={0} | all-to-all | bytes 2097152 | tf_op jit(solution)/shard_map/all_to_all | solution.py:442
  341.2 12.7 %all-to-all-start.14 = ((bf16[8,4,4096]{2,1,0:T(4,128)(2,1)}), bf16[8,4,4096]{2,1,0:T(4,128)(2,1)S(1)}, u32[]{:S(2)}, u32[]{:S(2)}) async-start(bf16[8,4,4096]{2,1,0:T(4,128)(2,1)} %reshape.754), calls=%async_computation.14 | async-start | bytes 524288 | tf_op jit(solution)/shard_map/all_to_all | solution.py:444
  353.9 13.6 %all-to-all-done.14 = bf16[8,4,4096]{2,1,0:T(4,128)(2,1)S(1)} async-done(((bf16[8,4,4096]{2,1,0:T(4,128)(2,1)}), bf16[8,4,4096]{2,1,0:T(4,128)(2,1)S(1)}, u32[]{:S(2)}, u32[]{:S(2)}) %all-to-all-start.14) | async-done | bytes 262176 | tf_op jit(solution)/shard_map/all_to_all | solution.py:444
  (233 shorter events, 88.4 us)
Async XLA Ops:
  12.5 20.9 %copy-start.40 = (s32[8,2]{0,1:T(2,128)S(1)}, s32[8,2]{0,1:T(2,128)}, u32[]{:S(2)}) copy-start(s32[8,2]{0,1:T(2,128)} %param.33) | copy-start | bytes 196
  12.5 21.2 %copy-start.39 = (s32[16]{0:T(128)S(1)}, s32[16]{0:T(128)}, u32[]{:S(2)}) copy-start(s32[16]{0:T(128)} %param.32) | copy-start | bytes 196
  12.6 28.5 %copy-start.32 = (s32[16,96]{1,0:T(8,128)S(1)}, s32[16,96]{1,0:T(8,128)}, u32[]{:S(2)}) copy-start(s32[16,96]{1,0:T(8,128)} %param.34) | copy-start | bytes 18436
  12.6 29.4 %copy-start.23 = (bf16[1,1024,128]{2,1,0:T(8,128)(2,1)S(1)}, bf16[1,1024,128]{2,1,0:T(8,128)(2,1)}, u32[]{:S(2)}) copy-start(bf16[1,1024,128]{2,1,0:T(8,128)(2,1)} %param.30) | copy-start | bytes 786436
  12.6 38.6 %collective-permute-start.1 = (bf16[256,512]{0,1:T(8,128)(2,1)S(1)}, bf16[256,512]{0,1:T(8,128)(2,1)}, u32[]{:S(2)}, u32[]{:S(2)}) collective-permute-start(bf16[256,512]{0,1:T(8,128)(2,1)S(1)} %pad_maximum_fusion.1), channel_id=1, source_target_pairs={{0,64},{64,0},{1,65},{65,1},{2,66},{66,2},{3,67},{67,3},{4,68},{68... | collective-permute-start | bytes 786440 | tf_op jit(solution)/shard_map/ppermute | solution.py:70
  28.8 17.5 %copy-start.13 = (bf16[128,4096]{1,0:T(8,128)(2,1)S(1)}, bf16[128,4096]{1,0:T(8,128)(2,1)}, u32[]{:S(2)}) copy-start(bf16[128,4096]{1,0:T(8,128)(2,1)} %param.18) | copy-start | bytes 3145732
  28.8 23.5 %all-to-all-start = ((bf16[4,256,512]{2,1,0:T(8,128)(2,1)}), bf16[4,256,512]{2,1,0:T(8,128)(2,1)S(1)}, u32[]{:S(2)}, u32[]{:S(2)}) async-start(bf16[4,256,512]{2,1,0:T(8,128)(2,1)} %broadcast_in_dim.81), calls=%async_computation | async-start | bytes 2097152 | tf_op jit(solution)/shard_map/all_to_all | solution.py:44
  53.4 19.1 %all-to-all-start.1 = ((bf16[4,256,512]{2,1,0:T(8,128)(2,1)}), bf16[4,256,512]{2,1,0:T(8,128)(2,1)S(1)}, u32[]{:S(2)}, u32[]{:S(2)}) async-start(bf16[4,256,512]{2,1,0:T(8,128)(2,1)} %broadcast_in_dim.82), calls=%async_computation.1 | async-start | bytes 2097152 | tf_op jit(solution)/shard_map/all_to_all | solution.py:44
  61.5 17.8 %collective-permute-start = (bf16[4,256,512]{2,1,0:T(8,128)(2,1)S(1)}, bf16[4,256,512]{2,1,0:T(8,128)(2,1)S(1)}, u32[]{:S(2)}, u32[]{:S(2)}) collective-permute-start(bf16[4,256,512]{2,1,0:T(8,128)(2,1)S(1)} %all-to-all-done.refs_0_), channel_id=1, source_target_pairs={{0,32},{32,0},{1,33},{33,1},{2,34},{34,2},{3,35},{35,3},{4,36},{36... | collective-permute-start | bytes 3145736 | tf_op jit(solution)/shard_map/ppermute | solution.py:70
  72.5 7.5 %collective-permute-start.2 = (bf16[4,256,512]{2,1,0:T(8,128)(2,1)S(1)}, bf16[4,256,512]{2,1,0:T(8,128)(2,1)S(1)}, u32[]{:S(2)}, u32[]{:S(2)}) collective-permute-start(bf16[4,256,512]{2,1,0:T(8,128)(2,1)S(1)} %all-to-all-done.1.refs_2_), channel_id=1, source_target_pairs={{0,32},{32,0},{1,33},{33,1},{2,34},{34,2},{3,35},{35,3},{4,36},{36... | collective-permute-start | bytes 3145736 | tf_op jit(solution)/shard_map/ppermute | solution.py:70
  82.7 24.0 %all-to-all-start.2 = ((f32[32,2,128]{2,1,0:T(2,128)}), f32[32,2,128]{2,1,0:T(2,128)}, u32[]{:S(2)}, u32[]{:S(2)}) async-start(f32[32,2,128]{2,1,0:T(2,128)} %broadcast_in_dim.83), calls=%async_computation.2 | async-start | bytes 65536 | tf_op jit(solution)/shard_map/all_to_all | solution.py:354
  93.6 131.8 %all-gather.8.cloned.1.call-start = ((), (), s32[]{:S(2)}) async-start(), calls=%async_computation.16 | async-start | bytes 1597440 | tf_op jit(solution)/shard_map/all_gather | solution.py:359
  108.1 152.9 %all-gather.10.cloned.1.call-start = ((), (), s32[]{:S(2)}) async-start(), calls=%async_computation.17 | async-start | bytes 2662400 | tf_op jit(solution)/shard_map/all_gather | solution.py:335
  116.3 46.7 %copy-start.37 = (s32[256]{0:T(256)S(1)}, s32[256]{0:T(256)}, u32[]{:S(2)}) copy-start(s32[256]{0:T(256)} %pad_add_fusion.1) | copy-start | bytes 3076
  116.4 13.9 %collective-permute-start.3 = (bf16[64,128]{1,0:T(8,128)(2,1)S(1)}, bf16[64,128]{1,0:T(8,128)(2,1)S(1)}, u32[]{:S(2)}, u32[]{:S(2)}) collective-permute-start(bf16[64,128]{1,0:T(8,128)(2,1)S(1)} %get-tuple-element.31), channel_id=1, source_target_pairs={{0,32},{32,0},{1,33},{33,1},{2,34},{34,2},{3,35},{35,3},{4,36},{36... | collective-permute-start | bytes 49160 | tf_op jit(solution)/shard_map/ppermute | solution.py:70
  119.0 26.9 %all-to-all-start.3 = ((bf16[2,128,128]{2,1,0:T(8,128)(2,1)}), bf16[2,128,128]{2,1,0:T(8,128)(2,1)S(1)}, u32[]{:S(2)}, u32[]{:S(2)}) async-start(bf16[2,128,128]{2,1,0:T(8,128)(2,1)} %broadcast_in_dim.84), calls=%async_computation.3 | async-start | bytes 131072 | tf_op jit(solution)/shard_map/all_to_all | solution.py:44
  146.7 11.1 %all-to-all-start.4 = ((bf16[4,2,128,128]{3,2,1,0:T(8,128)(2,1)}), bf16[4,2,128,128]{3,2,1,0:T(8,128)(2,1)}, u32[]{:S(2)}, u32[]{:S(2)}) async-start(bf16[4,2,128,128]{3,2,1,0:T(8,128)(2,1)} %broadcast_in_dim.85), calls=%async_computation.4 | async-start | bytes 524288 | tf_op jit(solution)/shard_map/all_to_all | solution.py:44
  169.7 28.8 %copy-start.35 = (f32[32]{0:T(128)S(1)}, f32[32]{0:T(128)}, u32[]{:S(2)}) copy-start(f32[32]{0:T(128)} %copy-done.34) | copy-start | bytes 388
  174.8 17.6 %all-to-all-start.6 = ((bf16[2,160,256]{2,1,0:T(8,128)(2,1)}), bf16[2,160,256]{2,1,0:T(8,128)(2,1)}, u32[]{:S(2)}, u32[]{:S(2)}) async-start(bf16[2,160,256]{2,1,0:T(8,128)(2,1)} %broadcast_in_dim.171), calls=%async_computation.6 | async-start | bytes 327680 | tf_op jit(solution)/shard_map/all_to_all | solution.py:44
  182.8 15.7 %copy-start.29 = (f32[32,64]{1,0:T(8,128)S(1)}, f32[32,64]{1,0:T(8,128)}, u32[]{:S(2)}) copy-start(f32[32,64]{1,0:T(8,128)} %copy-done.28) | copy-start | bytes 24580
  182.8 15.7 %copy-start.33 = (bf16[32,128]{1,0:T(8,128)(2,1)S(1)}, bf16[32,128]{1,0:T(8,128)(2,1)}, u32[]{:S(2)}) copy-start(bf16[32,128]{1,0:T(8,128)(2,1)} %get-tuple-element.84) | copy-start | bytes 24580
  182.8 15.7 %copy-start.42 = (f32[32]{0:T(128)S(1)}, f32[32]{0:T(128)}, u32[]{:S(2)}) copy-start(f32[32]{0:T(128)} %compare_select_fusion.6) | copy-start | bytes 388
  194.2 22.9 %all-to-all-start.7 = ((bf16[4,2,160,256]{3,2,1,0:T(8,128)(2,1)}), bf16[4,2,160,256]{3,2,1,0:T(8,128)(2,1)}, u32[]{:S(2)}, u32[]{:S(2)}) async-start(bf16[4,2,160,256]{3,2,1,0:T(8,128)(2,1)} %broadcast_in_dim.172), calls=%async_computation.7 | async-start | bytes 1310720 | tf_op jit(solution)/shard_map/all_to_all | solution.py:44
  198.4 67.8 %all-gather.6.cloned.1.call-start = ((), (), s32[]{:S(2)}) async-start(), calls=%async_computation.15 | async-start | bytes 2662400 | tf_op jit(solution)/shard_map/all_gather | solution.py:418
  227.6 54.8 %copy-start.30 = (f32[4096]{0:T(1024)S(1)}, f32[4096]{0:T(1024)}, u32[]{:S(2)}) copy-start(f32[4096]{0:T(1024)} %param.25) | copy-start | bytes 49156
  248.0 28.2 %all-to-all-start.10 = ((bf16[8,128,128]{2,1,0:T(8,128)(2,1)}), bf16[8,128,128]{2,1,0:T(8,128)(2,1)S(1)}, u32[]{:S(2)}, u32[]{:S(2)}) async-start(bf16[8,128,128]{2,1,0:T(8,128)(2,1)} %reduce_sum.130), calls=%async_computation.10 | async-start | bytes 524288 | tf_op jit(solution)/shard_map/all_to_all | solution.py:421
  261.0 44.3 %collective-permute-start.4 = (bf16[4,1040,256]{2,1,0:T(8,128)(2,1)}, bf16[4,1040,256]{2,1,0:T(8,128)(2,1)}, u32[]{:S(2)}, u32[]{:S(2)}) collective-permute-start(bf16[4,1040,256]{2,1,0:T(8,128)(2,1)} %bitcast.185), channel_id=1, source_target_pairs={{0,32},{32,0},{1,33},{33,1},{2,34},{34,2},{3,35},{35,3},{4,36},{36... | collective-permute-start | bytes 6389768 | tf_op jit(solution)/shard_map/ppermute | solution.py:70
  266.3 47.7 %collective-permute-start.5 = (bf16[4,1040,256]{2,1,0:T(8,128)(2,1)}, bf16[4,1040,256]{2,1,0:T(8,128)(2,1)}, u32[]{:S(2)}, u32[]{:S(2)}) collective-permute-start(bf16[4,1040,256]{2,1,0:T(8,128)(2,1)} %all-gather.6.cloned.1.call-done.refs_2_.refs_6_), channel_id=1, source_target_pairs={{0,32},{32,0},{1,33},{33,1},{2,34},{34,2},{3,35},{35,3},{4,36},{36... | collective-permute-start | bytes 6389768 | tf_op jit(solution)/shard_map/ppermute | solution.py:70
  276.9 21.3 %all-to-all-start.11 = ((bf16[8,128,128]{2,1,0:T(8,128)(2,1)}), bf16[8,128,128]{2,1,0:T(8,128)(2,1)S(1)}, u32[]{:S(2)}, u32[]{:S(2)}) async-start(bf16[8,128,128]{2,1,0:T(8,128)(2,1)} %broadcast_in_dim.174), calls=%async_computation.11 | async-start | bytes 524288 | tf_op jit(solution)/shard_map/all_to_all | solution.py:44
  299.4 14.5 %all-to-all-start.12 = ((bf16[4,8,128,128]{3,2,1,0:T(8,128)(2,1)}), bf16[4,8,128,128]{3,2,1,0:T(8,128)(2,1)S(1)}, u32[]{:S(2)}, u32[]{:S(2)}) async-start(bf16[4,8,128,128]{3,2,1,0:T(8,128)(2,1)} %broadcast_in_dim.175), calls=%async_computation.12 | async-start | bytes 2097152 | tf_op jit(solution)/shard_map/all_to_all | solution.py:44
  326.7 27.1 %copy-start.31 = (f32[4096]{0:T(1024)S(1)}, f32[4096]{0:T(1024)}, u32[]{:S(2)}) copy-start(f32[4096]{0:T(1024)} %param.29) | copy-start | bytes 49156
  341.2 26.4 %all-to-all-start.14 = ((bf16[8,4,4096]{2,1,0:T(4,128)(2,1)}), bf16[8,4,4096]{2,1,0:T(4,128)(2,1)S(1)}, u32[]{:S(2)}, u32[]{:S(2)}) async-start(bf16[8,4,4096]{2,1,0:T(4,128)(2,1)} %reshape.754), calls=%async_computation.14 | async-start | bytes 524288 | tf_op jit(solution)/shard_map/all_to_all | solution.py:444
  (31 other events, 139.8 us)
Sparse Core Ops, SparseCore 0:
  108.3 68.8 all-gather.7
  179.3 43.9 all-gather.9
  227.7 38.4 all-gather.5

commit v4 on v3

v4 whole, which is shorter than its diff:
```python
import functools
import math

import jax
import jax.numpy as jnp
from jax import lax
from jax.experimental import pallas as pl
from jax.experimental.pallas import tpu as pltpu
from jax.sharding import Mesh, PartitionSpec as P

HD = 128
PLEN = 1024
SEL = 96
PPR = 2
TOKN_DEV = 32
ROW_DEV = 128

EPSILON = 1e-06
ROPE_THETA = 500000.0
MASKED = -1e30

SEQ = ("y", "zh", "core")
BLK = ("zl", "x")
NY, NZH, NCORE, NZL, NX = 4, 2, 2, 8, 4
N_SEQ = NY * NZH * NCORE
bf16 = jnp.bfloat16
f32 = jnp.float32


def frequencies():
    indices = jnp.arange(HD // 2, dtype=f32)
    return jnp.exp(indices * (-2.0 * math.log(ROPE_THETA) / HD))


def copies_to_all(a, axis, count):
    return lax.all_to_all(
        jnp.broadcast_to(a[None], (count,) + a.shape), axis, 0, 0, tiled=True
    )


def gather_seq(a):
    a = copies_to_all(a, "zh", NZH)
    a = copies_to_all(a, "y", NY)
    a = copies_to_all(a, "core", NCORE)
    return a.reshape((N_SEQ,) + a.shape[3:])


def seq_slot(s):
    return (s % 2) * 8 + (s // 4) * 2 + (s // 2) % 2


def swap(a, axis, count):
    return lax.ppermute(a, axis, [(i, i ^ 1) for i in range(count)])


def layout(passage_order, separators, recompute_index, prompt_lengths):
    requests = N_SEQ // PPR
    slot_ids = jnp.arange(PPR, dtype=jnp.int32)
    opening = slot_ids[None, :] * PLEN + jnp.cumsum(separators, axis=1)
    flat = passage_order.reshape(-1)
    hit = flat[None, :] == jnp.arange(N_SEQ, dtype=jnp.int32)[:, None]
    starts = jnp.sum(jnp.where(hit, opening.reshape(-1)[None, :], 0), axis=1)
    place = jnp.sum(jnp.where(hit, jnp.arange(N_SEQ, dtype=jnp.int32)[None, :], 0), axis=1)
    owners = place // PPR
    prompt_start = opening[:, PPR - 1] + PLEN
    new_index = jnp.arange(PPR * TOKN_DEV, dtype=jnp.int32)
    new_positions = (prompt_start[:, None] + new_index[None, :]).reshape(N_SEQ, TOKN_DEV)
    new_live = (new_index[None, :] < prompt_lengths[:, None]).reshape(N_SEQ, TOKN_DEV)
    picked = starts[:, None] + recompute_index
    positions = jnp.concatenate([picked, new_positions], axis=1)
    return starts, owners, positions, new_live


def partial_attention(queries, keys, values, visible):
    scores = lax.dot_general(
        queries, keys, (((1,), (1,)), ((), ())), preferred_element_type=f32
    ) * HD ** (-0.5)
    scores = jnp.where(visible, scores, MASKED)
    peak = jnp.max(scores, axis=1, keepdims=True)
    weights = jnp.where(visible, jnp.exp(scores - peak), 0.0)
    total = jnp.sum(weights, axis=1, keepdims=True)
    some = total > 0.0
    safe = jnp.where(some, total, 1.0)
    out = jnp.dot(weights.astype(bf16), values, preferred_element_type=f32) / safe
    return out, jnp.where(some, peak + jnp.log(safe), MASKED)


def merge(parts):
    top = parts[0][1]
    for _, level in parts[1:]:
        top = jnp.maximum(top, level)
    num = 0.0
    den = 0.0
    for out, level in parts:
        w = jnp.exp(level - top)
        num = num + w * out
        den = den + w
    return num / den


def unpack(block):
    block = block.astype(f32)
    level = block[:, HD : HD + 1] + block[:, HD + 1 : HD + 2] + block[:, HD + 2 : HD + 3]
    return block[:, :HD], level


def whole(a):
    return pl.BlockSpec(a.shape, lambda *k: (0,) * a.ndim)


SMEM = pl.BlockSpec(memory_space=pltpu.SMEM)


def call(kernel, name, out_shape, *args, scratch=(), limit=24):
    small = [a.ndim == 1 for a in args]
    return pl.pallas_call(
        kernel,
        grid=(1,),
        out_shape=out_shape,
        in_specs=[SMEM if one else whole(a) for a, one in zip(args, small)],
        out_specs=jax.tree.map(whole, out_shape),
        scratch_shapes=list(scratch),
        compiler_params=pltpu.CompilerParams(vmem_limit_bytes=limit << 20),
        name=name,
    )(*args)


def shape(dims, dtype):
    return jax.ShapeDtypeStruct(dims, dtype)


def join_weights(query_weight, key_weight, value_weight, output_weight):
    depth, width = query_weight.shape

    def kernel(q_ref, k_ref, v_ref, o_ref, out_ref):
        for n, ref in enumerate((q_ref, k_ref, v_ref)):
            out_ref[:, n * width : (n + 1) * width] = ref[...]
        out_ref[:, 3 * width :] = jnp.transpose(o_ref[...].astype(f32)).astype(bf16)

    return call(
        kernel,
        "join_weights",
        shape((depth, 4 * width), bf16),
        query_weight,
        key_weight,
        value_weight,
        output_weight,
    )


def project(columns, hidden, weights, width, copies):
    rows = hidden.shape[0]
    count, depth, _ = weights[0].shape

    def kernel(c_ref, x_ref, *refs):
        weight_refs, (raw_ref, squares_ref) = refs[:-2], refs[-2:]
        raw = jnp.zeros((rows, 3 * width), f32)
        for m in range(len(weight_refs) * count):
            at = pl.multiple_of(c_ref[m] * depth, depth)
            raw = raw + jnp.dot(
                x_ref[:, pl.ds(at, depth)],
                weight_refs[m // count][m % count, :, : 3 * width],
                preferred_element_type=f32,
            )
        raw_ref[...] = raw
        query, key = raw[:, :width], raw[:, width : 2 * width]
        lane = lax.broadcasted_iota(jnp.int32, (rows, width), 1)
        sums = jnp.where(lane == 0, jnp.sum(query * query, axis=1, keepdims=True), 0.0)
        sums = jnp.where(lane == 1, jnp.sum(key * key, axis=1, keepdims=True), sums)
        sums = jnp.transpose(sums)[:8]
        for b in range(copies):
            squares_ref[b] = sums

    return call(
        kernel,
        "project",
        (shape((rows, 3 * width), f32), shape((copies, 8, rows), f32)),
        columns,
        hidden,
        *weights,
    )


def turn_by(x, cosine, sine):
    return x * cosine + pltpu.roll(x, HD // 2, 1) * sine


def finish_rows(raw, squares, query_gain, key_gain, cosine, sine, model):
    rows = raw.shape[0]
    width = query_gain.shape[1]
    copies = squares.shape[0]

    def kernel(raw_ref, s_ref, gq_ref, gk_ref, c_ref, t_ref, q_ref, k_ref, v_ref, new_ref):
        sums = s_ref[0]
        for b in range(1, copies):
            sums = sums + s_ref[b]
        sums = jnp.concatenate([sums, jnp.zeros((width - 8, rows), f32)], axis=0)
        scale = lax.rsqrt(jnp.transpose(sums) / model + EPSILON)
        raw = raw_ref[...]
        query = raw[:, :width] * scale[:, 0:1] * gq_ref[...]
        key = raw[:, width : 2 * width] * scale[:, 1:2] * gk_ref[...]
        query = turn_by(query, c_ref[...], t_ref[...]).astype(bf16)
        key = turn_by(key, c_ref[...], t_ref[...]).astype(bf16)
        value = raw[:, 2 * width :].astype(bf16)
        for z in range(NZH):
            q_ref[z] = query
        k_ref[...] = key
        v_ref[...] = value
        new_ref[:TOKN_DEV, :] = key[SEL:]
        new_ref[TOKN_DEV:, :] = value[SEL:]

    return call(
        kernel,
        "finish_rows",
        (
            shape((NZH, rows, width), bf16),
            shape((rows, width), bf16),
            shape((rows, width), bf16),
            shape((2 * TOKN_DEV, width), bf16),
        ),
        raw,
        squares,
        query_gain,
        key_gain,
        cosine,
        sine,
    )


def blend(picked, cosine, sine, keys, values, new_keys, new_values):
    _, length, width = keys.shape
    steps = 4
    chunk = length // steps

    def kernel(p_ref, c_ref, t_ref, k_ref, v_ref, nk_ref, nv_ref, bk_ref, bv_ref):
        at = lax.broadcasted_iota(jnp.int32, (chunk, width), 0) + pl.program_id(0) * chunk
        hit = (at == p_ref[...]).astype(f32)
        here = jnp.max(hit, axis=1, keepdims=True) > 0.0
        hit = hit.astype(bf16)
        turned = turn_by(k_ref[0].astype(f32), c_ref[...], t_ref[...])
        placed = jnp.dot(hit, nk_ref[...], preferred_element_type=f32)
        bk_ref[0] = jnp.where(here, placed, turned).astype(bf16)
        placed = jnp.dot(hit, nv_ref[...], preferred_element_type=f32)
        bv_ref[0] = jnp.where(here, placed, v_ref[0].astype(f32)).astype(bf16)

    tile = pl.BlockSpec((1, chunk, width), lambda k: (0, k, 0))
    return pl.pallas_call(
        kernel,
        grid=(steps,),
        out_shape=(shape(keys.shape, bf16), shape(keys.shape, bf16)),
        in_specs=[
            whole(picked),
            whole(cosine),
            whole(sine),
            tile,
            tile,
            whole(new_keys),
            whole(new_values),
        ],
        out_specs=(tile, tile),
        name="blend",
    )(picked, cosine, sine, keys, values, new_keys, new_values)


def attend(control, queries, keys, values, wanted_at, own, new_mine, new_other, new_at, new_key_at):
    width = keys.shape[2]
    length = keys.shape[1]
    cuts = [(0, SEL), (0, SEL), (SEL, ROW_DEV), (SEL, ROW_DEV)]
    count = sum(high - low for low, high in cuts)
    back = count - SEL
    step = 32

    def kernel(
        c_ref, q_ref, k_ref, v_ref, w_ref, own_ref, nm_ref, no_ref, na_ref, nk_ref,
        back_ref, kept_ref, new_ref, rows_ref,
    ):
        at = 0
        for i, (low, high) in enumerate(cuts):
            rows_ref[at : at + high - low, :] = q_ref[c_ref[i], low:high, :]
            at += high - low
        lane = lax.broadcasted_iota(jnp.int32, (step, width), 1)
        key_at = c_ref[4] + lax.broadcasted_iota(jnp.int32, (step, length), 1)
        for n in range(count // step):
            span = slice(n * step, (n + 1) * step)
            out, level = partial_attention(
                rows_ref[span, :], k_ref[0], v_ref[0], key_at <= w_ref[span, :]
            )
            if n * step < 2 * SEL:
                kept_ref[span, :width] = out
                kept_ref[span, width:] = jnp.broadcast_to(level, (step, width))
            if n * step >= SEL:
                high = level.astype(bf16).astype(f32)
                mid = (level - high).astype(bf16).astype(f32)
                low = level - high - mid
                pieces = jnp.where(lane == 0, high, jnp.where(lane == 1, mid, 0.0))
                pieces = jnp.where(lane == 2, low, pieces)
                to = slice(n * step - SEL, (n + 1) * step - SEL)
                for z in range(NZH):
                    back_ref[z, to, :width] = out.astype(bf16)
                    back_ref[z, to, width:] = pieces.astype(bf16)
        new_keys = jnp.concatenate([nm_ref[:TOKN_DEV, :], no_ref[:TOKN_DEV, :]], axis=0)
        new_values = jnp.concatenate([nm_ref[TOKN_DEV:, :], no_ref[TOKN_DEV:, :]], axis=0)
        out, level = partial_attention(
            own_ref[0, SEL:, :], new_keys, new_values, nk_ref[...] <= na_ref[...]
        )
        new_ref[:, :width] = out
        new_ref[:, width:] = jnp.broadcast_to(level, (TOKN_DEV, width))

    return call(
        kernel,
        "attend",
        (
            shape((NZH, back, 2 * width), bf16),
            shape((2 * SEL, 2 * width), f32),
            shape((TOKN_DEV, 2 * width), f32),
        ),
        control,
        queries,
        keys,
        values,
        wanted_at,
        own,
        new_mine,
        new_other,
        new_at,
        new_key_at,
        scratch=[pltpu.VMEM((count, width), bf16)],
    )


def merge_and_project(control, kept, new_part, returned, weights):
    width = new_part.shape[1] // 2
    count, part, _ = weights[0].shape
    halves = part // width
    blocks = len(weights) * count * halves

    def kernel(c_ref, kept_ref, new_ref, back_ref, *refs):
        weight_refs, (out_ref, att_ref) = refs[:-2], refs[-2:]
        first = c_ref[4] == 1
        kept = jnp.where(first, kept_ref[:SEL, :], kept_ref[SEL:, :])
        remote, remote_level = unpack(back_ref[c_ref[0], :SEL, :])
        remote_level = jnp.where(first, MASKED, remote_level)
        att_ref[:SEL, :] = merge(
            [(kept[:, :width], kept[:, width : width + 1]), (remote, remote_level)]
        )
        at = pl.multiple_of(SEL + c_ref[3] * TOKN_DEV, TOKN_DEV)
        parts = [(new_ref[:, :width], new_ref[:, width : width + 1])]
        for i in range(PPR):
            parts.append(unpack(back_ref[c_ref[1 + i], pl.ds(at, TOKN_DEV), :]))
        att_ref[SEL:, :] = merge(parts)
        attention = att_ref[...].astype(bf16)
        for j, ref in enumerate(weight_refs):
            for n in range(count):
                term = lax.dot_general(
                    attention, ref[n], (((1,), (1,)), ((), ())), preferred_element_type=f32
                ).astype(bf16)
                for h in range(halves):
                    out_ref[(j * count + n) * halves + h] = term[:, h * width : (h + 1) * width]

    out_weights = pl.BlockSpec((count, part, width), lambda i: (0, 0, 3))
    return pl.pallas_call(
        kernel,
        grid=(1,),
        out_shape=shape((blocks, ROW_DEV, width), bf16),
        in_specs=[SMEM, whole(kept), whole(new_part), whole(returned)]
        + [out_weights] * len(weights),
        out_specs=pl.BlockSpec((blocks, ROW_DEV, width), lambda i: (0, 0, 0)),
        scratch_shapes=[pltpu.VMEM((ROW_DEV, width), f32)],
        compiler_params=pltpu.CompilerParams(vmem_limit_bytes=24 << 20),
        name="merge_and_project",
    )(control, kept, new_part, returned, *weights)


def feed_forward(columns, summed, hidden, gain, parcels, units):
    blocks, rows, part = summed.shape
    model = blocks * part
    count, _, depth = parcels[0].shape
    group = 2
    half = count // group
    parts = len(parcels)
    steps = parts * half
    split = depth // part
    per = rows // (NZL * NX)
    contract_last = (((1,), (1,)), ((), ()))

    def kernel(c_ref, s_ref, x_ref, g_ref, *refs):
        within_refs, down_refs = refs[:parts], refs[parts : 2 * parts]
        out_ref, mixed_ref, norm_ref, acc_ref = refs[2 * parts :]
        k = pl.program_id(0)

        @pl.when(k == 0)
        def _():
            squares = jnp.zeros((rows, part), f32)
            for b in range(blocks):
                block = s_ref[b].astype(f32)
                squares = squares + block * block
            norm_ref[...] = lax.rsqrt(
                jnp.sum(squares, axis=1, keepdims=True) / model + EPSILON
            )
            acc_ref[...] = jnp.zeros_like(acc_ref)

        def add(ref):
            for n in range(group):
                m = k * group + n
                at = pl.multiple_of(c_ref[m] * depth, depth)
                cols = pl.ds(at, depth)
                summed = jnp.concatenate([s_ref[m * split + h] for h in range(split)], axis=1)
                mixed = (
                    x_ref[:, cols].astype(f32)
                    + summed.astype(f32) * norm_ref[...] * g_ref[:, cols]
                ).astype(bf16)
                mixed_ref[:, cols] = mixed
                acc_ref[...] += lax.dot_general(
                    ref[n], mixed, contract_last, preferred_element_type=f32
                )

        for j in range(parts):
            pl.when(k // half == j)(functools.partial(add, within_refs[j]))

        @pl.when(k == steps - 1)
        def _():
            to = lax.broadcasted_iota(jnp.int32, (rows, rows), 0)
            at = lax.broadcasted_iota(jnp.int32, (rows, rows), 1)
            source = (to // per) % NZL * (NX * per) + to // (NZL * per) * per + to % per
            move = jnp.where(at == source, 1.0, 0.0).astype(bf16)
            gate = acc_ref[:units, :]
            active = (gate / (1.0 + jnp.exp(-gate)) * acc_ref[units:, :]).astype(bf16)
            active = lax.dot_general(
                move, active, contract_last, preferred_element_type=f32
            ).astype(bf16)
            for m in range(parts * count):
                at_col = pl.multiple_of(c_ref[m] * depth, depth)
                out_ref[:, pl.ds(at_col, depth)] = jnp.dot(
                    active, down_refs[m // count][m % count], preferred_element_type=f32
                ).astype(bf16)

    return pl.pallas_call(
        kernel,
        grid=(steps,),
        out_shape=(shape((rows, model), bf16), shape((rows, model), bf16)),
        in_specs=[SMEM, whole(summed), whole(hidden), whole(gain)]
        + [
            pl.BlockSpec(
                (group, 2 * units, depth),
                lambda k, j=j: (jnp.clip(k - j * half, 0, half - 1), 0, 0),
            )
            for j in range(parts)
        ]
        + [pl.BlockSpec((count, units, depth), lambda k: (0, 2, 0))] * parts,
        out_specs=(
            pl.BlockSpec((rows, model), lambda k: (0, 0)),
            pl.BlockSpec((rows, model), lambda k: (0, 0)),
        ),
        scratch_shapes=[pltpu.VMEM((rows, 1), f32), pltpu.VMEM((2 * units, rows), f32)],
        compiler_params=pltpu.CompilerParams(vmem_limit_bytes=40 << 20),
        name="feed_forward",
    )(columns, summed, hidden, gain, *parcels, *parcels)


def shards(
    hidden_states,
    query_weight,
    key_weight,
    value_weight,
    output_weight,
    query_gain,
    key_gain,
    attention_gain,
    gate_weight,
    up_weight,
    down_weight,
    feedforward_gain,
    cached_keys,
    cached_values,
    passage_order,
    separators,
    recompute_index,
    prompt_lengths,
):
    y_at, zh, core = (lax.axis_index(a) for a in SEQ)
    zl, x_at = (lax.axis_index(a) for a in BLK)
    seq = y_at * 4 + zh * 2 + core
    width = query_weight.shape[1]
    hidden_units = gate_weight.shape[1]
    model = hidden_states.shape[1]
    blocks = NX * NZL
    rows = ROW_DEV // blocks

    mine = join_weights(query_weight, key_weight, value_weight, output_weight)
    theirs = swap(mine, "zh", NZH)
    near = copies_to_all(mine, "y", NY)
    parcel = jnp.concatenate([gate_weight.T, up_weight.T, down_weight])
    parcel = jnp.pad(parcel, ((0, -parcel.shape[0] % 16), (0, 0)))

    order_of = jnp.arange(N_SEQ, dtype=jnp.int32)
    columns = order_of % 4 * 4 + (zh ^ (order_of // 8)) * 2 + (core ^ (order_of // 4 % 2))
    starts, owners, positions, new_live = layout(
        passage_order, separators, recompute_index, prompt_lengths
    )

    def rows_of(table, s):
        return lax.dynamic_index_in_dim(table, s, 0, False)

    frequency = frequencies()
    my_positions = rows_of(positions, seq)
    angles = my_positions.astype(f32)[:, None] * frequency[None, :]
    cosine, sine = jnp.cos(angles), jnp.sin(angles)
    cosine = jnp.concatenate([cosine, cosine], axis=1)
    sine = jnp.concatenate([-sine, sine], axis=1)
    start = rows_of(starts, seq)
    turn = (start.astype(f32) * frequency)[None, :]
    turn_cosine, turn_sine = jnp.cos(turn), jnp.sin(turn)
    turn_cosine = jnp.concatenate([turn_cosine, turn_cosine], axis=1)
    turn_sine = jnp.concatenate([-turn_sine, turn_sine], axis=1)
    picked = jnp.pad(rows_of(recompute_index, seq), (0, width - SEL), constant_values=-1)[None]
    request = rows_of(owners, seq)
    order = passage_order.reshape(-1, PPR)
    chosen = rows_of(order, request)
    my_order = rows_of(order, seq // 2)
    sources = [chosen[0], chosen[1], request * 2, request * 2 + 1]
    cuts = [slice(0, SEL), slice(0, SEL), slice(SEL, None), slice(SEL, None)]
    wanted_at = jnp.concatenate([rows_of(positions, s)[c] for s, c in zip(sources, cuts)])[:, None]
    partner = seq + 1 - 2 * core
    far_away = jnp.int32(1 << 30)
    new_key_at = jnp.concatenate(
        [
            jnp.where(rows_of(new_live, s), rows_of(positions, s)[SEL:], far_away)
            for s in (seq, partner)
        ]
    )[None]
    new_at = my_positions[SEL:][:, None]
    first = chosen[0] == seq
    attend_control = jnp.stack([seq_slot(s) for s in sources] + [start]).astype(jnp.int32)
    merge_control = jnp.stack(
        [seq_slot(chosen[0]), seq_slot(my_order[0]), seq_slot(my_order[1]), core, first]
    ).astype(jnp.int32)
    tables = (
        columns,
        cosine,
        sine,
        turn_cosine,
        turn_sine,
        picked,
        wanted_at,
        new_key_at,
        new_at,
        attend_control,
        merge_control,
    )
    theirs, near, tables = lax.optimization_barrier((theirs, near, tables))
    (
        columns,
        cosine,
        sine,
        turn_cosine,
        turn_sine,
        picked,
        wanted_at,
        new_key_at,
        new_at,
        attend_control,
        merge_control,
    ) = tables

    near_other = swap(near, "core", NCORE)
    far = copies_to_all(theirs, "y", NY)
    far_other = swap(far, "core", NCORE)
    parcel_near = lax.all_gather(parcel, "y")
    weights = [near, near_other, far, far_other]
    raw, squares = project(columns, hidden_states, weights, width, blocks)
    squares = lax.all_to_all(squares, BLK, 0, 0, tiled=True)
    squares, parcel, parcel_near = lax.optimization_barrier((squares, parcel, parcel_near))
    pair = lax.all_gather(parcel, "zh")
    query, key, value, new_mine = finish_rows(
        raw, squares, query_gain[None], key_gain[None], cosine, sine, model
    )

    queries = lax.all_to_all(query, "zh", 0, 0, tiled=True)
    queries = copies_to_all(queries, "y", NY)
    queries = copies_to_all(queries, "core", NCORE).reshape(N_SEQ, ROW_DEV, width)
    new_other = swap(new_mine, "core", NCORE)
    blended_keys, blended_values = blend(
        picked, turn_cosine, turn_sine, cached_keys, cached_values, key, value
    )
    returned, kept, new_part = attend(
        attend_control,
        queries,
        blended_keys,
        blended_values,
        wanted_at,
        query,
        new_mine,
        new_other,
        new_at,
        new_key_at,
    )

    returned = lax.all_to_all(returned, "zh", 0, 0, tiled=True)
    returned = copies_to_all(returned, "y", NY)
    returned = copies_to_all(returned, "core", NCORE).reshape(N_SEQ, -1, 2 * width)

    terms = merge_and_project(merge_control, kept, new_part, returned, weights)
    terms, pair = lax.optimization_barrier((terms, pair))
    parcel_far = lax.all_gather(jnp.where(zh == 0, pair[1], pair[0]), "y")
    terms = lax.all_to_all(terms.reshape(NX, NZL, ROW_DEV, width), "x", 0, 0, tiled=True)
    terms = jnp.sum(terms.astype(f32), axis=0).astype(bf16)
    terms = lax.all_to_all(terms, "zl", 0, 0, tiled=True)
    summed = jnp.sum(terms.astype(f32), axis=0).astype(bf16)
    summed = copies_to_all(summed, "zl", NZL)
    summed = copies_to_all(summed, "x", NX).reshape(blocks, ROW_DEV, model // blocks)

    parcels = [parcel_near, swap(parcel_near, "core", NCORE)]
    parcels += [parcel_far, swap(parcel_far, "core", NCORE)]
    terms, mixed = feed_forward(
        columns, summed, hidden_states, attention_gain[None], parcels, hidden_units
    )
    terms = lax.all_to_all(terms.reshape(NX, NZL * rows, model), "x", 0, 0, tiled=True)
    terms = jnp.sum(terms.astype(f32), axis=0).astype(bf16)
    terms = lax.all_to_all(terms.reshape(NZL, rows, model), "zl", 0, 0, tiled=True)
    total = jnp.sum(terms.astype(f32), axis=0)
    norm = lax.rsqrt(jnp.mean(total * total, axis=1, keepdims=True) + EPSILON)
    my_rows = lax.dynamic_slice_in_dim(mixed, (zl * NX + x_at) * rows, rows, 0)
    hidden_out = (my_rows.astype(f32) + total * norm * feedforward_gain).astype(bf16)
    return (hidden_out, blended_keys, blended_values)


def solution(mesh):
    fine = Mesh(
        mesh.devices.reshape(NY, NZH, NCORE, NZL, NX), ("y", "zh", "core", "zl", "x")
    )
    by_both = P(SEQ, BLK)
    return jax.shard_map(
        shards,
        mesh=fine,
        in_specs=(
            P(SEQ, None),
            by_both,
            by_both,
            by_both,
            P(BLK, SEQ),
            P(BLK),
            P(BLK),
            P(),
            by_both,
            by_both,
            P(BLK, SEQ),
            P(),
            P(SEQ, None, BLK),
            P(SEQ, None, BLK),
            P(),
            P(),
            P(),
            P(),
        ),
        out_specs=(P(SEQ + BLK, None), P(SEQ, None, BLK), P(SEQ, None, BLK)),
        check_vma=False,
    )
```

time: 380 us -> 354 us (0.932)
  blocking collectives: 41.8 us -> 109 us
  local copies, waits for them, and re-layouts: 50 us -> 23.3 us
  starting transfers between devices: 101 us -> 77.5 us
  waiting for transfers between devices: 101 us -> 78.5 us
  other arithmetic: 34 us -> 12.2 us
  Pallas kernels: 10 us -> 20.7 us
  matrix products: 6.19 us -> 0 us
    all_to_all x0 -> x2, blocking collectives: none -> 49.6 us  [the longest x1 27.9 us: shards(): returned = lax.all_to_all(returned, 'zh', 0, 0, tiled=True)]
    all_to_all x8 -> x6, waiting for transfers between devices: 76.4 us -> 36.5 us  [copies_to_all(): lax.all_to_all(jnp.broadcast_to(a[None], (count,) + a.shape), axis, 0, 0,...]
    all_to_all x2, blocking collectives: 8.94 us -> 26 us  [copies_to_all(): lax.all_to_all(jnp.broadcast_to(a[None], (count,) + a.shape), axis, 0, 0,...]
    all_to_all x8 -> x6, starting transfers between devices: 39.5 us -> 24.3 us  [copies_to_all(): lax.all_to_all(jnp.broadcast_to(a[None], (count,) + a.shape), axis, 0, 0,...]
    all_to_all x1, waiting for transfers between devices: 0.01 us -> 13.2 us  [shards(): queries = lax.all_to_all(query, 'zh', 0, 0, tiled=True)]
    pallas_call x2 -> x7, Pallas kernels: 10 us -> 20.7 us  [the longest x1 8.46 us: feed_forward(): pl.pallas_call(kernel, grid=(steps,), out_shape=(shape((rows, model), bf1...]
    select_n x13 -> x1, other arithmetic: 7.84 us -> 0.59 us  [shards(): jnp.where(rows_of(new_live, s), rows_of(positions, s)[SEL:], far_away)]
    dot_general x8 -> x0, matrix products: 6.19 us -> none  [the longest x2 2.56 us: partial_attention(): jnp.dot(weights.astype(bf16), values, preferred_element_type=f32) / safe]
  transfers between devices with their start and end apart: 20 -> 18, of which waited for: 10 -> 10; matrix products, arithmetic and copies ran while one was open for 19% -> 5% of each run, Pallas kernels for 0% -> 3%
where the time goes in v4:
time: 354 us; the launch traced here: 352 us
  blocking collectives  109 us (31%)
  waiting for transfers between devices  78.5 us (22%)
  starting transfers between devices  77.5 us (22%)
  between operations  31.1 us (9%)
  local copies, waits for them, and re-layouts  23.3 us (7%)
  Pallas kernels  20.7 us (6%)
  other arithmetic  12.2 us (3%)
    all_to_all x6, waiting for transfers between devices, copies_to_all(): lax.all_to_all(jnp.broadcast_to(a[None], (count,) + a.shape), axis, 0, 0,...  36.5 us
    all_to_all x1, blocking collectives, shards(): returned = lax.all_to_all(returned, 'zh', 0, 0, tiled=True)  27.9 us
    all_to_all x2, blocking collectives, copies_to_all(): lax.all_to_all(jnp.broadcast_to(a[None], (count,) + a.shape), axis, 0, 0,...  26 us
    ppermute x6, starting transfers between devices, swap(): return lax.ppermute(a, axis, [(i, i ^ 1) for i in range(count)])  24.7 us
    all_to_all x6, starting transfers between devices, copies_to_all(): lax.all_to_all(jnp.broadcast_to(a[None], (count,) + a.shape), axis, 0, 0,...  24.3 us
    all_to_all x1, blocking collectives, shards(): squares = lax.all_to_all(squares, BLK, 0, 0, tiled=True)  21.7 us
    all_to_all x1, blocking collectives, shards(): lax.all_to_all(terms.reshape(NX, NZL, ROW_DEV, width), 'x', 0, 0, tiled=T...  19.7 us
    all_to_all x1, waiting for transfers between devices, shards(): lax.all_to_all(terms.reshape(NZL, rows, model), 'zl', 0, 0, tiled=True)  13.7 us
  transfers between devices with their start and end apart: 18, of which 10 were waited for; matrix products, arithmetic and copies ran while one was open for 5% of the time, Pallas kernels for 3%

profile of v4, /device:TPU:32, one launch (start us, length us, event | category | flops | bytes accessed | tf_op | source)
XLA Modules:
  0.0 351.9 jit_solution(14827939016415412047)
XLA Ops:
  10.7 14.8 %collective-permute-start = (bf16[256,512]{1,0:T(8,128)(2,1)S(1)}, bf16[256,512]{1,0:T(8,128)(2,1)S(1)}, u32[]{:S(2)}, u32[]{:S(2)}) collective-permute-start(bf16[256,512]{1,0:T(8,128)(2,1)S(1)} %join_weights.1), channel_id=1, source_target_pairs={{0,64},{64,0},{1,65},{65,1},{2,66},{66,2},{3,67},{67,3},{4,68},{68... | collective-permute-start | bytes 786440 | tf_op jit(solution)/shard_map/ppermute | solution.py:53
  25.5 1.9 fusion.4
  28.5 4.6 %all-to-all-start = ((bf16[4,256,512]{2,1,0:T(8,128)(2,1)}), bf16[4,256,512]{2,1,0:T(8,128)(2,1)S(1)}, u32[]{:S(2)}, u32[]{:S(2)}) async-start(bf16[4,256,512]{2,1,0:T(8,128)(2,1)} %broadcast_in_dim.53), calls=%async_computation | async-start | bytes 2097152 | tf_op jit(solution)/shard_map/all_to_all | solution.py:36
  58.8 4.9 %all-to-all-start.1 = ((bf16[4,256,512]{2,1,0:T(8,128)(2,1)}), bf16[4,256,512]{2,1,0:T(8,128)(2,1)S(1)}, u32[]{:S(2)}, u32[]{:S(2)}) async-start(bf16[4,256,512]{2,1,0:T(8,128)(2,1)} %broadcast_in_dim.62), calls=%async_computation.1 | async-start | bytes 2097152 | tf_op jit(solution)/shard_map/all_to_all | solution.py:36
  63.8 2.0 collective-permute-start.1
  65.8 12.2 %all-to-all-done.1.refs_2_ = bf16[4,256,512]{2,1,0:T(8,128)(2,1)S(1)} async-done(((bf16[4,256,512]{2,1,0:T(8,128)(2,1)}), bf16[4,256,512]{2,1,0:T(8,128)(2,1)S(1)}, u32[]{:S(2)}, u32[]{:S(2)}) %all-to-all-start.1) | async-done | bytes 1048608 | tf_op jit(solution)/shard_map/all_to_all | solution.py:36
  80.0 2.6 collective-permute-done.2.refs_3_
  82.6 2.5 project.1
  85.1 21.7 %all_to_all.75.s_ref = f32[32,8,128]{2,1,0:T(8,128)S(1)} all-to-all(f32[32,8,128]{2,1,0:T(8,128)S(1)} %get-tuple-element.40), channel_id=1, replica_groups=mesh['y'=4,'zh'=2,'core'=2,'zl'=8,'x'=4] {'zl','x'}, dimensions={0} | all-to-all | bytes 262144 | tf_op jit(solution)/shard_map/all_to_all | solution.py:571
  108.9 5.7 %all-to-all-start.3 = ((bf16[2,128,128]{2,1,0:T(8,128)(2,1)}), bf16[2,128,128]{2,1,0:T(8,128)(2,1)S(1)}, u32[]{:S(2)}, u32[]{:S(2)}) async-start(bf16[2,128,128]{2,1,0:T(8,128)(2,1)} %get-tuple-element.44.own_ref), calls=%async_computation.3 | async-start | bytes 131072 | tf_op jit(solution)/shard_map/all_to_all | solution.py:578
  115.3 13.2 %all-to-all-done.3 = bf16[2,128,128]{2,1,0:T(8,128)(2,1)S(1)} async-done(((bf16[2,128,128]{2,1,0:T(8,128)(2,1)}), bf16[2,128,128]{2,1,0:T(8,128)(2,1)S(1)}, u32[]{:S(2)}, u32[]{:S(2)}) %all-to-all-start.3) | async-done | bytes 65568 | tf_op jit(solution)/shard_map/all_to_all | solution.py:578
  129.2 3.4 all-to-all-start.4
  134.8 3.4 blend.1
  140.2 3.5 all-to-all-start.5
  145.4 3.7 %attend.1 = (bf16[2,160,256]{2,1,0:T(8,128)(2,1)S(1)}, f32[192,256]{1,0:T(8,128)S(1)}, f32[32,256]{1,0:T(8,128)S(1)}) custom-call(s32[5]{0:T(128)S(1)} %stack.39.c_ref, bf16[16,128,128]{2,1,0:T(8,128)(2,1)S(1)} %bitcast.58, bf16[1,1024,128]{2,1,0:T(8,128)(2,1)S(1)} %copy-done.10, bf16[1,1024,128]{2,1,0:T(8,128)(2,1)S(1)} %copy-done.11, ...), custom_call_target="tpu_custom_call" | custom-call | tf_op jit(solution)/shard_map/attend/pallas_call | solution.py:116
  149.8 27.9 %all_to_all.76 = bf16[2,160,256]{2,1,0:T(8,128)(2,1)S(1)} all-to-all(bf16[2,160,256]{2,1,0:T(8,128)(2,1)S(1)} %get-tuple-element.58), channel_id=1, replica_groups=mesh['y'=4,'zh'=2,'core'=2,'zl'=8,'x'=4] {'zh'}, dimensions={0} | all-to-all | bytes 327680 | tf_op jit(solution)/shard_map/all_to_all | solution.py:598
  178.6 4.2 %all-to-all-start.7 = ((bf16[4,2,160,256]{3,2,1,0:T(8,128)(2,1)}), bf16[4,2,160,256]{3,2,1,0:T(8,128)(2,1)S(1)}, u32[]{:S(2)}, u32[]{:S(2)}) async-start(bf16[4,2,160,256]{3,2,1,0:T(8,128)(2,1)} %broadcast_in_dim.120), calls=%async_computation.7 | async-start | bytes 1310720 | tf_op jit(solution)/shard_map/all_to_all | solution.py:36
  182.9 10.7 %all-to-all-done.7 = bf16[4,2,160,256]{3,2,1,0:T(8,128)(2,1)S(1)} async-done(((bf16[4,2,160,256]{3,2,1,0:T(8,128)(2,1)}), bf16[4,2,160,256]{3,2,1,0:T(8,128)(2,1)S(1)}, u32[]{:S(2)}, u32[]{:S(2)}) %all-to-all-start.7) | async-done | bytes 655392 | tf_op jit(solution)/shard_map/all_to_all | solution.py:36
  193.7 4.9 %all_to_all.77 = bf16[2,4,2,160,256]{4,3,2,1,0:T(8,128)(2,1)S(1)} all-to-all(bf16[2,4,2,160,256]{4,3,2,1,0:T(8,128)(2,1)S(1)} %broadcast_in_dim.121), channel_id=1, replica_groups=mesh['y'=4,'zh'=2,'core'=2,'zl'=8,'x'=4] {'core'}, dimensions={0} | all-to-all | bytes 2621440 | tf_op jit(solution)/shard_map/all_to_all | solution.py:36
  201.3 2.2 slice_select_fusion
  203.5 19.7 %all_to_all.78 = bf16[4,8,128,128]{3,2,1,0:T(8,128)(2,1)} all-to-all(bf16[4,8,128,128]{3,2,1,0:T(8,128)(2,1)S(1)} %bitcast.57), channel_id=1, replica_groups=mesh['y'=4,'zh'=2,'core'=2,'zl'=8,'x'=4] {'x'}, dimensions={0} | all-to-all | bytes 2097152 | tf_op jit(solution)/shard_map/all_to_all | solution.py:605
  223.2 2.2 reduce_sum.74
  225.3 10.1 %all-to-all-start.10 = ((bf16[8,128,128]{2,1,0:T(8,128)(2,1)}), bf16[8,128,128]{2,1,0:T(8,128)(2,1)S(1)}, u32[]{:S(2)}, u32[]{:S(2)}) async-start(bf16[8,128,128]{2,1,0:T(8,128)(2,1)} %reduce_sum.74), calls=%async_computation.10 | async-start | bytes 524288 | tf_op jit(solution)/shard_map/all_to_all | solution.py:607
  237.7 2.1 collective-permute-start.5
  239.8 11.4 %all-to-all-done.10 = bf16[8,128,128]{2,1,0:T(8,128)(2,1)S(1)} async-done(((bf16[8,128,128]{2,1,0:T(8,128)(2,1)}), bf16[8,128,128]{2,1,0:T(8,128)(2,1)S(1)}, u32[]{:S(2)}, u32[]{:S(2)}) %all-to-all-start.10) | async-done | bytes 262176 | tf_op jit(solution)/shard_map/all_to_all | solution.py:607
  251.3 21.1 %all_to_all.79 = bf16[8,128,128]{2,1,0:T(8,128)(2,1)S(1)} all-to-all(bf16[8,128,128]{2,1,0:T(8,128)(2,1)S(1)} %broadcast_in_dim.122), channel_id=1, replica_groups=mesh['y'=4,'zh'=2,'core'=2,'zl'=8,'x'=4] {'zl'}, dimensions={0} | all-to-all | bytes 524288 | tf_op jit(solution)/shard_map/all_to_all | solution.py:36
  273.7 3.6 %all-to-all-start.12 = ((bf16[4,8,128,128]{3,2,1,0:T(8,128)(2,1)}), bf16[4,8,128,128]{3,2,1,0:T(8,128)(2,1)S(1)}, u32[]{:S(2)}, u32[]{:S(2)}) async-start(bf16[4,8,128,128]{3,2,1,0:T(8,128)(2,1)} %broadcast_in_dim.123), calls=%async_computation.12 | async-start | bytes 2097152 | tf_op jit(solution)/shard_map/all_to_all | solution.py:36
  277.3 10.8 %all-to-all-done.12 = bf16[4,8,128,128]{3,2,1,0:T(8,128)(2,1)S(1)} async-done(((bf16[4,8,128,128]{3,2,1,0:T(8,128)(2,1)}), bf16[4,8,128,128]{3,2,1,0:T(8,128)(2,1)S(1)}, u32[]{:S(2)}, u32[]{:S(2)}) %all-to-all-start.12) | async-done | bytes 1048608 | tf_op jit(solution)/shard_map/all_to_all | solution.py:36
  293.2 8.5 %feed_forward.1 = (bf16[128,4096]{1,0:T(8,128)(2,1)S(1)}, bf16[128,4096]{1,0:T(8,128)(2,1)S(1)}) custom-call(s32[16]{0:T(128)S(1)} %fusion.11.c_ref, bf16[32,128,128]{2,1,0:T(8,128)(2,1)S(1)} %bitcast.56, bf16[128,4096]{1,0:T(8,128)(2,1)S(1)} %copy-done.5, f32[1,4096]{1,0:T(1,128)S(1)} %bitcast.60, bf16[4,1040,256]{2,1,0:T(8,128)(2,1)S(1)} %bitcast.53, ...), custom_call_target="tpu_custom_call" | custom-call | tf_op jit(solution)/shard_map/feed_forward/pallas_call | solution.py:437
  302.7 13.3 %all_to_all.80 = bf16[4,32,4096]{2,1,0:T(8,128)(2,1)S(1)} all-to-all(bf16[4,32,4096]{2,1,0:T(8,128)(2,1)S(1)} %bitcast.59), channel_id=1, replica_groups=mesh['y'=4,'zh'=2,'core'=2,'zl'=8,'x'=4] {'x'}, dimensions={0} | all-to-all | bytes 2097152 | tf_op jit(solution)/shard_map/all_to_all | solution.py:617
  317.0 12.7 %all-to-all-start.14 = ((bf16[8,4,4096]{2,1,0:T(4,128)(2,1)}), bf16[8,4,4096]{2,1,0:T(4,128)(2,1)S(1)}, u32[]{:S(2)}, u32[]{:S(2)}) async-start(bf16[8,4,4096]{2,1,0:T(4,128)(2,1)} %reshape.133), calls=%async_computation.14 | async-start | bytes 524288 | tf_op jit(solution)/shard_map/all_to_all | solution.py:619
  329.7 13.7 %all-to-all-done.14 = bf16[8,4,4096]{2,1,0:T(4,128)(2,1)S(1)} async-done(((bf16[8,4,4096]{2,1,0:T(4,128)(2,1)}), bf16[8,4,4096]{2,1,0:T(4,128)(2,1)S(1)}, u32[]{:S(2)}, u32[]{:S(2)}) %all-to-all-start.14) | async-done | bytes 262176 | tf_op jit(solution)/shard_map/all_to_all | solution.py:619
  (145 shorter events, 41.5 us)
Async XLA Ops:
  7.2 99.6 %all-gather.8.cloned.1.call-start = ((), (), s32[]{:S(2)}) async-start(), calls=%async_computation.16 | async-start | bytes 2662400 | tf_op jit(solution)/shard_map/all_gather | solution.py:568
  10.7 47.1 %collective-permute-start = (bf16[256,512]{1,0:T(8,128)(2,1)S(1)}, bf16[256,512]{1,0:T(8,128)(2,1)S(1)}, u32[]{:S(2)}, u32[]{:S(2)}) collective-permute-start(bf16[256,512]{1,0:T(8,128)(2,1)S(1)} %join_weights.1), channel_id=1, source_target_pairs={{0,64},{64,0},{1,65},{65,1},{2,66},{66,2},{3,67},{67,3},{4,68},{68... | collective-permute-start | bytes 786440 | tf_op jit(solution)/shard_map/ppermute | solution.py:53
  28.5 4.9 %copy-start.28 = (s32[16]{0:T(128)S(1)}, s32[16]{0:T(128)}, u32[]{:S(2)}) copy-start(s32[16]{0:T(128)} %param.32) | copy-start | bytes 196
  28.5 13.0 %copy-start.25 = (s32[16,96]{1,0:T(8,128)S(1)}, s32[16,96]{1,0:T(8,128)}, u32[]{:S(2)}) copy-start(s32[16,96]{1,0:T(8,128)} %param.34) | copy-start | bytes 18436
  28.5 14.4 %copy-start.30 = (s32[8]{0:T(128)S(1)}, s32[8]{0:T(128)}, u32[]{:S(2)}) copy-start(s32[8]{0:T(128)} %param.35) | copy-start | bytes 100
  28.5 29.2 %all-to-all-start = ((bf16[4,256,512]{2,1,0:T(8,128)(2,1)}), bf16[4,256,512]{2,1,0:T(8,128)(2,1)S(1)}, u32[]{:S(2)}, u32[]{:S(2)}) async-start(bf16[4,256,512]{2,1,0:T(8,128)(2,1)} %broadcast_in_dim.53), calls=%async_computation | async-start | bytes 2097152 | tf_op jit(solution)/shard_map/all_to_all | solution.py:36
  58.8 23.7 %copy-start.4 = (bf16[128,4096]{1,0:T(8,128)(2,1)S(1)}, bf16[128,4096]{1,0:T(8,128)(2,1)}, u32[]{:S(2)}) copy-start(bf16[128,4096]{1,0:T(8,128)(2,1)} %x_ref.3) | copy-start | bytes 3145732
  58.8 19.2 %all-to-all-start.1 = ((bf16[4,256,512]{2,1,0:T(8,128)(2,1)}), bf16[4,256,512]{2,1,0:T(8,128)(2,1)S(1)}, u32[]{:S(2)}, u32[]{:S(2)}) async-start(bf16[4,256,512]{2,1,0:T(8,128)(2,1)} %broadcast_in_dim.62), calls=%async_computation.1 | async-start | bytes 2097152 | tf_op jit(solution)/shard_map/all_to_all | solution.py:36
  63.8 43.0 %copy-start.22 = (f32[128]{0:T(128)S(1)}, f32[128]{0:T(128)}, u32[]{:S(2)}) copy-start(f32[128]{0:T(128)} %param.23) | copy-start | bytes 1540
  63.8 43.0 %copy-start.23 = (f32[128]{0:T(128)S(1)}, f32[128]{0:T(128)}, u32[]{:S(2)}) copy-start(f32[128]{0:T(128)} %param.24) | copy-start | bytes 1540
  63.8 16.2 %collective-permute-start.1 = (bf16[4,256,512]{2,1,0:T(8,128)(2,1)S(1)}, bf16[4,256,512]{2,1,0:T(8,128)(2,1)}, u32[]{:S(2)}, u32[]{:S(2)}) collective-permute-start(bf16[4,256,512]{2,1,0:T(8,128)(2,1)S(1)} %all-to-all-done.refs_0_), channel_id=1, source_target_pairs={{0,32},{32,0},{1,33},{33,1},{2,34},{34,2},{3,35},{35,3},{4,36},{36... | collective-permute-start | bytes 3145736 | tf_op jit(solution)/shard_map/ppermute | solution.py:53
  78.0 4.5 %collective-permute-start.2 = (bf16[4,256,512]{2,1,0:T(8,128)(2,1)S(1)}, bf16[4,256,512]{2,1,0:T(8,128)(2,1)S(1)}, u32[]{:S(2)}, u32[]{:S(2)}) collective-permute-start(bf16[4,256,512]{2,1,0:T(8,128)(2,1)S(1)} %all-to-all-done.1.refs_2_), channel_id=1, source_target_pairs={{0,32},{32,0},{1,33},{33,1},{2,34},{34,2},{3,35},{35,3},{4,36},{36... | collective-permute-start | bytes 3145736 | tf_op jit(solution)/shard_map/ppermute | solution.py:53
  85.0 49.5 %copy-start.27 = (s32[32,1]{0,1:T(1,128)S(1)}, s32[32,1]{0,1:T(1,128)}, u32[]{:S(2)}) copy-start(s32[32,1]{0,1:T(1,128)} %get-tuple-element.54) | copy-start | bytes 388
  106.7 27.9 %copy-start.26 = (s32[256]{0:T(256)S(1)}, s32[256]{0:T(256)}, u32[]{:S(2)}) copy-start(s32[256]{0:T(256)} %pad_add_fusion) | copy-start | bytes 3076
  108.9 19.6 %all-to-all-start.3 = ((bf16[2,128,128]{2,1,0:T(8,128)(2,1)}), bf16[2,128,128]{2,1,0:T(8,128)(2,1)S(1)}, u32[]{:S(2)}, u32[]{:S(2)}) async-start(bf16[2,128,128]{2,1,0:T(8,128)(2,1)} %get-tuple-element.44.own_ref), calls=%async_computation.3 | async-start | bytes 131072 | tf_op jit(solution)/shard_map/all_to_all | solution.py:578
  114.6 86.7 %all-gather.10.cloned.1.call-start = ((), (), s32[]{:S(2)}) async-start(), calls=%async_computation.17 | async-start | bytes 1597440 | tf_op jit(solution)/shard_map/all_gather | solution.py:573
  129.2 10.1 %all-to-all-start.4 = ((bf16[4,2,128,128]{3,2,1,0:T(8,128)(2,1)}), bf16[4,2,128,128]{3,2,1,0:T(8,128)(2,1)S(1)}, u32[]{:S(2)}, u32[]{:S(2)}) async-start(bf16[4,2,128,128]{3,2,1,0:T(8,128)(2,1)} %broadcast_in_dim.118), calls=%async_computation.4 | async-start | bytes 524288 | tf_op jit(solution)/shard_map/all_to_all | solution.py:36
  132.6 11.1 %collective-permute-start.3 = (bf16[64,128]{1,0:T(8,128)(2,1)S(1)}, bf16[64,128]{1,0:T(8,128)(2,1)S(1)}, u32[]{:S(2)}, u32[]{:S(2)}) collective-permute-start(bf16[64,128]{1,0:T(8,128)(2,1)S(1)} %get-tuple-element.53.nm_ref), channel_id=1, source_target_pairs={{0,32},{32,0},{1,33},{33,1},{2,34},{34,2},{3,35},{35,3},{4,36},{36... | collective-permute-start | bytes 49160 | tf_op jit(solution)/shard_map/ppermute | solution.py:53
  138.2 7.2 %copy-start.10 = (bf16[1,1024,128]{2,1,0:T(8,128)(2,1)S(1)}, bf16[1,1024,128]{2,1,0:T(8,128)(2,1)}, u32[]{:S(2)}) copy-start(bf16[1,1024,128]{2,1,0:T(8,128)(2,1)} %get-tuple-element.32.k_ref) | copy-start | bytes 786436
  138.2 7.2 %copy-start.11 = (bf16[1,1024,128]{2,1,0:T(8,128)(2,1)S(1)}, bf16[1,1024,128]{2,1,0:T(8,128)(2,1)}, u32[]{:S(2)}) copy-start(bf16[1,1024,128]{2,1,0:T(8,128)(2,1)} %get-tuple-element.33.v_ref) | copy-start | bytes 786436
  140.2 5.2 %all-to-all-start.5 = ((bf16[2,4,2,128,128]{4,3,2,1,0:T(8,128)(2,1)}), bf16[2,4,2,128,128]{4,3,2,1,0:T(8,128)(2,1)S(1)}, u32[]{:S(2)}, u32[]{:S(2)}) async-start(bf16[2,4,2,128,128]{4,3,2,1,0:T(8,128)(2,1)} %broadcast_in_dim.119), calls=%async_computation.5 | async-start | bytes 1048576 | tf_op jit(solution)/shard_map/all_to_all | solution.py:36
  178.6 14.9 %all-to-all-start.7 = ((bf16[4,2,160,256]{3,2,1,0:T(8,128)(2,1)}), bf16[4,2,160,256]{3,2,1,0:T(8,128)(2,1)S(1)}, u32[]{:S(2)}, u32[]{:S(2)}) async-start(bf16[4,2,160,256]{3,2,1,0:T(8,128)(2,1)} %broadcast_in_dim.120), calls=%async_computation.7 | async-start | bytes 1310720 | tf_op jit(solution)/shard_map/all_to_all | solution.py:36
  182.9 54.8 %all-gather.6.cloned.1.call-start = ((), (), s32[]{:S(2)}) async-start(), calls=%async_computation.15 | async-start | bytes 2662400 | tf_op jit(solution)/shard_map/all_gather | solution.py:604
  193.7 4.9 %copy-start.9 = (bf16[4,256,512]{2,1,0:T(8,128)(2,1)S(1)}, bf16[4,256,512]{2,1,0:T(8,128)(2,1)}, u32[]{:S(2)}) copy-start(bf16[4,256,512]{2,1,0:T(8,128)(2,1)} %copy-done.8) | copy-start | bytes 3145732
  203.5 32.0 %copy-start = (bf16[4160,256]{1,0:T(8,128)(2,1)S(1)}, bf16[4160,256]{1,0:T(8,128)(2,1)}, u32[]{:S(2)}) copy-start(bf16[4160,256]{1,0:T(8,128)(2,1)} %all-gather.8.cloned.1.call-done) | copy-start | bytes 6389764
  225.3 25.9 %all-to-all-start.10 = ((bf16[8,128,128]{2,1,0:T(8,128)(2,1)}), bf16[8,128,128]{2,1,0:T(8,128)(2,1)S(1)}, u32[]{:S(2)}, u32[]{:S(2)}) async-start(bf16[8,128,128]{2,1,0:T(8,128)(2,1)} %reduce_sum.74), calls=%async_computation.10 | async-start | bytes 524288 | tf_op jit(solution)/shard_map/all_to_all | solution.py:607
  235.5 41.9 %collective-permute-start.4 = (bf16[4,1040,256]{2,1,0:T(8,128)(2,1)S(1)}, bf16[4,1040,256]{2,1,0:T(8,128)(2,1)}, u32[]{:S(2)}, u32[]{:S(2)}) collective-permute-start(bf16[4,1040,256]{2,1,0:T(8,128)(2,1)S(1)} %bitcast.52), channel_id=1, source_target_pairs={{0,32},{32,0},{1,33},{33,1},{2,34},{34,2},{3,35},{35,3},{4,36},{36... | collective-permute-start | bytes 6389768 | tf_op jit(solution)/shard_map/ppermute | solution.py:53
  237.7 51.4 %collective-permute-start.5 = (bf16[4,1040,256]{2,1,0:T(8,128)(2,1)}, bf16[4,1040,256]{2,1,0:T(8,128)(2,1)}, u32[]{:S(2)}, u32[]{:S(2)}) collective-permute-start(bf16[4,1040,256]{2,1,0:T(8,128)(2,1)} %all-gather.6.cloned.1.call-done.refs_2_.refs_6_), channel_id=1, source_target_pairs={{0,32},{32,0},{1,33},{33,1},{2,34},{34,2},{3,35},{35,3},{4,36},{36... | collective-permute-start | bytes 6389768 | tf_op jit(solution)/shard_map/ppermute | solution.py:53
  273.7 15.5 %copy-start.20 = (f32[4096]{0:T(1024)S(1)}, f32[4096]{0:T(1024)}, u32[]{:S(2)}) copy-start(f32[4096]{0:T(1024)} %param.25) | copy-start | bytes 49156
  273.7 14.5 %all-to-all-start.12 = ((bf16[4,8,128,128]{3,2,1,0:T(8,128)(2,1)}), bf16[4,8,128,128]{3,2,1,0:T(8,128)(2,1)S(1)}, u32[]{:S(2)}, u32[]{:S(2)}) async-start(bf16[4,8,128,128]{3,2,1,0:T(8,128)(2,1)} %broadcast_in_dim.123), calls=%async_computation.12 | async-start | bytes 2097152 | tf_op jit(solution)/shard_map/all_to_all | solution.py:36
  316.0 27.9 %copy-start.24 = (f32[4096]{0:T(1024)S(1)}, f32[4096]{0:T(1024)}, u32[]{:S(2)}) copy-start(f32[4096]{0:T(1024)} %param.29) | copy-start | bytes 49156
  317.0 26.4 %all-to-all-start.14 = ((bf16[8,4,4096]{2,1,0:T(4,128)(2,1)}), bf16[8,4,4096]{2,1,0:T(4,128)(2,1)S(1)}, u32[]{:S(2)}, u32[]{:S(2)}) async-start(bf16[8,4,4096]{2,1,0:T(4,128)(2,1)} %reshape.133), calls=%async_computation.14 | async-start | bytes 524288 | tf_op jit(solution)/shard_map/all_to_all | solution.py:619
  (17 other events, 26.6 us)
Sparse Core Ops, SparseCore 0:
  27.6 37.7 all-gather.7
  117.5 72.5 all-gather.9
  203.6 34.0 all-gather.5

commit v5 on v4

--- a/solution.py
+++ b/solution.py
@@ -45,30 +45,8 @@
     return a.reshape((N_SEQ,) + a.shape[3:])
 
 
-def seq_slot(s):
-    return (s % 2) * 8 + (s // 4) * 2 + (s // 2) % 2
-
-
 def swap(a, axis, count):
     return lax.ppermute(a, axis, [(i, i ^ 1) for i in range(count)])
-
-
-def layout(passage_order, separators, recompute_index, prompt_lengths):
-    requests = N_SEQ // PPR
-    slot_ids = jnp.arange(PPR, dtype=jnp.int32)
-    opening = slot_ids[None, :] * PLEN + jnp.cumsum(separators, axis=1)
-    flat = passage_order.reshape(-1)
-    hit = flat[None, :] == jnp.arange(N_SEQ, dtype=jnp.int32)[:, None]
-    starts = jnp.sum(jnp.where(hit, opening.reshape(-1)[None, :], 0), axis=1)
-    place = jnp.sum(jnp.where(hit, jnp.arange(N_SEQ, dtype=jnp.int32)[None, :], 0), axis=1)
-    owners = place // PPR
-    prompt_start = opening[:, PPR - 1] + PLEN
-    new_index = jnp.arange(PPR * TOKN_DEV, dtype=jnp.int32)
-    new_positions = (prompt_start[:, None] + new_index[None, :]).reshape(N_SEQ, TOKN_DEV)
-    new_live = (new_index[None, :] < prompt_lengths[:, None]).reshape(N_SEQ, TOKN_DEV)
-    picked = starts[:, None] + recompute_index
-    positions = jnp.concatenate([picked, new_positions], axis=1)
-    return starts, owners, positions, new_live
 
 
 def partial_attention(queries, keys, values, visible):
@@ -105,20 +83,20 @@
 
 
 def whole(a):
-    return pl.BlockSpec(a.shape, lambda *k: (0,) * a.ndim)
+    return pl.BlockSpec(a.shape, lambda *k: (0,) * len(a.shape))
 
 
 SMEM = pl.BlockSpec(memory_space=pltpu.SMEM)
 
 
-def call(kernel, name, out_shape, *args, scratch=(), limit=24):
+def call(kernel, name, out_shape, *args, scratch=(), limit=16):
     small = [a.ndim == 1 for a in args]
     return pl.pallas_call(
         kernel,
         grid=(1,),
         out_shape=out_shape,
         in_specs=[SMEM if one else whole(a) for a, one in zip(args, small)],
-        out_specs=jax.tree.map(whole, out_shape),
+        out_specs=jax.tree.map(lambda a: SMEM if len(a.shape) == 1 else whole(a), out_shape),
         scratch_shapes=list(scratch),
         compiler_params=pltpu.CompilerParams(vmem_limit_bytes=limit << 20),
         name=name,
@@ -127,6 +105,91 @@
 
 def shape(dims, dtype):
     return jax.ShapeDtypeStruct(dims, dtype)
+
+
+def tables(seq, passage_order, separators, prompt_lengths, recompute_index):
+    spare = 8
+
+    def kernel(
+        s_ref, o_ref, sep_ref, len_ref, i_ref, t_ref,
+        at_ref, wanted_ref, picked_ref, new_ref, new_key_ref, attend_ref, merge_ref, column_ref,
+    ):
+        seq = s_ref[0]
+        place = jnp.int32(0)
+        for n in range(N_SEQ):
+            place = jnp.where(o_ref[n] == seq, n, place)
+
+        def start_of(request, slot):
+            first = sep_ref[2 * request]
+            return first + jnp.where(slot == 1, PLEN + sep_ref[2 * request + 1], 0)
+
+        request, mine = place >> 1, seq >> 1
+        chosen = [o_ref[2 * request + i] for i in range(PPR)]
+        start = start_of(request, place & 1)
+        base = start_of(request, 1) + PLEN
+        my_base = start_of(mine, 1) + PLEN
+        my_from = (seq & 1) * TOKN_DEV
+
+        lane = lax.broadcasted_iota(jnp.int32, (SEL, N_SEQ), 1)
+        index = t_ref[...].astype(f32)
+
+        def column(passage):
+            return jnp.sum(jnp.where(lane == passage, index, 0.0), axis=1, keepdims=True)
+
+        count = PPR * TOKN_DEV
+        down = lax.broadcasted_iota(jnp.int32, (count, 1), 0)
+        at_ref[:SEL, :] = column(seq) + start.astype(f32)
+        at_ref[SEL:ROW_DEV, :] = (my_base + my_from + down[:TOKN_DEV]).astype(f32)
+        at_ref[ROW_DEV:, :] = jnp.full((spare, 1), start, jnp.int32).astype(f32)
+        for i in range(PPR):
+            at = column(chosen[i]) + start_of(request, i).astype(f32)
+            wanted_ref[i * SEL : (i + 1) * SEL, :] = at.astype(jnp.int32)
+        wanted_ref[PPR * SEL :, :] = base + down
+        picked_ref[...] = jnp.full((1, HD), -1, jnp.int32)
+        picked_ref[:, :SEL] = i_ref[pl.ds(seq, 1), :]
+        new_ref[...] = my_base + my_from + down[:TOKN_DEV]
+        across = lax.broadcasted_iota(jnp.int32, (1, count), 1)
+        token = across ^ my_from
+        new_key_ref[...] = jnp.where(token < len_ref[mine], my_base + token, 1 << 30)
+
+        def slot(s):
+            return (s & 1) * 8 + (s >> 2) * 2 + ((s >> 1) & 1)
+
+        attend_ref[0] = slot(chosen[0])
+        attend_ref[1] = slot(chosen[1])
+        attend_ref[2] = slot(2 * request)
+        attend_ref[3] = slot(2 * request + 1)
+        attend_ref[4] = start
+        merge_ref[0] = slot(chosen[0])
+        merge_ref[1] = slot(o_ref[2 * mine])
+        merge_ref[2] = slot(o_ref[2 * mine + 1])
+        merge_ref[3] = seq & 1
+        merge_ref[4] = jnp.where(chosen[0] == seq, 1, 0)
+        for m in range(N_SEQ):
+            other = (m // 8) * 2 + m // 4 % 2
+            column_ref[m] = m % 4 * 4 + ((seq & 3) ^ other)
+
+    i32 = jnp.int32
+    return call(
+        kernel,
+        "tables",
+        (
+            shape((ROW_DEV + spare, 1), f32),
+            shape((PPR * (SEL + TOKN_DEV), 1), i32),
+            shape((1, HD), i32),
+            shape((TOKN_DEV, 1), i32),
+            shape((1, PPR * TOKN_DEV), i32),
+            shape((5,), i32),
+            shape((5,), i32),
+            shape((N_SEQ,), i32),
+        ),
+        seq[None],
+        passage_order,
+        separators.reshape(-1),
+        prompt_lengths,
+        recompute_index,
+        recompute_index.T,
+    )
 
 
 def join_weights(query_weight, key_weight, value_weight, output_weight):
@@ -258,6 +321,7 @@
             whole(new_values),
         ],
         out_specs=(tile, tile),
+        compiler_params=pltpu.CompilerParams(vmem_limit_bytes=8 << 20),
         name="blend",
     )(picked, cosine, sine, keys, values, new_keys, new_values)
 
@@ -366,7 +430,7 @@
         + [out_weights] * len(weights),
         out_specs=pl.BlockSpec((blocks, ROW_DEV, width), lambda i: (0, 0, 0)),
         scratch_shapes=[pltpu.VMEM((ROW_DEV, width), f32)],
-        compiler_params=pltpu.CompilerParams(vmem_limit_bytes=24 << 20),
+        compiler_params=pltpu.CompilerParams(vmem_limit_bytes=16 << 20),
         name="merge_and_project",
     )(control, kept, new_part, returned, *weights)
 
@@ -375,86 +439,85 @@
     blocks, rows, part = summed.shape
     model = blocks * part
     count, _, depth = parcels[0].shape
-    group = 2
-    half = count // group
     parts = len(parcels)
-    steps = parts * half
     split = depth // part
     per = rows // (NZL * NX)
     contract_last = (((1,), (1,)), ((), ()))
 
     def kernel(c_ref, s_ref, x_ref, g_ref, *refs):
-        within_refs, down_refs = refs[:parts], refs[parts : 2 * parts]
-        out_ref, mixed_ref, norm_ref, acc_ref = refs[2 * parts :]
-        k = pl.program_id(0)
-
-        @pl.when(k == 0)
-        def _():
-            squares = jnp.zeros((rows, part), f32)
-            for b in range(blocks):
-                block = s_ref[b].astype(f32)
-                squares = squares + block * block
-            norm_ref[...] = lax.rsqrt(
-                jnp.sum(squares, axis=1, keepdims=True) / model + EPSILON
+        parcel_refs = refs[:parts]
+        out_ref, mixed_ref, within_ref, down_ref, acc_ref, within_sem, down_sem = refs[parts:]
+        within = [
+            pltpu.make_async_copy(
+                parcel_refs[m // count].at[m % count, pl.ds(0, 2 * units)],
+                within_ref.at[m],
+                within_sem.at[m],
             )
-            acc_ref[...] = jnp.zeros_like(acc_ref)
-
-        def add(ref):
-            for n in range(group):
-                m = k * group + n
-                at = pl.multiple_of(c_ref[m] * depth, depth)
-                cols = pl.ds(at, depth)
-                summed = jnp.concatenate([s_ref[m * split + h] for h in range(split)], axis=1)
-                mixed = (
-                    x_ref[:, cols].astype(f32)
-                    + summed.astype(f32) * norm_ref[...] * g_ref[:, cols]
-                ).astype(bf16)
-                mixed_ref[:, cols] = mixed
-                acc_ref[...] += lax.dot_general(
-                    ref[n], mixed, contract_last, preferred_element_type=f32
-                )
-
-        for j in range(parts):
-            pl.when(k // half == j)(functools.partial(add, within_refs[j]))
-
-        @pl.when(k == steps - 1)
-        def _():
-            to = lax.broadcasted_iota(jnp.int32, (rows, rows), 0)
-            at = lax.broadcasted_iota(jnp.int32, (rows, rows), 1)
-            source = (to // per) % NZL * (NX * per) + to // (NZL * per) * per + to % per
-            move = jnp.where(at == source, 1.0, 0.0).astype(bf16)
-            gate = acc_ref[:units, :]
-            active = (gate / (1.0 + jnp.exp(-gate)) * acc_ref[units:, :]).astype(bf16)
-            active = lax.dot_general(
-                move, active, contract_last, preferred_element_type=f32
+            for m in range(parts * count)
+        ]
+        down = [
+            pltpu.make_async_copy(
+                parcel_refs[m // count].at[m % count, pl.ds(2 * units, units)],
+                down_ref.at[m],
+                down_sem.at[m],
+            )
+            for m in range(parts * count)
+        ]
+        for copy in within + down:
+            copy.start()
+        squares = jnp.zeros((rows, part), f32)
+        for b in range(blocks):
+            block = s_ref[b].astype(f32)
+            squares = squares + block * block
+        norm = lax.rsqrt(jnp.sum(squares, axis=1, keepdims=True) / model + EPSILON)
+        for m in range(parts * count):
+            cols = pl.ds(pl.multiple_of(c_ref[m] * depth, depth), depth)
+            summed = jnp.concatenate([s_ref[m * split + h] for h in range(split)], axis=1)
+            mixed = (
+                x_ref[:, cols].astype(f32) + summed.astype(f32) * norm * g_ref[:, cols]
             ).astype(bf16)
-            for m in range(parts * count):
-                at_col = pl.multiple_of(c_ref[m] * depth, depth)
-                out_ref[:, pl.ds(at_col, depth)] = jnp.dot(
-                    active, down_refs[m // count][m % count], preferred_element_type=f32
-                ).astype(bf16)
+            mixed_ref[:, cols] = mixed
+            within[m].wait()
+            product = lax.dot_general(
+                within_ref[m], mixed, contract_last, preferred_element_type=f32
+            )
+            acc_ref[...] = product if m == 0 else acc_ref[...] + product
+        to = lax.broadcasted_iota(jnp.int32, (rows, rows), 0)
+        at = lax.broadcasted_iota(jnp.int32, (rows, rows), 1)
+        source = (to // per) % NZL * (NX * per) + to // (NZL * per) * per + to % per
+        move = jnp.where(at == source, 1.0, 0.0).astype(bf16)
+        gate = acc_ref[:units, :]
+        active = (gate / (1.0 + jnp.exp(-gate)) * acc_ref[units:, :]).astype(bf16)
+        active = lax.dot_general(
+            move, active, contract_last, preferred_element_type=f32
+        ).astype(bf16)
+        for m in range(parts * count):
+            cols = pl.ds(pl.multiple_of(c_ref[m] * depth, depth), depth)
+            down[m].wait()
+            out_ref[:, cols] = jnp.dot(
+                active, down_ref[m], preferred_element_type=f32
+            ).astype(bf16)
 
     return pl.pallas_call(
         kernel,
-        grid=(steps,),
+        grid=(1,),
         out_shape=(shape((rows, model), bf16), shape((rows, model), bf16)),
         in_specs=[SMEM, whole(summed), whole(hidden), whole(gain)]
-        + [
-            pl.BlockSpec(
-                (group, 2 * units, depth),
-                lambda k, j=j: (jnp.clip(k - j * half, 0, half - 1), 0, 0),
-            )
-            for j in range(parts)
-        ]
-        + [pl.BlockSpec((count, units, depth), lambda k: (0, 2, 0))] * parts,
+        + [pl.BlockSpec(memory_space=pl.ANY)] * parts,
         out_specs=(
             pl.BlockSpec((rows, model), lambda k: (0, 0)),
             pl.BlockSpec((rows, model), lambda k: (0, 0)),
         ),
-        scratch_shapes=[pltpu.VMEM((rows, 1), f32), pltpu.VMEM((2 * units, rows), f32)],
-        compiler_params=pltpu.CompilerParams(vmem_limit_bytes=40 << 20),
+        scratch_shapes=[
+            pltpu.VMEM((parts * count, 2 * units, depth), bf16),
+            pltpu.VMEM((parts * count, units, depth), bf16),
+            pltpu.VMEM((2 * units, rows), f32),
+            pltpu.SemaphoreType.DMA((parts * count,)),
+            pltpu.SemaphoreType.DMA((parts * count,)),
+        ],
+        compiler_params=pltpu.CompilerParams(vmem_limit_bytes=24 << 20),
         name="feed_forward",
-    )(columns, summed, hidden, gain, *parcels, *parcels)
+    )(columns, summed, hidden, gain, *parcels)
 
 
 def shards(
@@ -492,75 +555,16 @@
     parcel = jnp.concatenate([gate_weight.T, up_weight.T, down_weight])
     parcel = jnp.pad(parcel, ((0, -parcel.shape[0] % 16), (0, 0)))
 
-    order_of = jnp.arange(N_SEQ, dtype=jnp.int32)
-    columns = order_of % 4 * 4 + (zh ^ (order_of // 8)) * 2 + (core ^ (order_of // 4 % 2))
-    starts, owners, positions, new_live = layout(
-        passage_order, separators, recompute_index, prompt_lengths
-    )
-
-    def rows_of(table, s):
-        return lax.dynamic_index_in_dim(table, s, 0, False)
-
+    at, wanted_at, picked, new_at, new_key_at, attend_control, merge_control, columns = tables(
+        seq, passage_order, separators, prompt_lengths, recompute_index
+    )
     frequency = frequencies()
-    my_positions = rows_of(positions, seq)
-    angles = my_positions.astype(f32)[:, None] * frequency[None, :]
-    cosine, sine = jnp.cos(angles), jnp.sin(angles)
-    cosine = jnp.concatenate([cosine, cosine], axis=1)
-    sine = jnp.concatenate([-sine, sine], axis=1)
-    start = rows_of(starts, seq)
-    turn = (start.astype(f32) * frequency)[None, :]
-    turn_cosine, turn_sine = jnp.cos(turn), jnp.sin(turn)
-    turn_cosine = jnp.concatenate([turn_cosine, turn_cosine], axis=1)
-    turn_sine = jnp.concatenate([-turn_sine, turn_sine], axis=1)
-    picked = jnp.pad(rows_of(recompute_index, seq), (0, width - SEL), constant_values=-1)[None]
-    request = rows_of(owners, seq)
-    order = passage_order.reshape(-1, PPR)
-    chosen = rows_of(order, request)
-    my_order = rows_of(order, seq // 2)
-    sources = [chosen[0], chosen[1], request * 2, request * 2 + 1]
-    cuts = [slice(0, SEL), slice(0, SEL), slice(SEL, None), slice(SEL, None)]
-    wanted_at = jnp.concatenate([rows_of(positions, s)[c] for s, c in zip(sources, cuts)])[:, None]
-    partner = seq + 1 - 2 * core
-    far_away = jnp.int32(1 << 30)
-    new_key_at = jnp.concatenate(
-        [
-            jnp.where(rows_of(new_live, s), rows_of(positions, s)[SEL:], far_away)
-            for s in (seq, partner)
-        ]
-    )[None]
-    new_at = my_positions[SEL:][:, None]
-    first = chosen[0] == seq
-    attend_control = jnp.stack([seq_slot(s) for s in sources] + [start]).astype(jnp.int32)
-    merge_control = jnp.stack(
-        [seq_slot(chosen[0]), seq_slot(my_order[0]), seq_slot(my_order[1]), core, first]
-    ).astype(jnp.int32)
-    tables = (
-        columns,
-        cosine,
-        sine,
-        turn_cosine,
-        turn_sine,
-        picked,
-        wanted_at,
-        new_key_at,
-        new_at,
-        attend_control,
-        merge_control,
-    )
-    theirs, near, tables = lax.optimization_barrier((theirs, near, tables))
-    (
-        columns,
-        cosine,
-        sine,
-        turn_cosine,
-        turn_sine,
-        picked,
-        wanted_at,
-        new_key_at,
-        new_at,
-        attend_control,
-        merge_control,
-    ) = tables
+    angles = at * jnp.concatenate([frequency, frequency])[None, :]
+    sign = jnp.where(jnp.arange(HD) < HD // 2, -1.0, 1.0).astype(f32)
+    cosine, sine = jnp.cos(angles), jnp.sin(angles) * sign
+    theirs, near, cosine, sine = lax.optimization_barrier((theirs, near, cosine, sine))
+    turn_cosine, turn_sine = cosine[ROW_DEV : ROW_DEV + 1], sine[ROW_DEV : ROW_DEV + 1]
+    cosine, sine = cosine[:ROW_DEV], sine[:ROW_DEV]
 
     near_other = swap(near, "core", NCORE)
     far = copies_to_all(theirs, "y", NY)
@@ -601,12 +605,13 @@
 
     terms = merge_and_project(merge_control, kept, new_part, returned, weights)
     terms, pair = lax.optimization_barrier((terms, pair))
-    parcel_far = lax.all_gather(jnp.where(zh == 0, pair[1], pair[0]), "y")
+    parcel_far = lax.all_gather(lax.dynamic_index_in_dim(pair, 1 - zh, 0, False), "y")
     terms = lax.all_to_all(terms.reshape(NX, NZL, ROW_DEV, width), "x", 0, 0, tiled=True)
     terms = jnp.sum(terms.astype(f32), axis=0).astype(bf16)
     terms = lax.all_to_all(terms, "zl", 0, 0, tiled=True)
     summed = jnp.sum(terms.astype(f32), axis=0).astype(bf16)
     summed = copies_to_all(summed, "zl", NZL)
+    summed, parcel_far = lax.optimization_barrier((summed, parcel_far))
     summed = copies_to_all(summed, "x", NX).reshape(blocks, ROW_DEV, model // blocks)
 
     parcels = [parcel_near, swap(parcel_near, "core", NCORE)]

time: 354 us -> 351 us (level)
  waiting for transfers between devices: 78.5 us -> 117 us
  between operations: 31.1 us -> 14.2 us
  blocking collectives: 109 us -> 93.9 us
  other arithmetic: 12.2 us -> 4.81 us
    all_to_all x2 -> x1, blocking collectives: 26 us -> 4.92 us  [copies_to_all(): lax.all_to_all(jnp.broadcast_to(a[None], (count,) + a.shape), axis, 0, 0,...]
    all_to_all x6 -> x7, waiting for transfers between devices: 36.5 us -> 56 us  [copies_to_all(): lax.all_to_all(jnp.broadcast_to(a[None], (count,) + a.shape), axis, 0, 0,...]
    ppermute x6, waiting for transfers between devices: 2.63 us -> 20.8 us  [swap(): return lax.ppermute(a, axis, [(i, i ^ 1) for i in range(count)])]
    all_to_all x1, starting transfers between devices: 12.7 us -> 5.47 us  [shards(): lax.all_to_all(terms.reshape(NZL, rows, model), 'zl', 0, 0, tiled=True)]
    all_to_all x6 -> x7, starting transfers between devices: 24.3 us -> 29.3 us  [copies_to_all(): lax.all_to_all(jnp.broadcast_to(a[None], (count,) + a.shape), axis, 0, 0,...]
    unnamed x62 -> x78, local copies, waits for them, and re-layouts: 12.3 us -> 7.59 us
    all_to_all x1, blocking collectives: 13.3 us -> 17.7 us  [shards(): lax.all_to_all(terms.reshape(NX, NZL * rows, model), 'x', 0, 0, tiled=True)]
    pallas_call x4 -> x5, Pallas kernels: 7.22 us -> 7.38 us  [call(): pl.pallas_call(kernel, grid=(1,), out_shape=out_shape, in_specs=[SMEM if...]
  transfers between devices with their start and end apart: 18 -> 19, of which waited for: 10 -> 11; matrix products, arithmetic and copies ran while one was open for 5% -> 3% of each run, Pallas kernels for 3% -> 3%
where the time goes in v5:
time: 351 us; the launch traced here: 350 us
  waiting for transfers between devices  117 us (33%)
  blocking collectives  93.9 us (27%)
  starting transfers between devices  79 us (23%)
  Pallas kernels  20.4 us (6%)
  local copies, waits for them, and re-layouts  20.2 us (6%)
  between operations  14.2 us (4%)
  other arithmetic  4.81 us (1%)
    all_to_all x7, waiting for transfers between devices, copies_to_all(): lax.all_to_all(jnp.broadcast_to(a[None], (count,) + a.shape), axis, 0, 0,...  56 us
    all_to_all x7, starting transfers between devices, copies_to_all(): lax.all_to_all(jnp.broadcast_to(a[None], (count,) + a.shape), axis, 0, 0,...  29.3 us
    all_to_all x1, blocking collectives, shards(): returned = lax.all_to_all(returned, 'zh', 0, 0, tiled=True)  28.5 us
    ppermute x6, starting transfers between devices, swap(): return lax.ppermute(a, axis, [(i, i ^ 1) for i in range(count)])  24.4 us
    all_to_all x1, blocking collectives, shards(): terms = lax.all_to_all(terms, 'zl', 0, 0, tiled=True)  23.7 us
    ppermute x6, waiting for transfers between devices, swap(): return lax.ppermute(a, axis, [(i, i ^ 1) for i in range(count)])  20.8 us
    all_to_all x1, blocking collectives, shards(): lax.all_to_all(terms.reshape(NX, NZL, ROW_DEV, width), 'x', 0, 0, tiled=T...  19 us
    all_to_all x1, blocking collectives, shards(): lax.all_to_all(terms.reshape(NX, NZL * rows, model), 'x', 0, 0, tiled=True)  17.7 us
  transfers between devices with their start and end apart: 19, of which 11 were waited for; matrix products, arithmetic and copies ran while one was open for 3% of the time, Pallas kernels for 3%

profile of v5, /device:TPU:32, one launch (start us, length us, event | category | flops | bytes accessed | tf_op | source)
XLA Modules:
  0.0 349.8 jit_solution(1442568166287822427)
XLA Ops:
  7.3 2.0 fusion.4
  10.5 4.6 %all-to-all-start = ((bf16[4,256,512]{2,1,0:T(8,128)(2,1)}), bf16[4,256,512]{2,1,0:T(8,128)(2,1)S(1)}, u32[]{:S(2)}, u32[]{:S(2)}) async-start(bf16[4,256,512]{2,1,0:T(8,128)(2,1)} %broadcast_in_dim.33), calls=%async_computation | async-start | bytes 2097152 | tf_op jit(solution)/shard_map/all_to_all | solution.py:36
  15.1 14.8 %collective-permute-start = (bf16[256,512]{1,0:T(8,128)(2,1)S(1)}, bf16[256,512]{1,0:T(8,128)(2,1)S(1)}, u32[]{:S(2)}, u32[]{:S(2)}) collective-permute-start(bf16[256,512]{1,0:T(8,128)(2,1)S(1)} %join_weights.1), channel_id=1, source_target_pairs={{0,64},{64,0},{1,65},{65,1},{2,66},{66,2},{3,67},{67,3},{4,68},{68... | collective-permute-start | bytes 786440 | tf_op jit(solution)/shard_map/ppermute | solution.py:49
  34.8 18.2 %collective-permute-done = bf16[256,512]{1,0:T(8,128)(2,1)S(1)} collective-permute-done((bf16[256,512]{1,0:T(8,128)(2,1)S(1)}, bf16[256,512]{1,0:T(8,128)(2,1)S(1)}, u32[]{:S(2)}, u32[]{:S(2)}) %collective-permute-start) | collective-permute-done | bytes 262176 | tf_op jit(solution)/shard_map/ppermute | solution.py:49
  54.0 4.5 %all-to-all-start.1 = ((bf16[4,256,512]{2,1,0:T(8,128)(2,1)}), bf16[4,256,512]{2,1,0:T(8,128)(2,1)S(1)}, u32[]{:S(2)}, u32[]{:S(2)}) async-start(bf16[4,256,512]{2,1,0:T(8,128)(2,1)} %broadcast_in_dim.36), calls=%async_computation.1 | async-start | bytes 2097152 | tf_op jit(solution)/shard_map/all_to_all | solution.py:36
  60.5 12.2 %all-to-all-done.1.refs_2_ = bf16[4,256,512]{2,1,0:T(8,128)(2,1)S(1)} async-done(((bf16[4,256,512]{2,1,0:T(8,128)(2,1)}), bf16[4,256,512]{2,1,0:T(8,128)(2,1)S(1)}, u32[]{:S(2)}, u32[]{:S(2)}) %all-to-all-start.1) | async-done | bytes 1048608 | tf_op jit(solution)/shard_map/all_to_all | solution.py:36
  72.7 1.9 collective-permute-start.2
  74.6 2.6 collective-permute-done.2.refs_3_
  80.9 11.5 %all-to-all-start.2 = ((f32[32,8,128]{2,1,0:T(8,128)}), f32[32,8,128]{2,1,0:T(8,128)S(1)}, u32[]{:S(2)}, u32[]{:S(2)}) async-start(f32[32,8,128]{2,1,0:T(8,128)} %copy-done.13), calls=%async_computation.2 | async-start | bytes 262144 | tf_op jit(solution)/shard_map/all_to_all | solution.py:575
  94.1 11.4 %all-to-all-done.2.s_ref = f32[32,8,128]{2,1,0:T(8,128)S(1)} async-done(((f32[32,8,128]{2,1,0:T(8,128)}), f32[32,8,128]{2,1,0:T(8,128)S(1)}, u32[]{:S(2)}, u32[]{:S(2)}) %all-to-all-start.2) | async-done | bytes 131104 | tf_op jit(solution)/shard_map/all_to_all | solution.py:575
  107.8 8.4 %all-to-all-start.3 = ((bf16[2,128,128]{2,1,0:T(8,128)(2,1)}), bf16[2,128,128]{2,1,0:T(8,128)(2,1)S(1)}, u32[]{:S(2)}, u32[]{:S(2)}) async-start(bf16[2,128,128]{2,1,0:T(8,128)(2,1)} %get-tuple-element.46.own_ref), calls=%async_computation.3 | async-start | bytes 131072 | tf_op jit(solution)/shard_map/all_to_all | solution.py:582
  117.0 13.2 %all-to-all-done.3 = bf16[2,128,128]{2,1,0:T(8,128)(2,1)S(1)} async-done(((bf16[2,128,128]{2,1,0:T(8,128)(2,1)}), bf16[2,128,128]{2,1,0:T(8,128)(2,1)S(1)}, u32[]{:S(2)}, u32[]{:S(2)}) %all-to-all-start.3) | async-done | bytes 65568 | tf_op jit(solution)/shard_map/all_to_all | solution.py:582
  130.9 3.4 all-to-all-start.4
  134.3 1.9 collective-permute-start.3
  141.8 3.5 all-to-all-start.5
  147.1 3.7 %attend.1 = (bf16[2,160,256]{2,1,0:T(8,128)(2,1)S(1)}, f32[192,256]{1,0:T(8,128)S(1)}, f32[32,256]{1,0:T(8,128)S(1)}) custom-call(s32[5]{0:T(128)S(1)} %copy-done.29, bf16[16,128,128]{2,1,0:T(8,128)(2,1)S(1)} %bitcast.17, bf16[1,1024,128]{2,1,0:T(8,128)(2,1)S(1)} %copy-done.9, bf16[1,1024,128]{2,1,0:T(8,128)(2,1)S(1)} %copy-done.10, ...), custom_call_target="tpu_custom_call" | custom-call | tf_op jit(solution)/shard_map/attend/pallas_call | solution.py:94
  150.8 28.5 %all_to_all.75 = bf16[2,160,256]{2,1,0:T(8,128)(2,1)S(1)} all-to-all(bf16[2,160,256]{2,1,0:T(8,128)(2,1)S(1)} %get-tuple-element.58), channel_id=1, replica_groups=mesh['y'=4,'zh'=2,'core'=2,'zl'=8,'x'=4] {'zh'}, dimensions={0} | all-to-all | bytes 327680 | tf_op jit(solution)/shard_map/all_to_all | solution.py:602
  180.3 4.1 %all-to-all-start.7 = ((bf16[4,2,160,256]{3,2,1,0:T(8,128)(2,1)}), bf16[4,2,160,256]{3,2,1,0:T(8,128)(2,1)S(1)}, u32[]{:S(2)}, u32[]{:S(2)}) async-start(bf16[4,2,160,256]{3,2,1,0:T(8,128)(2,1)} %broadcast_in_dim.41), calls=%async_computation.7 | async-start | bytes 1310720 | tf_op jit(solution)/shard_map/all_to_all | solution.py:36
  184.4 10.7 %all-to-all-done.7 = bf16[4,2,160,256]{3,2,1,0:T(8,128)(2,1)S(1)} async-done(((bf16[4,2,160,256]{3,2,1,0:T(8,128)(2,1)}), bf16[4,2,160,256]{3,2,1,0:T(8,128)(2,1)S(1)}, u32[]{:S(2)}, u32[]{:S(2)}) %all-to-all-start.7) | async-done | bytes 655392 | tf_op jit(solution)/shard_map/all_to_all | solution.py:36
  195.3 4.9 %all_to_all.76 = bf16[2,4,2,160,256]{4,3,2,1,0:T(8,128)(2,1)S(1)} all-to-all(bf16[2,4,2,160,256]{4,3,2,1,0:T(8,128)(2,1)S(1)} %broadcast_in_dim.42), channel_id=1, replica_groups=mesh['y'=4,'zh'=2,'core'=2,'zl'=8,'x'=4] {'core'}, dimensions={0} | all-to-all | bytes 2621440 | tf_op jit(solution)/shard_map/all_to_all | solution.py:36
  203.3 19.0 %all_to_all.77 = bf16[4,8,128,128]{3,2,1,0:T(8,128)(2,1)S(1)} all-to-all(bf16[4,8,128,128]{3,2,1,0:T(8,128)(2,1)S(1)} %bitcast.15), channel_id=1, replica_groups=mesh['y'=4,'zh'=2,'core'=2,'zl'=8,'x'=4] {'x'}, dimensions={0} | all-to-all | bytes 2097152 | tf_op jit(solution)/shard_map/all_to_all | solution.py:609
  222.5 23.7 %all_to_all.78 = bf16[8,128,128]{2,1,0:T(8,128)(2,1)S(1)} all-to-all(bf16[8,128,128]{2,1,0:T(8,128)(2,1)S(1)} %reduce_sum.54), channel_id=1, replica_groups=mesh['y'=4,'zh'=2,'core'=2,'zl'=8,'x'=4] {'zl'}, dimensions={0} | all-to-all | bytes 524288 | tf_op jit(solution)/shard_map/all_to_all | solution.py:611
  247.0 5.5 %all-to-all-start.11 = ((bf16[8,128,128]{2,1,0:T(8,128)(2,1)}), bf16[8,128,128]{2,1,0:T(8,128)(2,1)S(1)}, u32[]{:S(2)}, u32[]{:S(2)}) async-start(bf16[8,128,128]{2,1,0:T(8,128)(2,1)} %broadcast_in_dim.43), calls=%async_computation.11 | async-start | bytes 524288 | tf_op jit(solution)/shard_map/all_to_all | solution.py:36
  252.5 1.9 collective-permute-start.4
  254.4 13.9 %all-to-all-done.11 = bf16[8,128,128]{2,1,0:T(8,128)(2,1)S(1)} async-done(((bf16[8,128,128]{2,1,0:T(8,128)(2,1)}), bf16[8,128,128]{2,1,0:T(8,128)(2,1)S(1)}, u32[]{:S(2)}, u32[]{:S(2)}) %all-to-all-start.11) | async-done | bytes 262176 | tf_op jit(solution)/shard_map/all_to_all | solution.py:36
  268.3 1.9 collective-permute-start.5
  271.5 3.6 %all-to-all-start.12 = ((bf16[4,8,128,128]{3,2,1,0:T(8,128)(2,1)}), bf16[4,8,128,128]{3,2,1,0:T(8,128)(2,1)S(1)}, u32[]{:S(2)}, u32[]{:S(2)}) async-start(bf16[4,8,128,128]{3,2,1,0:T(8,128)(2,1)} %broadcast_in_dim.84), calls=%async_computation.12 | async-start | bytes 2097152 | tf_op jit(solution)/shard_map/all_to_all | solution.py:36
  275.1 16.0 %all-to-all-done.12 = bf16[4,8,128,128]{3,2,1,0:T(8,128)(2,1)S(1)} async-done(((bf16[4,8,128,128]{3,2,1,0:T(8,128)(2,1)}), bf16[4,8,128,128]{3,2,1,0:T(8,128)(2,1)S(1)}, u32[]{:S(2)}, u32[]{:S(2)}) %all-to-all-start.12) | async-done | bytes 1048608 | tf_op jit(solution)/shard_map/all_to_all | solution.py:36
  292.7 10.1 %feed_forward.1 = (bf16[128,4096]{1,0:T(8,128)(2,1)S(1)}, bf16[128,4096]{1,0:T(8,128)(2,1)S(1)}) custom-call(s32[16]{0:T(128)S(1)} %copy-done.23, bf16[32,128,128]{2,1,0:T(8,128)(2,1)S(1)} %bitcast.16, bf16[128,4096]{1,0:T(8,128)(2,1)S(1)} %copy-done.5, f32[1,4096]{1,0:T(1,128)S(1)} %bitcast.20, bf16[4,1040,256]{2,1,0:T(8,128)(2,1)} %bitcast.4.refs_0_, ...), custom_call_target="tpu_custom_call" | custom-call | tf_op jit(solution)/shard_map/feed_forward/pallas_call | solution.py:501
  302.8 17.7 %all_to_all.79 = bf16[4,32,4096]{2,1,0:T(8,128)(2,1)S(1)} all-to-all(bf16[4,32,4096]{2,1,0:T(8,128)(2,1)S(1)} %bitcast.18), channel_id=1, replica_groups=mesh['y'=4,'zh'=2,'core'=2,'zl'=8,'x'=4] {'x'}, dimensions={0} | all-to-all | bytes 2097152 | tf_op jit(solution)/shard_map/all_to_all | solution.py:622
  321.6 5.5 %all-to-all-start.14 = ((bf16[8,4,4096]{2,1,0:T(4,128)(2,1)}), bf16[8,4,4096]{2,1,0:T(4,128)(2,1)S(1)}, u32[]{:S(2)}, u32[]{:S(2)}) async-start(bf16[8,4,4096]{2,1,0:T(4,128)(2,1)} %reshape.56), calls=%async_computation.14 | async-start | bytes 524288 | tf_op jit(solution)/shard_map/all_to_all | solution.py:624
  327.0 15.0 %all-to-all-done.14 = bf16[8,4,4096]{2,1,0:T(4,128)(2,1)S(1)} async-done(((bf16[8,4,4096]{2,1,0:T(4,128)(2,1)}), bf16[8,4,4096]{2,1,0:T(4,128)(2,1)S(1)}, u32[]{:S(2)}, u32[]{:S(2)}) %all-to-all-start.14) | async-done | bytes 262176 | tf_op jit(solution)/shard_map/all_to_all | solution.py:624
  (127 shorter events, 35.6 us)
Async XLA Ops:
  7.2 98.4 %all-gather.8.cloned.1.call-start = ((), (), s32[]{:S(2)}) async-start(), calls=%async_computation.16 | async-start | bytes 2662400 | tf_op jit(solution)/shard_map/all_gather | solution.py:572
  10.4 19.7 %copy-start.20 = (s32[16,96]{1,0:T(8,128)S(1)}, s32[16,96]{1,0:T(8,128)}, u32[]{:S(2)}) copy-start(s32[16,96]{1,0:T(8,128)} %i_ref.1) | copy-start | bytes 18436
  10.5 19.8 %copy-start.30 = (s32[16]{0:T(128)S(1)}, s32[16]{0:T(128)}, u32[]{:S(2)}) copy-start(s32[16]{0:T(128)} %o_ref.2) | copy-start | bytes 196
  10.5 19.8 %copy-start.31 = (s32[8]{0:T(128)S(1)}, s32[8]{0:T(128)}, u32[]{:S(2)}) copy-start(s32[8]{0:T(128)} %len_ref.1) | copy-start | bytes 100
  10.5 42.5 %all-to-all-start = ((bf16[4,256,512]{2,1,0:T(8,128)(2,1)}), bf16[4,256,512]{2,1,0:T(8,128)(2,1)S(1)}, u32[]{:S(2)}, u32[]{:S(2)}) async-start(bf16[4,256,512]{2,1,0:T(8,128)(2,1)} %broadcast_in_dim.33), calls=%async_computation | async-start | bytes 2097152 | tf_op jit(solution)/shard_map/all_to_all | solution.py:36
  15.1 37.9 %collective-permute-start = (bf16[256,512]{1,0:T(8,128)(2,1)S(1)}, bf16[256,512]{1,0:T(8,128)(2,1)S(1)}, u32[]{:S(2)}, u32[]{:S(2)}) collective-permute-start(bf16[256,512]{1,0:T(8,128)(2,1)S(1)} %join_weights.1), channel_id=1, source_target_pairs={{0,64},{64,0},{1,65},{65,1},{2,66},{66,2},{3,67},{67,3},{4,68},{68... | collective-permute-start | bytes 786440 | tf_op jit(solution)/shard_map/ppermute | solution.py:49
  33.7 43.6 %copy-start.22 = (s32[16]{0:T(128)}, s32[16]{0:T(128)S(1)}, u32[]{:S(2)}) copy-start(s32[16]{0:T(128)S(1)} %get-tuple-element.35.c_ref) | copy-start | bytes 196
  54.0 18.6 %all-to-all-start.1 = ((bf16[4,256,512]{2,1,0:T(8,128)(2,1)}), bf16[4,256,512]{2,1,0:T(8,128)(2,1)S(1)}, u32[]{:S(2)}, u32[]{:S(2)}) async-start(bf16[4,256,512]{2,1,0:T(8,128)(2,1)} %broadcast_in_dim.36), calls=%async_computation.1 | async-start | bytes 2097152 | tf_op jit(solution)/shard_map/all_to_all | solution.py:36
  58.6 16.0 %collective-permute-start.1 = (bf16[4,256,512]{2,1,0:T(8,128)(2,1)S(1)}, bf16[4,256,512]{2,1,0:T(8,128)(2,1)S(1)}, u32[]{:S(2)}, u32[]{:S(2)}) collective-permute-start(bf16[4,256,512]{2,1,0:T(8,128)(2,1)S(1)} %all-to-all-done.refs_0_), channel_id=1, source_target_pairs={{0,32},{32,0},{1,33},{33,1},{2,34},{34,2},{3,35},{35,3},{4,36},{36... | collective-permute-start | bytes 3145736 | tf_op jit(solution)/shard_map/ppermute | solution.py:49
  72.7 4.5 %collective-permute-start.2 = (bf16[4,256,512]{2,1,0:T(8,128)(2,1)S(1)}, bf16[4,256,512]{2,1,0:T(8,128)(2,1)S(1)}, u32[]{:S(2)}, u32[]{:S(2)}) collective-permute-start(bf16[4,256,512]{2,1,0:T(8,128)(2,1)S(1)} %all-to-all-done.1.refs_2_), channel_id=1, source_target_pairs={{0,32},{32,0},{1,33},{33,1},{2,34},{34,2},{3,35},{35,3},{4,36},{36... | collective-permute-start | bytes 3145736 | tf_op jit(solution)/shard_map/ppermute | solution.py:49
  80.9 24.7 %all-to-all-start.2 = ((f32[32,8,128]{2,1,0:T(8,128)}), f32[32,8,128]{2,1,0:T(8,128)S(1)}, u32[]{:S(2)}, u32[]{:S(2)}) async-start(f32[32,8,128]{2,1,0:T(8,128)} %copy-done.13), calls=%async_computation.2 | async-start | bytes 262144 | tf_op jit(solution)/shard_map/all_to_all | solution.py:575
  92.4 45.2 %copy-start.33 = (s32[1,128]{1,0:T(1,128)S(1)}, s32[1,128]{1,0:T(1,128)}, u32[]{:S(2)}) copy-start(s32[1,128]{1,0:T(1,128)} %copy-done.32) | copy-start | bytes 1540
  93.2 44.4 %copy-start.7 = (bf16[1,1024,128]{2,1,0:T(8,128)(2,1)S(1)}, bf16[1,1024,128]{2,1,0:T(8,128)(2,1)}, u32[]{:S(2)}) copy-start(bf16[1,1024,128]{2,1,0:T(8,128)(2,1)} %k_ref.3) | copy-start | bytes 786436
  93.2 44.4 %copy-start.8 = (bf16[1,1024,128]{2,1,0:T(8,128)(2,1)S(1)}, bf16[1,1024,128]{2,1,0:T(8,128)(2,1)}, u32[]{:S(2)}) copy-start(bf16[1,1024,128]{2,1,0:T(8,128)(2,1)} %v_ref.3) | copy-start | bytes 786436
  107.8 22.3 %all-to-all-start.3 = ((bf16[2,128,128]{2,1,0:T(8,128)(2,1)}), bf16[2,128,128]{2,1,0:T(8,128)(2,1)S(1)}, u32[]{:S(2)}, u32[]{:S(2)}) async-start(bf16[2,128,128]{2,1,0:T(8,128)(2,1)} %get-tuple-element.46.own_ref), calls=%async_computation.3 | async-start | bytes 131072 | tf_op jit(solution)/shard_map/all_to_all | solution.py:582
  116.2 85.1 %all-gather.10.cloned.1.call-start = ((), (), s32[]{:S(2)}) async-start(), calls=%async_computation.17 | async-start | bytes 1597440 | tf_op jit(solution)/shard_map/all_gather | solution.py:577
  130.9 10.1 %all-to-all-start.4 = ((bf16[4,2,128,128]{3,2,1,0:T(8,128)(2,1)}), bf16[4,2,128,128]{3,2,1,0:T(8,128)(2,1)S(1)}, u32[]{:S(2)}, u32[]{:S(2)}) async-start(bf16[4,2,128,128]{3,2,1,0:T(8,128)(2,1)} %broadcast_in_dim.39), calls=%async_computation.4 | async-start | bytes 524288 | tf_op jit(solution)/shard_map/all_to_all | solution.py:36
  134.3 11.0 %collective-permute-start.3 = (bf16[64,128]{1,0:T(8,128)(2,1)S(1)}, bf16[64,128]{1,0:T(8,128)(2,1)S(1)}, u32[]{:S(2)}, u32[]{:S(2)}) collective-permute-start(bf16[64,128]{1,0:T(8,128)(2,1)S(1)} %get-tuple-element.53.nm_ref), channel_id=1, source_target_pairs={{0,32},{32,0},{1,33},{33,1},{2,34},{34,2},{3,35},{35,3},{4,36},{36... | collective-permute-start | bytes 49160 | tf_op jit(solution)/shard_map/ppermute | solution.py:49
  141.8 5.2 %all-to-all-start.5 = ((bf16[2,4,2,128,128]{4,3,2,1,0:T(8,128)(2,1)}), bf16[2,4,2,128,128]{4,3,2,1,0:T(8,128)(2,1)S(1)}, u32[]{:S(2)}, u32[]{:S(2)}) async-start(bf16[2,4,2,128,128]{4,3,2,1,0:T(8,128)(2,1)} %broadcast_in_dim.40), calls=%async_computation.5 | async-start | bytes 1048576 | tf_op jit(solution)/shard_map/all_to_all | solution.py:36
  150.8 28.6 %copy-start.18 = (f32[32,256]{1,0:T(8,128)}, f32[32,256]{1,0:T(8,128)S(1)}, u32[]{:S(2)}) copy-start(f32[32,256]{1,0:T(8,128)S(1)} %get-tuple-element.57.new_ref) | copy-start | bytes 98308
  150.8 29.5 %copy-start.11 = (f32[192,256]{1,0:T(8,128)}, f32[192,256]{1,0:T(8,128)S(1)}, u32[]{:S(2)}) copy-start(f32[192,256]{1,0:T(8,128)S(1)} %get-tuple-element.56.kept_ref) | copy-start | bytes 589828
  180.3 14.8 %all-to-all-start.7 = ((bf16[4,2,160,256]{3,2,1,0:T(8,128)(2,1)}), bf16[4,2,160,256]{3,2,1,0:T(8,128)(2,1)S(1)}, u32[]{:S(2)}, u32[]{:S(2)}) async-start(bf16[4,2,160,256]{3,2,1,0:T(8,128)(2,1)} %broadcast_in_dim.41), calls=%async_computation.7 | async-start | bytes 1310720 | tf_op jit(solution)/shard_map/all_to_all | solution.py:36
  184.4 83.9 %all-gather.6.cloned.1.call-start = ((), (), s32[]{:S(2)}) async-start(), calls=%async_computation.15 | async-start | bytes 2662400 | tf_op jit(solution)/shard_map/all_gather | solution.py:608
  247.0 21.3 %all-to-all-start.11 = ((bf16[8,128,128]{2,1,0:T(8,128)(2,1)}), bf16[8,128,128]{2,1,0:T(8,128)(2,1)S(1)}, u32[]{:S(2)}, u32[]{:S(2)}) async-start(bf16[8,128,128]{2,1,0:T(8,128)(2,1)} %broadcast_in_dim.43), calls=%async_computation.11 | async-start | bytes 524288 | tf_op jit(solution)/shard_map/all_to_all | solution.py:36
  252.5 22.6 %collective-permute-start.4 = (bf16[4,1040,256]{2,1,0:T(8,128)(2,1)}, bf16[4,1040,256]{2,1,0:T(8,128)(2,1)}, u32[]{:S(2)}, u32[]{:S(2)}) collective-permute-start(bf16[4,1040,256]{2,1,0:T(8,128)(2,1)} %bitcast.4.refs_0_), channel_id=1, source_target_pairs={{0,32},{32,0},{1,33},{33,1},{2,34},{34,2},{3,35},{35,3},{4,36},{36... | collective-permute-start | bytes 6389768 | tf_op jit(solution)/shard_map/ppermute | solution.py:49
  268.3 22.8 %collective-permute-start.5 = (bf16[4,1040,256]{2,1,0:T(8,128)(2,1)}, bf16[4,1040,256]{2,1,0:T(8,128)(2,1)}, u32[]{:S(2)}, u32[]{:S(2)}) collective-permute-start(bf16[4,1040,256]{2,1,0:T(8,128)(2,1)} %all-gather.6.cloned.1.call-done.refs_2_), channel_id=1, source_target_pairs={{0,32},{32,0},{1,33},{33,1},{2,34},{34,2},{3,35},{35,3},{4,36},{36... | collective-permute-start | bytes 6389768 | tf_op jit(solution)/shard_map/ppermute | solution.py:49
  271.5 19.7 %copy-start.5 = (bf16[128,4096]{1,0:T(8,128)(2,1)S(1)}, bf16[128,4096]{1,0:T(8,128)(2,1)}, u32[]{:S(2)}) copy-start(bf16[128,4096]{1,0:T(8,128)(2,1)} %x_ref.3) | copy-start | bytes 3145732
  271.5 19.7 %copy-start.21 = (f32[4096]{0:T(1024)S(1)}, f32[4096]{0:T(1024)}, u32[]{:S(2)}) copy-start(f32[4096]{0:T(1024)} %param.25) | copy-start | bytes 49156
  271.5 19.7 %copy-start.23 = (s32[16]{0:T(128)S(1)}, s32[16]{0:T(128)}, u32[]{:S(2)}) copy-start(s32[16]{0:T(128)} %copy-done.22) | copy-start | bytes 196
  271.5 19.7 %all-to-all-start.12 = ((bf16[4,8,128,128]{3,2,1,0:T(8,128)(2,1)}), bf16[4,8,128,128]{3,2,1,0:T(8,128)(2,1)S(1)}, u32[]{:S(2)}, u32[]{:S(2)}) async-start(bf16[4,8,128,128]{3,2,1,0:T(8,128)(2,1)} %broadcast_in_dim.84), calls=%async_computation.12 | async-start | bytes 2097152 | tf_op jit(solution)/shard_map/all_to_all | solution.py:36
  320.5 22.0 %copy-start.36 = (f32[4096]{0:T(1024)S(1)}, f32[4096]{0:T(1024)}, u32[]{:S(2)}) copy-start(f32[4096]{0:T(1024)} %param.29) | copy-start | bytes 49156
  321.6 20.5 %all-to-all-start.14 = ((bf16[8,4,4096]{2,1,0:T(4,128)(2,1)}), bf16[8,4,4096]{2,1,0:T(4,128)(2,1)S(1)}, u32[]{:S(2)}, u32[]{:S(2)}) async-start(bf16[8,4,4096]{2,1,0:T(4,128)(2,1)} %reshape.56), calls=%async_computation.14 | async-start | bytes 524288 | tf_op jit(solution)/shard_map/all_to_all | solution.py:624
  (25 other events, 99.0 us)
Sparse Core Ops, SparseCore 0:
  10.1 42.9 all-gather.7
  119.2 72.5 all-gather.9
  203.4 32.3 all-gather.5

commit v6 on v5

--- a/solution.py
+++ b/solution.py
@@ -14,6 +14,7 @@
 PPR = 2
 TOKN_DEV = 32
 ROW_DEV = 128
+LEVEL_ROWS = 16
 
 EPSILON = 1e-06
 ROPE_THETA = 500000.0
@@ -76,10 +77,10 @@
     return num / den
 
 
-def unpack(block):
-    block = block.astype(f32)
-    level = block[:, HD : HD + 1] + block[:, HD + 1 : HD + 2] + block[:, HD + 2 : HD + 3]
-    return block[:, :HD], level
+def pieces_of(level):
+    high = level.astype(bf16).astype(f32)
+    mid = (level - high).astype(bf16).astype(f32)
+    return high, mid, level - high - mid
 
 
 def whole(a):
@@ -336,32 +337,34 @@
 
     def kernel(
         c_ref, q_ref, k_ref, v_ref, w_ref, own_ref, nm_ref, no_ref, na_ref, nk_ref,
-        back_ref, kept_ref, new_ref, rows_ref,
+        back_ref, kept_ref, new_ref, rows_ref, level_ref,
     ):
         at = 0
         for i, (low, high) in enumerate(cuts):
             rows_ref[at : at + high - low, :] = q_ref[c_ref[i], low:high, :]
             at += high - low
-        lane = lax.broadcasted_iota(jnp.int32, (step, width), 1)
         key_at = c_ref[4] + lax.broadcasted_iota(jnp.int32, (step, length), 1)
         for n in range(count // step):
             span = slice(n * step, (n + 1) * step)
             out, level = partial_attention(
                 rows_ref[span, :], k_ref[0], v_ref[0], key_at <= w_ref[span, :]
             )
+            level = jnp.broadcast_to(level, (step, width))
             if n * step < 2 * SEL:
                 kept_ref[span, :width] = out
-                kept_ref[span, width:] = jnp.broadcast_to(level, (step, width))
+                kept_ref[span, width:] = level
             if n * step >= SEL:
-                high = level.astype(bf16).astype(f32)
-                mid = (level - high).astype(bf16).astype(f32)
-                low = level - high - mid
-                pieces = jnp.where(lane == 0, high, jnp.where(lane == 1, mid, 0.0))
-                pieces = jnp.where(lane == 2, low, pieces)
                 to = slice(n * step - SEL, (n + 1) * step - SEL)
+                level_ref[to, :] = level
                 for z in range(NZH):
-                    back_ref[z, to, :width] = out.astype(bf16)
-                    back_ref[z, to, width:] = pieces.astype(bf16)
+                    back_ref[z, to, :] = out.astype(bf16)
+        level_ref[back:, :] = jnp.zeros((2 * width - back, width), f32)
+        lines = [jnp.transpose(level_ref[i * width : (i + 1) * width, :])[:1] for i in range(2)]
+        lines = [piece for line in lines for piece in pieces_of(line)]
+        lines.append(jnp.zeros((LEVEL_ROWS - len(lines), width), f32))
+        lines = jnp.concatenate(lines, axis=0).astype(bf16)
+        for z in range(NZH):
+            back_ref[z, back:, :] = lines
         new_keys = jnp.concatenate([nm_ref[:TOKN_DEV, :], no_ref[:TOKN_DEV, :]], axis=0)
         new_values = jnp.concatenate([nm_ref[TOKN_DEV:, :], no_ref[TOKN_DEV:, :]], axis=0)
         out, level = partial_attention(
@@ -374,7 +377,7 @@
         kernel,
         "attend",
         (
-            shape((NZH, back, 2 * width), bf16),
+            shape((NZH, back + LEVEL_ROWS, width), bf16),
             shape((2 * SEL, 2 * width), f32),
             shape((TOKN_DEV, 2 * width), f32),
         ),
@@ -388,7 +391,7 @@
         new_other,
         new_at,
         new_key_at,
-        scratch=[pltpu.VMEM((count, width), bf16)],
+        scratch=[pltpu.VMEM((count, width), bf16), pltpu.VMEM((2 * width, width), f32)],
     )
 
 
@@ -397,20 +400,32 @@
     count, part, _ = weights[0].shape
     halves = part // width
     blocks = len(weights) * count * halves
+    back = returned.shape[1] - LEVEL_ROWS
 
     def kernel(c_ref, kept_ref, new_ref, back_ref, *refs):
         weight_refs, (out_ref, att_ref) = refs[:-2], refs[-2:]
+        def levels(source):
+            lines = back_ref[source, back:, :].astype(f32)
+            lines = jnp.concatenate([lines, jnp.zeros((width - LEVEL_ROWS, width), f32)], axis=0)
+            lines = jnp.transpose(lines)
+            return [
+                lines[:, n : n + 1] + lines[:, n + 1 : n + 2] + lines[:, n + 2 : n + 3]
+                for n in (0, 3)
+            ]
+
         first = c_ref[4] == 1
         kept = jnp.where(first, kept_ref[:SEL, :], kept_ref[SEL:, :])
-        remote, remote_level = unpack(back_ref[c_ref[0], :SEL, :])
-        remote_level = jnp.where(first, MASKED, remote_level)
+        remote = back_ref[c_ref[0], :SEL, :].astype(f32)
+        remote_level = jnp.where(first, MASKED, levels(c_ref[0])[0][:SEL])
         att_ref[:SEL, :] = merge(
             [(kept[:, :width], kept[:, width : width + 1]), (remote, remote_level)]
         )
         at = pl.multiple_of(SEL + c_ref[3] * TOKN_DEV, TOKN_DEV)
         parts = [(new_ref[:, :width], new_ref[:, width : width + 1])]
         for i in range(PPR):
-            parts.append(unpack(back_ref[c_ref[1 + i], pl.ds(at, TOKN_DEV), :]))
+            column = levels(c_ref[1 + i])
+            level = jnp.where(c_ref[3] == 0, column[0][SEL:], column[1][:TOKN_DEV])
+            parts.append((back_ref[c_ref[1 + i], pl.ds(at, TOKN_DEV), :].astype(f32), level))
         att_ref[SEL:, :] = merge(parts)
         attention = att_ref[...].astype(bf16)
         for j, ref in enumerate(weight_refs):
@@ -569,11 +584,10 @@
     near_other = swap(near, "core", NCORE)
     far = copies_to_all(theirs, "y", NY)
     far_other = swap(far, "core", NCORE)
-    parcel_near = lax.all_gather(parcel, "y")
     weights = [near, near_other, far, far_other]
     raw, squares = project(columns, hidden_states, weights, width, blocks)
     squares = lax.all_to_all(squares, BLK, 0, 0, tiled=True)
-    squares, parcel, parcel_near = lax.optimization_barrier((squares, parcel, parcel_near))
+    squares, parcel = lax.optimization_barrier((squares, parcel))
     pair = lax.all_gather(parcel, "zh")
     query, key, value, new_mine = finish_rows(
         raw, squares, query_gain[None], key_gain[None], cosine, sine, model
@@ -601,17 +615,18 @@
 
     returned = lax.all_to_all(returned, "zh", 0, 0, tiled=True)
     returned = copies_to_all(returned, "y", NY)
-    returned = copies_to_all(returned, "core", NCORE).reshape(N_SEQ, -1, 2 * width)
+    returned = copies_to_all(returned, "core", NCORE).reshape(N_SEQ, -1, width)
 
     terms = merge_and_project(merge_control, kept, new_part, returned, weights)
-    terms, pair = lax.optimization_barrier((terms, pair))
+    terms, pair, parcel = lax.optimization_barrier((terms, pair, parcel))
+    parcel_near = lax.all_gather(parcel, "y")
     parcel_far = lax.all_gather(lax.dynamic_index_in_dim(pair, 1 - zh, 0, False), "y")
     terms = lax.all_to_all(terms.reshape(NX, NZL, ROW_DEV, width), "x", 0, 0, tiled=True)
     terms = jnp.sum(terms.astype(f32), axis=0).astype(bf16)
     terms = lax.all_to_all(terms, "zl", 0, 0, tiled=True)
     summed = jnp.sum(terms.astype(f32), axis=0).astype(bf16)
     summed = copies_to_all(summed, "zl", NZL)
-    summed, parcel_far = lax.optimization_barrier((summed, parcel_far))
+    summed, parcel_near, parcel_far = lax.optimization_barrier((summed, parcel_near, parcel_far))
     summed = copies_to_all(summed, "x", NX).reshape(blocks, ROW_DEV, model // blocks)
 
     parcels = [parcel_near, swap(parcel_near, "core", NCORE)]

time: 351 us -> 359 us (1.023)
  blocking collectives: 93.9 us -> 162 us
  waiting for transfers between devices: 117 us -> 71.2 us
  starting transfers between devices: 79 us -> 63.7 us
    all_to_all x1 -> x4, blocking collectives: 4.92 us -> 54.6 us  [copies_to_all(): lax.all_to_all(jnp.broadcast_to(a[None], (count,) + a.shape), axis, 0, 0,...]
    all_to_all x7 -> x4, waiting for transfers between devices: 56 us -> 16.7 us  [copies_to_all(): lax.all_to_all(jnp.broadcast_to(a[None], (count,) + a.shape), axis, 0, 0,...]
    all_to_all x0 -> x1, blocking collectives: none -> 22.2 us  [shards(): queries = lax.all_to_all(query, 'zh', 0, 0, tiled=True)]
    all_to_all x1 -> x0, waiting for transfers between devices: 13.2 us -> none  [shards(): queries = lax.all_to_all(query, 'zh', 0, 0, tiled=True)]
    all_to_all x7 -> x4, starting transfers between devices: 29.3 us -> 16.6 us  [copies_to_all(): lax.all_to_all(jnp.broadcast_to(a[None], (count,) + a.shape), axis, 0, 0,...]
    all_to_all x1 -> x0, starting transfers between devices: 8.42 us -> none  [shards(): queries = lax.all_to_all(query, 'zh', 0, 0, tiled=True)]
    all_gather x1, waiting for transfers between devices: 0.01 us -> 7.99 us  [shards(): lax.all_gather(lax.dynamic_index_in_dim(pair, 1 - zh, 0, False), 'y')]
    all_to_all x1, starting transfers between devices: 5.47 us -> 10.5 us  [shards(): lax.all_to_all(terms.reshape(NZL, rows, model), 'zl', 0, 0, tiled=True)]
  transfers between devices with their start and end apart: 19 -> 15, of which waited for: 11 -> 8; matrix products, arithmetic and copies ran while one was open for 3% -> 2% of each run, Pallas kernels for 3% -> 2%
where the time goes in v6:
time: 359 us; the launch traced here: 357 us
  blocking collectives  162 us (45%)
  waiting for transfers between devices  71.2 us (20%)
  starting transfers between devices  63.7 us (18%)
  Pallas kernels  23.9 us (7%)
  local copies, waits for them, and re-layouts  17 us (5%)
  between operations  14.2 us (4%)
  other arithmetic  4.79 us (1%)
    all_to_all x4, blocking collectives, copies_to_all(): lax.all_to_all(jnp.broadcast_to(a[None], (count,) + a.shape), axis, 0, 0,...  54.6 us
    all_to_all x1, blocking collectives, shards(): returned = lax.all_to_all(returned, 'zh', 0, 0, tiled=True)  28.8 us
    ppermute x6, starting transfers between devices, swap(): return lax.ppermute(a, axis, [(i, i ^ 1) for i in range(count)])  24.9 us
    all_to_all x1, blocking collectives, shards(): queries = lax.all_to_all(query, 'zh', 0, 0, tiled=True)  22.2 us
    all_to_all x1, blocking collectives, shards(): terms = lax.all_to_all(terms, 'zl', 0, 0, tiled=True)  22 us
    ppermute x6, waiting for transfers between devices, swap(): return lax.ppermute(a, axis, [(i, i ^ 1) for i in range(count)])  21.4 us
    all_to_all x1, blocking collectives, shards(): lax.all_to_all(terms.reshape(NX, NZL, ROW_DEV, width), 'x', 0, 0, tiled=T...  18.1 us
    all_to_all x4, waiting for transfers between devices, copies_to_all(): lax.all_to_all(jnp.broadcast_to(a[None], (count,) + a.shape), axis, 0, 0,...  16.7 us
  transfers between devices with their start and end apart: 15, of which 8 were waited for; matrix products, arithmetic and copies ran while one was open for 2% of the time, Pallas kernels for 2%

profile of v6, /device:TPU:32, one launch (start us, length us, event | category | flops | bytes accessed | tf_op | source)
XLA Modules:
  0.0 357.1 jit_solution(12145902932335581956)
XLA Ops:
  11.7 4.6 %all-to-all-start = ((bf16[4,256,512]{2,1,0:T(8,128)(2,1)}), bf16[4,256,512]{2,1,0:T(8,128)(2,1)S(1)}, u32[]{:S(2)}, u32[]{:S(2)}) async-start(bf16[4,256,512]{2,1,0:T(8,128)(2,1)} %broadcast_in_dim.33), calls=%async_computation | async-start | bytes 2097152 | tf_op jit(solution)/shard_map/all_to_all | solution.py:37
  16.3 14.8 %collective-permute-start = (bf16[256,512]{1,0:T(8,128)(2,1)S(1)}, bf16[256,512]{1,0:T(8,128)(2,1)S(1)}, u32[]{:S(2)}, u32[]{:S(2)}) collective-permute-start(bf16[256,512]{1,0:T(8,128)(2,1)S(1)} %join_weights.1), channel_id=1, source_target_pairs={{0,64},{64,0},{1,65},{65,1},{2,66},{66,2},{3,67},{67,3},{4,68},{68... | collective-permute-start | bytes 786440 | tf_op jit(solution)/shard_map/ppermute | solution.py:50
  35.5 18.8 %collective-permute-done = bf16[256,512]{1,0:T(8,128)(2,1)S(1)} collective-permute-done((bf16[256,512]{1,0:T(8,128)(2,1)S(1)}, bf16[256,512]{1,0:T(8,128)(2,1)S(1)}, u32[]{:S(2)}, u32[]{:S(2)}) %collective-permute-start) | collective-permute-done | bytes 262176 | tf_op jit(solution)/shard_map/ppermute | solution.py:50
  55.3 4.5 %all-to-all-start.1 = ((bf16[4,256,512]{2,1,0:T(8,128)(2,1)}), bf16[4,256,512]{2,1,0:T(8,128)(2,1)S(1)}, u32[]{:S(2)}, u32[]{:S(2)}) async-start(bf16[4,256,512]{2,1,0:T(8,128)(2,1)} %broadcast_in_dim.36), calls=%async_computation.1 | async-start | bytes 2097152 | tf_op jit(solution)/shard_map/all_to_all | solution.py:37
  59.8 1.9 collective-permute-start.1
  61.8 12.2 %all-to-all-done.1.refs_2_ = bf16[4,256,512]{2,1,0:T(8,128)(2,1)S(1)} async-done(((bf16[4,256,512]{2,1,0:T(8,128)(2,1)}), bf16[4,256,512]{2,1,0:T(8,128)(2,1)S(1)}, u32[]{:S(2)}, u32[]{:S(2)}) %all-to-all-start.1) | async-done | bytes 1048608 | tf_op jit(solution)/shard_map/all_to_all | solution.py:37
  73.9 1.9 collective-permute-start.2
  75.9 2.6 collective-permute-done.2.refs_3_
  82.2 11.6 %all-to-all-start.2 = ((f32[32,8,128]{2,1,0:T(8,128)}), f32[32,8,128]{2,1,0:T(8,128)S(1)}, u32[]{:S(2)}, u32[]{:S(2)}) async-start(f32[32,8,128]{2,1,0:T(8,128)} %copy-done.12), calls=%async_computation.2 | async-start | bytes 262144 | tf_op jit(solution)/shard_map/all_to_all | solution.py:589
  93.8 1.9 fusion.4
  95.8 11.2 %all-to-all-done.2.s_ref = f32[32,8,128]{2,1,0:T(8,128)S(1)} async-done(((f32[32,8,128]{2,1,0:T(8,128)}), f32[32,8,128]{2,1,0:T(8,128)S(1)}, u32[]{:S(2)}, u32[]{:S(2)}) %all-to-all-start.2) | async-done | bytes 131104 | tf_op jit(solution)/shard_map/all_to_all | solution.py:589
  107.4 22.2 %all_to_all.75 = bf16[2,128,128]{2,1,0:T(8,128)(2,1)S(1)} all-to-all(bf16[2,128,128]{2,1,0:T(8,128)(2,1)S(1)} %get-tuple-element.47.own_ref), channel_id=1, replica_groups=mesh['y'=4,'zh'=2,'core'=2,'zl'=8,'x'=4] {'zh'}, dimensions={0} | all-to-all | bytes 131072 | tf_op jit(solution)/shard_map/all_to_all | solution.py:596
  130.3 4.0 %all-to-all-start.4 = ((bf16[4,2,128,128]{3,2,1,0:T(8,128)(2,1)}), bf16[4,2,128,128]{3,2,1,0:T(8,128)(2,1)}, u32[]{:S(2)}, u32[]{:S(2)}) async-start(bf16[4,2,128,128]{3,2,1,0:T(8,128)(2,1)} %broadcast_in_dim.39), calls=%async_computation.4 | async-start | bytes 524288 | tf_op jit(solution)/shard_map/all_to_all | solution.py:37
  134.4 1.9 collective-permute-start.3
  138.2 2.9 all-to-all-done.4
  142.9 3.5 all-to-all-start.5
  148.2 3.4 attend.1
  151.6 28.8 %all_to_all.76 = bf16[2,176,128]{2,1,0:T(8,128)(2,1)S(1)} all-to-all(bf16[2,176,128]{2,1,0:T(8,128)(2,1)S(1)} %get-tuple-element.59), channel_id=1, replica_groups=mesh['y'=4,'zh'=2,'core'=2,'zl'=8,'x'=4] {'zh'}, dimensions={0} | all-to-all | bytes 180224 | tf_op jit(solution)/shard_map/all_to_all | solution.py:616
  180.5 9.6 %all_to_all.77 = bf16[4,2,176,128]{3,2,1,0:T(8,128)(2,1)S(1)} all-to-all(bf16[4,2,176,128]{3,2,1,0:T(8,128)(2,1)S(1)} %broadcast_in_dim.41), channel_id=1, replica_groups=mesh['y'=4,'zh'=2,'core'=2,'zl'=8,'x'=4] {'y'}, dimensions={0} | all-to-all | bytes 720896 | tf_op jit(solution)/shard_map/all_to_all | solution.py:37
  190.2 4.4 %all_to_all.78 = bf16[2,4,2,176,128]{4,3,2,1,0:T(8,128)(2,1)S(1)} all-to-all(bf16[2,4,2,176,128]{4,3,2,1,0:T(8,128)(2,1)S(1)} %broadcast_in_dim.42), channel_id=1, replica_groups=mesh['y'=4,'zh'=2,'core'=2,'zl'=8,'x'=4] {'core'}, dimensions={0} | all-to-all | bytes 1441792 | tf_op jit(solution)/shard_map/all_to_all | solution.py:37
  196.0 1.9 constant_dynamic-slice_fusion
  197.9 18.1 %all_to_all.79 = bf16[4,8,128,128]{3,2,1,0:T(8,128)(2,1)S(1)} all-to-all(bf16[4,8,128,128]{3,2,1,0:T(8,128)(2,1)S(1)} %bitcast.14), channel_id=1, replica_groups=mesh['y'=4,'zh'=2,'core'=2,'zl'=8,'x'=4] {'x'}, dimensions={0} | all-to-all | bytes 2097152 | tf_op jit(solution)/shard_map/all_to_all | solution.py:624
  216.2 22.0 %all_to_all.80 = bf16[8,128,128]{2,1,0:T(8,128)(2,1)S(1)} all-to-all(bf16[8,128,128]{2,1,0:T(8,128)(2,1)S(1)} %reduce_sum.54), channel_id=1, replica_groups=mesh['y'=4,'zh'=2,'core'=2,'zl'=8,'x'=4] {'zl'}, dimensions={0} | all-to-all | bytes 524288 | tf_op jit(solution)/shard_map/all_to_all | solution.py:626
  238.3 21.1 %all_to_all.81 = bf16[8,128,128]{2,1,0:T(8,128)(2,1)S(1)} all-to-all(bf16[8,128,128]{2,1,0:T(8,128)(2,1)S(1)} %broadcast_in_dim.43), channel_id=1, replica_groups=mesh['y'=4,'zh'=2,'core'=2,'zl'=8,'x'=4] {'zl'}, dimensions={0} | all-to-all | bytes 524288 | tf_op jit(solution)/shard_map/all_to_all | solution.py:37
  259.4 8.0 %all-gather.6.cloned.1.call-done.refs_2_ = bf16[4,1040,256]{2,1,0:T(8,128)(2,1)} async-done(((bf16[1,1040,256]{2,1,0:T(8,128)(2,1)}), bf16[4,1040,256]{2,1,0:T(8,128)(2,1)}) %all-gather.6.cloned.1.call-update) | async-done | bytes 2129936 | tf_op jit(solution)/shard_map/all_gather | solution.py:623
  267.4 1.9 collective-permute-start.4
  269.3 2.4 collective-permute-start.5
  272.0 19.5 %all_to_all.82 = bf16[4,8,128,128]{3,2,1,0:T(8,128)(2,1)S(1)} all-to-all(bf16[4,8,128,128]{3,2,1,0:T(8,128)(2,1)S(1)} %broadcast_in_dim.84), channel_id=1, replica_groups=mesh['y'=4,'zh'=2,'core'=2,'zl'=8,'x'=4] {'x'}, dimensions={0} | all-to-all | bytes 2097152 | tf_op jit(solution)/shard_map/all_to_all | solution.py:37
  293.1 14.4 %feed_forward.1 = (bf16[128,4096]{1,0:T(8,128)(2,1)S(1)}, bf16[128,4096]{1,0:T(8,128)(2,1)S(1)}) custom-call(s32[16]{0:T(128)S(1)} %copy-done.20, bf16[32,128,128]{2,1,0:T(8,128)(2,1)S(1)} %bitcast.15, bf16[128,4096]{1,0:T(8,128)(2,1)S(1)} %copy-done.5, f32[1,4096]{1,0:T(1,128)S(1)} %bitcast.22, bf16[4,1040,256]{2,1,0:T(8,128)(2,1)S(1)} %bitcast.18, ...), custom_call_target="tpu_custom_call" | custom-call | tf_op jit(solution)/shard_map/feed_forward/pallas_call | solution.py:516
  307.5 16.5 %all_to_all.83 = bf16[4,32,4096]{2,1,0:T(8,128)(2,1)S(1)} all-to-all(bf16[4,32,4096]{2,1,0:T(8,128)(2,1)S(1)} %bitcast.20), channel_id=1, replica_groups=mesh['y'=4,'zh'=2,'core'=2,'zl'=8,'x'=4] {'x'}, dimensions={0} | all-to-all | bytes 2097152 | tf_op jit(solution)/shard_map/all_to_all | solution.py:637
  325.1 10.5 %all-to-all-start.14 = ((bf16[8,4,4096]{2,1,0:T(4,128)(2,1)}), bf16[8,4,4096]{2,1,0:T(4,128)(2,1)S(1)}, u32[]{:S(2)}, u32[]{:S(2)}) async-start(bf16[8,4,4096]{2,1,0:T(4,128)(2,1)} %reshape.56), calls=%async_computation.14 | async-start | bytes 524288 | tf_op jit(solution)/shard_map/all_to_all | solution.py:639
  335.5 13.8 %all-to-all-done.14 = bf16[8,4,4096]{2,1,0:T(4,128)(2,1)S(1)} async-done(((bf16[8,4,4096]{2,1,0:T(4,128)(2,1)}), bf16[8,4,4096]{2,1,0:T(4,128)(2,1)S(1)}, u32[]{:S(2)}, u32[]{:S(2)}) %all-to-all-start.14) | async-done | bytes 262176 | tf_op jit(solution)/shard_map/all_to_all | solution.py:639
  (121 shorter events, 26.0 us)
Async XLA Ops:
  11.7 19.5 %copy-start.36 = (s32[8,2]{0,1:T(2,128)S(1)}, s32[8,2]{0,1:T(2,128)}, u32[]{:S(2)}) copy-start(s32[8,2]{0,1:T(2,128)} %param.33) | copy-start | bytes 196
  11.7 19.7 %copy-start.17 = (s32[16,96]{1,0:T(8,128)S(1)}, s32[16,96]{1,0:T(8,128)}, u32[]{:S(2)}) copy-start(s32[16,96]{1,0:T(8,128)} %i_ref.1) | copy-start | bytes 18436
  11.7 19.8 %copy-start.29 = (s32[16]{0:T(128)S(1)}, s32[16]{0:T(128)}, u32[]{:S(2)}) copy-start(s32[16]{0:T(128)} %o_ref.2) | copy-start | bytes 196
  11.7 19.8 %copy-start.30 = (s32[8]{0:T(128)S(1)}, s32[8]{0:T(128)}, u32[]{:S(2)}) copy-start(s32[8]{0:T(128)} %len_ref.1) | copy-start | bytes 100
  11.7 42.5 %all-to-all-start = ((bf16[4,256,512]{2,1,0:T(8,128)(2,1)}), bf16[4,256,512]{2,1,0:T(8,128)(2,1)S(1)}, u32[]{:S(2)}, u32[]{:S(2)}) async-start(bf16[4,256,512]{2,1,0:T(8,128)(2,1)} %broadcast_in_dim.33), calls=%async_computation | async-start | bytes 2097152 | tf_op jit(solution)/shard_map/all_to_all | solution.py:37
  16.3 37.9 %collective-permute-start = (bf16[256,512]{1,0:T(8,128)(2,1)S(1)}, bf16[256,512]{1,0:T(8,128)(2,1)S(1)}, u32[]{:S(2)}, u32[]{:S(2)}) collective-permute-start(bf16[256,512]{1,0:T(8,128)(2,1)S(1)} %join_weights.1), channel_id=1, source_target_pairs={{0,64},{64,0},{1,65},{65,1},{2,66},{66,2},{3,67},{67,3},{4,68},{68... | collective-permute-start | bytes 786440 | tf_op jit(solution)/shard_map/ppermute | solution.py:50
  34.4 21.0 %copy-start.27 = (s32[5]{0:T(128)}, s32[5]{0:T(128)S(1)}, u32[]{:S(2)}) copy-start(s32[5]{0:T(128)S(1)} %get-tuple-element.38.c_ref) | copy-start | bytes 64
  34.4 44.1 %copy-start.19 = (s32[16]{0:T(128)}, s32[16]{0:T(128)S(1)}, u32[]{:S(2)}) copy-start(s32[16]{0:T(128)S(1)} %get-tuple-element.36.c_ref) | copy-start | bytes 196
  55.3 18.6 %all-to-all-start.1 = ((bf16[4,256,512]{2,1,0:T(8,128)(2,1)}), bf16[4,256,512]{2,1,0:T(8,128)(2,1)S(1)}, u32[]{:S(2)}, u32[]{:S(2)}) async-start(bf16[4,256,512]{2,1,0:T(8,128)(2,1)} %broadcast_in_dim.36), calls=%async_computation.1 | async-start | bytes 2097152 | tf_op jit(solution)/shard_map/all_to_all | solution.py:37
  59.8 16.0 %collective-permute-start.1 = (bf16[4,256,512]{2,1,0:T(8,128)(2,1)S(1)}, bf16[4,256,512]{2,1,0:T(8,128)(2,1)S(1)}, u32[]{:S(2)}, u32[]{:S(2)}) collective-permute-start(bf16[4,256,512]{2,1,0:T(8,128)(2,1)S(1)} %all-to-all-done.refs_0_), channel_id=1, source_target_pairs={{0,32},{32,0},{1,33},{33,1},{2,34},{34,2},{3,35},{35,3},{4,36},{36... | collective-permute-start | bytes 3145736 | tf_op jit(solution)/shard_map/ppermute | solution.py:50
  73.9 4.5 %collective-permute-start.2 = (bf16[4,256,512]{2,1,0:T(8,128)(2,1)S(1)}, bf16[4,256,512]{2,1,0:T(8,128)(2,1)S(1)}, u32[]{:S(2)}, u32[]{:S(2)}) collective-permute-start(bf16[4,256,512]{2,1,0:T(8,128)(2,1)S(1)} %all-to-all-done.1.refs_2_), channel_id=1, source_target_pairs={{0,32},{32,0},{1,33},{33,1},{2,34},{34,2},{3,35},{35,3},{4,36},{36... | collective-permute-start | bytes 3145736 | tf_op jit(solution)/shard_map/ppermute | solution.py:50
  82.2 24.9 %copy-start.34 = (f32[136,128]{1,0:T(8,128)S(1)}, f32[136,128]{1,0:T(8,128)}, u32[]{:S(2)}) copy-start(f32[136,128]{1,0:T(8,128)} %get-tuple-element.45) | copy-start | bytes 208900
  82.2 24.9 %copy-start.33 = (f32[136,128]{1,0:T(8,128)S(1)}, f32[136,128]{1,0:T(8,128)}, u32[]{:S(2)}) copy-start(f32[136,128]{1,0:T(8,128)} %get-tuple-element.46) | copy-start | bytes 208900
  82.2 24.9 %copy-start.21 = (f32[128]{0:T(128)S(1)}, f32[128]{0:T(128)}, u32[]{:S(2)}) copy-start(f32[128]{0:T(128)} %param.23) | copy-start | bytes 1540
  82.2 24.9 %copy-start.22 = (f32[128]{0:T(128)S(1)}, f32[128]{0:T(128)}, u32[]{:S(2)}) copy-start(f32[128]{0:T(128)} %param.24) | copy-start | bytes 1540
  82.2 24.8 %all-to-all-start.2 = ((f32[32,8,128]{2,1,0:T(8,128)}), f32[32,8,128]{2,1,0:T(8,128)S(1)}, u32[]{:S(2)}, u32[]{:S(2)}) async-start(f32[32,8,128]{2,1,0:T(8,128)} %copy-done.12), calls=%async_computation.2 | async-start | bytes 262144 | tf_op jit(solution)/shard_map/all_to_all | solution.py:589
  93.8 102.1 %all-gather.8.cloned.1.call-start = ((), (), s32[]{:S(2)}) async-start(), calls=%async_computation.16 | async-start | bytes 1597440 | tf_op jit(solution)/shard_map/all_gather | solution.py:591
  95.8 40.6 %copy-start.8 = (bf16[1,1024,128]{2,1,0:T(8,128)(2,1)S(1)}, bf16[1,1024,128]{2,1,0:T(8,128)(2,1)}, u32[]{:S(2)}) copy-start(bf16[1,1024,128]{2,1,0:T(8,128)(2,1)} %k_ref.3) | copy-start | bytes 786436
  95.8 40.6 %copy-start.9 = (bf16[1,1024,128]{2,1,0:T(8,128)(2,1)S(1)}, bf16[1,1024,128]{2,1,0:T(8,128)(2,1)}, u32[]{:S(2)}) copy-start(bf16[1,1024,128]{2,1,0:T(8,128)(2,1)} %v_ref.3) | copy-start | bytes 786436
  95.8 40.6 %copy-start.32 = (s32[1,128]{1,0:T(1,128)S(1)}, s32[1,128]{1,0:T(1,128)}, u32[]{:S(2)}) copy-start(s32[1,128]{1,0:T(1,128)} %copy-done.31) | copy-start | bytes 1540
  130.3 10.8 %all-to-all-start.4 = ((bf16[4,2,128,128]{3,2,1,0:T(8,128)(2,1)}), bf16[4,2,128,128]{3,2,1,0:T(8,128)(2,1)}, u32[]{:S(2)}, u32[]{:S(2)}) async-start(bf16[4,2,128,128]{3,2,1,0:T(8,128)(2,1)} %broadcast_in_dim.39), calls=%async_computation.4 | async-start | bytes 524288 | tf_op jit(solution)/shard_map/all_to_all | solution.py:37
  134.4 12.1 %collective-permute-start.3 = (bf16[64,128]{1,0:T(8,128)(2,1)S(1)}, bf16[64,128]{1,0:T(8,128)(2,1)S(1)}, u32[]{:S(2)}, u32[]{:S(2)}) collective-permute-start(bf16[64,128]{1,0:T(8,128)(2,1)S(1)} %get-tuple-element.54.nm_ref), channel_id=1, source_target_pairs={{0,32},{32,0},{1,33},{33,1},{2,34},{34,2},{3,35},{35,3},{4,36},{36... | collective-permute-start | bytes 49160 | tf_op jit(solution)/shard_map/ppermute | solution.py:50
  142.9 5.2 %all-to-all-start.5 = ((bf16[2,4,2,128,128]{4,3,2,1,0:T(8,128)(2,1)}), bf16[2,4,2,128,128]{4,3,2,1,0:T(8,128)(2,1)S(1)}, u32[]{:S(2)}, u32[]{:S(2)}) async-start(bf16[2,4,2,128,128]{4,3,2,1,0:T(8,128)(2,1)} %broadcast_in_dim.40), calls=%async_computation.5 | async-start | bytes 1048576 | tf_op jit(solution)/shard_map/all_to_all | solution.py:37
  146.4 113.0 %all-gather.10.cloned.1.call-start = ((), (), s32[]{:S(2)}) async-start(), calls=%async_computation.17 | async-start | bytes 2662400 | tf_op jit(solution)/shard_map/all_gather | solution.py:622
  195.9 71.5 %all-gather.6.cloned.1.call-start = ((), (), s32[]{:S(2)}) async-start(), calls=%async_computation.15 | async-start | bytes 2662400 | tf_op jit(solution)/shard_map/all_gather | solution.py:623
  267.4 24.1 %collective-permute-start.4 = (bf16[4,1040,256]{2,1,0:T(8,128)(2,1)}, bf16[4,1040,256]{2,1,0:T(8,128)(2,1)S(1)}, u32[]{:S(2)}, u32[]{:S(2)}) collective-permute-start(bf16[4,1040,256]{2,1,0:T(8,128)(2,1)} %bitcast.17), channel_id=1, source_target_pairs={{0,32},{32,0},{1,33},{33,1},{2,34},{34,2},{3,35},{35,3},{4,36},{36... | collective-permute-start | bytes 6389768 | tf_op jit(solution)/shard_map/ppermute | solution.py:50
  269.3 22.2 %collective-permute-start.5 = (bf16[4,1040,256]{2,1,0:T(8,128)(2,1)}, bf16[4,1040,256]{2,1,0:T(8,128)(2,1)S(1)}, u32[]{:S(2)}, u32[]{:S(2)}) collective-permute-start(bf16[4,1040,256]{2,1,0:T(8,128)(2,1)} %all-gather.6.cloned.1.call-done.refs_2_), channel_id=1, source_target_pairs={{0,32},{32,0},{1,33},{33,1},{2,34},{34,2},{3,35},{35,3},{4,36},{36... | collective-permute-start | bytes 6389768 | tf_op jit(solution)/shard_map/ppermute | solution.py:50
  271.8 19.7 %copy-start.6 = (bf16[4160,256]{1,0:T(8,128)(2,1)S(1)}, bf16[4160,256]{1,0:T(8,128)(2,1)}, u32[]{:S(2)}) copy-start(bf16[4160,256]{1,0:T(8,128)(2,1)} %all-gather.10.cloned.1.call-done) | copy-start | bytes 6389764
  272.0 19.5 %copy-start.5 = (bf16[128,4096]{1,0:T(8,128)(2,1)S(1)}, bf16[128,4096]{1,0:T(8,128)(2,1)}, u32[]{:S(2)}) copy-start(bf16[128,4096]{1,0:T(8,128)(2,1)} %x_ref.3) | copy-start | bytes 3145732
  272.0 19.5 %copy-start.18 = (f32[4096]{0:T(1024)S(1)}, f32[4096]{0:T(1024)}, u32[]{:S(2)}) copy-start(f32[4096]{0:T(1024)} %param.25) | copy-start | bytes 49156
  324.1 25.8 %copy-start.35 = (f32[4096]{0:T(1024)S(1)}, f32[4096]{0:T(1024)}, u32[]{:S(2)}) copy-start(f32[4096]{0:T(1024)} %param.29) | copy-start | bytes 49156
  325.1 24.3 %all-to-all-start.14 = ((bf16[8,4,4096]{2,1,0:T(4,128)(2,1)}), bf16[8,4,4096]{2,1,0:T(4,128)(2,1)S(1)}, u32[]{:S(2)}, u32[]{:S(2)}) async-start(bf16[8,4,4096]{2,1,0:T(4,128)(2,1)} %reshape.56), calls=%async_computation.14 | async-start | bytes 524288 | tf_op jit(solution)/shard_map/all_to_all | solution.py:639
  (20 other events, 90.4 us)
Sparse Core Ops, SparseCore 0:
  107.1 57.3 all-gather.7
  196.1 30.2 all-gather.9
  228.5 38.8 all-gather.5

commit v7 on v6

--- a/solution.py
+++ b/solution.py
@@ -88,16 +88,16 @@
 
 
 SMEM = pl.BlockSpec(memory_space=pltpu.SMEM)
+VMEM = pl.BlockSpec(memory_space=pltpu.VMEM)
 
 
 def call(kernel, name, out_shape, *args, scratch=(), limit=16):
     small = [a.ndim == 1 for a in args]
     return pl.pallas_call(
         kernel,
-        grid=(1,),
         out_shape=out_shape,
-        in_specs=[SMEM if one else whole(a) for a, one in zip(args, small)],
-        out_specs=jax.tree.map(lambda a: SMEM if len(a.shape) == 1 else whole(a), out_shape),
+        in_specs=[SMEM if one else VMEM for one in small],
+        out_specs=jax.tree.map(lambda a: SMEM if len(a.shape) == 1 else VMEM, out_shape),
         scratch_shapes=list(scratch),
         compiler_params=pltpu.CompilerParams(vmem_limit_bytes=limit << 20),
         name=name,
@@ -431,23 +431,25 @@
         for j, ref in enumerate(weight_refs):
             for n in range(count):
                 term = lax.dot_general(
-                    attention, ref[n], (((1,), (1,)), ((), ())), preferred_element_type=f32
+                    attention,
+                    ref[n, :, 3 * width :],
+                    (((1,), (1,)), ((), ())),
+                    preferred_element_type=f32,
                 ).astype(bf16)
                 for h in range(halves):
                     out_ref[(j * count + n) * halves + h] = term[:, h * width : (h + 1) * width]
 
-    out_weights = pl.BlockSpec((count, part, width), lambda i: (0, 0, 3))
-    return pl.pallas_call(
-        kernel,
-        grid=(1,),
-        out_shape=shape((blocks, ROW_DEV, width), bf16),
-        in_specs=[SMEM, whole(kept), whole(new_part), whole(returned)]
-        + [out_weights] * len(weights),
-        out_specs=pl.BlockSpec((blocks, ROW_DEV, width), lambda i: (0, 0, 0)),
-        scratch_shapes=[pltpu.VMEM((ROW_DEV, width), f32)],
-        compiler_params=pltpu.CompilerParams(vmem_limit_bytes=16 << 20),
-        name="merge_and_project",
-    )(control, kept, new_part, returned, *weights)
+    return call(
+        kernel,
+        "merge_and_project",
+        shape((blocks, ROW_DEV, width), bf16),
+        control,
+        kept,
+        new_part,
+        returned,
+        *weights,
+        scratch=[pltpu.VMEM((ROW_DEV, width), f32)],
+    )
 
 
 def feed_forward(columns, summed, hidden, gain, parcels, units):
@@ -461,25 +463,7 @@
 
     def kernel(c_ref, s_ref, x_ref, g_ref, *refs):
         parcel_refs = refs[:parts]
-        out_ref, mixed_ref, within_ref, down_ref, acc_ref, within_sem, down_sem = refs[parts:]
-        within = [
-            pltpu.make_async_copy(
-                parcel_refs[m // count].at[m % count, pl.ds(0, 2 * units)],
-                within_ref.at[m],
-                within_sem.at[m],
-            )
-            for m in range(parts * count)
-        ]
-        down = [
-            pltpu.make_async_copy(
-                parcel_refs[m // count].at[m % count, pl.ds(2 * units, units)],
-                down_ref.at[m],
-                down_sem.at[m],
-            )
-            for m in range(parts * count)
-        ]
-        for copy in within + down:
-            copy.start()
+        out_ref, mixed_ref, acc_ref = refs[parts:]
         squares = jnp.zeros((rows, part), f32)
         for b in range(blocks):
             block = s_ref[b].astype(f32)
@@ -492,9 +476,11 @@
                 x_ref[:, cols].astype(f32) + summed.astype(f32) * norm * g_ref[:, cols]
             ).astype(bf16)
             mixed_ref[:, cols] = mixed
-            within[m].wait()
             product = lax.dot_general(
-                within_ref[m], mixed, contract_last, preferred_element_type=f32
+                parcel_refs[m // count][m % count, : 2 * units],
+                mixed,
+                contract_last,
+                preferred_element_type=f32,
             )
             acc_ref[...] = product if m == 0 else acc_ref[...] + product
         to = lax.broadcasted_iota(jnp.int32, (rows, rows), 0)
@@ -508,31 +494,20 @@
         ).astype(bf16)
         for m in range(parts * count):
             cols = pl.ds(pl.multiple_of(c_ref[m] * depth, depth), depth)
-            down[m].wait()
-            out_ref[:, cols] = jnp.dot(
-                active, down_ref[m], preferred_element_type=f32
-            ).astype(bf16)
-
-    return pl.pallas_call(
-        kernel,
-        grid=(1,),
-        out_shape=(shape((rows, model), bf16), shape((rows, model), bf16)),
-        in_specs=[SMEM, whole(summed), whole(hidden), whole(gain)]
-        + [pl.BlockSpec(memory_space=pl.ANY)] * parts,
-        out_specs=(
-            pl.BlockSpec((rows, model), lambda k: (0, 0)),
-            pl.BlockSpec((rows, model), lambda k: (0, 0)),
-        ),
-        scratch_shapes=[
-            pltpu.VMEM((parts * count, 2 * units, depth), bf16),
-            pltpu.VMEM((parts * count, units, depth), bf16),
-            pltpu.VMEM((2 * units, rows), f32),
-            pltpu.SemaphoreType.DMA((parts * count,)),
-            pltpu.SemaphoreType.DMA((parts * count,)),
-        ],
-        compiler_params=pltpu.CompilerParams(vmem_limit_bytes=24 << 20),
-        name="feed_forward",
-    )(columns, summed, hidden, gain, *parcels)
+            down = parcel_refs[m // count][m % count, 2 * units : 3 * units]
+            out_ref[:, cols] = jnp.dot(active, down, preferred_element_type=f32).astype(bf16)
+
+    return call(
+        kernel,
+        "feed_forward",
+        (shape((rows, model), bf16), shape((rows, model), bf16)),
+        columns,
+        summed,
+        hidden,
+        gain,
+        *parcels,
+        scratch=[pltpu.VMEM((2 * units, rows), f32)],
+    )
 
 
 def shards(
@@ -583,6 +558,8 @@
 
     near_other = swap(near, "core", NCORE)
     far = copies_to_all(theirs, "y", NY)
+    far, near_parcel = lax.optimization_barrier((far, parcel))
+    parcel_near = lax.all_gather(near_parcel, "y")
     far_other = swap(far, "core", NCORE)
     weights = [near, near_other, far, far_other]
     raw, squares = project(columns, hidden_states, weights, width, blocks)
@@ -594,6 +571,7 @@
     )
 
     queries = lax.all_to_all(query, "zh", 0, 0, tiled=True)
+    queries, parcel_near = lax.optimization_barrier((queries, parcel_near))
     queries = copies_to_all(queries, "y", NY)
     queries = copies_to_all(queries, "core", NCORE).reshape(N_SEQ, ROW_DEV, width)
     new_other = swap(new_mine, "core", NCORE)
@@ -618,15 +596,14 @@
     returned = copies_to_all(returned, "core", NCORE).reshape(N_SEQ, -1, width)
 
     terms = merge_and_project(merge_control, kept, new_part, returned, weights)
-    terms, pair, parcel = lax.optimization_barrier((terms, pair, parcel))
-    parcel_near = lax.all_gather(parcel, "y")
+    terms, pair = lax.optimization_barrier((terms, pair))
     parcel_far = lax.all_gather(lax.dynamic_index_in_dim(pair, 1 - zh, 0, False), "y")
     terms = lax.all_to_all(terms.reshape(NX, NZL, ROW_DEV, width), "x", 0, 0, tiled=True)
     terms = jnp.sum(terms.astype(f32), axis=0).astype(bf16)
     terms = lax.all_to_all(terms, "zl", 0, 0, tiled=True)
     summed = jnp.sum(terms.astype(f32), axis=0).astype(bf16)
     summed = copies_to_all(summed, "zl", NZL)
-    summed, parcel_near, parcel_far = lax.optimization_barrier((summed, parcel_near, parcel_far))
+    summed, parcel_far = lax.optimization_barrier((summed, parcel_far))
     summed = copies_to_all(summed, "x", NX).reshape(blocks, ROW_DEV, model // blocks)
 
     parcels = [parcel_near, swap(parcel_near, "core", NCORE)]

time: 359 us -> 354 us (0.986)
  blocking collectives: 162 us -> 143 us
  waiting for transfers between devices: 71.2 us -> 88.6 us
  local copies, waits for them, and re-layouts: 17 us -> 25.6 us
  Pallas kernels: 23.9 us -> 16.4 us
  starting transfers between devices: 63.7 us -> 59.9 us
    all_to_all x4 -> x1, blocking collectives: 54.6 us -> 4.44 us  [copies_to_all(): lax.all_to_all(jnp.broadcast_to(a[None], (count,) + a.shape), axis, 0, 0,...]
    all_to_all x4 -> x7, waiting for transfers between devices: 16.7 us -> 52.5 us  [copies_to_all(): lax.all_to_all(jnp.broadcast_to(a[None], (count,) + a.shape), axis, 0, 0,...]
    all_to_all x0 -> x1, blocking collectives: none -> 24.7 us  [shards(): squares = lax.all_to_all(squares, BLK, 0, 0, tiled=True)]
    all_to_all x4 -> x7, starting transfers between devices: 16.6 us -> 29.5 us  [copies_to_all(): lax.all_to_all(jnp.broadcast_to(a[None], (count,) + a.shape), axis, 0, 0,...]
    all_to_all x1, blocking collectives: 22 us -> 34.1 us  [shards(): terms = lax.all_to_all(terms, 'zl', 0, 0, tiled=True)]
    all_to_all x1 -> x0, starting transfers between devices: 11.6 us -> none  [shards(): squares = lax.all_to_all(squares, BLK, 0, 0, tiled=True)]
    all_to_all x1 -> x0, waiting for transfers between devices: 11.2 us -> none  [shards(): squares = lax.all_to_all(squares, BLK, 0, 0, tiled=True)]
    all_gather x1, waiting for transfers between devices: 7.99 us -> 0.01 us  [shards(): lax.all_gather(lax.dynamic_index_in_dim(pair, 1 - zh, 0, False), 'y')]
  transfers between devices with their start and end apart: 15 -> 17, of which waited for: 8 -> 10; matrix products, arithmetic and copies ran while one was open for 2% -> 3% of each run, Pallas kernels for 2% -> 3%
where the time goes in v7:
time: 354 us; the launch traced here: 353 us
  blocking collectives  143 us (40%)
  waiting for transfers between devices  88.6 us (25%)
  starting transfers between devices  59.9 us (17%)
  local copies, waits for them, and re-layouts  25.6 us (7%)
  Pallas kernels  16.4 us (5%)
  between operations  14.1 us (4%)
  other arithmetic  4.77 us (1%)
    all_to_all x7, waiting for transfers between devices, copies_to_all(): lax.all_to_all(jnp.broadcast_to(a[None], (count,) + a.shape), axis, 0, 0,...  52.5 us
    all_to_all x1, blocking collectives, shards(): terms = lax.all_to_all(terms, 'zl', 0, 0, tiled=True)  34.1 us
    all_to_all x7, starting transfers between devices, copies_to_all(): lax.all_to_all(jnp.broadcast_to(a[None], (count,) + a.shape), axis, 0, 0,...  29.5 us
    ppermute x6, starting transfers between devices, swap(): return lax.ppermute(a, axis, [(i, i ^ 1) for i in range(count)])  24.9 us
    all_to_all x1, blocking collectives, shards(): squares = lax.all_to_all(squares, BLK, 0, 0, tiled=True)  24.7 us
    all_to_all x1, blocking collectives, shards(): queries = lax.all_to_all(query, 'zh', 0, 0, tiled=True)  22.1 us
    ppermute x6, waiting for transfers between devices, swap(): return lax.ppermute(a, axis, [(i, i ^ 1) for i in range(count)])  21 us
    all_to_all x1, blocking collectives, shards(): returned = lax.all_to_all(returned, 'zh', 0, 0, tiled=True)  21 us
  transfers between devices with their start and end apart: 17, of which 10 were waited for; matrix products, arithmetic and copies ran while one was open for 3% of the time, Pallas kernels for 3%

profile of v7, /device:TPU:32, one launch (start us, length us, event | category | flops | bytes accessed | tf_op | source)
XLA Modules:
  0.0 352.6 jit_solution(15237833177942508855)
XLA Ops:
  11.8 4.6 %all-to-all-start = ((bf16[4,256,512]{2,1,0:T(8,128)(2,1)}), bf16[4,256,512]{2,1,0:T(8,128)(2,1)S(1)}, u32[]{:S(2)}, u32[]{:S(2)}) async-start(bf16[4,256,512]{2,1,0:T(8,128)(2,1)} %broadcast_in_dim.33), calls=%async_computation | async-start | bytes 2097152 | tf_op jit(solution)/shard_map/all_to_all | solution.py:37
  16.4 14.8 %collective-permute-start = (bf16[256,512]{1,0:T(8,128)(2,1)S(1)}, bf16[256,512]{1,0:T(8,128)(2,1)S(1)}, u32[]{:S(2)}, u32[]{:S(2)}) collective-permute-start(bf16[256,512]{1,0:T(8,128)(2,1)S(1)} %join_weights.1), channel_id=1, source_target_pairs={{0,64},{64,0},{1,65},{65,1},{2,66},{66,2},{3,67},{67,3},{4,68},{68... | collective-permute-start | bytes 786440 | tf_op jit(solution)/shard_map/ppermute | solution.py:50
  35.5 18.7 %collective-permute-done = bf16[256,512]{1,0:T(8,128)(2,1)S(1)} collective-permute-done((bf16[256,512]{1,0:T(8,128)(2,1)S(1)}, bf16[256,512]{1,0:T(8,128)(2,1)S(1)}, u32[]{:S(2)}, u32[]{:S(2)}) %collective-permute-start) | collective-permute-done | bytes 262176 | tf_op jit(solution)/shard_map/ppermute | solution.py:50
  55.4 4.6 %all-to-all-start.1 = ((bf16[4,256,512]{2,1,0:T(8,128)(2,1)}), bf16[4,256,512]{2,1,0:T(8,128)(2,1)S(1)}, u32[]{:S(2)}, u32[]{:S(2)}) async-start(bf16[4,256,512]{2,1,0:T(8,128)(2,1)} %broadcast_in_dim.36), calls=%async_computation.1 | async-start | bytes 2097152 | tf_op jit(solution)/shard_map/all_to_all | solution.py:37
  60.1 1.9 fusion.4
  62.0 12.2 %all-to-all-done.1.refs_2_ = bf16[4,256,512]{2,1,0:T(8,128)(2,1)S(1)} async-done(((bf16[4,256,512]{2,1,0:T(8,128)(2,1)}), bf16[4,256,512]{2,1,0:T(8,128)(2,1)S(1)}, u32[]{:S(2)}, u32[]{:S(2)}) %all-to-all-start.1) | async-done | bytes 1048608 | tf_op jit(solution)/shard_map/all_to_all | solution.py:37
  74.2 1.9 collective-permute-start.1
  76.2 2.4 collective-permute-start.2
  78.8 2.1 collective-permute-done.2.refs_3_
  82.3 24.7 %all_to_all.75.s_ref = f32[32,8,128]{2,1,0:T(8,128)S(1)} all-to-all(f32[32,8,128]{2,1,0:T(8,128)S(1)} %get-tuple-element.46), channel_id=1, replica_groups=mesh['y'=4,'zh'=2,'core'=2,'zl'=8,'x'=4] {'zl','x'}, dimensions={0} | all-to-all | bytes 262144 | tf_op jit(solution)/shard_map/all_to_all | solution.py:566
  110.4 22.1 %all_to_all.76 = bf16[2,128,128]{2,1,0:T(8,128)(2,1)S(1)} all-to-all(bf16[2,128,128]{2,1,0:T(8,128)(2,1)S(1)} %get-tuple-element.50.own_ref), channel_id=1, replica_groups=mesh['y'=4,'zh'=2,'core'=2,'zl'=8,'x'=4] {'zh'}, dimensions={0} | all-to-all | bytes 131072 | tf_op jit(solution)/shard_map/all_to_all | solution.py:573
  133.2 3.4 all-to-all-start.4
  136.6 1.9 collective-permute-start.3
  139.9 1.9 blend.1
  144.2 3.5 all-to-all-start.5
  152.1 3.4 attend.1
  156.2 21.0 %all_to_all.77 = bf16[2,176,128]{2,1,0:T(8,128)(2,1)S(1)} all-to-all(bf16[2,176,128]{2,1,0:T(8,128)(2,1)S(1)} %get-tuple-element.64), channel_id=1, replica_groups=mesh['y'=4,'zh'=2,'core'=2,'zl'=8,'x'=4] {'zh'}, dimensions={0} | all-to-all | bytes 180224 | tf_op jit(solution)/shard_map/all_to_all | solution.py:594
  177.9 4.2 %all-to-all-start.7 = ((bf16[4,2,176,128]{3,2,1,0:T(8,128)(2,1)}), bf16[4,2,176,128]{3,2,1,0:T(8,128)(2,1)S(1)}, u32[]{:S(2)}, u32[]{:S(2)}) async-start(bf16[4,2,176,128]{3,2,1,0:T(8,128)(2,1)} %broadcast_in_dim.41), calls=%async_computation.7 | async-start | bytes 720896 | tf_op jit(solution)/shard_map/all_to_all | solution.py:37
  182.2 7.9 %all-to-all-done.7 = bf16[4,2,176,128]{3,2,1,0:T(8,128)(2,1)S(1)} async-done(((bf16[4,2,176,128]{3,2,1,0:T(8,128)(2,1)}), bf16[4,2,176,128]{3,2,1,0:T(8,128)(2,1)S(1)}, u32[]{:S(2)}, u32[]{:S(2)}) %all-to-all-start.7) | async-done | bytes 360480 | tf_op jit(solution)/shard_map/all_to_all | solution.py:37
  190.1 4.4 %all_to_all.78 = bf16[2,4,2,176,128]{4,3,2,1,0:T(8,128)(2,1)S(1)} all-to-all(bf16[2,4,2,176,128]{4,3,2,1,0:T(8,128)(2,1)S(1)} %broadcast_in_dim.42), channel_id=1, replica_groups=mesh['y'=4,'zh'=2,'core'=2,'zl'=8,'x'=4] {'core'}, dimensions={0} | all-to-all | bytes 1441792 | tf_op jit(solution)/shard_map/all_to_all | solution.py:37
  198.7 19.3 %all_to_all.79 = bf16[4,8,128,128]{3,2,1,0:T(8,128)(2,1)S(1)} all-to-all(bf16[4,8,128,128]{3,2,1,0:T(8,128)(2,1)S(1)} %bitcast.14), channel_id=1, replica_groups=mesh['y'=4,'zh'=2,'core'=2,'zl'=8,'x'=4] {'x'}, dimensions={0} | all-to-all | bytes 2097152 | tf_op jit(solution)/shard_map/all_to_all | solution.py:601
  218.2 34.1 %all_to_all.80 = bf16[8,128,128]{2,1,0:T(8,128)(2,1)S(1)} all-to-all(bf16[8,128,128]{2,1,0:T(8,128)(2,1)S(1)} %reduce_sum.54), channel_id=1, replica_groups=mesh['y'=4,'zh'=2,'core'=2,'zl'=8,'x'=4] {'zl'}, dimensions={0} | all-to-all | bytes 524288 | tf_op jit(solution)/shard_map/all_to_all | solution.py:603
  253.0 5.5 %all-to-all-start.11 = ((bf16[8,128,128]{2,1,0:T(8,128)(2,1)}), bf16[8,128,128]{2,1,0:T(8,128)(2,1)S(1)}, u32[]{:S(2)}, u32[]{:S(2)}) async-start(bf16[8,128,128]{2,1,0:T(8,128)(2,1)} %broadcast_in_dim.43), calls=%async_computation.11 | async-start | bytes 524288 | tf_op jit(solution)/shard_map/all_to_all | solution.py:37
  258.5 1.9 collective-permute-start.4
  260.5 13.9 %all-to-all-done.11 = bf16[8,128,128]{2,1,0:T(8,128)(2,1)S(1)} async-done(((bf16[8,128,128]{2,1,0:T(8,128)(2,1)}), bf16[8,128,128]{2,1,0:T(8,128)(2,1)S(1)}, u32[]{:S(2)}, u32[]{:S(2)}) %all-to-all-start.11) | async-done | bytes 262176 | tf_op jit(solution)/shard_map/all_to_all | solution.py:37
  274.4 1.9 collective-permute-start.5
  277.5 3.6 %all-to-all-start.12 = ((bf16[4,8,128,128]{3,2,1,0:T(8,128)(2,1)}), bf16[4,8,128,128]{3,2,1,0:T(8,128)(2,1)S(1)}, u32[]{:S(2)}, u32[]{:S(2)}) async-start(bf16[4,8,128,128]{3,2,1,0:T(8,128)(2,1)} %broadcast_in_dim.84), calls=%async_computation.12 | async-start | bytes 2097152 | tf_op jit(solution)/shard_map/all_to_all | solution.py:37
  281.2 16.0 %all-to-all-done.12 = bf16[4,8,128,128]{3,2,1,0:T(8,128)(2,1)S(1)} async-done(((bf16[4,8,128,128]{3,2,1,0:T(8,128)(2,1)}), bf16[4,8,128,128]{3,2,1,0:T(8,128)(2,1)S(1)}, u32[]{:S(2)}, u32[]{:S(2)}) %all-to-all-start.12) | async-done | bytes 1048608 | tf_op jit(solution)/shard_map/all_to_all | solution.py:37
  298.8 6.9 %feed_forward.1 = (bf16[128,4096]{1,0:T(8,128)(2,1)S(1)}, bf16[128,4096]{1,0:T(8,128)(2,1)S(1)}) custom-call(s32[16]{0:T(128)S(1)} %copy-done.26, bf16[32,128,128]{2,1,0:T(8,128)(2,1)S(1)} %bitcast.15, bf16[128,4096]{1,0:T(8,128)(2,1)S(1)} %copy-done.5, f32[1,4096]{1,0:T(1,128)S(1)} %bitcast.20, bf16[4,1040,256]{2,1,0:T(8,128)(2,1)} %bitcast.6.refs_0_, ...), custom_call_target="tpu_custom_call" | custom-call | tf_op jit(solution)/shard_map/feed_forward/pallas_call | solution.py:96
  305.7 17.7 %all_to_all.81 = bf16[4,32,4096]{2,1,0:T(8,128)(2,1)S(1)} all-to-all(bf16[4,32,4096]{2,1,0:T(8,128)(2,1)S(1)} %bitcast.18), channel_id=1, replica_groups=mesh['y'=4,'zh'=2,'core'=2,'zl'=8,'x'=4] {'x'}, dimensions={0} | all-to-all | bytes 2097152 | tf_op jit(solution)/shard_map/all_to_all | solution.py:614
  324.4 5.5 %all-to-all-start.14 = ((bf16[8,4,4096]{2,1,0:T(4,128)(2,1)}), bf16[8,4,4096]{2,1,0:T(4,128)(2,1)S(1)}, u32[]{:S(2)}, u32[]{:S(2)}) async-start(bf16[8,4,4096]{2,1,0:T(4,128)(2,1)} %reshape.56), calls=%async_computation.14 | async-start | bytes 524288 | tf_op jit(solution)/shard_map/all_to_all | solution.py:616
  329.9 15.0 %all-to-all-done.14 = bf16[8,4,4096]{2,1,0:T(4,128)(2,1)S(1)} async-done(((bf16[8,4,4096]{2,1,0:T(4,128)(2,1)}), bf16[8,4,4096]{2,1,0:T(4,128)(2,1)S(1)}, u32[]{:S(2)}, u32[]{:S(2)}) %all-to-all-start.14) | async-done | bytes 262176 | tf_op jit(solution)/shard_map/all_to_all | solution.py:616
  (133 shorter events, 35.6 us)
Async XLA Ops:
  11.8 19.7 %copy-start.19 = (s32[16,96]{1,0:T(8,128)S(1)}, s32[16,96]{1,0:T(8,128)}, u32[]{:S(2)}) copy-start(s32[16,96]{1,0:T(8,128)} %i_ref.1) | copy-start | bytes 18436
  11.8 19.8 %copy-start.35 = (s32[16]{0:T(128)S(1)}, s32[16]{0:T(128)}, u32[]{:S(2)}) copy-start(s32[16]{0:T(128)} %o_ref.2) | copy-start | bytes 196
  11.8 19.8 %copy-start.36 = (s32[8]{0:T(128)S(1)}, s32[8]{0:T(128)}, u32[]{:S(2)}) copy-start(s32[8]{0:T(128)} %len_ref.1) | copy-start | bytes 100
  11.8 42.5 %all-to-all-start = ((bf16[4,256,512]{2,1,0:T(8,128)(2,1)}), bf16[4,256,512]{2,1,0:T(8,128)(2,1)S(1)}, u32[]{:S(2)}, u32[]{:S(2)}) async-start(bf16[4,256,512]{2,1,0:T(8,128)(2,1)} %broadcast_in_dim.33), calls=%async_computation | async-start | bytes 2097152 | tf_op jit(solution)/shard_map/all_to_all | solution.py:37
  16.4 37.9 %collective-permute-start = (bf16[256,512]{1,0:T(8,128)(2,1)S(1)}, bf16[256,512]{1,0:T(8,128)(2,1)S(1)}, u32[]{:S(2)}, u32[]{:S(2)}) collective-permute-start(bf16[256,512]{1,0:T(8,128)(2,1)S(1)} %join_weights.1), channel_id=1, source_target_pairs={{0,64},{64,0},{1,65},{65,1},{2,66},{66,2},{3,67},{67,3},{4,68},{68... | collective-permute-start | bytes 786440 | tf_op jit(solution)/shard_map/ppermute | solution.py:50
  34.4 21.0 %copy-start.33 = (s32[5]{0:T(128)}, s32[5]{0:T(128)S(1)}, u32[]{:S(2)}) copy-start(s32[5]{0:T(128)S(1)} %get-tuple-element.40.c_ref) | copy-start | bytes 64
  34.4 46.4 %copy-start.25 = (s32[16]{0:T(128)}, s32[16]{0:T(128)S(1)}, u32[]{:S(2)}) copy-start(s32[16]{0:T(128)S(1)} %get-tuple-element.38.c_ref) | copy-start | bytes 196
  55.4 18.8 %all-to-all-start.1 = ((bf16[4,256,512]{2,1,0:T(8,128)(2,1)}), bf16[4,256,512]{2,1,0:T(8,128)(2,1)S(1)}, u32[]{:S(2)}, u32[]{:S(2)}) async-start(bf16[4,256,512]{2,1,0:T(8,128)(2,1)} %broadcast_in_dim.36), calls=%async_computation.1 | async-start | bytes 2097152 | tf_op jit(solution)/shard_map/all_to_all | solution.py:37
  60.1 20.8 %copy-start.4 = (bf16[128,4096]{1,0:T(8,128)(2,1)S(1)}, bf16[128,4096]{1,0:T(8,128)(2,1)}, u32[]{:S(2)}) copy-start(bf16[128,4096]{1,0:T(8,128)(2,1)} %x_ref.3) | copy-start | bytes 3145732
  60.1 72.4 %all-gather.8.cloned.1.call-start = ((), (), s32[]{:S(2)}) async-start(), calls=%async_computation.16 | async-start | bytes 2662400 | tf_op jit(solution)/shard_map/all_gather | solution.py:562
  74.2 122.6 %all-gather.10.cloned.1.call-start = ((), (), s32[]{:S(2)}) async-start(), calls=%async_computation.17 | async-start | bytes 1597440 | tf_op jit(solution)/shard_map/all_gather | solution.py:568
  74.2 4.6 %collective-permute-start.1 = (bf16[4,256,512]{2,1,0:T(8,128)(2,1)S(1)}, bf16[4,256,512]{2,1,0:T(8,128)(2,1)S(1)}, u32[]{:S(2)}, u32[]{:S(2)}) collective-permute-start(bf16[4,256,512]{2,1,0:T(8,128)(2,1)S(1)} %all-to-all-done.refs_0_), channel_id=1, source_target_pairs={{0,32},{32,0},{1,33},{33,1},{2,34},{34,2},{3,35},{35,3},{4,36},{36... | collective-permute-start | bytes 3145736 | tf_op jit(solution)/shard_map/ppermute | solution.py:50
  76.2 4.7 %collective-permute-start.2 = (bf16[4,256,512]{2,1,0:T(8,128)(2,1)S(1)}, bf16[4,256,512]{2,1,0:T(8,128)(2,1)S(1)}, u32[]{:S(2)}, u32[]{:S(2)}) collective-permute-start(bf16[4,256,512]{2,1,0:T(8,128)(2,1)S(1)} %all-to-all-done.1.refs_2_), channel_id=1, source_target_pairs={{0,32},{32,0},{1,33},{33,1},{2,34},{34,2},{3,35},{35,3},{4,36},{36... | collective-permute-start | bytes 3145736 | tf_op jit(solution)/shard_map/ppermute | solution.py:50
  106.9 33.0 %copy-start.7 = (bf16[1,1024,128]{2,1,0:T(8,128)(2,1)S(1)}, bf16[1,1024,128]{2,1,0:T(8,128)(2,1)}, u32[]{:S(2)}) copy-start(bf16[1,1024,128]{2,1,0:T(8,128)(2,1)} %k_ref.3) | copy-start | bytes 786436
  106.9 33.0 %copy-start.8 = (bf16[1,1024,128]{2,1,0:T(8,128)(2,1)S(1)}, bf16[1,1024,128]{2,1,0:T(8,128)(2,1)}, u32[]{:S(2)}) copy-start(bf16[1,1024,128]{2,1,0:T(8,128)(2,1)} %v_ref.3) | copy-start | bytes 786436
  106.9 33.0 %copy-start.38 = (s32[1,128]{1,0:T(1,128)S(1)}, s32[1,128]{1,0:T(1,128)}, u32[]{:S(2)}) copy-start(s32[1,128]{1,0:T(1,128)} %copy-done.37) | copy-start | bytes 1540
  110.3 33.8 %copy-start.21 = (bf16[64,128]{1,0:T(8,128)(2,1)}, bf16[64,128]{1,0:T(8,128)(2,1)S(1)}, u32[]{:S(2)}) copy-start(bf16[64,128]{1,0:T(8,128)(2,1)S(1)} %get-tuple-element.59.nm_ref) | copy-start | bytes 49156
  133.2 10.1 %all-to-all-start.4 = ((bf16[4,2,128,128]{3,2,1,0:T(8,128)(2,1)}), bf16[4,2,128,128]{3,2,1,0:T(8,128)(2,1)S(1)}, u32[]{:S(2)}, u32[]{:S(2)}) async-start(bf16[4,2,128,128]{3,2,1,0:T(8,128)(2,1)} %broadcast_in_dim.39), calls=%async_computation.4 | async-start | bytes 524288 | tf_op jit(solution)/shard_map/all_to_all | solution.py:37
  136.6 11.1 %collective-permute-start.3 = (bf16[64,128]{1,0:T(8,128)(2,1)S(1)}, bf16[64,128]{1,0:T(8,128)(2,1)S(1)}, u32[]{:S(2)}, u32[]{:S(2)}) collective-permute-start(bf16[64,128]{1,0:T(8,128)(2,1)S(1)} %get-tuple-element.59.nm_ref), channel_id=1, source_target_pairs={{0,32},{32,0},{1,33},{33,1},{2,34},{34,2},{3,35},{35,3},{4,36},{36... | collective-permute-start | bytes 49160 | tf_op jit(solution)/shard_map/ppermute | solution.py:50
  144.2 5.2 %all-to-all-start.5 = ((bf16[2,4,2,128,128]{4,3,2,1,0:T(8,128)(2,1)}), bf16[2,4,2,128,128]{4,3,2,1,0:T(8,128)(2,1)S(1)}, u32[]{:S(2)}, u32[]{:S(2)}) async-start(bf16[2,4,2,128,128]{4,3,2,1,0:T(8,128)(2,1)} %broadcast_in_dim.40), calls=%async_computation.5 | async-start | bytes 1048576 | tf_op jit(solution)/shard_map/all_to_all | solution.py:37
  156.2 33.9 %copy-start.11 = (f32[192,256]{1,0:T(8,128)}, f32[192,256]{1,0:T(8,128)S(1)}, u32[]{:S(2)}) copy-start(f32[192,256]{1,0:T(8,128)S(1)} %get-tuple-element.62.kept_ref) | copy-start | bytes 589828
  177.9 12.1 %all-to-all-start.7 = ((bf16[4,2,176,128]{3,2,1,0:T(8,128)(2,1)}), bf16[4,2,176,128]{3,2,1,0:T(8,128)(2,1)S(1)}, u32[]{:S(2)}, u32[]{:S(2)}) async-start(bf16[4,2,176,128]{3,2,1,0:T(8,128)(2,1)} %broadcast_in_dim.41), calls=%async_computation.7 | async-start | bytes 720896 | tf_op jit(solution)/shard_map/all_to_all | solution.py:37
  182.1 92.2 %all-gather.6.cloned.1.call-start = ((), (), s32[]{:S(2)}) async-start(), calls=%async_computation.15 | async-start | bytes 2662400 | tf_op jit(solution)/shard_map/all_gather | solution.py:600
  253.0 21.3 %all-to-all-start.11 = ((bf16[8,128,128]{2,1,0:T(8,128)(2,1)}), bf16[8,128,128]{2,1,0:T(8,128)(2,1)S(1)}, u32[]{:S(2)}, u32[]{:S(2)}) async-start(bf16[8,128,128]{2,1,0:T(8,128)(2,1)} %broadcast_in_dim.43), calls=%async_computation.11 | async-start | bytes 524288 | tf_op jit(solution)/shard_map/all_to_all | solution.py:37
  258.5 22.6 %collective-permute-start.4 = (bf16[4,1040,256]{2,1,0:T(8,128)(2,1)}, bf16[4,1040,256]{2,1,0:T(8,128)(2,1)}, u32[]{:S(2)}, u32[]{:S(2)}) collective-permute-start(bf16[4,1040,256]{2,1,0:T(8,128)(2,1)} %bitcast.6.refs_0_), channel_id=1, source_target_pairs={{0,32},{32,0},{1,33},{33,1},{2,34},{34,2},{3,35},{35,3},{4,36},{36... | collective-permute-start | bytes 6389768 | tf_op jit(solution)/shard_map/ppermute | solution.py:50
  274.4 22.8 %collective-permute-start.5 = (bf16[4,1040,256]{2,1,0:T(8,128)(2,1)}, bf16[4,1040,256]{2,1,0:T(8,128)(2,1)}, u32[]{:S(2)}, u32[]{:S(2)}) collective-permute-start(bf16[4,1040,256]{2,1,0:T(8,128)(2,1)} %all-gather.6.cloned.1.call-done.refs_2_), channel_id=1, source_target_pairs={{0,32},{32,0},{1,33},{33,1},{2,34},{34,2},{3,35},{35,3},{4,36},{36... | collective-permute-start | bytes 6389768 | tf_op jit(solution)/shard_map/ppermute | solution.py:50
  277.5 19.7 %copy-start.5 = (bf16[128,4096]{1,0:T(8,128)(2,1)S(1)}, bf16[128,4096]{1,0:T(8,128)(2,1)}, u32[]{:S(2)}) copy-start(bf16[128,4096]{1,0:T(8,128)(2,1)} %x_ref.3) | copy-start | bytes 3145732
  277.5 19.7 %copy-start.20 = (f32[4096]{0:T(1024)S(1)}, f32[4096]{0:T(1024)}, u32[]{:S(2)}) copy-start(f32[4096]{0:T(1024)} %param.25) | copy-start | bytes 49156
  277.5 19.7 %copy-start.26 = (s32[16]{0:T(128)S(1)}, s32[16]{0:T(128)}, u32[]{:S(2)}) copy-start(s32[16]{0:T(128)} %copy-done.25) | copy-start | bytes 196
  277.5 19.7 %all-to-all-start.12 = ((bf16[4,8,128,128]{3,2,1,0:T(8,128)(2,1)}), bf16[4,8,128,128]{3,2,1,0:T(8,128)(2,1)S(1)}, u32[]{:S(2)}, u32[]{:S(2)}) async-start(bf16[4,8,128,128]{3,2,1,0:T(8,128)(2,1)} %broadcast_in_dim.84), calls=%async_computation.12 | async-start | bytes 2097152 | tf_op jit(solution)/shard_map/all_to_all | solution.py:37
  323.4 22.0 %copy-start.40 = (f32[4096]{0:T(1024)S(1)}, f32[4096]{0:T(1024)}, u32[]{:S(2)}) copy-start(f32[4096]{0:T(1024)} %param.29) | copy-start | bytes 49156
  324.4 20.5 %all-to-all-start.14 = ((bf16[8,4,4096]{2,1,0:T(4,128)(2,1)}), bf16[8,4,4096]{2,1,0:T(4,128)(2,1)S(1)}, u32[]{:S(2)}, u32[]{:S(2)}) async-start(bf16[8,4,4096]{2,1,0:T(4,128)(2,1)} %reshape.56), calls=%async_computation.14 | async-start | bytes 524288 | tf_op jit(solution)/shard_map/all_to_all | solution.py:616
  (27 other events, 91.0 us)
Sparse Core Ops, SparseCore 0:
  74.3 37.8 all-gather.7
  114.3 72.6 all-gather.9
  198.8 43.6 all-gather.5

commit v8 on v7

--- a/solution.py
+++ b/solution.py
@@ -263,8 +263,8 @@
         raw = raw_ref[...]
         query = raw[:, :width] * scale[:, 0:1] * gq_ref[...]
         key = raw[:, width : 2 * width] * scale[:, 1:2] * gk_ref[...]
-        query = turn_by(query, c_ref[...], t_ref[...]).astype(bf16)
-        key = turn_by(key, c_ref[...], t_ref[...]).astype(bf16)
+        query = turn_by(query, c_ref[:ROW_DEV, :], t_ref[:ROW_DEV, :]).astype(bf16)
+        key = turn_by(key, c_ref[:ROW_DEV, :], t_ref[:ROW_DEV, :]).astype(bf16)
         value = raw[:, 2 * width :].astype(bf16)
         for z in range(NZH):
             q_ref[z] = query
@@ -301,7 +301,8 @@
         hit = (at == p_ref[...]).astype(f32)
         here = jnp.max(hit, axis=1, keepdims=True) > 0.0
         hit = hit.astype(bf16)
-        turned = turn_by(k_ref[0].astype(f32), c_ref[...], t_ref[...])
+        turn = slice(ROW_DEV, ROW_DEV + 1)
+        turned = turn_by(k_ref[0].astype(f32), c_ref[turn, :], t_ref[turn, :])
         placed = jnp.dot(hit, nk_ref[...], preferred_element_type=f32)
         bk_ref[0] = jnp.where(here, placed, turned).astype(bf16)
         placed = jnp.dot(hit, nv_ref[...], preferred_element_type=f32)
@@ -553,8 +554,6 @@
     sign = jnp.where(jnp.arange(HD) < HD // 2, -1.0, 1.0).astype(f32)
     cosine, sine = jnp.cos(angles), jnp.sin(angles) * sign
     theirs, near, cosine, sine = lax.optimization_barrier((theirs, near, cosine, sine))
-    turn_cosine, turn_sine = cosine[ROW_DEV : ROW_DEV + 1], sine[ROW_DEV : ROW_DEV + 1]
-    cosine, sine = cosine[:ROW_DEV], sine[:ROW_DEV]
 
     near_other = swap(near, "core", NCORE)
     far = copies_to_all(theirs, "y", NY)
@@ -565,7 +564,7 @@
     raw, squares = project(columns, hidden_states, weights, width, blocks)
     squares = lax.all_to_all(squares, BLK, 0, 0, tiled=True)
     squares, parcel = lax.optimization_barrier((squares, parcel))
-    pair = lax.all_gather(parcel, "zh")
+    parcel_other = swap(parcel, "zh", NZH)
     query, key, value, new_mine = finish_rows(
         raw, squares, query_gain[None], key_gain[None], cosine, sine, model
     )
@@ -576,7 +575,7 @@
     queries = copies_to_all(queries, "core", NCORE).reshape(N_SEQ, ROW_DEV, width)
     new_other = swap(new_mine, "core", NCORE)
     blended_keys, blended_values = blend(
-        picked, turn_cosine, turn_sine, cached_keys, cached_values, key, value
+        picked, cosine, sine, cached_keys, cached_values, key, value
     )
     returned, kept, new_part = attend(
         attend_control,
@@ -596,8 +595,8 @@
     returned = copies_to_all(returned, "core", NCORE).reshape(N_SEQ, -1, width)
 
     terms = merge_and_project(merge_control, kept, new_part, returned, weights)
-    terms, pair = lax.optimization_barrier((terms, pair))
-    parcel_far = lax.all_gather(lax.dynamic_index_in_dim(pair, 1 - zh, 0, False), "y")
+    terms, parcel_other = lax.optimization_barrier((terms, parcel_other))
+    parcel_far = lax.all_gather(parcel_other, "y")
     terms = lax.all_to_all(terms.reshape(NX, NZL, ROW_DEV, width), "x", 0, 0, tiled=True)
     terms = jnp.sum(terms.astype(f32), axis=0).astype(bf16)
     terms = lax.all_to_all(terms, "zl", 0, 0, tiled=True)

time: 354 us -> 351 us (level)
  blocking collectives: 143 us -> 162 us
  local copies, waits for them, and re-layouts: 25.6 us -> 13.1 us
  waiting for transfers between devices: 88.6 us -> 81.8 us
    all_to_all x1, blocking collectives: 21 us -> 41.1 us  [shards(): returned = lax.all_to_all(returned, 'zh', 0, 0, tiled=True)]
    all_to_all x1, blocking collectives: 34.1 us -> 21.8 us  [shards(): terms = lax.all_to_all(terms, 'zl', 0, 0, tiled=True)]
    all_to_all x1 -> x2, blocking collectives: 4.44 us -> 16.6 us  [copies_to_all(): lax.all_to_all(jnp.broadcast_to(a[None], (count,) + a.shape), axis, 0, 0,...]
    all_to_all x7 -> x6, waiting for transfers between devices: 52.5 us -> 44.5 us  [copies_to_all(): lax.all_to_all(jnp.broadcast_to(a[None], (count,) + a.shape), axis, 0, 0,...]
    unnamed x86 -> x64, local copies, waits for them, and re-layouts: 13 us -> 6.32 us
    all_to_all x7 -> x6, starting transfers between devices: 29.5 us -> 25.1 us  [copies_to_all(): lax.all_to_all(jnp.broadcast_to(a[None], (count,) + a.shape), axis, 0, 0,...]
    ppermute x6 -> x7, starting transfers between devices: 24.9 us -> 26.8 us  [swap(): return lax.ppermute(a, axis, [(i, i ^ 1) for i in range(count)])]
    ppermute x6 -> x7, waiting for transfers between devices: 21 us -> 22.2 us  [swap(): return lax.ppermute(a, axis, [(i, i ^ 1) for i in range(count)])]
  transfers between devices with their start and end apart: 17 -> 16, of which waited for: 10 -> 9; matrix products, arithmetic and copies ran while one was open for 3% -> 2% of each run, Pallas kernels for 3% -> 3%
where the time goes in v8:
time: 351 us; the launch traced here: 350 us
  blocking collectives  162 us (46%)
  waiting for transfers between devices  81.8 us (23%)
  starting transfers between devices  57.5 us (16%)
  Pallas kernels  16.5 us (5%)
  between operations  14.4 us (4%)
  local copies, waits for them, and re-layouts  13.1 us (4%)
  other arithmetic  4.2 us (1%)
    all_to_all x6, waiting for transfers between devices, copies_to_all(): lax.all_to_all(jnp.broadcast_to(a[None], (count,) + a.shape), axis, 0, 0,...  44.5 us
    all_to_all x1, blocking collectives, shards(): returned = lax.all_to_all(returned, 'zh', 0, 0, tiled=True)  41.1 us
    ppermute x7, starting transfers between devices, swap(): return lax.ppermute(a, axis, [(i, i ^ 1) for i in range(count)])  26.8 us
    all_to_all x6, starting transfers between devices, copies_to_all(): lax.all_to_all(jnp.broadcast_to(a[None], (count,) + a.shape), axis, 0, 0,...  25.1 us
    all_to_all x1, blocking collectives, shards(): squares = lax.all_to_all(squares, BLK, 0, 0, tiled=True)  24.8 us
    ppermute x7, waiting for transfers between devices, swap(): return lax.ppermute(a, axis, [(i, i ^ 1) for i in range(count)])  22.2 us
    all_to_all x1, blocking collectives, shards(): queries = lax.all_to_all(query, 'zh', 0, 0, tiled=True)  22.1 us
    all_to_all x1, blocking collectives, shards(): terms = lax.all_to_all(terms, 'zl', 0, 0, tiled=True)  21.8 us
  transfers between devices with their start and end apart: 16, of which 9 were waited for; matrix products, arithmetic and copies ran while one was open for 2% of the time, Pallas kernels for 3%

profile of v8, /device:TPU:32, one launch (start us, length us, event | category | flops | bytes accessed | tf_op | source)
XLA Modules:
  0.0 349.5 jit_solution(1469634968438536577)
XLA Ops:
  11.7 4.6 %all-to-all-start = ((bf16[4,256,512]{2,1,0:T(8,128)(2,1)}), bf16[4,256,512]{2,1,0:T(8,128)(2,1)S(1)}, u32[]{:S(2)}, u32[]{:S(2)}) async-start(bf16[4,256,512]{2,1,0:T(8,128)(2,1)} %broadcast_in_dim.33), calls=%async_computation | async-start | bytes 2097152 | tf_op jit(solution)/shard_map/all_to_all | solution.py:37
  16.3 14.8 %collective-permute-start = (bf16[256,512]{1,0:T(8,128)(2,1)S(1)}, bf16[256,512]{1,0:T(8,128)(2,1)S(1)}, u32[]{:S(2)}, u32[]{:S(2)}) collective-permute-start(bf16[256,512]{1,0:T(8,128)(2,1)S(1)} %join_weights.1), channel_id=1, source_target_pairs={{0,64},{64,0},{1,65},{65,1},{2,66},{66,2},{3,67},{67,3},{4,68},{68... | collective-permute-start | bytes 786440 | tf_op jit(solution)/shard_map/ppermute | solution.py:50
  34.3 19.9 %collective-permute-done = bf16[256,512]{1,0:T(8,128)(2,1)S(1)} collective-permute-done((bf16[256,512]{1,0:T(8,128)(2,1)S(1)}, bf16[256,512]{1,0:T(8,128)(2,1)S(1)}, u32[]{:S(2)}, u32[]{:S(2)}) %collective-permute-start) | collective-permute-done | bytes 262176 | tf_op jit(solution)/shard_map/ppermute | solution.py:50
  55.3 4.5 %all-to-all-start.1 = ((bf16[4,256,512]{2,1,0:T(8,128)(2,1)}), bf16[4,256,512]{2,1,0:T(8,128)(2,1)S(1)}, u32[]{:S(2)}, u32[]{:S(2)}) async-start(bf16[4,256,512]{2,1,0:T(8,128)(2,1)} %broadcast_in_dim.36), calls=%async_computation.1 | async-start | bytes 2097152 | tf_op jit(solution)/shard_map/all_to_all | solution.py:37
  59.9 2.0 fusion.4
  61.9 12.1 %all-to-all-done.1.refs_2_ = bf16[4,256,512]{2,1,0:T(8,128)(2,1)S(1)} async-done(((bf16[4,256,512]{2,1,0:T(8,128)(2,1)}), bf16[4,256,512]{2,1,0:T(8,128)(2,1)S(1)}, u32[]{:S(2)}, u32[]{:S(2)}) %all-to-all-start.1) | async-done | bytes 1048608 | tf_op jit(solution)/shard_map/all_to_all | solution.py:37
  74.0 1.9 collective-permute-start.1
  75.9 2.4 collective-permute-start.2
  78.5 2.1 collective-permute-done.2.refs_3_
  82.1 24.8 %all_to_all.75.s_ref = f32[32,8,128]{2,1,0:T(8,128)S(1)} all-to-all(f32[32,8,128]{2,1,0:T(8,128)S(1)} %get-tuple-element.46), channel_id=1, replica_groups=mesh['y'=4,'zh'=2,'core'=2,'zl'=8,'x'=4] {'zl','x'}, dimensions={0} | all-to-all | bytes 262144 | tf_op jit(solution)/shard_map/all_to_all | solution.py:565
  107.2 22.1 %all_to_all.76 = bf16[2,128,128]{2,1,0:T(8,128)(2,1)S(1)} all-to-all(bf16[2,128,128]{2,1,0:T(8,128)(2,1)S(1)} %get-tuple-element.50.own_ref), channel_id=1, replica_groups=mesh['y'=4,'zh'=2,'core'=2,'zl'=8,'x'=4] {'zh'}, dimensions={0} | all-to-all | bytes 131072 | tf_op jit(solution)/shard_map/all_to_all | solution.py:572
  130.1 3.4 all-to-all-start.4
  133.5 1.9 collective-permute-start.4
  135.4 1.9 collective-permute-start.3
  137.4 1.9 blend.1
  141.1 3.5 all-to-all-start.5
  146.3 3.4 attend.1
  149.7 41.1 %all_to_all.77 = bf16[2,176,128]{2,1,0:T(8,128)(2,1)S(1)} all-to-all(bf16[2,176,128]{2,1,0:T(8,128)(2,1)S(1)} %get-tuple-element.64), channel_id=1, replica_groups=mesh['y'=4,'zh'=2,'core'=2,'zl'=8,'x'=4] {'zh'}, dimensions={0} | all-to-all | bytes 180224 | tf_op jit(solution)/shard_map/all_to_all | solution.py:593
  190.8 12.1 %all_to_all.78 = bf16[4,2,176,128]{3,2,1,0:T(8,128)(2,1)S(1)} all-to-all(bf16[4,2,176,128]{3,2,1,0:T(8,128)(2,1)S(1)} %broadcast_in_dim.41), channel_id=1, replica_groups=mesh['y'=4,'zh'=2,'core'=2,'zl'=8,'x'=4] {'y'}, dimensions={0} | all-to-all | bytes 720896 | tf_op jit(solution)/shard_map/all_to_all | solution.py:37
  203.1 4.4 %all_to_all.79 = bf16[2,4,2,176,128]{4,3,2,1,0:T(8,128)(2,1)S(1)} all-to-all(bf16[2,4,2,176,128]{4,3,2,1,0:T(8,128)(2,1)S(1)} %broadcast_in_dim.42), channel_id=1, replica_groups=mesh['y'=4,'zh'=2,'core'=2,'zl'=8,'x'=4] {'core'}, dimensions={0} | all-to-all | bytes 1441792 | tf_op jit(solution)/shard_map/all_to_all | solution.py:37
  208.8 18.1 %all_to_all.80 = bf16[4,8,128,128]{3,2,1,0:T(8,128)(2,1)S(1)} all-to-all(bf16[4,8,128,128]{3,2,1,0:T(8,128)(2,1)S(1)} %bitcast.14), channel_id=1, replica_groups=mesh['y'=4,'zh'=2,'core'=2,'zl'=8,'x'=4] {'x'}, dimensions={0} | all-to-all | bytes 2097152 | tf_op jit(solution)/shard_map/all_to_all | solution.py:600
  227.1 21.8 %all_to_all.81 = bf16[8,128,128]{2,1,0:T(8,128)(2,1)S(1)} all-to-all(bf16[8,128,128]{2,1,0:T(8,128)(2,1)S(1)} %reduce_sum.54), channel_id=1, replica_groups=mesh['y'=4,'zh'=2,'core'=2,'zl'=8,'x'=4] {'zl'}, dimensions={0} | all-to-all | bytes 524288 | tf_op jit(solution)/shard_map/all_to_all | solution.py:602
  249.7 5.5 %all-to-all-start.11 = ((bf16[8,128,128]{2,1,0:T(8,128)(2,1)}), bf16[8,128,128]{2,1,0:T(8,128)(2,1)S(1)}, u32[]{:S(2)}, u32[]{:S(2)}) async-start(bf16[8,128,128]{2,1,0:T(8,128)(2,1)} %broadcast_in_dim.43), calls=%async_computation.11 | async-start | bytes 524288 | tf_op jit(solution)/shard_map/all_to_all | solution.py:37
  255.1 1.9 collective-permute-start.5
  257.1 13.9 %all-to-all-done.11 = bf16[8,128,128]{2,1,0:T(8,128)(2,1)S(1)} async-done(((bf16[8,128,128]{2,1,0:T(8,128)(2,1)}), bf16[8,128,128]{2,1,0:T(8,128)(2,1)S(1)}, u32[]{:S(2)}, u32[]{:S(2)}) %all-to-all-start.11) | async-done | bytes 262176 | tf_op jit(solution)/shard_map/all_to_all | solution.py:37
  271.0 1.9 collective-permute-start.6
  274.1 3.6 %all-to-all-start.12 = ((bf16[4,8,128,128]{3,2,1,0:T(8,128)(2,1)}), bf16[4,8,128,128]{3,2,1,0:T(8,128)(2,1)S(1)}, u32[]{:S(2)}, u32[]{:S(2)}) async-start(bf16[4,8,128,128]{3,2,1,0:T(8,128)(2,1)} %broadcast_in_dim.84), calls=%async_computation.12 | async-start | bytes 2097152 | tf_op jit(solution)/shard_map/all_to_all | solution.py:37
  277.8 16.0 %all-to-all-done.12 = bf16[4,8,128,128]{3,2,1,0:T(8,128)(2,1)S(1)} async-done(((bf16[4,8,128,128]{3,2,1,0:T(8,128)(2,1)}), bf16[4,8,128,128]{3,2,1,0:T(8,128)(2,1)S(1)}, u32[]{:S(2)}, u32[]{:S(2)}) %all-to-all-start.12) | async-done | bytes 1048608 | tf_op jit(solution)/shard_map/all_to_all | solution.py:37
  295.4 6.9 %feed_forward.1 = (bf16[128,4096]{1,0:T(8,128)(2,1)S(1)}, bf16[128,4096]{1,0:T(8,128)(2,1)S(1)}) custom-call(s32[16]{0:T(128)S(1)} %copy-done.18, bf16[32,128,128]{2,1,0:T(8,128)(2,1)S(1)} %bitcast.15, bf16[128,4096]{1,0:T(8,128)(2,1)S(1)} %copy-done.5, f32[1,4096]{1,0:T(1,128)S(1)} %bitcast.22, bf16[4,1040,256]{2,1,0:T(8,128)(2,1)} %bitcast.6.refs_0_, ...), custom_call_target="tpu_custom_call" | custom-call | tf_op jit(solution)/shard_map/feed_forward/pallas_call | solution.py:96
  302.3 17.7 %all_to_all.82 = bf16[4,32,4096]{2,1,0:T(8,128)(2,1)S(1)} all-to-all(bf16[4,32,4096]{2,1,0:T(8,128)(2,1)S(1)} %bitcast.20), channel_id=1, replica_groups=mesh['y'=4,'zh'=2,'core'=2,'zl'=8,'x'=4] {'x'}, dimensions={0} | all-to-all | bytes 2097152 | tf_op jit(solution)/shard_map/all_to_all | solution.py:613
  321.0 5.5 %all-to-all-start.14 = ((bf16[8,4,4096]{2,1,0:T(4,128)(2,1)}), bf16[8,4,4096]{2,1,0:T(4,128)(2,1)S(1)}, u32[]{:S(2)}, u32[]{:S(2)}) async-start(bf16[8,4,4096]{2,1,0:T(4,128)(2,1)} %reshape.56), calls=%async_computation.14 | async-start | bytes 524288 | tf_op jit(solution)/shard_map/all_to_all | solution.py:615
  326.5 15.0 %all-to-all-done.14 = bf16[8,4,4096]{2,1,0:T(4,128)(2,1)S(1)} async-done(((bf16[8,4,4096]{2,1,0:T(4,128)(2,1)}), bf16[8,4,4096]{2,1,0:T(4,128)(2,1)S(1)}, u32[]{:S(2)}, u32[]{:S(2)}) %all-to-all-start.14) | async-done | bytes 262176 | tf_op jit(solution)/shard_map/all_to_all | solution.py:615
  (104 shorter events, 22.4 us)
Async XLA Ops:
  11.7 19.5 %copy-start.30 = (s32[8,2]{0,1:T(2,128)S(1)}, s32[8,2]{0,1:T(2,128)}, u32[]{:S(2)}) copy-start(s32[8,2]{0,1:T(2,128)} %param.33) | copy-start | bytes 196
  11.7 19.7 %copy-start.15 = (s32[16,96]{1,0:T(8,128)S(1)}, s32[16,96]{1,0:T(8,128)}, u32[]{:S(2)}) copy-start(s32[16,96]{1,0:T(8,128)} %i_ref.1) | copy-start | bytes 18436
  11.7 19.8 %copy-start.27 = (s32[16]{0:T(128)S(1)}, s32[16]{0:T(128)}, u32[]{:S(2)}) copy-start(s32[16]{0:T(128)} %o_ref.2) | copy-start | bytes 196
  11.7 19.8 %copy-start.28 = (s32[8]{0:T(128)S(1)}, s32[8]{0:T(128)}, u32[]{:S(2)}) copy-start(s32[8]{0:T(128)} %len_ref.1) | copy-start | bytes 100
  11.7 42.5 %all-to-all-start = ((bf16[4,256,512]{2,1,0:T(8,128)(2,1)}), bf16[4,256,512]{2,1,0:T(8,128)(2,1)S(1)}, u32[]{:S(2)}, u32[]{:S(2)}) async-start(bf16[4,256,512]{2,1,0:T(8,128)(2,1)} %broadcast_in_dim.33), calls=%async_computation | async-start | bytes 2097152 | tf_op jit(solution)/shard_map/all_to_all | solution.py:37
  16.3 37.9 %collective-permute-start = (bf16[256,512]{1,0:T(8,128)(2,1)S(1)}, bf16[256,512]{1,0:T(8,128)(2,1)S(1)}, u32[]{:S(2)}, u32[]{:S(2)}) collective-permute-start(bf16[256,512]{1,0:T(8,128)(2,1)S(1)} %join_weights.1), channel_id=1, source_target_pairs={{0,64},{64,0},{1,65},{65,1},{2,66},{66,2},{3,67},{67,3},{4,68},{68... | collective-permute-start | bytes 786440 | tf_op jit(solution)/shard_map/ppermute | solution.py:50
  33.9 21.5 %copy-start.25 = (s32[5]{0:T(128)}, s32[5]{0:T(128)S(1)}, u32[]{:S(2)}) copy-start(s32[5]{0:T(128)S(1)} %get-tuple-element.40.c_ref) | copy-start | bytes 64
  33.9 46.7 %copy-start.17 = (s32[16]{0:T(128)}, s32[16]{0:T(128)S(1)}, u32[]{:S(2)}) copy-start(s32[16]{0:T(128)S(1)} %get-tuple-element.38.c_ref) | copy-start | bytes 196
  55.3 18.6 %all-to-all-start.1 = ((bf16[4,256,512]{2,1,0:T(8,128)(2,1)}), bf16[4,256,512]{2,1,0:T(8,128)(2,1)S(1)}, u32[]{:S(2)}, u32[]{:S(2)}) async-start(bf16[4,256,512]{2,1,0:T(8,128)(2,1)} %broadcast_in_dim.36), calls=%async_computation.1 | async-start | bytes 2097152 | tf_op jit(solution)/shard_map/all_to_all | solution.py:37
  59.9 20.7 %copy-start.4 = (bf16[128,4096]{1,0:T(8,128)(2,1)S(1)}, bf16[128,4096]{1,0:T(8,128)(2,1)}, u32[]{:S(2)}) copy-start(bf16[128,4096]{1,0:T(8,128)(2,1)} %x_ref.3) | copy-start | bytes 3145732
  59.9 69.4 %all-gather.5.cloned.1.call-start = ((), (), s32[]{:S(2)}) async-start(), calls=%async_computation.15 | async-start | bytes 2662400 | tf_op jit(solution)/shard_map/all_gather | solution.py:561
  74.0 4.6 %collective-permute-start.1 = (bf16[4,256,512]{2,1,0:T(8,128)(2,1)S(1)}, bf16[4,256,512]{2,1,0:T(8,128)(2,1)S(1)}, u32[]{:S(2)}, u32[]{:S(2)}) collective-permute-start(bf16[4,256,512]{2,1,0:T(8,128)(2,1)S(1)} %all-to-all-done.refs_0_), channel_id=1, source_target_pairs={{0,32},{32,0},{1,33},{33,1},{2,34},{34,2},{3,35},{35,3},{4,36},{36... | collective-permute-start | bytes 3145736 | tf_op jit(solution)/shard_map/ppermute | solution.py:50
  75.9 4.7 %collective-permute-start.2 = (bf16[4,256,512]{2,1,0:T(8,128)(2,1)S(1)}, bf16[4,256,512]{2,1,0:T(8,128)(2,1)S(1)}, u32[]{:S(2)}, u32[]{:S(2)}) collective-permute-start(bf16[4,256,512]{2,1,0:T(8,128)(2,1)S(1)} %all-to-all-done.1.refs_2_), channel_id=1, source_target_pairs={{0,32},{32,0},{1,33},{33,1},{2,34},{34,2},{3,35},{35,3},{4,36},{36... | collective-permute-start | bytes 3145736 | tf_op jit(solution)/shard_map/ppermute | solution.py:50
  80.6 26.3 %copy-start.19 = (f32[128]{0:T(128)S(1)}, f32[128]{0:T(128)}, u32[]{:S(2)}) copy-start(f32[128]{0:T(128)} %param.23) | copy-start | bytes 1540
  80.6 26.3 %copy-start.20 = (f32[128]{0:T(128)S(1)}, f32[128]{0:T(128)}, u32[]{:S(2)}) copy-start(f32[128]{0:T(128)} %param.24) | copy-start | bytes 1540
  82.0 55.3 %copy-start.7 = (bf16[1,1024,128]{2,1,0:T(8,128)(2,1)S(1)}, bf16[1,1024,128]{2,1,0:T(8,128)(2,1)}, u32[]{:S(2)}) copy-start(bf16[1,1024,128]{2,1,0:T(8,128)(2,1)} %k_ref.3) | copy-start | bytes 786436
  82.0 55.3 %copy-start.8 = (bf16[1,1024,128]{2,1,0:T(8,128)(2,1)S(1)}, bf16[1,1024,128]{2,1,0:T(8,128)(2,1)}, u32[]{:S(2)}) copy-start(bf16[1,1024,128]{2,1,0:T(8,128)(2,1)} %v_ref.3) | copy-start | bytes 786436
  130.1 10.1 %all-to-all-start.4 = ((bf16[4,2,128,128]{3,2,1,0:T(8,128)(2,1)}), bf16[4,2,128,128]{3,2,1,0:T(8,128)(2,1)S(1)}, u32[]{:S(2)}, u32[]{:S(2)}) async-start(bf16[4,2,128,128]{3,2,1,0:T(8,128)(2,1)} %broadcast_in_dim.39), calls=%async_computation.4 | async-start | bytes 524288 | tf_op jit(solution)/shard_map/all_to_all | solution.py:37
  133.5 75.3 %collective-permute-start.4 = (bf16[1040,256]{1,0:T(8,128)(2,1)}, bf16[1040,256]{1,0:T(8,128)(2,1)}, u32[]{:S(2)}, u32[]{:S(2)}) collective-permute-start(bf16[1040,256]{1,0:T(8,128)(2,1)} %fusion.4), channel_id=1, source_target_pairs={{0,64},{64,0},{1,65},{65,1},{2,66},{66,2},{3,67},{67,3},{4,68},{68... | collective-permute-start | bytes 1597448 | tf_op jit(solution)/shard_map/ppermute | solution.py:50
  135.4 9.2 %collective-permute-start.3 = (bf16[64,128]{1,0:T(8,128)(2,1)S(1)}, bf16[64,128]{1,0:T(8,128)(2,1)S(1)}, u32[]{:S(2)}, u32[]{:S(2)}) collective-permute-start(bf16[64,128]{1,0:T(8,128)(2,1)S(1)} %get-tuple-element.59.nm_ref), channel_id=1, source_target_pairs={{0,32},{32,0},{1,33},{33,1},{2,34},{34,2},{3,35},{35,3},{4,36},{36... | collective-permute-start | bytes 49160 | tf_op jit(solution)/shard_map/ppermute | solution.py:50
  139.3 7.0 %copy-start.26 = (s32[5]{0:T(128)S(1)}, s32[5]{0:T(128)}, u32[]{:S(2)}) copy-start(s32[5]{0:T(128)} %copy-done.25) | copy-start | bytes 64
  141.1 5.2 %all-to-all-start.5 = ((bf16[2,4,2,128,128]{4,3,2,1,0:T(8,128)(2,1)}), bf16[2,4,2,128,128]{4,3,2,1,0:T(8,128)(2,1)S(1)}, u32[]{:S(2)}, u32[]{:S(2)}) async-start(bf16[2,4,2,128,128]{4,3,2,1,0:T(8,128)(2,1)} %broadcast_in_dim.40), calls=%async_computation.5 | async-start | bytes 1048576 | tf_op jit(solution)/shard_map/all_to_all | solution.py:37
  144.6 126.4 %all-gather.7.cloned.1.call-start = ((), (), s32[]{:S(2)}) async-start(), calls=%async_computation.16 | async-start | bytes 2662400 | tf_op jit(solution)/shard_map/all_gather | solution.py:599
  249.7 21.3 %all-to-all-start.11 = ((bf16[8,128,128]{2,1,0:T(8,128)(2,1)}), bf16[8,128,128]{2,1,0:T(8,128)(2,1)S(1)}, u32[]{:S(2)}, u32[]{:S(2)}) async-start(bf16[8,128,128]{2,1,0:T(8,128)(2,1)} %broadcast_in_dim.43), calls=%async_computation.11 | async-start | bytes 524288 | tf_op jit(solution)/shard_map/all_to_all | solution.py:37
  255.1 22.6 %collective-permute-start.5 = (bf16[4,1040,256]{2,1,0:T(8,128)(2,1)}, bf16[4,1040,256]{2,1,0:T(8,128)(2,1)}, u32[]{:S(2)}, u32[]{:S(2)}) collective-permute-start(bf16[4,1040,256]{2,1,0:T(8,128)(2,1)} %bitcast.6.refs_0_), channel_id=1, source_target_pairs={{0,32},{32,0},{1,33},{33,1},{2,34},{34,2},{3,35},{35,3},{4,36},{36... | collective-permute-start | bytes 6389768 | tf_op jit(solution)/shard_map/ppermute | solution.py:50
  271.0 22.8 %collective-permute-start.6 = (bf16[4,1040,256]{2,1,0:T(8,128)(2,1)}, bf16[4,1040,256]{2,1,0:T(8,128)(2,1)}, u32[]{:S(2)}, u32[]{:S(2)}) collective-permute-start(bf16[4,1040,256]{2,1,0:T(8,128)(2,1)} %bitcast.17), channel_id=1, source_target_pairs={{0,32},{32,0},{1,33},{33,1},{2,34},{34,2},{3,35},{35,3},{4,36},{36... | collective-permute-start | bytes 6389768 | tf_op jit(solution)/shard_map/ppermute | solution.py:50
  274.1 19.7 %copy-start.5 = (bf16[128,4096]{1,0:T(8,128)(2,1)S(1)}, bf16[128,4096]{1,0:T(8,128)(2,1)}, u32[]{:S(2)}) copy-start(bf16[128,4096]{1,0:T(8,128)(2,1)} %x_ref.3) | copy-start | bytes 3145732
  274.1 19.7 %copy-start.16 = (f32[4096]{0:T(1024)S(1)}, f32[4096]{0:T(1024)}, u32[]{:S(2)}) copy-start(f32[4096]{0:T(1024)} %param.25) | copy-start | bytes 49156
  274.1 19.7 %copy-start.18 = (s32[16]{0:T(128)S(1)}, s32[16]{0:T(128)}, u32[]{:S(2)}) copy-start(s32[16]{0:T(128)} %copy-done.17) | copy-start | bytes 196
  274.1 19.7 %all-to-all-start.12 = ((bf16[4,8,128,128]{3,2,1,0:T(8,128)(2,1)}), bf16[4,8,128,128]{3,2,1,0:T(8,128)(2,1)S(1)}, u32[]{:S(2)}, u32[]{:S(2)}) async-start(bf16[4,8,128,128]{3,2,1,0:T(8,128)(2,1)} %broadcast_in_dim.84), calls=%async_computation.12 | async-start | bytes 2097152 | tf_op jit(solution)/shard_map/all_to_all | solution.py:37
  320.0 22.0 %copy-start.29 = (f32[4096]{0:T(1024)S(1)}, f32[4096]{0:T(1024)}, u32[]{:S(2)}) copy-start(f32[4096]{0:T(1024)} %param.29) | copy-start | bytes 49156
  321.0 20.5 %all-to-all-start.14 = ((bf16[8,4,4096]{2,1,0:T(4,128)(2,1)}), bf16[8,4,4096]{2,1,0:T(4,128)(2,1)S(1)}, u32[]{:S(2)}, u32[]{:S(2)}) async-start(bf16[8,4,4096]{2,1,0:T(4,128)(2,1)} %reshape.56), calls=%async_computation.14 | async-start | bytes 524288 | tf_op jit(solution)/shard_map/all_to_all | solution.py:615
  (15 other events, 45.7 us)
Sparse Core Ops, SparseCore 0:
  74.1 37.8 all-gather.4
  208.9 34.0 all-gather.6

commit v9 on v8

--- a/solution.py
+++ b/solution.py
@@ -456,15 +456,16 @@
 def feed_forward(columns, summed, hidden, gain, parcels, units):
     blocks, rows, part = summed.shape
     model = blocks * part
-    count, _, depth = parcels[0].shape
+    count, _, depth = parcels[0][0].shape
     parts = len(parcels)
     split = depth // part
     per = rows // (NZL * NX)
     contract_last = (((1,), (1,)), ((), ()))
 
     def kernel(c_ref, s_ref, x_ref, g_ref, *refs):
-        parcel_refs = refs[:parts]
-        out_ref, mixed_ref, acc_ref = refs[parts:]
+        refs = list(refs)
+        held = [[refs.pop(0) for _ in pieces] for pieces in parcels]
+        out_ref, mixed_ref, acc_ref = refs
         squares = jnp.zeros((rows, part), f32)
         for b in range(blocks):
             block = s_ref[b].astype(f32)
@@ -477,13 +478,18 @@
                 x_ref[:, cols].astype(f32) + summed.astype(f32) * norm * g_ref[:, cols]
             ).astype(bf16)
             mixed_ref[:, cols] = mixed
-            product = lax.dot_general(
-                parcel_refs[m // count][m % count, : 2 * units],
-                mixed,
-                contract_last,
-                preferred_element_type=f32,
-            )
-            acc_ref[...] = product if m == 0 else acc_ref[...] + product
+            low = 0
+            for ref in held[m // count]:
+                high = min(low + ref.shape[1], 2 * units)
+                product = lax.dot_general(
+                    ref[m % count, : high - low],
+                    mixed,
+                    contract_last,
+                    preferred_element_type=f32,
+                )
+                span = slice(low, high)
+                acc_ref[span, :] = product if m == 0 else acc_ref[span, :] + product
+                low = high
         to = lax.broadcasted_iota(jnp.int32, (rows, rows), 0)
         at = lax.broadcasted_iota(jnp.int32, (rows, rows), 1)
         source = (to // per) % NZL * (NX * per) + to // (NZL * per) * per + to % per
@@ -495,7 +501,9 @@
         ).astype(bf16)
         for m in range(parts * count):
             cols = pl.ds(pl.multiple_of(c_ref[m] * depth, depth), depth)
-            down = parcel_refs[m // count][m % count, 2 * units : 3 * units]
+            pieces = held[m // count]
+            at_row = 2 * units - sum(ref.shape[1] for ref in pieces[:-1])
+            down = pieces[-1][m % count, at_row : at_row + units]
             out_ref[:, cols] = jnp.dot(active, down, preferred_element_type=f32).astype(bf16)
 
     return call(
@@ -506,7 +514,7 @@
         summed,
         hidden,
         gain,
-        *parcels,
+        *[piece for pieces in parcels for piece in pieces],
         scratch=[pltpu.VMEM((2 * units, rows), f32)],
     )
 
@@ -564,13 +572,14 @@
     raw, squares = project(columns, hidden_states, weights, width, blocks)
     squares = lax.all_to_all(squares, BLK, 0, 0, tiled=True)
     squares, parcel = lax.optimization_barrier((squares, parcel))
-    parcel_other = swap(parcel, "zh", NZH)
+    early, late = jnp.split(parcel, 2)
     query, key, value, new_mine = finish_rows(
         raw, squares, query_gain[None], key_gain[None], cosine, sine, model
     )
 
     queries = lax.all_to_all(query, "zh", 0, 0, tiled=True)
-    queries, parcel_near = lax.optimization_barrier((queries, parcel_near))
+    queries, parcel_near, early = lax.optimization_barrier((queries, parcel_near, early))
+    early = swap(early, "zh", NZH)
     queries = copies_to_all(queries, "y", NY)
     queries = copies_to_all(queries, "core", NCORE).reshape(N_SEQ, ROW_DEV, width)
     new_other = swap(new_mine, "core", NCORE)
@@ -590,23 +599,27 @@
         new_key_at,
     )
 
+    returned, early = lax.optimization_barrier((returned, early))
+    early = lax.all_gather(early, "y")
     returned = lax.all_to_all(returned, "zh", 0, 0, tiled=True)
+    returned, late = lax.optimization_barrier((returned, late))
+    late = swap(late, "zh", NZH)
     returned = copies_to_all(returned, "y", NY)
     returned = copies_to_all(returned, "core", NCORE).reshape(N_SEQ, -1, width)
 
     terms = merge_and_project(merge_control, kept, new_part, returned, weights)
-    terms, parcel_other = lax.optimization_barrier((terms, parcel_other))
-    parcel_far = lax.all_gather(parcel_other, "y")
     terms = lax.all_to_all(terms.reshape(NX, NZL, ROW_DEV, width), "x", 0, 0, tiled=True)
+    terms, late = lax.optimization_barrier((terms, late))
+    late = lax.all_gather(late, "y")
     terms = jnp.sum(terms.astype(f32), axis=0).astype(bf16)
     terms = lax.all_to_all(terms, "zl", 0, 0, tiled=True)
     summed = jnp.sum(terms.astype(f32), axis=0).astype(bf16)
     summed = copies_to_all(summed, "zl", NZL)
-    summed, parcel_far = lax.optimization_barrier((summed, parcel_far))
+    summed, early, late = lax.optimization_barrier((summed, early, late))
     summed = copies_to_all(summed, "x", NX).reshape(blocks, ROW_DEV, model // blocks)
 
-    parcels = [parcel_near, swap(parcel_near, "core", NCORE)]
-    parcels += [parcel_far, swap(parcel_far, "core", NCORE)]
+    parcels = [(parcel_near,), (swap(parcel_near, "core", NCORE),)]
+    parcels += [(early, late), (swap(early, "core", NCORE), swap(late, "core", NCORE))]
     terms, mixed = feed_forward(
         columns, summed, hidden_states, attention_gain[None], parcels, hidden_units
     )

time: 351 us -> 377 us (1.074)
  blocking collectives: 162 us -> 83.9 us
  waiting for transfers between devices: 81.8 us -> 136 us
  starting transfers between devices: 57.5 us -> 87 us
  local copies, waits for them, and re-layouts: 13.1 us -> 30 us
    all_to_all x3 -> x0, blocking collectives: 62 us -> none  [the longest x1 22.1 us: shards(): queries = lax.all_to_all(query, 'zh', 0, 0, tiled=True)]
    ppermute x7 -> x9, waiting for transfers between devices: 22.2 us -> 49 us  [swap(): return lax.ppermute(a, axis, [(i, i ^ 1) for i in range(count)])]
    all_to_all x0 -> x3, waiting for transfers between devices: none -> 25.8 us  [the longest x1 13.6 us: shards(): terms = lax.all_to_all(terms, 'zl', 0, 0, tiled=True)]
    all_to_all x0 -> x3, starting transfers between devices: none -> 18 us  [the longest x1 8.55 us: shards(): queries = lax.all_to_all(query, 'zh', 0, 0, tiled=True)]
    all_to_all x1, blocking collectives: 41.1 us -> 26 us  [shards(): returned = lax.all_to_all(returned, 'zh', 0, 0, tiled=True)]
    unnamed x64 -> x104, local copies, waits for them, and re-layouts: 6.32 us -> 19.5 us
    all_gather x1 -> x2, waiting for transfers between devices: 0.01 us -> 9.81 us  [the longest x1 9.81 us: shards(): late = lax.all_gather(late, 'y')]
    ppermute x7 -> x9, starting transfers between devices: 26.8 us -> 35.8 us  [swap(): return lax.ppermute(a, axis, [(i, i ^ 1) for i in range(count)])]
  transfers between devices with their start and end apart: 16 -> 22, of which waited for: 9 -> 14; matrix products, arithmetic and copies ran while one was open for 2% -> 3% of each run, Pallas kernels for 3% -> 3%
where the time goes in v9:
time: 377 us; the launch traced here: 375 us
  waiting for transfers between devices  136 us (36%)
  starting transfers between devices  87 us (23%)
  blocking collectives  83.9 us (22%)
  local copies, waits for them, and re-layouts  30 us (8%)
  Pallas kernels  18.5 us (5%)
  between operations  14.1 us (4%)
  other arithmetic  4.63 us (1%)
    ppermute x9, waiting for transfers between devices, swap(): return lax.ppermute(a, axis, [(i, i ^ 1) for i in range(count)])  49 us
    all_to_all x6, waiting for transfers between devices, copies_to_all(): lax.all_to_all(jnp.broadcast_to(a[None], (count,) + a.shape), axis, 0, 0,...  36.8 us
    ppermute x9, starting transfers between devices, swap(): return lax.ppermute(a, axis, [(i, i ^ 1) for i in range(count)])  35.8 us
    all_to_all x6, starting transfers between devices, copies_to_all(): lax.all_to_all(jnp.broadcast_to(a[None], (count,) + a.shape), axis, 0, 0,...  27.6 us
    all_to_all x1, blocking collectives, shards(): returned = lax.all_to_all(returned, 'zh', 0, 0, tiled=True)  26 us
    all_to_all x1, blocking collectives, shards(): squares = lax.all_to_all(squares, BLK, 0, 0, tiled=True)  24.7 us
    unnamed x104, local copies, waits for them, and re-layouts  19.5 us
    all_to_all x1, blocking collectives, shards(): lax.all_to_all(terms.reshape(NX, NZL * rows, model), 'x', 0, 0, tiled=True)  16.8 us
  transfers between devices with their start and end apart: 22, of which 14 were waited for; matrix products, arithmetic and copies ran while one was open for 3% of the time, Pallas kernels for 3%

profile of v9, /device:TPU:32, one launch (start us, length us, event | category | flops | bytes accessed | tf_op | source)
XLA Modules:
  0.0 374.6 jit_solution(13804685067759612064)
XLA Ops:
  11.7 4.6 %all-to-all-start = ((bf16[4,256,512]{2,1,0:T(8,128)(2,1)}), bf16[4,256,512]{2,1,0:T(8,128)(2,1)S(1)}, u32[]{:S(2)}, u32[]{:S(2)}) async-start(bf16[4,256,512]{2,1,0:T(8,128)(2,1)} %broadcast_in_dim.33), calls=%async_computation | async-start | bytes 2097152 | tf_op jit(solution)/shard_map/all_to_all | solution.py:37
  16.3 14.8 %collective-permute-start = (bf16[256,512]{1,0:T(8,128)(2,1)S(1)}, bf16[256,512]{1,0:T(8,128)(2,1)S(1)}, u32[]{:S(2)}, u32[]{:S(2)}) collective-permute-start(bf16[256,512]{1,0:T(8,128)(2,1)S(1)} %join_weights.1), channel_id=1, source_target_pairs={{0,64},{64,0},{1,65},{65,1},{2,66},{66,2},{3,67},{67,3},{4,68},{68... | collective-permute-start | bytes 786440 | tf_op jit(solution)/shard_map/ppermute | solution.py:50
  36.1 18.1 %collective-permute-done = bf16[256,512]{1,0:T(8,128)(2,1)S(1)} collective-permute-done((bf16[256,512]{1,0:T(8,128)(2,1)S(1)}, bf16[256,512]{1,0:T(8,128)(2,1)S(1)}, u32[]{:S(2)}, u32[]{:S(2)}) %collective-permute-start) | collective-permute-done | bytes 262176 | tf_op jit(solution)/shard_map/ppermute | solution.py:50
  55.3 4.6 %all-to-all-start.1 = ((bf16[4,256,512]{2,1,0:T(8,128)(2,1)}), bf16[4,256,512]{2,1,0:T(8,128)(2,1)S(1)}, u32[]{:S(2)}, u32[]{:S(2)}) async-start(bf16[4,256,512]{2,1,0:T(8,128)(2,1)} %broadcast_in_dim.36), calls=%async_computation.1 | async-start | bytes 2097152 | tf_op jit(solution)/shard_map/all_to_all | solution.py:37
  60.8 13.2 %all-to-all-done.1.refs_2_ = bf16[4,256,512]{2,1,0:T(8,128)(2,1)S(1)} async-done(((bf16[4,256,512]{2,1,0:T(8,128)(2,1)}), bf16[4,256,512]{2,1,0:T(8,128)(2,1)S(1)}, u32[]{:S(2)}, u32[]{:S(2)}) %all-to-all-start.1) | async-done | bytes 1048608 | tf_op jit(solution)/shard_map/all_to_all | solution.py:37
  76.0 2.4 collective-permute-start.2
  78.7 2.1 collective-permute-done.2.refs_3_
  83.7 24.7 %all_to_all.75.s_ref = f32[32,8,128]{2,1,0:T(8,128)S(1)} all-to-all(f32[32,8,128]{2,1,0:T(8,128)S(1)} %get-tuple-element.52), channel_id=1, replica_groups=mesh['y'=4,'zh'=2,'core'=2,'zl'=8,'x'=4] {'zl','x'}, dimensions={0} | all-to-all | bytes 262144 | tf_op jit(solution)/shard_map/all_to_all | solution.py:573
  111.2 8.6 %all-to-all-start.3 = ((bf16[2,128,128]{2,1,0:T(8,128)(2,1)}), bf16[2,128,128]{2,1,0:T(8,128)(2,1)}, u32[]{:S(2)}, u32[]{:S(2)}) async-start(bf16[2,128,128]{2,1,0:T(8,128)(2,1)} %get-tuple-element.56.own_ref), calls=%async_computation.3 | async-start | bytes 131072 | tf_op jit(solution)/shard_map/all_to_all | solution.py:580
  121.6 12.1 %all-to-all-done.3 = bf16[2,128,128]{2,1,0:T(8,128)(2,1)} async-done(((bf16[2,128,128]{2,1,0:T(8,128)(2,1)}), bf16[2,128,128]{2,1,0:T(8,128)(2,1)}, u32[]{:S(2)}, u32[]{:S(2)}) %all-to-all-start.3) | async-done | bytes 65568 | tf_op jit(solution)/shard_map/all_to_all | solution.py:580
  137.2 4.0 %all-to-all-start.4 = ((bf16[4,2,128,128]{3,2,1,0:T(8,128)(2,1)}), bf16[4,2,128,128]{3,2,1,0:T(8,128)(2,1)}, u32[]{:S(2)}, u32[]{:S(2)}) async-start(bf16[4,2,128,128]{3,2,1,0:T(8,128)(2,1)} %broadcast_in_dim.39), calls=%async_computation.4 | async-start | bytes 524288 | tf_op jit(solution)/shard_map/all_to_all | solution.py:37
  149.9 4.2 %all-to-all-start.5 = ((bf16[2,4,2,128,128]{4,3,2,1,0:T(8,128)(2,1)}), bf16[2,4,2,128,128]{4,3,2,1,0:T(8,128)(2,1)}, u32[]{:S(2)}, u32[]{:S(2)}) async-start(bf16[2,4,2,128,128]{4,3,2,1,0:T(8,128)(2,1)} %broadcast_in_dim.40), calls=%async_computation.5 | async-start | bytes 1048576 | tf_op jit(solution)/shard_map/all_to_all | solution.py:37
  158.9 4.0 %attend.1 = (bf16[2,176,128]{2,1,0:T(8,128)(2,1)S(1)}, f32[192,256]{1,0:T(8,128)S(1)}, f32[32,256]{1,0:T(8,128)S(1)}) custom-call(s32[5]{0:T(128)S(1)} %copy-done.41, bf16[16,128,128]{2,1,0:T(8,128)(2,1)} %bitcast.7.q_ref, bf16[1,1024,128]{2,1,0:T(8,128)(2,1)S(1)} %copy-done.8, bf16[1,1024,128]{2,1,0:T(8,128)(2,1)S(1)} %copy-done.9, ...), custom_call_target="tpu_custom_call" | custom-call | tf_op jit(solution)/shard_map/attend/pallas_call | solution.py:96
  165.4 26.0 %all_to_all.76 = bf16[2,176,128]{2,1,0:T(8,128)(2,1)S(1)} all-to-all(bf16[2,176,128]{2,1,0:T(8,128)(2,1)} %copy-done.14), channel_id=1, replica_groups=mesh['y'=4,'zh'=2,'core'=2,'zl'=8,'x'=4] {'zh'}, dimensions={0} | all-to-all | bytes 180224 | tf_op jit(solution)/shard_map/all_to_all | solution.py:604
  191.5 12.0 %all_to_all.77 = bf16[4,2,176,128]{3,2,1,0:T(8,128)(2,1)S(1)} all-to-all(bf16[4,2,176,128]{3,2,1,0:T(8,128)(2,1)S(1)} %broadcast_in_dim.41), channel_id=1, replica_groups=mesh['y'=4,'zh'=2,'core'=2,'zl'=8,'x'=4] {'y'}, dimensions={0} | all-to-all | bytes 720896 | tf_op jit(solution)/shard_map/all_to_all | solution.py:37
  203.6 4.4 %all_to_all.78 = bf16[2,4,2,176,128]{4,3,2,1,0:T(8,128)(2,1)S(1)} all-to-all(bf16[2,4,2,176,128]{4,3,2,1,0:T(8,128)(2,1)S(1)} %broadcast_in_dim.42), channel_id=1, replica_groups=mesh['y'=4,'zh'=2,'core'=2,'zl'=8,'x'=4] {'core'}, dimensions={0} | all-to-all | bytes 1441792 | tf_op jit(solution)/shard_map/all_to_all | solution.py:37
  208.0 2.2 merge_and_project.1
  210.3 3.6 all-to-all-start.9
  213.9 6.6 %collective-permute-start.5 = (bf16[520,256]{1,0:T(8,128)(2,1)S(1)}, bf16[520,256]{1,0:T(8,128)(2,1)S(1)}, u32[]{:S(2)}, u32[]{:S(2)}) collective-permute-start(bf16[520,256]{1,0:T(8,128)(2,1)S(1)} %copy-done.45), channel_id=1, source_target_pairs={{0,64},{64,0},{1,65},{65,1},{2,66},{66,2},{3,67},{67,3},{4,68},{68... | collective-permute-start | bytes 798728 | tf_op jit(solution)/shard_map/ppermute | solution.py:50
  220.6 28.0 %collective-permute-done.5 = bf16[520,256]{1,0:T(8,128)(2,1)S(1)} collective-permute-done((bf16[520,256]{1,0:T(8,128)(2,1)S(1)}, bf16[520,256]{1,0:T(8,128)(2,1)S(1)}, u32[]{:S(2)}, u32[]{:S(2)}) %collective-permute-start.5) | collective-permute-done | bytes 266272 | tf_op jit(solution)/shard_map/ppermute | solution.py:50
  249.6 5.8 %all-to-all-start.10 = ((bf16[8,128,128]{2,1,0:T(8,128)(2,1)}), bf16[8,128,128]{2,1,0:T(8,128)(2,1)S(1)}, u32[]{:S(2)}, u32[]{:S(2)}) async-start(bf16[8,128,128]{2,1,0:T(8,128)(2,1)} %reduce_sum.54), calls=%async_computation.10 | async-start | bytes 524288 | tf_op jit(solution)/shard_map/all_to_all | solution.py:615
  258.1 13.6 %all-to-all-done.10 = bf16[8,128,128]{2,1,0:T(8,128)(2,1)S(1)} async-done(((bf16[8,128,128]{2,1,0:T(8,128)(2,1)}), bf16[8,128,128]{2,1,0:T(8,128)(2,1)S(1)}, u32[]{:S(2)}, u32[]{:S(2)}) %all-to-all-start.10) | async-done | bytes 262176 | tf_op jit(solution)/shard_map/all_to_all | solution.py:615
  272.5 5.5 %all-to-all-start.11 = ((bf16[8,128,128]{2,1,0:T(8,128)(2,1)}), bf16[8,128,128]{2,1,0:T(8,128)(2,1)S(1)}, u32[]{:S(2)}, u32[]{:S(2)}) async-start(bf16[8,128,128]{2,1,0:T(8,128)(2,1)} %broadcast_in_dim.43), calls=%async_computation.11 | async-start | bytes 524288 | tf_op jit(solution)/shard_map/all_to_all | solution.py:37
  278.0 9.8 %all-gather.11.cloned.1.call-done = bf16[2080,256]{1,0:T(8,128)(2,1)} async-done(((bf16[520,256]{1,0:T(8,128)(2,1)}), bf16[2080,256]{1,0:T(8,128)(2,1)}) %all-gather.11.cloned.1.call-update) | async-done | bytes 1064976 | tf_op jit(solution)/shard_map/all_gather | solution.py:613
  287.8 6.0 %all-to-all-done.11 = bf16[8,128,128]{2,1,0:T(8,128)(2,1)S(1)} async-done(((bf16[8,128,128]{2,1,0:T(8,128)(2,1)}), bf16[8,128,128]{2,1,0:T(8,128)(2,1)S(1)}, u32[]{:S(2)}, u32[]{:S(2)}) %all-to-all-start.11) | async-done | bytes 262176 | tf_op jit(solution)/shard_map/all_to_all | solution.py:37
  295.8 2.4 collective-permute-start.8
  299.4 4.6 %all-to-all-start.12 = ((bf16[4,8,128,128]{3,2,1,0:T(8,128)(2,1)}), bf16[4,8,128,128]{3,2,1,0:T(8,128)(2,1)S(1)}, u32[]{:S(2)}, u32[]{:S(2)}) async-start(bf16[4,8,128,128]{3,2,1,0:T(8,128)(2,1)} %broadcast_in_dim.84), calls=%async_computation.12 | async-start | bytes 2097152 | tf_op jit(solution)/shard_map/all_to_all | solution.py:37
  304.1 15.3 %all-to-all-done.12 = bf16[4,8,128,128]{3,2,1,0:T(8,128)(2,1)S(1)} async-done(((bf16[4,8,128,128]{3,2,1,0:T(8,128)(2,1)}), bf16[4,8,128,128]{3,2,1,0:T(8,128)(2,1)S(1)}, u32[]{:S(2)}, u32[]{:S(2)}) %all-to-all-start.12) | async-done | bytes 1048608 | tf_op jit(solution)/shard_map/all_to_all | solution.py:37
  320.6 6.8 %feed_forward.1 = (bf16[128,4096]{1,0:T(8,128)(2,1)S(1)}, bf16[128,4096]{1,0:T(8,128)(2,1)S(1)}) custom-call(s32[16]{0:T(128)S(1)} %copy-done.32, bf16[32,128,128]{2,1,0:T(8,128)(2,1)S(1)} %bitcast.15, bf16[128,4096]{1,0:T(8,128)(2,1)S(1)} %copy-done.3, f32[1,4096]{1,0:T(1,128)S(1)} %bitcast.23, bf16[4,1040,256]{2,1,0:T(8,128)(2,1)} %bitcast.6.refs_0_, ...), custom_call_target="tpu_custom_call" | custom-call | tf_op jit(solution)/shard_map/feed_forward/pallas_call | solution.py:96
  328.4 16.8 %all_to_all.79 = bf16[4,32,4096]{2,1,0:T(8,128)(2,1)S(1)} all-to-all(bf16[4,32,4096]{2,1,0:T(8,128)(2,1)S(1)} %bitcast.21), channel_id=1, replica_groups=mesh['y'=4,'zh'=2,'core'=2,'zl'=8,'x'=4] {'x'}, dimensions={0} | all-to-all | bytes 2097152 | tf_op jit(solution)/shard_map/all_to_all | solution.py:626
  346.2 5.5 %all-to-all-start.14 = ((bf16[8,4,4096]{2,1,0:T(4,128)(2,1)}), bf16[8,4,4096]{2,1,0:T(4,128)(2,1)S(1)}, u32[]{:S(2)}, u32[]{:S(2)}) async-start(bf16[8,4,4096]{2,1,0:T(4,128)(2,1)} %reshape.56), calls=%async_computation.14 | async-start | bytes 524288 | tf_op jit(solution)/shard_map/all_to_all | solution.py:628
  351.7 14.3 %all-to-all-done.14 = bf16[8,4,4096]{2,1,0:T(4,128)(2,1)S(1)} async-done(((bf16[8,4,4096]{2,1,0:T(4,128)(2,1)}), bf16[8,4,4096]{2,1,0:T(4,128)(2,1)S(1)}, u32[]{:S(2)}, u32[]{:S(2)}) %all-to-all-start.14) | async-done | bytes 262176 | tf_op jit(solution)/shard_map/all_to_all | solution.py:628
  (155 shorter events, 53.5 us)
Async XLA Ops:
  11.7 19.8 %copy-start.43 = (s32[8]{0:T(128)S(1)}, s32[8]{0:T(128)}, u32[]{:S(2)}) copy-start(s32[8]{0:T(128)} %len_ref.1) | copy-start | bytes 100
  11.7 42.5 %all-to-all-start = ((bf16[4,256,512]{2,1,0:T(8,128)(2,1)}), bf16[4,256,512]{2,1,0:T(8,128)(2,1)S(1)}, u32[]{:S(2)}, u32[]{:S(2)}) async-start(bf16[4,256,512]{2,1,0:T(8,128)(2,1)} %broadcast_in_dim.33), calls=%async_computation | async-start | bytes 2097152 | tf_op jit(solution)/shard_map/all_to_all | solution.py:37
  16.3 37.9 %collective-permute-start = (bf16[256,512]{1,0:T(8,128)(2,1)S(1)}, bf16[256,512]{1,0:T(8,128)(2,1)S(1)}, u32[]{:S(2)}, u32[]{:S(2)}) collective-permute-start(bf16[256,512]{1,0:T(8,128)(2,1)S(1)} %join_weights.1), channel_id=1, source_target_pairs={{0,64},{64,0},{1,65},{65,1},{2,66},{66,2},{3,67},{67,3},{4,68},{68... | collective-permute-start | bytes 786440 | tf_op jit(solution)/shard_map/ppermute | solution.py:50
  35.7 45.1 %copy-start.31 = (s32[16]{0:T(128)}, s32[16]{0:T(128)S(1)}, u32[]{:S(2)}) copy-start(s32[16]{0:T(128)S(1)} %get-tuple-element.44.c_ref) | copy-start | bytes 196
  55.3 18.8 %all-to-all-start.1 = ((bf16[4,256,512]{2,1,0:T(8,128)(2,1)}), bf16[4,256,512]{2,1,0:T(8,128)(2,1)S(1)}, u32[]{:S(2)}, u32[]{:S(2)}) async-start(bf16[4,256,512]{2,1,0:T(8,128)(2,1)} %broadcast_in_dim.36), calls=%async_computation.1 | async-start | bytes 2097152 | tf_op jit(solution)/shard_map/all_to_all | solution.py:37
  60.0 73.7 %all-gather.7.cloned.1.call-start = ((), (), s32[]{:S(2)}) async-start(), calls=%async_computation.15 | async-start | bytes 2662400 | tf_op jit(solution)/shard_map/all_gather | solution.py:569
  74.1 4.6 %collective-permute-start.1 = (bf16[4,256,512]{2,1,0:T(8,128)(2,1)S(1)}, bf16[4,256,512]{2,1,0:T(8,128)(2,1)S(1)}, u32[]{:S(2)}, u32[]{:S(2)}) collective-permute-start(bf16[4,256,512]{2,1,0:T(8,128)(2,1)S(1)} %all-to-all-done.refs_0_), channel_id=1, source_target_pairs={{0,32},{32,0},{1,33},{33,1},{2,34},{34,2},{3,35},{35,3},{4,36},{36... | collective-permute-start | bytes 3145736 | tf_op jit(solution)/shard_map/ppermute | solution.py:50
  76.0 4.7 %collective-permute-start.2 = (bf16[4,256,512]{2,1,0:T(8,128)(2,1)S(1)}, bf16[4,256,512]{2,1,0:T(8,128)(2,1)S(1)}, u32[]{:S(2)}, u32[]{:S(2)}) collective-permute-start(bf16[4,256,512]{2,1,0:T(8,128)(2,1)S(1)} %all-to-all-done.1.refs_2_), channel_id=1, source_target_pairs={{0,32},{32,0},{1,33},{33,1},{2,34},{34,2},{3,35},{35,3},{4,36},{36... | collective-permute-start | bytes 3145736 | tf_op jit(solution)/shard_map/ppermute | solution.py:50
  82.3 26.1 %copy-start.34 = (f32[128]{0:T(128)S(1)}, f32[128]{0:T(128)}, u32[]{:S(2)}) copy-start(f32[128]{0:T(128)} %param.23) | copy-start | bytes 1540
  82.3 26.1 %copy-start.35 = (f32[128]{0:T(128)S(1)}, f32[128]{0:T(128)}, u32[]{:S(2)}) copy-start(f32[128]{0:T(128)} %param.24) | copy-start | bytes 1540
  111.2 32.1 %copy-start.6 = (bf16[1,1024,128]{2,1,0:T(8,128)(2,1)S(1)}, bf16[1,1024,128]{2,1,0:T(8,128)(2,1)}, u32[]{:S(2)}) copy-start(bf16[1,1024,128]{2,1,0:T(8,128)(2,1)} %k_ref.3) | copy-start | bytes 786436
  111.2 22.6 %all-to-all-start.3 = ((bf16[2,128,128]{2,1,0:T(8,128)(2,1)}), bf16[2,128,128]{2,1,0:T(8,128)(2,1)}, u32[]{:S(2)}, u32[]{:S(2)}) async-start(bf16[2,128,128]{2,1,0:T(8,128)(2,1)} %get-tuple-element.56.own_ref), calls=%async_computation.3 | async-start | bytes 131072 | tf_op jit(solution)/shard_map/all_to_all | solution.py:580
  133.7 31.6 %collective-permute-start.4 = (bf16[520,256]{1,0:T(8,128)(2,1)}, bf16[520,256]{1,0:T(8,128)(2,1)}, u32[]{:S(2)}, u32[]{:S(2)}) collective-permute-start(bf16[520,256]{1,0:T(8,128)(2,1)} %get-tuple-element.72), channel_id=1, source_target_pairs={{0,64},{64,0},{1,65},{65,1},{2,66},{66,2},{3,67},{67,3},{4,68},{68... | collective-permute-start | bytes 798728 | tf_op jit(solution)/shard_map/ppermute | solution.py:50
  137.2 10.8 %all-to-all-start.4 = ((bf16[4,2,128,128]{3,2,1,0:T(8,128)(2,1)}), bf16[4,2,128,128]{3,2,1,0:T(8,128)(2,1)}, u32[]{:S(2)}, u32[]{:S(2)}) async-start(bf16[4,2,128,128]{3,2,1,0:T(8,128)(2,1)} %broadcast_in_dim.39), calls=%async_computation.4 | async-start | bytes 524288 | tf_op jit(solution)/shard_map/all_to_all | solution.py:37
  141.3 12.9 %collective-permute-start.3 = (bf16[64,128]{1,0:T(8,128)(2,1)}, bf16[64,128]{1,0:T(8,128)(2,1)}, u32[]{:S(2)}, u32[]{:S(2)}) collective-permute-start(bf16[64,128]{1,0:T(8,128)(2,1)} %copy-done.29), channel_id=1, source_target_pairs={{0,32},{32,0},{1,33},{33,1},{2,34},{34,2},{3,35},{35,3},{4,36},{36... | collective-permute-start | bytes 49160 | tf_op jit(solution)/shard_map/ppermute | solution.py:50
  149.9 6.1 %all-to-all-start.5 = ((bf16[2,4,2,128,128]{4,3,2,1,0:T(8,128)(2,1)}), bf16[2,4,2,128,128]{4,3,2,1,0:T(8,128)(2,1)}, u32[]{:S(2)}, u32[]{:S(2)}) async-start(bf16[2,4,2,128,128]{4,3,2,1,0:T(8,128)(2,1)} %broadcast_in_dim.40), calls=%async_computation.5 | async-start | bytes 1048576 | tf_op jit(solution)/shard_map/all_to_all | solution.py:37
  154.1 123.9 %all-gather.9.cloned.1.call-start = ((), (), s32[]{:S(2)}) async-start(), calls=%async_computation.16 | async-start | bytes 1331200 | tf_op jit(solution)/shard_map/all_gather | solution.py:603
  210.3 38.3 %all-to-all-start.9 = ((bf16[4,8,128,128]{3,2,1,0:T(8,128)(2,1)}), bf16[4,8,128,128]{3,2,1,0:T(8,128)(2,1)S(1)}, u32[]{:S(2)}, u32[]{:S(2)}) async-start(bf16[4,8,128,128]{3,2,1,0:T(8,128)(2,1)} %bitcast.9), calls=%async_computation.9 | async-start | bytes 2097152 | tf_op jit(solution)/shard_map/all_to_all | solution.py:611
  213.9 34.7 %collective-permute-start.5 = (bf16[520,256]{1,0:T(8,128)(2,1)S(1)}, bf16[520,256]{1,0:T(8,128)(2,1)S(1)}, u32[]{:S(2)}, u32[]{:S(2)}) collective-permute-start(bf16[520,256]{1,0:T(8,128)(2,1)S(1)} %copy-done.45), channel_id=1, source_target_pairs={{0,64},{64,0},{1,65},{65,1},{2,66},{66,2},{3,67},{67,3},{4,68},{68... | collective-permute-start | bytes 798728 | tf_op jit(solution)/shard_map/ppermute | solution.py:50
  249.6 22.1 %all-to-all-start.10 = ((bf16[8,128,128]{2,1,0:T(8,128)(2,1)}), bf16[8,128,128]{2,1,0:T(8,128)(2,1)S(1)}, u32[]{:S(2)}, u32[]{:S(2)}) async-start(bf16[8,128,128]{2,1,0:T(8,128)(2,1)} %reduce_sum.54), calls=%async_computation.10 | async-start | bytes 524288 | tf_op jit(solution)/shard_map/all_to_all | solution.py:615
  255.4 32.4 %all-gather.11.cloned.1.call-start = ((), (), s32[]{:S(2)}) async-start(), calls=%async_computation.17 | async-start | bytes 1331200 | tf_op jit(solution)/shard_map/all_gather | solution.py:613
  256.1 48.0 %collective-permute-start.6 = (bf16[4,1040,256]{2,1,0:T(8,128)(2,1)}, bf16[4,1040,256]{2,1,0:T(8,128)(2,1)}, u32[]{:S(2)}, u32[]{:S(2)}) collective-permute-start(bf16[4,1040,256]{2,1,0:T(8,128)(2,1)} %bitcast.6.refs_0_), channel_id=1, source_target_pairs={{0,32},{32,0},{1,33},{33,1},{2,34},{34,2},{3,35},{35,3},{4,36},{36... | collective-permute-start | bytes 6389768 | tf_op jit(solution)/shard_map/ppermute | solution.py:50
  272.5 21.3 %all-to-all-start.11 = ((bf16[8,128,128]{2,1,0:T(8,128)(2,1)}), bf16[8,128,128]{2,1,0:T(8,128)(2,1)S(1)}, u32[]{:S(2)}, u32[]{:S(2)}) async-start(bf16[8,128,128]{2,1,0:T(8,128)(2,1)} %broadcast_in_dim.43), calls=%async_computation.11 | async-start | bytes 524288 | tf_op jit(solution)/shard_map/all_to_all | solution.py:37
  293.9 25.5 %collective-permute-start.7 = (bf16[4,520,256]{2,1,0:T(8,128)(2,1)}, bf16[4,520,256]{2,1,0:T(8,128)(2,1)}, u32[]{:S(2)}, u32[]{:S(2)}) collective-permute-start(bf16[4,520,256]{2,1,0:T(8,128)(2,1)} %bitcast.17), channel_id=1, source_target_pairs={{0,32},{32,0},{1,33},{33,1},{2,34},{34,2},{3,35},{35,3},{4,36},{36... | collective-permute-start | bytes 3194888 | tf_op jit(solution)/shard_map/ppermute | solution.py:50
  295.8 23.6 %collective-permute-start.8 = (bf16[4,520,256]{2,1,0:T(8,128)(2,1)}, bf16[4,520,256]{2,1,0:T(8,128)(2,1)}, u32[]{:S(2)}, u32[]{:S(2)}) collective-permute-start(bf16[4,520,256]{2,1,0:T(8,128)(2,1)} %bitcast.19), channel_id=1, source_target_pairs={{0,32},{32,0},{1,33},{33,1},{2,34},{34,2},{3,35},{35,3},{4,36},{36... | collective-permute-start | bytes 3194888 | tf_op jit(solution)/shard_map/ppermute | solution.py:50
  298.2 21.2 %copy-start.4 = (bf16[2080,256]{1,0:T(8,128)(2,1)S(1)}, bf16[2080,256]{1,0:T(8,128)(2,1)}, u32[]{:S(2)}) copy-start(bf16[2080,256]{1,0:T(8,128)(2,1)} %all-gather.9.cloned.1.call-done) | copy-start | bytes 3194884
  299.4 19.9 %copy-start.3 = (bf16[128,4096]{1,0:T(8,128)(2,1)S(1)}, bf16[128,4096]{1,0:T(8,128)(2,1)}, u32[]{:S(2)}) copy-start(bf16[128,4096]{1,0:T(8,128)(2,1)} %x_ref.3) | copy-start | bytes 3145732
  299.4 19.9 %copy-start.26 = (f32[4096]{0:T(1024)S(1)}, f32[4096]{0:T(1024)}, u32[]{:S(2)}) copy-start(f32[4096]{0:T(1024)} %param.25) | copy-start | bytes 49156
  299.4 20.0 %copy-start.32 = (s32[16]{0:T(128)S(1)}, s32[16]{0:T(128)}, u32[]{:S(2)}) copy-start(s32[16]{0:T(128)} %copy-done.31) | copy-start | bytes 196
  299.4 19.9 %all-to-all-start.12 = ((bf16[4,8,128,128]{3,2,1,0:T(8,128)(2,1)}), bf16[4,8,128,128]{3,2,1,0:T(8,128)(2,1)S(1)}, u32[]{:S(2)}, u32[]{:S(2)}) async-start(bf16[4,8,128,128]{3,2,1,0:T(8,128)(2,1)} %broadcast_in_dim.84), calls=%async_computation.12 | async-start | bytes 2097152 | tf_op jit(solution)/shard_map/all_to_all | solution.py:37
  345.2 21.4 %copy-start.49 = (f32[4096]{0:T(1024)S(1)}, f32[4096]{0:T(1024)}, u32[]{:S(2)}) copy-start(f32[4096]{0:T(1024)} %param.29) | copy-start | bytes 49156
  346.2 19.8 %all-to-all-start.14 = ((bf16[8,4,4096]{2,1,0:T(4,128)(2,1)}), bf16[8,4,4096]{2,1,0:T(4,128)(2,1)S(1)}, u32[]{:S(2)}, u32[]{:S(2)}) async-start(bf16[8,4,4096]{2,1,0:T(4,128)(2,1)} %reshape.56), calls=%async_computation.14 | async-start | bytes 524288 | tf_op jit(solution)/shard_map/all_to_all | solution.py:628
  (41 other events, 149.3 us)
Sparse Core Ops, SparseCore 0:
  74.2 37.8 all-gather.6
  165.5 30.5 all-gather.8
  258.3 29.4 all-gather.10

commit v10 on v8

--- a/solution.py
+++ b/solution.py
@@ -557,20 +557,18 @@
 
     near_other = swap(near, "core", NCORE)
     far = copies_to_all(theirs, "y", NY)
-    far, near_parcel = lax.optimization_barrier((far, parcel))
-    parcel_near = lax.all_gather(near_parcel, "y")
     far_other = swap(far, "core", NCORE)
+    parcel_near = lax.all_gather(parcel, "y")
     weights = [near, near_other, far, far_other]
     raw, squares = project(columns, hidden_states, weights, width, blocks)
     squares = lax.all_to_all(squares, BLK, 0, 0, tiled=True)
-    squares, parcel = lax.optimization_barrier((squares, parcel))
-    parcel_other = swap(parcel, "zh", NZH)
+    squares, parcel, parcel_near = lax.optimization_barrier((squares, parcel, parcel_near))
+    pair = lax.all_gather(parcel, "zh")
     query, key, value, new_mine = finish_rows(
         raw, squares, query_gain[None], key_gain[None], cosine, sine, model
     )
 
     queries = lax.all_to_all(query, "zh", 0, 0, tiled=True)
-    queries, parcel_near = lax.optimization_barrier((queries, parcel_near))
     queries = copies_to_all(queries, "y", NY)
     queries = copies_to_all(queries, "core", NCORE).reshape(N_SEQ, ROW_DEV, width)
     new_other = swap(new_mine, "core", NCORE)
@@ -595,8 +593,8 @@
     returned = copies_to_all(returned, "core", NCORE).reshape(N_SEQ, -1, width)
 
     terms = merge_and_project(merge_control, kept, new_part, returned, weights)
-    terms, parcel_other = lax.optimization_barrier((terms, parcel_other))
-    parcel_far = lax.all_gather(parcel_other, "y")
+    terms, pair = lax.optimization_barrier((terms, pair))
+    parcel_far = lax.all_gather(lax.dynamic_index_in_dim(pair, 1 - zh, 0, False), "y")
     terms = lax.all_to_all(terms.reshape(NX, NZL, ROW_DEV, width), "x", 0, 0, tiled=True)
     terms = jnp.sum(terms.astype(f32), axis=0).astype(bf16)
     terms = lax.all_to_all(terms, "zl", 0, 0, tiled=True)

time: 351 us -> 340 us (0.969)
  blocking collectives: 162 us -> 133 us
  waiting for transfers between devices: 81.8 us -> 90.4 us
  local copies, waits for them, and re-layouts: 13.1 us -> 20.4 us
    all_to_all x1, blocking collectives: 41.1 us -> 25.4 us  [shards(): returned = lax.all_to_all(returned, 'zh', 0, 0, tiled=True)]
    all_to_all x2 -> x1, blocking collectives: 16.6 us -> 4.44 us  [copies_to_all(): lax.all_to_all(jnp.broadcast_to(a[None], (count,) + a.shape), axis, 0, 0,...]
    all_to_all x6 -> x7, waiting for transfers between devices: 44.5 us -> 53.3 us  [copies_to_all(): lax.all_to_all(jnp.broadcast_to(a[None], (count,) + a.shape), axis, 0, 0,...]
    all_to_all x6 -> x7, starting transfers between devices: 25.1 us -> 30.2 us  [copies_to_all(): lax.all_to_all(jnp.broadcast_to(a[None], (count,) + a.shape), axis, 0, 0,...]
    unnamed x64 -> x84, local copies, waits for them, and re-layouts: 6.32 us -> 10 us
    ppermute x7 -> x6, starting transfers between devices: 26.8 us -> 24.4 us  [swap(): return lax.ppermute(a, axis, [(i, i ^ 1) for i in range(count)])]
    ppermute x7 -> x6, waiting for transfers between devices: 22.2 us -> 21.9 us  [swap(): return lax.ppermute(a, axis, [(i, i ^ 1) for i in range(count)])]
  transfers between devices with their start and end apart: 16 -> 17, of which waited for: 9 -> 9; matrix products, arithmetic and copies ran while one was open for 2% -> 3% of each run, Pallas kernels for 3% -> 3%
where the time goes in v10:
time: 340 us; the launch traced here: 338 us
  blocking collectives  133 us (39%)
  waiting for transfers between devices  90.4 us (27%)
  starting transfers between devices  60.1 us (18%)
  local copies, waits for them, and re-layouts  20.4 us (6%)
  Pallas kernels  16.4 us (5%)
  between operations  14.2 us (4%)
  other arithmetic  4.14 us (1%)
    all_to_all x7, waiting for transfers between devices, copies_to_all(): lax.all_to_all(jnp.broadcast_to(a[None], (count,) + a.shape), axis, 0, 0,...  53.3 us
    all_to_all x7, starting transfers between devices, copies_to_all(): lax.all_to_all(jnp.broadcast_to(a[None], (count,) + a.shape), axis, 0, 0,...  30.2 us
    all_to_all x1, blocking collectives, shards(): returned = lax.all_to_all(returned, 'zh', 0, 0, tiled=True)  25.4 us
    all_to_all x1, blocking collectives, shards(): squares = lax.all_to_all(squares, BLK, 0, 0, tiled=True)  24.5 us
    ppermute x6, starting transfers between devices, swap(): return lax.ppermute(a, axis, [(i, i ^ 1) for i in range(count)])  24.4 us
    all_to_all x1, blocking collectives, shards(): queries = lax.all_to_all(query, 'zh', 0, 0, tiled=True)  22.2 us
    ppermute x6, waiting for transfers between devices, swap(): return lax.ppermute(a, axis, [(i, i ^ 1) for i in range(count)])  21.9 us
    all_to_all x1, blocking collectives, shards(): terms = lax.all_to_all(terms, 'zl', 0, 0, tiled=True)  20.5 us
  transfers between devices with their start and end apart: 17, of which 9 were waited for; matrix products, arithmetic and copies ran while one was open for 3% of the time, Pallas kernels for 3%

profile of v10, /device:TPU:32, one launch (start us, length us, event | category | flops | bytes accessed | tf_op | source)
XLA Modules:
  0.0 338.4 jit_solution(16748852360471275218)
XLA Ops:
  7.3 2.0 fusion.4
  10.5 4.6 %all-to-all-start = ((bf16[4,256,512]{2,1,0:T(8,128)(2,1)}), bf16[4,256,512]{2,1,0:T(8,128)(2,1)S(1)}, u32[]{:S(2)}, u32[]{:S(2)}) async-start(bf16[4,256,512]{2,1,0:T(8,128)(2,1)} %broadcast_in_dim.33), calls=%async_computation | async-start | bytes 2097152 | tf_op jit(solution)/shard_map/all_to_all | solution.py:37
  15.1 14.8 %collective-permute-start = (bf16[256,512]{1,0:T(8,128)(2,1)S(1)}, bf16[256,512]{1,0:T(8,128)(2,1)S(1)}, u32[]{:S(2)}, u32[]{:S(2)}) collective-permute-start(bf16[256,512]{1,0:T(8,128)(2,1)S(1)} %join_weights.1), channel_id=1, source_target_pairs={{0,64},{64,0},{1,65},{65,1},{2,66},{66,2},{3,67},{67,3},{4,68},{68... | collective-permute-start | bytes 786440 | tf_op jit(solution)/shard_map/ppermute | solution.py:50
  33.7 19.3 %collective-permute-done = bf16[256,512]{1,0:T(8,128)(2,1)S(1)} collective-permute-done((bf16[256,512]{1,0:T(8,128)(2,1)S(1)}, bf16[256,512]{1,0:T(8,128)(2,1)S(1)}, u32[]{:S(2)}, u32[]{:S(2)}) %collective-permute-start) | collective-permute-done | bytes 262176 | tf_op jit(solution)/shard_map/ppermute | solution.py:50
  54.1 4.5 %all-to-all-start.1 = ((bf16[4,256,512]{2,1,0:T(8,128)(2,1)}), bf16[4,256,512]{2,1,0:T(8,128)(2,1)S(1)}, u32[]{:S(2)}, u32[]{:S(2)}) async-start(bf16[4,256,512]{2,1,0:T(8,128)(2,1)} %broadcast_in_dim.36), calls=%async_computation.1 | async-start | bytes 2097152 | tf_op jit(solution)/shard_map/all_to_all | solution.py:37
  58.6 1.9 collective-permute-start.1
  60.5 12.2 %all-to-all-done.1.refs_2_ = bf16[4,256,512]{2,1,0:T(8,128)(2,1)S(1)} async-done(((bf16[4,256,512]{2,1,0:T(8,128)(2,1)}), bf16[4,256,512]{2,1,0:T(8,128)(2,1)S(1)}, u32[]{:S(2)}, u32[]{:S(2)}) %all-to-all-start.1) | async-done | bytes 1048608 | tf_op jit(solution)/shard_map/all_to_all | solution.py:37
  72.7 1.9 collective-permute-start.2
  74.6 2.6 collective-permute-done.2.refs_3_
  80.2 24.5 %all_to_all.75.s_ref = f32[32,8,128]{2,1,0:T(8,128)S(1)} all-to-all(f32[32,8,128]{2,1,0:T(8,128)S(1)} %get-tuple-element.42), channel_id=1, replica_groups=mesh['y'=4,'zh'=2,'core'=2,'zl'=8,'x'=4] {'zl','x'}, dimensions={0} | all-to-all | bytes 262144 | tf_op jit(solution)/shard_map/all_to_all | solution.py:564
  105.1 22.2 %all_to_all.76 = bf16[2,128,128]{2,1,0:T(8,128)(2,1)S(1)} all-to-all(bf16[2,128,128]{2,1,0:T(8,128)(2,1)S(1)} %get-tuple-element.46.own_ref), channel_id=1, replica_groups=mesh['y'=4,'zh'=2,'core'=2,'zl'=8,'x'=4] {'zh'}, dimensions={0} | all-to-all | bytes 131072 | tf_op jit(solution)/shard_map/all_to_all | solution.py:571
  128.0 4.0 %all-to-all-start.4 = ((bf16[4,2,128,128]{3,2,1,0:T(8,128)(2,1)}), bf16[4,2,128,128]{3,2,1,0:T(8,128)(2,1)}, u32[]{:S(2)}, u32[]{:S(2)}) async-start(bf16[4,2,128,128]{3,2,1,0:T(8,128)(2,1)} %broadcast_in_dim.39), calls=%async_computation.4 | async-start | bytes 524288 | tf_op jit(solution)/shard_map/all_to_all | solution.py:37
  132.1 1.9 collective-permute-start.3
  135.9 2.9 all-to-all-done.4
  140.7 3.5 %all-to-all-start.5 = ((bf16[2,4,2,128,128]{4,3,2,1,0:T(8,128)(2,1)}), bf16[2,4,2,128,128]{4,3,2,1,0:T(8,128)(2,1)S(1)}, u32[]{:S(2)}, u32[]{:S(2)}) async-start(bf16[2,4,2,128,128]{4,3,2,1,0:T(8,128)(2,1)} %broadcast_in_dim.40), calls=%async_computation.5 | async-start | bytes 1048576 | tf_op jit(solution)/shard_map/all_to_all | solution.py:37
  148.6 3.4 %attend.1 = (bf16[2,176,128]{2,1,0:T(8,128)(2,1)S(1)}, f32[192,256]{1,0:T(8,128)S(1)}, f32[32,256]{1,0:T(8,128)S(1)}) custom-call(s32[5]{0:T(128)S(1)} %copy-done.36, bf16[16,128,128]{2,1,0:T(8,128)(2,1)S(1)} %bitcast.17, bf16[1,1024,128]{2,1,0:T(8,128)(2,1)S(1)} %copy-done.9, bf16[1,1024,128]{2,1,0:T(8,128)(2,1)S(1)} %copy-done.10, ...), custom_call_target="tpu_custom_call" | custom-call | tf_op jit(solution)/shard_map/attend/pallas_call | solution.py:96
  152.7 25.4 %all_to_all.77 = bf16[2,176,128]{2,1,0:T(8,128)(2,1)S(1)} all-to-all(bf16[2,176,128]{2,1,0:T(8,128)(2,1)S(1)} %get-tuple-element.58), channel_id=1, replica_groups=mesh['y'=4,'zh'=2,'core'=2,'zl'=8,'x'=4] {'zh'}, dimensions={0} | all-to-all | bytes 180224 | tf_op jit(solution)/shard_map/all_to_all | solution.py:591
  178.9 4.4 %all-to-all-start.7 = ((bf16[4,2,176,128]{3,2,1,0:T(8,128)(2,1)}), bf16[4,2,176,128]{3,2,1,0:T(8,128)(2,1)S(1)}, u32[]{:S(2)}, u32[]{:S(2)}) async-start(bf16[4,2,176,128]{3,2,1,0:T(8,128)(2,1)} %broadcast_in_dim.41), calls=%async_computation.7 | async-start | bytes 720896 | tf_op jit(solution)/shard_map/all_to_all | solution.py:37
  183.3 7.2 %all-to-all-done.7 = bf16[4,2,176,128]{3,2,1,0:T(8,128)(2,1)S(1)} async-done(((bf16[4,2,176,128]{3,2,1,0:T(8,128)(2,1)}), bf16[4,2,176,128]{3,2,1,0:T(8,128)(2,1)S(1)}, u32[]{:S(2)}, u32[]{:S(2)}) %all-to-all-start.7) | async-done | bytes 360480 | tf_op jit(solution)/shard_map/all_to_all | solution.py:37
  190.6 4.4 %all_to_all.78 = bf16[2,4,2,176,128]{4,3,2,1,0:T(8,128)(2,1)S(1)} all-to-all(bf16[2,4,2,176,128]{4,3,2,1,0:T(8,128)(2,1)S(1)} %broadcast_in_dim.42), channel_id=1, replica_groups=mesh['y'=4,'zh'=2,'core'=2,'zl'=8,'x'=4] {'core'}, dimensions={0} | all-to-all | bytes 1441792 | tf_op jit(solution)/shard_map/all_to_all | solution.py:37
  199.1 18.1 %all_to_all.79 = bf16[4,8,128,128]{3,2,1,0:T(8,128)(2,1)S(1)} all-to-all(bf16[4,8,128,128]{3,2,1,0:T(8,128)(2,1)S(1)} %bitcast.14), channel_id=1, replica_groups=mesh['y'=4,'zh'=2,'core'=2,'zl'=8,'x'=4] {'x'}, dimensions={0} | all-to-all | bytes 2097152 | tf_op jit(solution)/shard_map/all_to_all | solution.py:598
  217.5 20.5 %all_to_all.80 = bf16[8,128,128]{2,1,0:T(8,128)(2,1)S(1)} all-to-all(bf16[8,128,128]{2,1,0:T(8,128)(2,1)S(1)} %reduce_sum.54), channel_id=1, replica_groups=mesh['y'=4,'zh'=2,'core'=2,'zl'=8,'x'=4] {'zl'}, dimensions={0} | all-to-all | bytes 524288 | tf_op jit(solution)/shard_map/all_to_all | solution.py:600
  238.8 5.5 %all-to-all-start.11 = ((bf16[8,128,128]{2,1,0:T(8,128)(2,1)}), bf16[8,128,128]{2,1,0:T(8,128)(2,1)S(1)}, u32[]{:S(2)}, u32[]{:S(2)}) async-start(bf16[8,128,128]{2,1,0:T(8,128)(2,1)} %broadcast_in_dim.43), calls=%async_computation.11 | async-start | bytes 524288 | tf_op jit(solution)/shard_map/all_to_all | solution.py:37
  244.3 1.9 collective-permute-start.4
  246.2 13.9 %all-to-all-done.11 = bf16[8,128,128]{2,1,0:T(8,128)(2,1)S(1)} async-done(((bf16[8,128,128]{2,1,0:T(8,128)(2,1)}), bf16[8,128,128]{2,1,0:T(8,128)(2,1)S(1)}, u32[]{:S(2)}, u32[]{:S(2)}) %all-to-all-start.11) | async-done | bytes 262176 | tf_op jit(solution)/shard_map/all_to_all | solution.py:37
  260.1 1.9 collective-permute-start.5
  263.2 3.6 %all-to-all-start.12 = ((bf16[4,8,128,128]{3,2,1,0:T(8,128)(2,1)}), bf16[4,8,128,128]{3,2,1,0:T(8,128)(2,1)S(1)}, u32[]{:S(2)}, u32[]{:S(2)}) async-start(bf16[4,8,128,128]{3,2,1,0:T(8,128)(2,1)} %broadcast_in_dim.84), calls=%async_computation.12 | async-start | bytes 2097152 | tf_op jit(solution)/shard_map/all_to_all | solution.py:37
  266.9 16.0 %all-to-all-done.12 = bf16[4,8,128,128]{3,2,1,0:T(8,128)(2,1)S(1)} async-done(((bf16[4,8,128,128]{3,2,1,0:T(8,128)(2,1)}), bf16[4,8,128,128]{3,2,1,0:T(8,128)(2,1)S(1)}, u32[]{:S(2)}, u32[]{:S(2)}) %all-to-all-start.12) | async-done | bytes 1048608 | tf_op jit(solution)/shard_map/all_to_all | solution.py:37
  284.5 6.9 %feed_forward.1 = (bf16[128,4096]{1,0:T(8,128)(2,1)S(1)}, bf16[128,4096]{1,0:T(8,128)(2,1)S(1)}) custom-call(s32[16]{0:T(128)S(1)} %copy-done.28, bf16[32,128,128]{2,1,0:T(8,128)(2,1)S(1)} %bitcast.15, bf16[128,4096]{1,0:T(8,128)(2,1)S(1)} %copy-done.5, f32[1,4096]{1,0:T(1,128)S(1)} %bitcast.20, bf16[4,1040,256]{2,1,0:T(8,128)(2,1)} %bitcast.4.refs_0_, ...), custom_call_target="tpu_custom_call" | custom-call | tf_op jit(solution)/shard_map/feed_forward/pallas_call | solution.py:96
  291.4 17.7 %all_to_all.81 = bf16[4,32,4096]{2,1,0:T(8,128)(2,1)S(1)} all-to-all(bf16[4,32,4096]{2,1,0:T(8,128)(2,1)S(1)} %bitcast.18), channel_id=1, replica_groups=mesh['y'=4,'zh'=2,'core'=2,'zl'=8,'x'=4] {'x'}, dimensions={0} | all-to-all | bytes 2097152 | tf_op jit(solution)/shard_map/all_to_all | solution.py:611
  310.1 5.5 %all-to-all-start.14 = ((bf16[8,4,4096]{2,1,0:T(4,128)(2,1)}), bf16[8,4,4096]{2,1,0:T(4,128)(2,1)S(1)}, u32[]{:S(2)}, u32[]{:S(2)}) async-start(bf16[8,4,4096]{2,1,0:T(4,128)(2,1)} %reshape.56), calls=%async_computation.14 | async-start | bytes 524288 | tf_op jit(solution)/shard_map/all_to_all | solution.py:613
  315.6 15.1 %all-to-all-done.14 = bf16[8,4,4096]{2,1,0:T(4,128)(2,1)S(1)} async-done(((bf16[8,4,4096]{2,1,0:T(4,128)(2,1)}), bf16[8,4,4096]{2,1,0:T(4,128)(2,1)S(1)}, u32[]{:S(2)}, u32[]{:S(2)}) %all-to-all-start.14) | async-done | bytes 262176 | tf_op jit(solution)/shard_map/all_to_all | solution.py:613
  (127 shorter events, 29.9 us)
Async XLA Ops:
  7.2 97.5 %all-gather.8.cloned.1.call-start = ((), (), s32[]{:S(2)}) async-start(), calls=%async_computation.16 | async-start | bytes 2662400 | tf_op jit(solution)/shard_map/all_gather | solution.py:561
  10.5 19.7 %copy-start.21 = (s32[16,96]{1,0:T(8,128)S(1)}, s32[16,96]{1,0:T(8,128)}, u32[]{:S(2)}) copy-start(s32[16,96]{1,0:T(8,128)} %i_ref.1) | copy-start | bytes 18436
  10.5 19.8 %copy-start.37 = (s32[16]{0:T(128)S(1)}, s32[16]{0:T(128)}, u32[]{:S(2)}) copy-start(s32[16]{0:T(128)} %o_ref.2) | copy-start | bytes 196
  10.5 19.8 %copy-start.38 = (s32[8]{0:T(128)S(1)}, s32[8]{0:T(128)}, u32[]{:S(2)}) copy-start(s32[8]{0:T(128)} %len_ref.1) | copy-start | bytes 100
  10.5 42.5 %all-to-all-start = ((bf16[4,256,512]{2,1,0:T(8,128)(2,1)}), bf16[4,256,512]{2,1,0:T(8,128)(2,1)S(1)}, u32[]{:S(2)}, u32[]{:S(2)}) async-start(bf16[4,256,512]{2,1,0:T(8,128)(2,1)} %broadcast_in_dim.33), calls=%async_computation | async-start | bytes 2097152 | tf_op jit(solution)/shard_map/all_to_all | solution.py:37
  15.1 37.9 %collective-permute-start = (bf16[256,512]{1,0:T(8,128)(2,1)S(1)}, bf16[256,512]{1,0:T(8,128)(2,1)S(1)}, u32[]{:S(2)}, u32[]{:S(2)}) collective-permute-start(bf16[256,512]{1,0:T(8,128)(2,1)S(1)} %join_weights.1), channel_id=1, source_target_pairs={{0,64},{64,0},{1,65},{65,1},{2,66},{66,2},{3,67},{67,3},{4,68},{68... | collective-permute-start | bytes 786440 | tf_op jit(solution)/shard_map/ppermute | solution.py:50
  33.2 20.8 %copy-start.35 = (s32[5]{0:T(128)}, s32[5]{0:T(128)S(1)}, u32[]{:S(2)}) copy-start(s32[5]{0:T(128)S(1)} %get-tuple-element.37.c_ref) | copy-start | bytes 64
  33.2 44.0 %copy-start.27 = (s32[16]{0:T(128)}, s32[16]{0:T(128)S(1)}, u32[]{:S(2)}) copy-start(s32[16]{0:T(128)S(1)} %get-tuple-element.35.c_ref) | copy-start | bytes 196
  54.1 18.6 %all-to-all-start.1 = ((bf16[4,256,512]{2,1,0:T(8,128)(2,1)}), bf16[4,256,512]{2,1,0:T(8,128)(2,1)S(1)}, u32[]{:S(2)}, u32[]{:S(2)}) async-start(bf16[4,256,512]{2,1,0:T(8,128)(2,1)} %broadcast_in_dim.36), calls=%async_computation.1 | async-start | bytes 2097152 | tf_op jit(solution)/shard_map/all_to_all | solution.py:37
  58.6 138.7 %all-gather.10.cloned.1.call-start = ((), (), s32[]{:S(2)}) async-start(), calls=%async_computation.17 | async-start | bytes 1597440 | tf_op jit(solution)/shard_map/all_gather | solution.py:566
  58.6 16.0 %collective-permute-start.1 = (bf16[4,256,512]{2,1,0:T(8,128)(2,1)S(1)}, bf16[4,256,512]{2,1,0:T(8,128)(2,1)S(1)}, u32[]{:S(2)}, u32[]{:S(2)}) collective-permute-start(bf16[4,256,512]{2,1,0:T(8,128)(2,1)S(1)} %all-to-all-done.refs_0_), channel_id=1, source_target_pairs={{0,32},{32,0},{1,33},{33,1},{2,34},{34,2},{3,35},{35,3},{4,36},{36... | collective-permute-start | bytes 3145736 | tf_op jit(solution)/shard_map/ppermute | solution.py:50
  72.7 4.5 %collective-permute-start.2 = (bf16[4,256,512]{2,1,0:T(8,128)(2,1)S(1)}, bf16[4,256,512]{2,1,0:T(8,128)(2,1)S(1)}, u32[]{:S(2)}, u32[]{:S(2)}) collective-permute-start(bf16[4,256,512]{2,1,0:T(8,128)(2,1)S(1)} %all-to-all-done.1.refs_2_), channel_id=1, source_target_pairs={{0,32},{32,0},{1,33},{33,1},{2,34},{34,2},{3,35},{35,3},{4,36},{36... | collective-permute-start | bytes 3145736 | tf_op jit(solution)/shard_map/ppermute | solution.py:50
  78.8 25.9 %copy-start.29 = (f32[128]{0:T(128)S(1)}, f32[128]{0:T(128)}, u32[]{:S(2)}) copy-start(f32[128]{0:T(128)} %param.23) | copy-start | bytes 1540
  78.8 25.9 %copy-start.30 = (f32[128]{0:T(128)S(1)}, f32[128]{0:T(128)}, u32[]{:S(2)}) copy-start(f32[128]{0:T(128)} %param.24) | copy-start | bytes 1540
  104.7 29.3 %copy-start.7 = (bf16[1,1024,128]{2,1,0:T(8,128)(2,1)S(1)}, bf16[1,1024,128]{2,1,0:T(8,128)(2,1)}, u32[]{:S(2)}) copy-start(bf16[1,1024,128]{2,1,0:T(8,128)(2,1)} %k_ref.3) | copy-start | bytes 786436
  104.7 29.3 %copy-start.8 = (bf16[1,1024,128]{2,1,0:T(8,128)(2,1)S(1)}, bf16[1,1024,128]{2,1,0:T(8,128)(2,1)}, u32[]{:S(2)}) copy-start(bf16[1,1024,128]{2,1,0:T(8,128)(2,1)} %v_ref.3) | copy-start | bytes 786436
  105.1 35.6 %copy-start.23 = (bf16[64,128]{1,0:T(8,128)(2,1)}, bf16[64,128]{1,0:T(8,128)(2,1)S(1)}, u32[]{:S(2)}) copy-start(bf16[64,128]{1,0:T(8,128)(2,1)S(1)} %get-tuple-element.53.nm_ref) | copy-start | bytes 49156
  128.0 10.8 %all-to-all-start.4 = ((bf16[4,2,128,128]{3,2,1,0:T(8,128)(2,1)}), bf16[4,2,128,128]{3,2,1,0:T(8,128)(2,1)}, u32[]{:S(2)}, u32[]{:S(2)}) async-start(bf16[4,2,128,128]{3,2,1,0:T(8,128)(2,1)} %broadcast_in_dim.39), calls=%async_computation.4 | async-start | bytes 524288 | tf_op jit(solution)/shard_map/all_to_all | solution.py:37
  132.1 12.1 %collective-permute-start.3 = (bf16[64,128]{1,0:T(8,128)(2,1)S(1)}, bf16[64,128]{1,0:T(8,128)(2,1)S(1)}, u32[]{:S(2)}, u32[]{:S(2)}) collective-permute-start(bf16[64,128]{1,0:T(8,128)(2,1)S(1)} %get-tuple-element.53.nm_ref), channel_id=1, source_target_pairs={{0,32},{32,0},{1,33},{33,1},{2,34},{34,2},{3,35},{35,3},{4,36},{36... | collective-permute-start | bytes 49160 | tf_op jit(solution)/shard_map/ppermute | solution.py:50
  140.7 5.2 %all-to-all-start.5 = ((bf16[2,4,2,128,128]{4,3,2,1,0:T(8,128)(2,1)}), bf16[2,4,2,128,128]{4,3,2,1,0:T(8,128)(2,1)S(1)}, u32[]{:S(2)}, u32[]{:S(2)}) async-start(bf16[2,4,2,128,128]{4,3,2,1,0:T(8,128)(2,1)} %broadcast_in_dim.40), calls=%async_computation.5 | async-start | bytes 1048576 | tf_op jit(solution)/shard_map/all_to_all | solution.py:37
  152.7 37.9 %copy-start.11 = (f32[192,256]{1,0:T(8,128)}, f32[192,256]{1,0:T(8,128)S(1)}, u32[]{:S(2)}) copy-start(f32[192,256]{1,0:T(8,128)S(1)} %get-tuple-element.56.kept_ref) | copy-start | bytes 589828
  178.9 11.6 %all-to-all-start.7 = ((bf16[4,2,176,128]{3,2,1,0:T(8,128)(2,1)}), bf16[4,2,176,128]{3,2,1,0:T(8,128)(2,1)S(1)}, u32[]{:S(2)}, u32[]{:S(2)}) async-start(bf16[4,2,176,128]{3,2,1,0:T(8,128)(2,1)} %broadcast_in_dim.41), calls=%async_computation.7 | async-start | bytes 720896 | tf_op jit(solution)/shard_map/all_to_all | solution.py:37
  183.3 76.8 %all-gather.6.cloned.1.call-start = ((), (), s32[]{:S(2)}) async-start(), calls=%async_computation.15 | async-start | bytes 2662400 | tf_op jit(solution)/shard_map/all_gather | solution.py:597
  238.8 21.3 %all-to-all-start.11 = ((bf16[8,128,128]{2,1,0:T(8,128)(2,1)}), bf16[8,128,128]{2,1,0:T(8,128)(2,1)S(1)}, u32[]{:S(2)}, u32[]{:S(2)}) async-start(bf16[8,128,128]{2,1,0:T(8,128)(2,1)} %broadcast_in_dim.43), calls=%async_computation.11 | async-start | bytes 524288 | tf_op jit(solution)/shard_map/all_to_all | solution.py:37
  244.3 22.6 %collective-permute-start.4 = (bf16[4,1040,256]{2,1,0:T(8,128)(2,1)}, bf16[4,1040,256]{2,1,0:T(8,128)(2,1)}, u32[]{:S(2)}, u32[]{:S(2)}) collective-permute-start(bf16[4,1040,256]{2,1,0:T(8,128)(2,1)} %bitcast.4.refs_0_), channel_id=1, source_target_pairs={{0,32},{32,0},{1,33},{33,1},{2,34},{34,2},{3,35},{35,3},{4,36},{36... | collective-permute-start | bytes 6389768 | tf_op jit(solution)/shard_map/ppermute | solution.py:50
  260.1 22.8 %collective-permute-start.5 = (bf16[4,1040,256]{2,1,0:T(8,128)(2,1)}, bf16[4,1040,256]{2,1,0:T(8,128)(2,1)}, u32[]{:S(2)}, u32[]{:S(2)}) collective-permute-start(bf16[4,1040,256]{2,1,0:T(8,128)(2,1)} %all-gather.6.cloned.1.call-done.refs_2_), channel_id=1, source_target_pairs={{0,32},{32,0},{1,33},{33,1},{2,34},{34,2},{3,35},{35,3},{4,36},{36... | collective-permute-start | bytes 6389768 | tf_op jit(solution)/shard_map/ppermute | solution.py:50
  263.2 19.7 %copy-start.5 = (bf16[128,4096]{1,0:T(8,128)(2,1)S(1)}, bf16[128,4096]{1,0:T(8,128)(2,1)}, u32[]{:S(2)}) copy-start(bf16[128,4096]{1,0:T(8,128)(2,1)} %x_ref.3) | copy-start | bytes 3145732
  263.2 19.7 %copy-start.22 = (f32[4096]{0:T(1024)S(1)}, f32[4096]{0:T(1024)}, u32[]{:S(2)}) copy-start(f32[4096]{0:T(1024)} %param.25) | copy-start | bytes 49156
  263.2 19.7 %copy-start.28 = (s32[16]{0:T(128)S(1)}, s32[16]{0:T(128)}, u32[]{:S(2)}) copy-start(s32[16]{0:T(128)} %copy-done.27) | copy-start | bytes 196
  263.2 19.7 %all-to-all-start.12 = ((bf16[4,8,128,128]{3,2,1,0:T(8,128)(2,1)}), bf16[4,8,128,128]{3,2,1,0:T(8,128)(2,1)S(1)}, u32[]{:S(2)}, u32[]{:S(2)}) async-start(bf16[4,8,128,128]{3,2,1,0:T(8,128)(2,1)} %broadcast_in_dim.84), calls=%async_computation.12 | async-start | bytes 2097152 | tf_op jit(solution)/shard_map/all_to_all | solution.py:37
  309.1 22.1 %copy-start.39 = (f32[4096]{0:T(1024)S(1)}, f32[4096]{0:T(1024)}, u32[]{:S(2)}) copy-start(f32[4096]{0:T(1024)} %param.29) | copy-start | bytes 49156
  310.1 20.5 %all-to-all-start.14 = ((bf16[8,4,4096]{2,1,0:T(4,128)(2,1)}), bf16[8,4,4096]{2,1,0:T(4,128)(2,1)S(1)}, u32[]{:S(2)}, u32[]{:S(2)}) async-start(bf16[8,4,4096]{2,1,0:T(4,128)(2,1)} %reshape.56), calls=%async_computation.14 | async-start | bytes 524288 | tf_op jit(solution)/shard_map/all_to_all | solution.py:613
  (26 other events, 108.9 us)
Sparse Core Ops, SparseCore 0:
  10.1 42.9 all-gather.7
  104.9 57.3 all-gather.9
  199.3 32.0 all-gather.5
